TPU v7x, 32 devices: a whole 2x2x4 slice. The times are simulated.
32 devices in a mesh: pb: 8 (over z, y), ka: 4 (over x, core).
Axes of the slice: x: 2, y: 2, z: 4, core: 2. Of those that a mesh axis runs over, the one named last changes fastest.
Arguments:
- queries: bfloat16 [1, 4096, 4096], P(None, 'pb', 'ka'), may hold values from -12 to 12
- keys: bfloat16 [4096, 512], P('ka'), may hold values from -8 to 8
- values: bfloat16 [4096, 512], P('ka'), may hold values from -18 to 18
- block_ids: int32 [1, 8, 16], P(None, 'pb'), may hold values from 0 to 32, as said below
- counts: int32 [1, 8], P(None, 'pb'), may hold values from 1 to 16, as said below
- refresh: int32 [1, 8], P(None, 'pb'), may hold values 0 or 1
- cached_attn: bfloat16 [1, 4096, 4096], P(None, 'pb', 'ka'), may hold values from -3 to 3
- wo: bfloat16 [4096, 8192], P('pb', 'ka'), may hold values from -0.09375 to 0.09375
Outputs:
- mixed: bfloat16 [1, 4096, 8192], P(None, 'pb', 'ka')
Inputs may be any that keep to these rules, and one draw needn't show every extreme that they name: `block_ids`: row (r, p) lists counts[r, p] distinct key-block numbers in ascending order in its first slots; the other slots hold 32. `counts`: some query block has exactly 16 active key blocks and some has exactly one.
All inputs are finite; a program needn't handle non-finite values. No bound on the sum of `refresh` on one device may be relied on, other than what follows from the above.
Results may differ from a plain program's by a relative error of at most 0.014.
Values may be sent and summed in bfloat16 or wider, within the bound.
No kernel may reach another device: no remote copies, remote signals or barrier semaphores. Data moves between devices by JAX's collectives and lax.ppermute only.
A program may use at most 128 MiB of HBM per device.

v0:
```python
import functools
import math

import jax
import jax.numpy as jnp
from jax import lax
from jax.experimental import pallas as pl
from jax.experimental.pallas import tpu as pltpu
from jax.sharding import PartitionSpec as P

HEAD_SIZE = 128
QUERY_HEAD_COUNT = 32
KEY_VALUE_HEADS = 4
QUERY_BLOCK_SIZE = 512
KEY_BLOCK_TOKENS = 128
RATIO = QUERY_HEAD_COUNT // KEY_VALUE_HEADS
LOWEST = -1e30
EXP2_SCALE = math.log2(math.e) / math.sqrt(HEAD_SIZE)


def attention_kernel(heads, meta_ref, q_ref, kv_ref, old_ref, out_ref, peak_ref, denom_ref, acc_ref):
    live = meta_ref[0]
    flag = meta_ref[1]

    @pl.when(flag <= 0)
    def _():
        out_ref[...] = old_ref[...]

    @pl.when(flag > 0)
    def _():
        peak_ref[...] = jnp.full_like(peak_ref, LOWEST)
        denom_ref[...] = jnp.zeros_like(denom_ref)
        acc_ref[...] = jnp.zeros_like(acc_ref)

        def pair(step, carry):
            second = 2 * step + 1 < live
            first_row = pl.multiple_of(meta_ref[2 + 2 * step] * KEY_BLOCK_TOKENS, KEY_BLOCK_TOKENS)
            second_block = jnp.where(
                second, meta_ref[jnp.minimum(3 + 2 * step, meta_ref.shape[0] - 1)], 0
            )
            second_row = pl.multiple_of(second_block * KEY_BLOCK_TOKENS, KEY_BLOCK_TOKENS)
            bias = jnp.where(second, 0.0, LOWEST).astype(jnp.float32)
            tile = jnp.concatenate(
                [
                    kv_ref[pl.ds(first_row, KEY_BLOCK_TOKENS), :],
                    kv_ref[pl.ds(second_row, KEY_BLOCK_TOKENS), :],
                ],
                axis=0,
            )
            key_tile = tile[:, :HEAD_SIZE]
            value_tile = tile[:, HEAD_SIZE:]
            for head in range(heads):
                query = q_ref[:, head * HEAD_SIZE : (head + 1) * HEAD_SIZE]
                scores = lax.dot_general(
                    key_tile, query, (((1,), (1,)), ((), ())), preferred_element_type=jnp.float32
                )
                upper = scores[:KEY_BLOCK_TOKENS]
                lower = scores[KEY_BLOCK_TOKENS:] + bias
                old_peak = peak_ref[head]
                peak = jnp.maximum(
                    old_peak, jnp.max(jnp.maximum(upper, lower), axis=0, keepdims=True)
                )
                decay = jnp.exp2((old_peak - peak) * EXP2_SCALE)
                upper = jnp.exp2((upper - peak) * EXP2_SCALE)
                lower = jnp.exp2((lower - peak) * EXP2_SCALE)
                peak_ref[head] = peak
                denom_ref[head] = denom_ref[head] * decay + jnp.sum(
                    upper + lower, axis=0, keepdims=True
                )
                weights = jnp.concatenate(
                    [upper.astype(jnp.bfloat16), lower.astype(jnp.bfloat16)], axis=0
                )
                update = lax.dot_general(
                    value_tile, weights, (((0,), (0,)), ((), ())), preferred_element_type=jnp.float32
                )
                acc_ref[head] = acc_ref[head] * decay + update
            return carry

        lax.fori_loop(0, (live + 1) // 2, pair, 0)
        for head in range(heads):
            result = acc_ref[head] / denom_ref[head]
            out_ref[:, head * HEAD_SIZE : (head + 1) * HEAD_SIZE] = result.T.astype(jnp.bfloat16)


def attend(meta, queries, kv, old):
    rows, width = queries.shape
    heads = width // HEAD_SIZE
    whole = pl.BlockSpec(memory_space=pltpu.VMEM)
    return pl.pallas_call(
        functools.partial(attention_kernel, heads),
        out_shape=jax.ShapeDtypeStruct((rows, width), jnp.bfloat16),
        in_specs=[pl.BlockSpec(memory_space=pltpu.SMEM), whole, whole, whole],
        out_specs=whole,
        scratch_shapes=[
            pltpu.VMEM((heads, 1, rows), jnp.float32),
            pltpu.VMEM((heads, 1, rows), jnp.float32),
            pltpu.VMEM((heads, HEAD_SIZE, rows), jnp.float32),
        ],
        compiler_params=pltpu.CompilerParams(vmem_limit_bytes=40 << 20),
        cost_estimate=pl.CostEstimate(
            flops=4 * rows * width * 16 * KEY_BLOCK_TOKENS,
            transcendentals=rows * heads * 16 * KEY_BLOCK_TOKENS,
            bytes_accessed=2 * (3 * rows * width + kv.size),
        ),
        name="attend",
    )(meta, queries, kv, old)


def own_head_keys_values(keys, values, groups):
    rows = keys.shape[0]
    both = jnp.concatenate(
        [
            keys.reshape(rows, KEY_VALUE_HEADS, HEAD_SIZE),
            values.reshape(rows, KEY_VALUE_HEADS, HEAD_SIZE),
        ],
        axis=2,
    )
    both = jnp.repeat(both, groups // KEY_VALUE_HEADS, axis=1)
    return lax.all_to_all(
        both.reshape(rows, groups * 2 * HEAD_SIZE), "ka", split_axis=1, concat_axis=0, tiled=True
    )


def ring_of(pb_size):
    if pb_size == 8:
        return [0, 2, 4, 6, 7, 5, 3, 1]
    return list(range(pb_size))


def project_ring(attn, wo):
    pb_size = lax.axis_size("pb")
    depth, columns = wo.shape
    ring = ring_of(pb_size)
    place_of = [ring.index(p) for p in range(pb_size)]
    forward = [(ring[i], ring[(i + 1) % pb_size]) for i in range(pb_size)]
    backward = [(b, a) for a, b in forward]
    here = jnp.asarray(place_of, jnp.int32)[lax.axis_index("pb")]
    order = jnp.asarray(ring, jnp.int32)
    half = columns // 2
    far = pb_size // 2
    slabs = [[(0, wo[:, :half])], [(0, wo[:, half:])]]
    moving = [[slabs[0][0][1]] * 2, [slabs[1][0][1]] * 2]
    for hop in range(1, far + 1):
        for part in range(2):
            if hop < far or part == 0:
                moving[part][0] = lax.ppermute(moving[part][0], "pb", forward)
                slabs[part].append((-hop, moving[part][0]))
            if hop < far or part == 1:
                moving[part][1] = lax.ppermute(moving[part][1], "pb", backward)
                slabs[part].append((hop, moving[part][1]))
    attn_blocks = attn
    results = []
    for part in range(2):
        total = None
        for offset, slab in slabs[part]:
            source = order[(here + offset + pb_size) % pb_size]
            left = attn_blocks(source)
            term = jnp.dot(left, slab, preferred_element_type=jnp.float32)
            total = term if total is None else total + term
        results.append(total.astype(jnp.bfloat16))
    return jnp.concatenate(results, axis=1)


def shards(queries, keys, values, block_ids, counts, refresh, cached_attn, wo):
    groups = lax.axis_size("ka")
    pb_size = lax.axis_size("pb")
    me = lax.axis_index("ka")
    width = QUERY_HEAD_COUNT * HEAD_SIZE
    depth = wo.shape[0]
    kv = own_head_keys_values(keys, values, groups)
    meta = jnp.concatenate([counts[0], refresh[0], block_ids[0, 0]])
    attn = attend(meta, queries[0], kv, cached_attn[0])
    if pb_size == 8 and groups == 4:
        across = lax.ppermute(attn, "ka", [(i, i ^ 2) for i in range(4)])
        beside = lax.ppermute(attn, "ka", [(i, i ^ 1) for i in range(4)])
        corner = lax.ppermute(across, "ka", [(i, i ^ 1) for i in range(4)])
        pieces = jnp.stack([attn, beside, across, corner])
        per = attn.shape[1] // depth

        def block(source):
            slot = jnp.bitwise_xor(source // per, me)
            return lax.dynamic_slice(
                pieces, (slot, 0, (source % per) * depth), (1, attn.shape[0], depth)
            )[0]

        mixed = project_ring(block, wo)
    else:
        attn_full = lax.all_gather(attn, "ka", axis=1, tiled=True)
        mixed = jnp.dot(
            attn_full, lax.all_gather(wo, "pb", axis=0, tiled=True), preferred_element_type=jnp.float32
        ).astype(jnp.bfloat16)
    return mixed[None]


def solution(mesh):
    placed = (
        P(None, "pb", "ka"),
        P("ka", None),
        P("ka", None),
        P(None, "pb", None),
        P(None, "pb"),
        P(None, "pb"),
        P(None, "pb", "ka"),
        P("pb", "ka"),
    )
    return jax.shard_map(
        shards, mesh=mesh, in_specs=placed, out_specs=P(None, "pb", "ka"), check_vma=False
    )
```

profile of v0, /device:TPU:0, one launch (start us, length us, event | category | flops | bytes accessed | tf_op | source)
XLA Modules:
  0.0 191.4 jit_solution(8581926883161246718)
XLA Ops:
  1.2 1.6 copy_bitcast_fusion
  2.9 1.5 pad_maximum_fusion.1
  4.4 4.2 %all-to-all-start = ((bf16[1024,4,256]{2,0,1:T(8,128)(2,1)}), bf16[1024,4,256]{2,0,1:T(8,128)(2,1)S(1)}, u32[]{:S(2)}, u32[]{:S(2)}) async-start(bf16[1024,4,256]{2,0,1:T(8,128)(2,1)} %pad_maximum_fusion.1), calls=%async_computation | async-start | bytes 4194304 | tf_op jit(solution)/shard_map/all_to_all | solution.py:119
  8.6 2.7 %fusion.64 = (bf16[512,1024]{1,0:T(8,128)(2,1)}, bf16[512,1024]{1,0:T(8,128)(2,1)S(1)}) fusion(bf16[512,2048]{1,0:T(8,128)(2,1)} %param.17), kind=kLoop, calls=%fused_computation.72 | loop fusion | bytes 4194304 | tf_op jit(solution)/shard_map/slice | solution.py:141
  11.3 2.4 %collective-permute-start.11 = (bf16[512,1024]{1,0:T(8,128)(2,1)S(1)}, bf16[512,1024]{1,0:T(8,128)(2,1)}, u32[]{:S(2)}, u32[]{:S(2)}) collective-permute-start(bf16[512,1024]{1,0:T(8,128)(2,1)S(1)} %get-tuple-element.6), channel_id=1, source_target_pairs={{8,0},{16,8},{24,16},{28,24},{20,28},{12,20},{4,12},{0,4},{9,1},{1... | collective-permute-start | bytes 3145736 | tf_op jit(solution)/shard_map/ppermute | solution.py:149
  13.8 2.0 %collective-permute-start.3 = (bf16[512,1024]{1,0:T(8,128)(2,1)}, bf16[512,1024]{1,0:T(8,128)(2,1)}, u32[]{:S(2)}, u32[]{:S(2)}) collective-permute-start(bf16[512,1024]{1,0:T(8,128)(2,1)} %get-tuple-element.5), channel_id=1, source_target_pairs={{0,8},{8,16},{16,24},{24,28},{28,20},{20,12},{12,4},{4,0},{1,9},{9... | collective-permute-start | bytes 3145736 | tf_op jit(solution)/shard_map/ppermute | solution.py:146
  17.2 20.7 %collective-permute-done.11 = bf16[512,1024]{1,0:T(8,128)(2,1)} collective-permute-done((bf16[512,1024]{1,0:T(8,128)(2,1)S(1)}, bf16[512,1024]{1,0:T(8,128)(2,1)}, u32[]{:S(2)}, u32[]{:S(2)}) %collective-permute-start.11) | collective-permute-done | bytes 1048608 | tf_op jit(solution)/shard_map/ppermute | solution.py:149
  37.9 1.9 collective-permute-start.13
  39.9 22.4 %collective-permute-done.3 = bf16[512,1024]{1,0:T(8,128)(2,1)} collective-permute-done((bf16[512,1024]{1,0:T(8,128)(2,1)}, bf16[512,1024]{1,0:T(8,128)(2,1)}, u32[]{:S(2)}, u32[]{:S(2)}) %collective-permute-start.3) | collective-permute-done | bytes 1048608 | tf_op jit(solution)/shard_map/ppermute | solution.py:146
  62.3 1.2 copy-done.2
  65.4 2.1 %collective-permute-start.1 = (bf16[512,1024]{1,0:T(8,128)(2,1)S(1)}, bf16[512,1024]{1,0:T(8,128)(2,1)}, u32[]{:S(2)}, u32[]{:S(2)}) collective-permute-start(bf16[512,1024]{1,0:T(8,128)(2,1)S(1)} %attend.1), channel_id=1, source_target_pairs={{0,2},{1,3},{2,0},{3,1},{4,6},{5,7},{6,4},{7,5},{8,10},{9,11},{10,... | collective-permute-start | bytes 3145736 | tf_op jit(solution)/shard_map/ppermute | solution.py:174
  67.5 2.0 %collective-permute-start.6 = (bf16[512,1024]{1,0:T(8,128)(2,1)}, bf16[512,1024]{1,0:T(8,128)(2,1)S(1)}, u32[]{:S(2)}, u32[]{:S(2)}) collective-permute-start(bf16[512,1024]{1,0:T(8,128)(2,1)} %collective-permute-done.4), channel_id=1, source_target_pairs={{8,0},{16,8},{24,16},{28,24},{20,28},{12,20},{4,12},{0,4},{9,1},{1... | collective-permute-start | bytes 3145736 | tf_op jit(solution)/shard_map/ppermute | solution.py:149
  69.5 13.1 %collective-permute-done.13 = bf16[512,1024]{1,0:T(8,128)(2,1)} collective-permute-done((bf16[512,1024]{1,0:T(8,128)(2,1)}, bf16[512,1024]{1,0:T(8,128)(2,1)}, u32[]{:S(2)}, u32[]{:S(2)}) %collective-permute-start.13) | collective-permute-done | bytes 1048608 | tf_op jit(solution)/shard_map/ppermute | solution.py:149
  82.6 2.1 %collective-permute-done.12 = bf16[512,1024]{1,0:T(8,128)(2,1)} collective-permute-done((bf16[512,1024]{1,0:T(8,128)(2,1)}, bf16[512,1024]{1,0:T(8,128)(2,1)}, u32[]{:S(2)}, u32[]{:S(2)}) %collective-permute-start.12) | collective-permute-done | bytes 1048608 | tf_op jit(solution)/shard_map/ppermute | solution.py:146
  84.7 1.6 collective-permute-start.15
  86.3 20.1 %collective-permute-done.5 = bf16[512,1024]{1,0:T(8,128)(2,1)} collective-permute-done((bf16[512,1024]{1,0:T(8,128)(2,1)}, bf16[512,1024]{1,0:T(8,128)(2,1)}, u32[]{:S(2)}, u32[]{:S(2)}) %collective-permute-start.5) | collective-permute-done | bytes 1048608 | tf_op jit(solution)/shard_map/ppermute | solution.py:146
  136.6 1.8 collective-permute-start.14
  138.7 1.7 collective-permute-start.16
  140.8 2.3 %pad_maximum_fusion = bf16[4,512,1024]{2,1,0:T(8,128)(2,1)S(1)} fusion(bf16[1,512,1024]{2,1,0:T(8,128)(2,1)} %bitcast.10, bf16[1,512,1024]{2,1,0:T(8,128)(2,1)} %bitcast.9, bf16[1,512,1024]{2,1,0:T(8,128)(2,1)} %bitcast.8, bf16[1,512,1024]{2,1,0:T(8,128)(2,1)S(1)} %bitcast.100), kind=kLoop, calls=%fused_computation | loop fusion | flops 6291456 | bytes 8388608 | tf_op jit(solution)/shard_map/stack | solution.py:177
  144.8 1.9 %fusion.10 = f32[512,1024]{1,0:T(8,128)S(1)} fusion(bf16[512,1024]{1,0:T(8,128)(2,1)} %collective-permute-done.13, bf16[4,512,1024]{2,1,0:T(8,128)(2,1)S(1)} %pad_maximum_fusion, s32[]{:T(128)S(6)} %select_n.271, s32[]{:T(128)S(6)} %select_n.273), kind=kOutput, calls=%fused_computation.17 | convolution fusion | flops 536870912 | bytes 3670024 | tf_op jit(solution)/shard_map/dot_general | solution.py:158
  147.4 2.0 %fusion.14 = f32[512,1024]{1,0:T(8,128)S(1)} fusion(bf16[512,1024]{1,0:T(8,128)(2,1)} %collective-permute-done.12, bf16[4,512,1024]{2,1,0:T(8,128)(2,1)S(1)} %pad_maximum_fusion, s32[]{:T(128)S(6)} %select_n.265, s32[]{:T(128)S(6)} %select_n.267), kind=kOutput, calls=%fused_computation.21 | convolution fusion | flops 536870912 | bytes 3670024 | tf_op jit(solution)/shard_map/dot_general | solution.py:158
  149.4 2.0 %fusion.16 = f32[512,1024]{1,0:T(8,128)S(1)} fusion(bf16[512,1024]{1,0:T(8,128)(2,1)} %collective-permute-done.5, bf16[4,512,1024]{2,1,0:T(8,128)(2,1)S(1)} %pad_maximum_fusion, s32[]{:T(128)S(6)} %select_n.265, s32[]{:T(128)S(6)} %select_n.267), kind=kOutput, calls=%fused_computation.23 | convolution fusion | flops 536870912 | bytes 3670024 | tf_op jit(solution)/shard_map/dot_general | solution.py:158
  151.4 1.9 %fusion.18 = f32[512,1024]{1,0:T(8,128)S(1)} fusion(bf16[512,1024]{1,0:T(8,128)(2,1)} %collective-permute-done.11, bf16[4,512,1024]{2,1,0:T(8,128)(2,1)S(1)} %pad_maximum_fusion, s32[]{:T(128)S(6)} %select_n.259, s32[]{:T(128)S(6)} %select_n.261), kind=kOutput, calls=%fused_computation.25 | convolution fusion | flops 536870912 | bytes 3670024 | tf_op jit(solution)/shard_map/dot_general | solution.py:158
  153.3 1.9 %fusion.20 = f32[512,1024]{1,0:T(8,128)S(1)} fusion(bf16[512,1024]{1,0:T(8,128)(2,1)} %collective-permute-done.4, bf16[4,512,1024]{2,1,0:T(8,128)(2,1)S(1)} %pad_maximum_fusion, s32[]{:T(128)S(6)} %select_n.259, s32[]{:T(128)S(6)} %select_n.261), kind=kOutput, calls=%fused_computation.27 | convolution fusion | flops 536870912 | bytes 3670024 | tf_op jit(solution)/shard_map/dot_general | solution.py:158
  155.3 2.0 %fusion.22 = f32[512,1024]{1,0:T(8,128)S(1)} fusion(bf16[512,1024]{1,0:T(8,128)(2,1)} %collective-permute-done.10, bf16[4,512,1024]{2,1,0:T(8,128)(2,1)S(1)} %pad_maximum_fusion, s32[]{:T(128)S(6)} %select_n.253, s32[]{:T(128)S(6)} %select_n.255), kind=kOutput, calls=%fused_computation.29 | convolution fusion | flops 536870912 | bytes 3670024 | tf_op jit(solution)/shard_map/dot_general | solution.py:158
  157.3 2.0 %fusion.24 = f32[512,1024]{1,0:T(8,128)S(1)} fusion(bf16[512,1024]{1,0:T(8,128)(2,1)} %collective-permute-done.3, bf16[4,512,1024]{2,1,0:T(8,128)(2,1)S(1)} %pad_maximum_fusion, s32[]{:T(128)S(6)} %select_n.253, s32[]{:T(128)S(6)} %select_n.255), kind=kOutput, calls=%fused_computation.31 | convolution fusion | flops 536870912 | bytes 3670024 | tf_op jit(solution)/shard_map/dot_general | solution.py:158
  159.2 2.0 %fusion.8 = f32[512,1024]{1,0:T(8,128)S(1)} fusion(bf16[512,1024]{1,0:T(8,128)(2,1)} %collective-permute-done.7, bf16[4,512,1024]{2,1,0:T(8,128)(2,1)S(1)} %pad_maximum_fusion, s32[]{:T(128)S(6)} %select_n.277, s32[]{:T(128)S(6)} %select_n.279), kind=kOutput, calls=%fused_computation.15 | convolution fusion | flops 536870912 | bytes 3670024 | tf_op jit(solution)/shard_map/dot_general | solution.py:158
  161.2 1.7 collective-permute-done.14
  163.6 1.9 %fusion.2 = f32[512,1024]{1,0:T(8,128)S(1)} fusion(bf16[512,1024]{1,0:T(8,128)(2,1)} %collective-permute-done.15, bf16[4,512,1024]{2,1,0:T(8,128)(2,1)S(1)} %pad_maximum_fusion, s32[]{:T(128)S(6)} %select_n.283, s32[]{:T(128)S(6)} %select_n.285), kind=kOutput, calls=%fused_computation.9 | convolution fusion | flops 536870912 | bytes 3670024 | tf_op jit(solution)/shard_map/dot_general | solution.py:158
  166.3 20.0 %collective-permute-done.16 = bf16[512,1024]{1,0:T(8,128)(2,1)} collective-permute-done((bf16[512,1024]{1,0:T(8,128)(2,1)}, bf16[512,1024]{1,0:T(8,128)(2,1)}, u32[]{:S(2)}, u32[]{:S(2)}) %collective-permute-start.16) | collective-permute-done | bytes 1048608 | tf_op jit(solution)/shard_map/ppermute | solution.py:149
  186.3 2.4 %add_convert_fusion = bf16[512,1024]{1,0:T(8,128)(2,1)S(1)} fusion(f32[512,1024]{1,0:T(8,128)S(1)} %fusion.2, f32[512,1024]{1,0:T(8,128)S(1)} %fusion.6, f32[512,1024]{1,0:T(8,128)S(1)} %fusion.10, f32[512,1024]{1,0:T(8,128)S(1)} %fusion.14, f32[512,1024]{1,0:T(8,128)S(1)} %fusion.18, f32[512,1024]{1,0:T(8,128)S(1)} %fusion.26, f32[512,1024]{1,0:T(8,128)S(1)} %fusion.22, ...), kind=kOutput, calls=%fused_computation.3 | convolution fusion | flops 541065216 | bytes 17301512 | tf_op jit(solution)/shard_map/dot_general | solution.py:158
  189.9 1.5 maximum_bitcast_fusion
  (45 shorter events, 10.7 us)
Async XLA Ops:
  0.0 1.2 copy-start
  4.4 57.9 %all-to-all-start = ((bf16[1024,4,256]{2,0,1:T(8,128)(2,1)}), bf16[1024,4,256]{2,0,1:T(8,128)(2,1)S(1)}, u32[]{:S(2)}, u32[]{:S(2)}) async-start(bf16[1024,4,256]{2,0,1:T(8,128)(2,1)} %pad_maximum_fusion.1), calls=%async_computation | async-start | bytes 4194304 | tf_op jit(solution)/shard_map/all_to_all | solution.py:119
  8.6 8.5 %copy-start.6 = (s32[1,1,16]{2,1,0:T(1,128)S(1)}, s32[1,1,16]{2,1,0:T(1,128)}, u32[]{:S(2)}) copy-start(s32[1,1,16]{2,1,0:T(1,128)} %param.13) | copy-start | bytes 196
  11.3 26.5 %collective-permute-start.11 = (bf16[512,1024]{1,0:T(8,128)(2,1)S(1)}, bf16[512,1024]{1,0:T(8,128)(2,1)}, u32[]{:S(2)}, u32[]{:S(2)}) collective-permute-start(bf16[512,1024]{1,0:T(8,128)(2,1)S(1)} %get-tuple-element.6), channel_id=1, source_target_pairs={{8,0},{16,8},{24,16},{28,24},{20,28},{12,20},{4,12},{0,4},{9,1},{1... | collective-permute-start | bytes 3145736 | tf_op jit(solution)/shard_map/ppermute | solution.py:149
  13.7 26.1 %collective-permute-start.10 = (bf16[512,1024]{1,0:T(8,128)(2,1)S(1)}, bf16[512,1024]{1,0:T(8,128)(2,1)}, u32[]{:S(2)}, u32[]{:S(2)}) collective-permute-start(bf16[512,1024]{1,0:T(8,128)(2,1)S(1)} %get-tuple-element.6), channel_id=1, source_target_pairs={{0,8},{8,16},{16,24},{24,28},{28,20},{20,12},{12,4},{4,0},{1,9},{9... | collective-permute-start | bytes 3145736 | tf_op jit(solution)/shard_map/ppermute | solution.py:146
  13.8 48.5 %collective-permute-start.3 = (bf16[512,1024]{1,0:T(8,128)(2,1)}, bf16[512,1024]{1,0:T(8,128)(2,1)}, u32[]{:S(2)}, u32[]{:S(2)}) collective-permute-start(bf16[512,1024]{1,0:T(8,128)(2,1)} %get-tuple-element.5), channel_id=1, source_target_pairs={{0,8},{8,16},{16,24},{24,28},{28,20},{20,12},{12,4},{4,0},{1,9},{9... | collective-permute-start | bytes 3145736 | tf_op jit(solution)/shard_map/ppermute | solution.py:146
  15.8 51.7 %collective-permute-start.4 = (bf16[512,1024]{1,0:T(8,128)(2,1)}, bf16[512,1024]{1,0:T(8,128)(2,1)}, u32[]{:S(2)}, u32[]{:S(2)}) collective-permute-start(bf16[512,1024]{1,0:T(8,128)(2,1)} %get-tuple-element.5), channel_id=1, source_target_pairs={{8,0},{16,8},{24,16},{28,24},{20,28},{12,20},{4,12},{0,4},{9,1},{1... | collective-permute-start | bytes 3145736 | tf_op jit(solution)/shard_map/ppermute | solution.py:149
  37.9 44.7 %collective-permute-start.13 = (bf16[512,1024]{1,0:T(8,128)(2,1)}, bf16[512,1024]{1,0:T(8,128)(2,1)}, u32[]{:S(2)}, u32[]{:S(2)}) collective-permute-start(bf16[512,1024]{1,0:T(8,128)(2,1)} %collective-permute-done.11), channel_id=1, source_target_pairs={{8,0},{16,8},{24,16},{28,24},{20,28},{12,20},{4,12},{0,4},{9,1},{1... | collective-permute-start | bytes 3145736 | tf_op jit(solution)/shard_map/ppermute | solution.py:149
  39.8 44.9 %collective-permute-start.12 = (bf16[512,1024]{1,0:T(8,128)(2,1)}, bf16[512,1024]{1,0:T(8,128)(2,1)}, u32[]{:S(2)}, u32[]{:S(2)}) collective-permute-start(bf16[512,1024]{1,0:T(8,128)(2,1)} %collective-permute-done.10), channel_id=1, source_target_pairs={{0,8},{8,16},{16,24},{24,28},{28,20},{20,12},{12,4},{4,0},{1,9},{9... | collective-permute-start | bytes 3145736 | tf_op jit(solution)/shard_map/ppermute | solution.py:146
  62.3 44.2 %collective-permute-start.5 = (bf16[512,1024]{1,0:T(8,128)(2,1)}, bf16[512,1024]{1,0:T(8,128)(2,1)}, u32[]{:S(2)}, u32[]{:S(2)}) collective-permute-start(bf16[512,1024]{1,0:T(8,128)(2,1)} %collective-permute-done.3), channel_id=1, source_target_pairs={{0,8},{8,16},{16,24},{24,28},{28,20},{20,12},{12,4},{4,0},{1,9},{9... | collective-permute-start | bytes 3145736 | tf_op jit(solution)/shard_map/ppermute | solution.py:146
  62.3 1.2 copy-start.2
  63.5 1.2 copy-start.3
  64.7 42.1 %copy-start.7 = (s32[8]{0:T(128)S(1)}, s32[8]{0:T(128)}, u32[]{:S(2)}) copy-start(s32[8]{0:T(128)} %constant.248.clone) | copy-start | bytes 100
  64.8 48.7 %copy-start.5 = (s32[8]{0:T(128)S(1)}, s32[8]{0:T(128)}, u32[]{:S(2)}) copy-start(s32[8]{0:T(128)} %constant.249.clone) | copy-start | bytes 100
  65.4 41.4 %collective-permute-start.1 = (bf16[512,1024]{1,0:T(8,128)(2,1)S(1)}, bf16[512,1024]{1,0:T(8,128)(2,1)}, u32[]{:S(2)}, u32[]{:S(2)}) collective-permute-start(bf16[512,1024]{1,0:T(8,128)(2,1)S(1)} %attend.1), channel_id=1, source_target_pairs={{0,2},{1,3},{2,0},{3,1},{4,6},{5,7},{6,4},{7,5},{8,10},{9,11},{10,... | collective-permute-start | bytes 3145736 | tf_op jit(solution)/shard_map/ppermute | solution.py:174
  67.5 69.2 %collective-permute-start.6 = (bf16[512,1024]{1,0:T(8,128)(2,1)}, bf16[512,1024]{1,0:T(8,128)(2,1)S(1)}, u32[]{:S(2)}, u32[]{:S(2)}) collective-permute-start(bf16[512,1024]{1,0:T(8,128)(2,1)} %collective-permute-done.4), channel_id=1, source_target_pairs={{8,0},{16,8},{24,16},{28,24},{20,28},{12,20},{4,12},{0,4},{9,1},{1... | collective-permute-start | bytes 3145736 | tf_op jit(solution)/shard_map/ppermute | solution.py:149
  82.6 55.9 %collective-permute-start = (bf16[512,1024]{1,0:T(8,128)(2,1)S(1)}, bf16[512,1024]{1,0:T(8,128)(2,1)}, u32[]{:S(2)}, u32[]{:S(2)}) collective-permute-start(bf16[512,1024]{1,0:T(8,128)(2,1)S(1)} %attend.1), channel_id=1, source_target_pairs={{0,1},{1,0},{2,3},{3,2},{4,5},{5,4},{6,7},{7,6},{8,9},{9,8},{10,11... | collective-permute-start | bytes 3145736 | tf_op jit(solution)/shard_map/ppermute | solution.py:175
  84.7 54.0 %collective-permute-start.15 = (bf16[512,1024]{1,0:T(8,128)(2,1)}, bf16[512,1024]{1,0:T(8,128)(2,1)}, u32[]{:S(2)}, u32[]{:S(2)}) collective-permute-start(bf16[512,1024]{1,0:T(8,128)(2,1)} %collective-permute-done.13), channel_id=1, source_target_pairs={{8,0},{16,8},{24,16},{28,24},{20,28},{12,20},{4,12},{0,4},{9,1},{1... | collective-permute-start | bytes 3145736 | tf_op jit(solution)/shard_map/ppermute | solution.py:149
  106.5 34.0 %collective-permute-start.7 = (bf16[512,1024]{1,0:T(8,128)(2,1)}, bf16[512,1024]{1,0:T(8,128)(2,1)}, u32[]{:S(2)}, u32[]{:S(2)}) collective-permute-start(bf16[512,1024]{1,0:T(8,128)(2,1)} %collective-permute-done.5), channel_id=1, source_target_pairs={{0,8},{8,16},{16,24},{24,28},{28,20},{20,12},{12,4},{4,0},{1,9},{9... | collective-permute-start | bytes 3145736 | tf_op jit(solution)/shard_map/ppermute | solution.py:146
  106.8 34.0 %collective-permute-start.2 = (bf16[512,1024]{1,0:T(8,128)(2,1)}, bf16[512,1024]{1,0:T(8,128)(2,1)}, u32[]{:S(2)}, u32[]{:S(2)}) collective-permute-start(bf16[512,1024]{1,0:T(8,128)(2,1)} %collective-permute-done.1), channel_id=1, source_target_pairs={{0,1},{1,0},{2,3},{3,2},{4,5},{5,4},{6,7},{7,6},{8,9},{9,8},{10,11... | collective-permute-start | bytes 3145736 | tf_op jit(solution)/shard_map/ppermute | solution.py:176
  136.6 26.2 %collective-permute-start.14 = (bf16[512,1024]{1,0:T(8,128)(2,1)}, bf16[512,1024]{1,0:T(8,128)(2,1)S(1)}, u32[]{:S(2)}, u32[]{:S(2)}) collective-permute-start(bf16[512,1024]{1,0:T(8,128)(2,1)} %collective-permute-done.12), channel_id=1, source_target_pairs={{0,8},{8,16},{16,24},{24,28},{28,20},{20,12},{12,4},{4,0},{1,9},{9... | collective-permute-start | bytes 3145736 | tf_op jit(solution)/shard_map/ppermute | solution.py:146
  138.4 27.1 %collective-permute-start.8 = (bf16[512,1024]{1,0:T(8,128)(2,1)S(1)}, bf16[512,1024]{1,0:T(8,128)(2,1)S(1)}, u32[]{:S(2)}, u32[]{:S(2)}) collective-permute-start(bf16[512,1024]{1,0:T(8,128)(2,1)S(1)} %collective-permute-done.6), channel_id=1, source_target_pairs={{8,0},{16,8},{24,16},{28,24},{20,28},{12,20},{4,12},{0,4},{9,1},{1... | collective-permute-start | bytes 3145736 | tf_op jit(solution)/shard_map/ppermute | solution.py:149
  138.7 47.6 %collective-permute-start.16 = (bf16[512,1024]{1,0:T(8,128)(2,1)}, bf16[512,1024]{1,0:T(8,128)(2,1)}, u32[]{:S(2)}, u32[]{:S(2)}) collective-permute-start(bf16[512,1024]{1,0:T(8,128)(2,1)} %collective-permute-done.15), channel_id=1, source_target_pairs={{8,0},{16,8},{24,16},{28,24},{20,28},{12,20},{4,12},{0,4},{9,1},{1... | collective-permute-start | bytes 3145736 | tf_op jit(solution)/shard_map/ppermute | solution.py:149
  140.4 48.3 %collective-permute-start.9 = (bf16[512,1024]{1,0:T(8,128)(2,1)}, bf16[512,1024]{1,0:T(8,128)(2,1)S(1)}, u32[]{:S(2)}, u32[]{:S(2)}) collective-permute-start(bf16[512,1024]{1,0:T(8,128)(2,1)} %collective-permute-done.7), channel_id=1, source_target_pairs={{0,8},{8,16},{16,24},{24,28},{28,20},{20,12},{12,4},{4,0},{1,9},{9... | collective-permute-start | bytes 3145736 | tf_op jit(solution)/shard_map/ppermute | solution.py:146
  140.8 2.5 %copy-start.4 = (bf16[512,2048]{1,0:T(8,128)(2,1)S(1)}, bf16[512,2048]{1,0:T(8,128)(2,1)}, u32[]{:S(2)}) copy-start(bf16[512,2048]{1,0:T(8,128)(2,1)} %param.17) | copy-start | bytes 6291460
  188.7 2.7 %copy-start.1 = (bf16[1024,512]{1,0:T(8,128)(2,1)S(1)}, bf16[1024,512]{1,0:T(8,128)(2,1)}, u32[]{:S(2)}) copy-start(bf16[1024,512]{1,0:T(8,128)(2,1)} %param.11) | copy-start | bytes 3145732
where the time goes:
time: 193 us; the launch traced here: 191 us
  waiting for transfers between devices  100 us (52%)
  between operations  30 us (16%)
  matrix products  24.8 us (13%)
  starting transfers between devices  20.8 us (11%)
  local copies, waits for them, and re-layouts  9.56 us (5%)
  other arithmetic  5.39 us (3%)
    ppermute x7, waiting for transfers between devices, project_ring(): moving[part][1] = lax.ppermute(moving[part][1], 'pb', backward)  53.8 us
    ppermute x7, waiting for transfers between devices, project_ring(): moving[part][0] = lax.ppermute(moving[part][0], 'pb', forward)  46.4 us
    dot_general x16, matrix products, project_ring(): term = jnp.dot(left, slab, preferred_element_type=jnp.float32)  24.8 us
    ppermute x7, starting transfers between devices, project_ring(): moving[part][1] = lax.ppermute(moving[part][1], 'pb', backward)  9.84 us
    ppermute x7, starting transfers between devices, project_ring(): moving[part][0] = lax.ppermute(moving[part][0], 'pb', forward)  4.68 us
    all_to_all x1, starting transfers between devices, own_head_keys_values(): lax.all_to_all(both.reshape(rows, groups * 2 * HEAD_SIZE), 'ka', split_ax...  4.21 us
    unnamed x16, local copies, waits for them, and re-layouts  3.96 us
  transfers between devices with their start and end apart: 18, of which 7 were waited for; matrix products, arithmetic and copies ran while one was open for 16% of the time, Pallas kernels for 0%

commit v1 on v0

--- a/solution.py
+++ b/solution.py
@@ -121,69 +121,198 @@
     )
 
 
-def ring_of(pb_size):
-    if pb_size == 8:
-        return [0, 2, 4, 6, 7, 5, 3, 1]
-    return list(range(pb_size))
-
-
-def project_ring(attn, wo):
-    pb_size = lax.axis_size("pb")
+def place_kernel(chunks, place_ref, *refs):
+    own, received = refs[: len(chunks)], refs[len(chunks) : 2 * len(chunks)]
+    out_ref, sems = refs[2 * len(chunks)], refs[2 * len(chunks) + 1]
+    y = place_ref[1]
+    half = out_ref.shape[1] // 2
+    copies = []
+    for side, pieces in enumerate((own, received)):
+        start = 0
+        for index, piece in enumerate(pieces):
+            column = pl.multiple_of(jnp.bitwise_xor(y, side) * half + start, HEAD_SIZE)
+            copies.append(
+                pltpu.make_async_copy(
+                    piece, out_ref.at[:, pl.ds(column, chunks[index])], sems.at[side, index]
+                )
+            )
+            start += chunks[index]
+    for copy in copies:
+        copy.start()
+    for copy in copies:
+        copy.wait()
+
+
+def place(chunks, where, own, received, columns):
+    rows = own[0].shape[0]
+    return pl.pallas_call(
+        functools.partial(place_kernel, chunks),
+        out_shape=jax.ShapeDtypeStruct((rows, columns), jnp.bfloat16),
+        in_specs=[pl.BlockSpec(memory_space=pltpu.SMEM)]
+        + [pl.BlockSpec(memory_space=pl.ANY)] * (2 * len(chunks)),
+        out_specs=pl.BlockSpec(memory_space=pl.ANY),
+        scratch_shapes=[pltpu.SemaphoreType.DMA((2, len(chunks)))],
+        name="place",
+    )(where, *own, *received)
+
+
+def partial_kernel(first, chunks, place_ref, *refs):
+    z, y, me = place_ref[0], place_ref[1], place_ref[2]
+    own_rows, other_rows, slabs, refs = refs[:4], refs[4:8], refs[8:15], refs[15:]
+    if first:
+        outs, refs = refs[: len(chunks)], refs[len(chunks) :]
+    else:
+        base_ref, own_out, other_out, refs = refs[0], refs[1], refs[2], refs[3:]
+    left, right, sems = refs
+    rows, depth = own_rows[0].shape[0], slabs[0].shape[0]
+    parity = y if first else 1 - y
+    column = pl.multiple_of(parity * depth, depth)
+
+    def left_copy(target, slot, side):
+        source = (own_rows, other_rows)[side][slot]
+        return pltpu.make_async_copy(
+            source.at[:, pl.ds(column, depth)],
+            left.at[pl.ds(side * rows, rows), pl.ds(target * depth, depth)],
+            sems.at[target, side],
+        )
+
+    def slab_copy(target, slot):
+        return pltpu.make_async_copy(
+            slabs[slot], right.at[pl.ds(target * depth, depth), :], sems.at[target, 2]
+        )
+
+    for target in range(4):
+        slot_here = jnp.bitwise_xor(me, target)
+        for slot in range(4):
+
+            @pl.when(slot_here == slot)
+            def _(slot=slot):
+                left_copy(target, slot, 0).start()
+                left_copy(target, slot, 1).start()
+
+        for position in range(4):
+
+            @pl.when(z == position)
+            def _(position=position):
+                distance = target - position
+                slab_copy(target, -distance if distance <= 0 else 3 + distance).start()
+
+    for target in range(4):
+        left_copy(target, 0, 0).wait()
+        left_copy(target, 0, 1).wait()
+        slab_copy(target, 0).wait()
+
+    tile = 256
+
+    def rows_tile(step, carry):
+        at = pl.ds(pl.multiple_of(step * tile, tile), tile)
+        product = jnp.dot(left[at, :], right[...], preferred_element_type=jnp.float32)
+        if first:
+            start = 0
+            for out, chunk in zip(outs, chunks):
+                out[at, :] = product[:, start : start + chunk]
+                start += chunk
+        else:
+            total = (product + base_ref[at, :]).astype(jnp.bfloat16)
+
+            @pl.when(step < rows // tile)
+            def _():
+                own_out[at, :] = total
+
+            @pl.when(step >= rows // tile)
+            def _():
+                back = pl.ds(pl.multiple_of(step * tile - rows, tile), tile)
+                other_out[back, :] = total
+
+        return carry
+
+    lax.fori_loop(0, 2 * rows // tile, rows_tile, 0)
+
+
+def partial_product(where, own_rows, other_rows, slabs, chunks=None, base=None):
+    rows = own_rows[0].shape[0]
+    depth, columns = slabs[0].shape
+    first = base is None
+    if first:
+        out_shape = [jax.ShapeDtypeStruct((2 * rows, chunk), jnp.float32) for chunk in chunks]
+    else:
+        out_shape = [jax.ShapeDtypeStruct((rows, columns), jnp.bfloat16)] * 2
+    whole = pl.BlockSpec(memory_space=pltpu.VMEM)
+    return pl.pallas_call(
+        functools.partial(partial_kernel, first, chunks),
+        out_shape=out_shape,
+        in_specs=[pl.BlockSpec(memory_space=pltpu.SMEM)]
+        + [pl.BlockSpec(memory_space=pl.ANY)] * 15
+        + ([] if first else [whole]),
+        out_specs=[whole] * len(out_shape),
+        scratch_shapes=[
+            pltpu.VMEM((2 * rows, 4 * depth), jnp.bfloat16),
+            pltpu.VMEM((4 * depth, columns), jnp.bfloat16),
+            pltpu.SemaphoreType.DMA((4, 3)),
+        ],
+        compiler_params=pltpu.CompilerParams(vmem_limit_bytes=32 << 20),
+        cost_estimate=pl.CostEstimate(
+            flops=2 * 2 * rows * 4 * depth * columns,
+            transcendentals=0,
+            bytes_accessed=2 * (2 * rows * 4 * depth + 4 * depth * columns) + 8 * rows * columns,
+        ),
+        name="partial_first" if first else "partial_rest",
+    )(where, *own_rows, *other_rows, *slabs, *([] if first else [base]))
+
+
+UP = [[(i, i + 2) for i in range(2 * s, 6)] for s in range(3)]
+DOWN = [[(i + 2, i) for i in range(6 - 2 * s)] for s in range(3)]
+ACROSS_Y = [(i, i ^ 1) for i in range(8)]
+ACROSS_X = [(i, i ^ 2) for i in range(4)]
+ACROSS_CORE = [(i, i ^ 1) for i in range(4)]
+
+
+def along_z(piece):
+    below, above = [piece], [piece]
+    for hop in range(3):
+        below.append(lax.ppermute(below[-1], "pb", UP[hop]))
+        above.append(lax.ppermute(above[-1], "pb", DOWN[hop]))
+    return [piece] + below[1:] + above[1:]
+
+
+def project(where, attn, wo):
+    y = where[1]
     depth, columns = wo.shape
-    ring = ring_of(pb_size)
-    place_of = [ring.index(p) for p in range(pb_size)]
-    forward = [(ring[i], ring[(i + 1) % pb_size]) for i in range(pb_size)]
-    backward = [(b, a) for a, b in forward]
-    here = jnp.asarray(place_of, jnp.int32)[lax.axis_index("pb")]
-    order = jnp.asarray(ring, jnp.int32)
     half = columns // 2
-    far = pb_size // 2
-    slabs = [[(0, wo[:, :half])], [(0, wo[:, half:])]]
-    moving = [[slabs[0][0][1]] * 2, [slabs[1][0][1]] * 2]
-    for hop in range(1, far + 1):
-        for part in range(2):
-            if hop < far or part == 0:
-                moving[part][0] = lax.ppermute(moving[part][0], "pb", forward)
-                slabs[part].append((-hop, moving[part][0]))
-            if hop < far or part == 1:
-                moving[part][1] = lax.ppermute(moving[part][1], "pb", backward)
-                slabs[part].append((hop, moving[part][1]))
-    attn_blocks = attn
-    results = []
-    for part in range(2):
-        total = None
-        for offset, slab in slabs[part]:
-            source = order[(here + offset + pb_size) % pb_size]
-            left = attn_blocks(source)
-            term = jnp.dot(left, slab, preferred_element_type=jnp.float32)
-            total = term if total is None else total + term
-        results.append(total.astype(jnp.bfloat16))
-    return jnp.concatenate(results, axis=1)
+    chunks = (half * 5 // 8, half // 4, half // 8)
+    kept = lax.dynamic_slice(wo, (0, y * half), (depth, half))
+    kept_slabs = along_z(kept)
+    rest_slabs = []
+    start = 0
+    for chunk in chunks:
+        given = lax.dynamic_slice(wo, (0, (1 - y) * half + start), (depth, chunk))
+        rest_slabs.append(along_z(lax.ppermute(given, "pb", ACROSS_Y)))
+        start += chunk
+    across_x = lax.ppermute(attn, "ka", ACROSS_X)
+    across_y = lax.ppermute(attn, "pb", ACROSS_Y)
+    corner = lax.ppermute(across_y, "ka", ACROSS_X)
+    own_rows = [attn, lax.ppermute(attn, "ka", ACROSS_CORE), across_x, lax.ppermute(across_x, "ka", ACROSS_CORE)]
+    other_rows = [across_y, lax.ppermute(across_y, "ka", ACROSS_CORE), corner, lax.ppermute(corner, "ka", ACROSS_CORE)]
+    bases = partial_product(where, own_rows, other_rows, kept_slabs, chunks=chunks)
+    own_out, received = [], []
+    for base, slabs in zip(bases, rest_slabs):
+        own, other = partial_product(where, own_rows, other_rows, slabs, base=base)
+        own_out.append(own)
+        received.append(lax.ppermute(other, "pb", ACROSS_Y))
+    return place(chunks, where, own_out, received, columns)
 
 
 def shards(queries, keys, values, block_ids, counts, refresh, cached_attn, wo):
     groups = lax.axis_size("ka")
     pb_size = lax.axis_size("pb")
     me = lax.axis_index("ka")
-    width = QUERY_HEAD_COUNT * HEAD_SIZE
-    depth = wo.shape[0]
     kv = own_head_keys_values(keys, values, groups)
     meta = jnp.concatenate([counts[0], refresh[0], block_ids[0, 0]])
     attn = attend(meta, queries[0], kv, cached_attn[0])
     if pb_size == 8 and groups == 4:
-        across = lax.ppermute(attn, "ka", [(i, i ^ 2) for i in range(4)])
-        beside = lax.ppermute(attn, "ka", [(i, i ^ 1) for i in range(4)])
-        corner = lax.ppermute(across, "ka", [(i, i ^ 1) for i in range(4)])
-        pieces = jnp.stack([attn, beside, across, corner])
-        per = attn.shape[1] // depth
-
-        def block(source):
-            slot = jnp.bitwise_xor(source // per, me)
-            return lax.dynamic_slice(
-                pieces, (slot, 0, (source % per) * depth), (1, attn.shape[0], depth)
-            )[0]
-
-        mixed = project_ring(block, wo)
+        pb = lax.axis_index("pb")
+        where = jnp.stack([pb // 2, pb % 2, me]).astype(jnp.int32)
+        mixed = project(where, attn, wo)
     else:
         attn_full = lax.all_gather(attn, "ka", axis=1, tiled=True)
         mixed = jnp.dot(

time: 193 us -> 287 us (1.49)
  Pallas kernels: 0.62 us -> 116 us
  starting transfers between devices: 20.8 us -> 59.3 us
  between operations: 30 us -> 1.9 us
  matrix products: 24.8 us -> 0 us
  waiting for transfers between devices: 100 us -> 89.5 us
  local copies, waits for them, and re-layouts: 9.56 us -> 18.5 us
  other arithmetic: 5.39 us -> 1.7 us
    pallas_call x0 -> x5, Pallas kernels: none -> 90.2 us  [the longest x1 65.3 us: place(): pl.pallas_call(functools.partial(place_kernel, chunks), out_shape=jax.Sha...]
    ppermute x17 -> x37, starting transfers between devices: 16.6 us -> 54.8 us  [the longest x12 28.3 us: along_z(): below.append(lax.ppermute(below[-1], 'pb', UP[hop]))]
    dot_general x16 -> x0, matrix products: 24.8 us -> none  [project_ring(): term = jnp.dot(left, slab, preferred_element_type=jnp.float32)]
    pallas_call x1, Pallas kernels: 0.62 us -> 25.4 us  [attend(): pl.pallas_call(functools.partial(attention_kernel, heads), out_shape=jax....]
    unnamed x16 -> x46, local copies, waits for them, and re-layouts: 3.96 us -> 15.1 us
    ppermute x17 -> x37, waiting for transfers between devices: 100 us -> 89.5 us  [the longest x12 58.5 us: along_z(): above.append(lax.ppermute(above[-1], 'pb', DOWN[hop]))]
  transfers between devices with their start and end apart: 18 -> 38, of which waited for: 7 -> 9; matrix products, arithmetic and copies ran while one was open for 16% -> 0% of each run, Pallas kernels for 0% -> 18%
where the time goes in v1:
time: 287 us; the launch traced here: 286 us
  Pallas kernels  116 us (40%)
  waiting for transfers between devices  89.5 us (31%)
  starting transfers between devices  59.3 us (21%)
  local copies, waits for them, and re-layouts  18.5 us (6%)
    pallas_call x1, Pallas kernels, place(): pl.pallas_call(functools.partial(place_kernel, chunks), out_shape=jax.Sha...  65.3 us
    ppermute x12, waiting for transfers between devices, along_z(): above.append(lax.ppermute(above[-1], 'pb', DOWN[hop]))  58.5 us
    ppermute x12, starting transfers between devices, along_z(): below.append(lax.ppermute(below[-1], 'pb', UP[hop]))  28.3 us
    pallas_call x1, Pallas kernels, attend(): pl.pallas_call(functools.partial(attention_kernel, heads), out_shape=jax....  25.4 us
    pallas_call x4, Pallas kernels, partial_product(): pl.pallas_call(functools.partial(partial_kernel, first, chunks), out_shap...  24.9 us
    ppermute x3, waiting for transfers between devices, project(): rest_slabs.append(along_z(lax.ppermute(given, 'pb', ACROSS_Y)))  20.8 us
    ppermute x12, starting transfers between devices, along_z(): above.append(lax.ppermute(above[-1], 'pb', DOWN[hop]))  15.4 us
    unnamed x46, local copies, waits for them, and re-layouts  15.1 us
  transfers between devices with their start and end apart: 38, of which 9 were waited for; matrix products, arithmetic and copies ran while one was open for 0% of the time, Pallas kernels for 18%

profile of v1, /device:TPU:0, one launch (start us, length us, event | category | flops | bytes accessed | tf_op | source)
XLA Modules:
  0.0 286.4 jit_solution(6799060741506493826)
XLA Ops:
  0.0 2.1 copy_bitcast_fusion
  2.1 1.5 pad_maximum_fusion
  3.6 4.5 %all-to-all-start = ((bf16[1024,4,256]{2,0,1:T(8,128)(2,1)}), bf16[1024,4,256]{2,0,1:T(8,128)(2,1)}, u32[]{:S(2)}, u32[]{:S(2)}) async-start(bf16[1024,4,256]{2,0,1:T(8,128)(2,1)} %pad_maximum_fusion), calls=%async_computation | async-start | bytes 4194304 | tf_op jit(solution)/shard_map/all_to_all | solution.py:119
  8.2 3.0 %collective-permute-start.7 = (bf16[512,640]{1,0:T(8,128)(2,1)S(1)}, bf16[512,640]{1,0:T(8,128)(2,1)}, u32[]{:S(2)}, u32[]{:S(2)}) collective-permute-start(bf16[512,640]{1,0:T(8,128)(2,1)S(1)} %constant_dynamic-slice_fusion.3), channel_id=1, source_target_pairs={{0,4},{4,0},{8,12},{12,8},{16,20},{20,16},{24,28},{28,24},{1,5},{5... | collective-permute-start | bytes 1966088 | tf_op jit(solution)/shard_map/ppermute | solution.py:289
  11.4 20.8 %collective-permute-done.20.refs_8_ = bf16[512,256]{1,0:T(8,128)(2,1)S(1)} collective-permute-done((bf16[512,256]{1,0:T(8,128)(2,1)S(1)}, bf16[512,256]{1,0:T(8,128)(2,1)S(1)}, u32[]{:S(2)}, u32[]{:S(2)}) %collective-permute-start.20) | collective-permute-done | bytes 262176 | tf_op jit(solution)/shard_map/ppermute | solution.py:289
  32.2 3.7 %collective-permute-start.21 = (bf16[512,256]{1,0:T(8,128)(2,1)S(1)}, bf16[512,256]{1,0:T(8,128)(2,1)S(1)}, u32[]{:S(2)}, u32[]{:S(2)}) collective-permute-start(bf16[512,256]{1,0:T(8,128)(2,1)S(1)} %collective-permute-done.20.refs_8_), channel_id=1, source_target_pairs={{0,8},{4,12},{8,16},{12,20},{16,24},{20,28},{1,9},{5,13},{9,17},{1... | collective-permute-start | bytes 786440 | tf_op jit(solution)/shard_map/ppermute | solution.py:273
  37.0 4.5 %collective-permute-start.14 = (bf16[512,1024]{1,0:T(8,128)(2,1)}, bf16[512,1024]{1,0:T(8,128)(2,1)}, u32[]{:S(2)}, u32[]{:S(2)}) collective-permute-start(bf16[512,1024]{1,0:T(8,128)(2,1)} %constant_dynamic-slice_fusion.2.refs_8_), channel_id=1, source_target_pairs={{0,8},{4,12},{8,16},{12,20},{16,24},{20,28},{1,9},{5,13},{9,17},{1... | collective-permute-start | bytes 3145736 | tf_op jit(solution)/shard_map/ppermute | solution.py:273
  45.5 6.1 %collective-permute-start.8 = (bf16[512,640]{1,0:T(8,128)(2,1)}, bf16[512,640]{1,0:T(8,128)(2,1)}, u32[]{:S(2)}, u32[]{:S(2)}) collective-permute-start(bf16[512,640]{1,0:T(8,128)(2,1)} %collective-permute-done.7.refs_8_), channel_id=1, source_target_pairs={{0,8},{4,12},{8,16},{12,20},{16,24},{20,28},{1,9},{5,13},{9,17},{1... | collective-permute-start | bytes 1966088 | tf_op jit(solution)/shard_map/ppermute | solution.py:273
  55.3 25.4 %attend.1.refs_0_ = bf16[512,1024]{1,0:T(8,128)(2,1)S(1)} custom-call(s32[18]{0:T(128)S(1)} %pad_add_fusion.1.meta_ref, bf16[512,1024]{1,0:T(8,128)(2,1)S(1)} %bitcast.24, bf16[4096,256]{1,0:T(8,128)(2,1)} %bitcast.8.kv_ref, bf16[512,1024]{1,0:T(8,128)(2,1)S(1)} %bitcast.25), custom_call_target="tpu_custom_call" | custom-call | flops 4294967296 | bytes 5242880 | tf_op jit(solution)/shard_map/attend/pallas_call | solution.py:89
  80.8 1.5 collective-permute-start.9
  82.3 5.3 %collective-permute-done.11.refs_12_ = bf16[512,640]{1,0:T(8,128)(2,1)} collective-permute-done((bf16[512,640]{1,0:T(8,128)(2,1)}, bf16[512,640]{1,0:T(8,128)(2,1)}, u32[]{:S(2)}, u32[]{:S(2)}) %collective-permute-start.11) | collective-permute-done | bytes 655392 | tf_op jit(solution)/shard_map/ppermute | solution.py:274
  89.6 1.3 collective-permute-start.18
  90.9 1.4 collective-permute-start.1
  92.3 15.1 %collective-permute-done.12.refs_13_ = bf16[512,640]{1,0:T(8,128)(2,1)} collective-permute-done((bf16[512,640]{1,0:T(8,128)(2,1)}, bf16[512,640]{1,0:T(8,128)(2,1)}, u32[]{:S(2)}, u32[]{:S(2)}) %collective-permute-start.12) | collective-permute-done | bytes 655392 | tf_op jit(solution)/shard_map/ppermute | solution.py:274
  107.5 1.3 collective-permute-start.5
  110.5 16.6 %collective-permute-done.18.refs_13_ = bf16[512,1024]{1,0:T(8,128)(2,1)S(1)} collective-permute-done((bf16[512,1024]{1,0:T(8,128)(2,1)}, bf16[512,1024]{1,0:T(8,128)(2,1)S(1)}, u32[]{:S(2)}, u32[]{:S(2)}) %collective-permute-start.18) | collective-permute-done | bytes 1048608 | tf_op jit(solution)/shard_map/ppermute | solution.py:274
  130.8 6.1 %collective-permute-done.5.refs_6_ = bf16[512,1024]{1,0:T(8,128)(2,1)} collective-permute-done((bf16[512,1024]{1,0:T(8,128)(2,1)}, bf16[512,1024]{1,0:T(8,128)(2,1)}, u32[]{:S(2)}, u32[]{:S(2)}) %collective-permute-start.5) | collective-permute-done | bytes 1048608 | tf_op jit(solution)/shard_map/ppermute | solution.py:293
  138.0 1.5 collective-permute-start.10
  139.5 12.0 %collective-permute-done.19.refs_14_ = bf16[512,1024]{1,0:T(8,128)(2,1)S(1)} collective-permute-done((bf16[512,1024]{1,0:T(8,128)(2,1)S(1)}, bf16[512,1024]{1,0:T(8,128)(2,1)S(1)}, u32[]{:S(2)}, u32[]{:S(2)}) %collective-permute-start.19) | collective-permute-done | bytes 1048608 | tf_op jit(solution)/shard_map/ppermute | solution.py:274
  153.9 1.6 collective-permute-start.27
  156.1 1.3 collective-permute-start.25
  163.6 8.2 %partial_first.1 = (f32[1024,640]{1,0:T(8,128)S(1)}, f32[1024,256]{1,0:T(8,128)S(1)}, f32[1024,128]{1,0:T(8,128)S(1)}) custom-call(s32[3]{0:T(128)S(1)} %pad_add_fusion.place_ref, bf16[512,1024]{1,0:T(8,128)(2,1)S(1)} %attend.1.refs_0_, bf16[512,1024]{1,0:T(8,128)(2,1)S(1)} %copy-done.2, bf16[512,1024]{1,0:T(8,128)(2,1)} %collective-permute-done.1.refs_2_, ...), custom_call_target="tpu_custom_call" | custom-call | flops 4294967296 | bytes 12582912 | tf_op jit(solution)/shard_map/partial_first/pallas_call | solution.py:241
  171.9 7.5 %partial_rest.3 = (bf16[512,640]{1,0:T(8,128)(2,1)S(1)}, bf16[512,640]{1,0:T(8,128)(2,1)S(1)}) custom-call(s32[3]{0:T(128)S(1)} %pad_add_fusion.place_ref, bf16[512,1024]{1,0:T(8,128)(2,1)S(1)} %attend.1.refs_0_, bf16[512,1024]{1,0:T(8,128)(2,1)S(1)} %copy-done.2, bf16[512,1024]{1,0:T(8,128)(2,1)} %collective-permute-done.1.refs_2_, ...), custom_call_target="tpu_custom_call" | custom-call | flops 2684354560 | bytes 9437184 | tf_op jit(solution)/shard_map/partial_rest/pallas_call | solution.py:241
  180.0 6.9 %collective-permute-start.28 = (bf16[512,128]{1,0:T(8,128)(2,1)S(1)}, bf16[512,128]{1,0:T(8,128)(2,1)S(1)}, u32[]{:S(2)}, u32[]{:S(2)}) collective-permute-start(bf16[512,128]{1,0:T(8,128)(2,1)S(1)} %collective-permute-done.27.refs_8_), channel_id=1, source_target_pairs={{0,8},{4,12},{8,16},{12,20},{16,24},{20,28},{1,9},{5,13},{9,17},{1... | collective-permute-start | bytes 393224 | tf_op jit(solution)/shard_map/ppermute | solution.py:273
  186.9 1.3 collective-permute-start.31
  190.9 2.9 %collective-permute-done.31.refs_12_ = bf16[512,128]{1,0:T(8,128)(2,1)S(1)} collective-permute-done((bf16[512,128]{1,0:T(8,128)(2,1)S(1)}, bf16[512,128]{1,0:T(8,128)(2,1)S(1)}, u32[]{:S(2)}, u32[]{:S(2)}) %collective-permute-start.31) | collective-permute-done | bytes 131104 | tf_op jit(solution)/shard_map/ppermute | solution.py:274
  195.8 6.6 %collective-permute-done.32.refs_13_ = bf16[512,128]{1,0:T(8,128)(2,1)S(1)} collective-permute-done((bf16[512,128]{1,0:T(8,128)(2,1)S(1)}, bf16[512,128]{1,0:T(8,128)(2,1)S(1)}, u32[]{:S(2)}, u32[]{:S(2)}) %collective-permute-start.32) | collective-permute-done | bytes 131104 | tf_op jit(solution)/shard_map/ppermute | solution.py:274
  203.7 4.5 %partial_rest.4 = (bf16[512,256]{1,0:T(8,128)(2,1)S(1)}, bf16[512,256]{1,0:T(8,128)(2,1)S(1)}) custom-call(s32[3]{0:T(128)S(1)} %pad_add_fusion.place_ref, bf16[512,1024]{1,0:T(8,128)(2,1)S(1)} %attend.1.refs_0_, bf16[512,1024]{1,0:T(8,128)(2,1)S(1)} %copy-done.2, bf16[512,1024]{1,0:T(8,128)(2,1)} %collective-permute-done.1.refs_2_, ...), custom_call_target="tpu_custom_call" | custom-call | flops 1073741824 | bytes 6291456 | tf_op jit(solution)/shard_map/partial_rest/pallas_call | solution.py:241
  208.2 1.6 collective-permute-start.35
  209.8 4.6 %partial_rest.5 = (bf16[512,128]{1,0:T(8,128)(2,1)S(1)}, bf16[512,128]{1,0:T(8,128)(2,1)S(1)}) custom-call(s32[3]{0:T(128)S(1)} %pad_add_fusion.place_ref, bf16[512,1024]{1,0:T(8,128)(2,1)S(1)} %attend.1.refs_0_, bf16[512,1024]{1,0:T(8,128)(2,1)S(1)} %copy-done.2, bf16[512,1024]{1,0:T(8,128)(2,1)} %collective-permute-done.1.refs_2_, ...), custom_call_target="tpu_custom_call" | custom-call | flops 536870912 | bytes 5242880 | tf_op jit(solution)/shard_map/partial_rest/pallas_call | solution.py:241
  216.0 4.1 %collective-permute-done.36.refs_5_ = bf16[512,128]{1,0:T(8,128)(2,1)S(1)} collective-permute-done((bf16[512,128]{1,0:T(8,128)(2,1)S(1)}, bf16[512,128]{1,0:T(8,128)(2,1)S(1)}, u32[]{:S(2)}, u32[]{:S(2)}) %collective-permute-start.36) | collective-permute-done | bytes 131104 | tf_op jit(solution)/shard_map/ppermute | solution.py:301
  221.0 65.3 %place.1 = bf16[512,2048]{1,0:T(8,128)(2,1)} custom-call(s32[3]{0:T(128)} %copy-done.8, bf16[512,640]{1,0:T(8,128)(2,1)} %copy-done.3, bf16[512,256]{1,0:T(8,128)(2,1)} %copy-done.6, bf16[512,128]{1,0:T(8,128)(2,1)} %copy-done.7, bf16[512,640]{1,0:T(8,128)(2,1)} %copy-done.19, bf16[512,256]{1,0:T(8,128)(2,1)} %copy-done.20, bf16[512,128]{1,0:T(8,128)(2,1)} %copy-done.21), custom_call_target="tpu_custom_call" | custom-call | tf_op jit(solution)/shard_map/place/pallas_call | solution.py:148
  (104 shorter events, 34.4 us)
Async XLA Ops:
  3.6 49.2 %all-to-all-start = ((bf16[1024,4,256]{2,0,1:T(8,128)(2,1)}), bf16[1024,4,256]{2,0,1:T(8,128)(2,1)}, u32[]{:S(2)}, u32[]{:S(2)}) async-start(bf16[1024,4,256]{2,0,1:T(8,128)(2,1)} %pad_maximum_fusion), calls=%async_computation | async-start | bytes 4194304 | tf_op jit(solution)/shard_map/all_to_all | solution.py:119
  8.2 37.2 %collective-permute-start.7 = (bf16[512,640]{1,0:T(8,128)(2,1)S(1)}, bf16[512,640]{1,0:T(8,128)(2,1)}, u32[]{:S(2)}, u32[]{:S(2)}) collective-permute-start(bf16[512,640]{1,0:T(8,128)(2,1)S(1)} %constant_dynamic-slice_fusion.3), channel_id=1, source_target_pairs={{0,4},{4,0},{8,12},{12,8},{16,20},{20,16},{24,28},{28,24},{1,5},{5... | collective-permute-start | bytes 1966088 | tf_op jit(solution)/shard_map/ppermute | solution.py:289
  11.3 20.9 %collective-permute-start.20 = (bf16[512,256]{1,0:T(8,128)(2,1)S(1)}, bf16[512,256]{1,0:T(8,128)(2,1)S(1)}, u32[]{:S(2)}, u32[]{:S(2)}) collective-permute-start(bf16[512,256]{1,0:T(8,128)(2,1)S(1)} %constant_dynamic-slice_fusion.1), channel_id=1, source_target_pairs={{0,4},{4,0},{8,12},{12,8},{16,20},{20,16},{24,28},{28,24},{1,5},{5... | collective-permute-start | bytes 786440 | tf_op jit(solution)/shard_map/ppermute | solution.py:289
  32.2 19.3 %collective-permute-start.21 = (bf16[512,256]{1,0:T(8,128)(2,1)S(1)}, bf16[512,256]{1,0:T(8,128)(2,1)S(1)}, u32[]{:S(2)}, u32[]{:S(2)}) collective-permute-start(bf16[512,256]{1,0:T(8,128)(2,1)S(1)} %collective-permute-done.20.refs_8_), channel_id=1, source_target_pairs={{0,8},{4,12},{8,16},{12,20},{16,24},{20,28},{1,9},{5,13},{9,17},{1... | collective-permute-start | bytes 786440 | tf_op jit(solution)/shard_map/ppermute | solution.py:273
  37.0 51.9 %collective-permute-start.14 = (bf16[512,1024]{1,0:T(8,128)(2,1)}, bf16[512,1024]{1,0:T(8,128)(2,1)}, u32[]{:S(2)}, u32[]{:S(2)}) collective-permute-start(bf16[512,1024]{1,0:T(8,128)(2,1)} %constant_dynamic-slice_fusion.2.refs_8_), channel_id=1, source_target_pairs={{0,8},{4,12},{8,16},{12,20},{16,24},{20,28},{1,9},{5,13},{9,17},{1... | collective-permute-start | bytes 3145736 | tf_op jit(solution)/shard_map/ppermute | solution.py:273
  41.5 48.1 %collective-permute-start.17 = (bf16[512,1024]{1,0:T(8,128)(2,1)}, bf16[512,1024]{1,0:T(8,128)(2,1)}, u32[]{:S(2)}, u32[]{:S(2)}) collective-permute-start(bf16[512,1024]{1,0:T(8,128)(2,1)} %constant_dynamic-slice_fusion.2.refs_8_), channel_id=1, source_target_pairs={{8,0},{12,4},{16,8},{20,12},{24,16},{28,20},{9,1},{13,5},{17,9},{2... | collective-permute-start | bytes 3145736 | tf_op jit(solution)/shard_map/ppermute | solution.py:274
  44.2 36.5 %collective-permute-start.24 = (bf16[512,256]{1,0:T(8,128)(2,1)S(1)}, bf16[512,256]{1,0:T(8,128)(2,1)}, u32[]{:S(2)}, u32[]{:S(2)}) collective-permute-start(bf16[512,256]{1,0:T(8,128)(2,1)S(1)} %collective-permute-done.20.refs_8_), channel_id=1, source_target_pairs={{8,0},{12,4},{16,8},{20,12},{24,16},{28,20},{9,1},{13,5},{17,9},{2... | collective-permute-start | bytes 786440 | tf_op jit(solution)/shard_map/ppermute | solution.py:274
  45.5 35.3 %collective-permute-start.8 = (bf16[512,640]{1,0:T(8,128)(2,1)}, bf16[512,640]{1,0:T(8,128)(2,1)}, u32[]{:S(2)}, u32[]{:S(2)}) collective-permute-start(bf16[512,640]{1,0:T(8,128)(2,1)} %collective-permute-done.7.refs_8_), channel_id=1, source_target_pairs={{0,8},{4,12},{8,16},{12,20},{16,24},{20,28},{1,9},{5,13},{9,17},{1... | collective-permute-start | bytes 1966088 | tf_op jit(solution)/shard_map/ppermute | solution.py:273
  51.5 36.1 %collective-permute-start.11 = (bf16[512,640]{1,0:T(8,128)(2,1)}, bf16[512,640]{1,0:T(8,128)(2,1)}, u32[]{:S(2)}, u32[]{:S(2)}) collective-permute-start(bf16[512,640]{1,0:T(8,128)(2,1)} %collective-permute-done.7.refs_8_), channel_id=1, source_target_pairs={{8,0},{12,4},{16,8},{20,12},{24,16},{28,20},{9,1},{13,5},{17,9},{2... | collective-permute-start | bytes 1966088 | tf_op jit(solution)/shard_map/ppermute | solution.py:274
  80.7 26.8 %collective-permute-start.3 = (bf16[512,1024]{1,0:T(8,128)(2,1)S(1)}, bf16[512,1024]{1,0:T(8,128)(2,1)}, u32[]{:S(2)}, u32[]{:S(2)}) collective-permute-start(bf16[512,1024]{1,0:T(8,128)(2,1)S(1)} %attend.1.refs_0_), channel_id=1, source_target_pairs={{0,4},{4,0},{8,12},{12,8},{16,20},{20,16},{24,28},{28,24},{1,5},{5... | collective-permute-start | bytes 3145736 | tf_op jit(solution)/shard_map/ppermute | solution.py:292
  87.6 19.9 %collective-permute-start.12 = (bf16[512,640]{1,0:T(8,128)(2,1)}, bf16[512,640]{1,0:T(8,128)(2,1)}, u32[]{:S(2)}, u32[]{:S(2)}) collective-permute-start(bf16[512,640]{1,0:T(8,128)(2,1)} %collective-permute-done.11.refs_12_), channel_id=1, source_target_pairs={{8,0},{12,4},{16,8},{20,12},{9,1},{13,5},{17,9},{21,13},{10,2},{14... | collective-permute-start | bytes 1966088 | tf_op jit(solution)/shard_map/ppermute | solution.py:274
  88.9 19.9 %collective-permute-start.15 = (bf16[512,1024]{1,0:T(8,128)(2,1)}, bf16[512,1024]{1,0:T(8,128)(2,1)S(1)}, u32[]{:S(2)}, u32[]{:S(2)}) collective-permute-start(bf16[512,1024]{1,0:T(8,128)(2,1)} %collective-permute-done.14.refs_9_), channel_id=1, source_target_pairs={{8,16},{12,20},{16,24},{20,28},{9,17},{13,21},{17,25},{21,29},{10,... | collective-permute-start | bytes 3145736 | tf_op jit(solution)/shard_map/ppermute | solution.py:273
  89.6 37.4 %collective-permute-start.18 = (bf16[512,1024]{1,0:T(8,128)(2,1)}, bf16[512,1024]{1,0:T(8,128)(2,1)S(1)}, u32[]{:S(2)}, u32[]{:S(2)}) collective-permute-start(bf16[512,1024]{1,0:T(8,128)(2,1)} %collective-permute-done.17.refs_12_), channel_id=1, source_target_pairs={{8,0},{12,4},{16,8},{20,12},{9,1},{13,5},{17,9},{21,13},{10,2},{14... | collective-permute-start | bytes 3145736 | tf_op jit(solution)/shard_map/ppermute | solution.py:274
  90.9 38.4 %collective-permute-start.1 = (bf16[512,1024]{1,0:T(8,128)(2,1)S(1)}, bf16[512,1024]{1,0:T(8,128)(2,1)}, u32[]{:S(2)}, u32[]{:S(2)}) collective-permute-start(bf16[512,1024]{1,0:T(8,128)(2,1)S(1)} %attend.1.refs_0_), channel_id=1, source_target_pairs={{0,2},{1,3},{2,0},{3,1},{4,6},{5,7},{6,4},{7,5},{8,10},{9,11},{10,... | collective-permute-start | bytes 3145736 | tf_op jit(solution)/shard_map/ppermute | solution.py:291
  107.5 21.9 %collective-permute-start = (bf16[512,1024]{1,0:T(8,128)(2,1)S(1)}, bf16[512,1024]{1,0:T(8,128)(2,1)S(1)}, u32[]{:S(2)}, u32[]{:S(2)}) collective-permute-start(bf16[512,1024]{1,0:T(8,128)(2,1)S(1)} %attend.1.refs_0_), channel_id=1, source_target_pairs={{0,1},{1,0},{2,3},{3,2},{4,5},{5,4},{6,7},{7,6},{8,9},{9,8},{10,11... | collective-permute-start | bytes 3145736 | tf_op jit(solution)/shard_map/ppermute | solution.py:294
  107.5 29.4 %collective-permute-start.5 = (bf16[512,1024]{1,0:T(8,128)(2,1)}, bf16[512,1024]{1,0:T(8,128)(2,1)}, u32[]{:S(2)}, u32[]{:S(2)}) collective-permute-start(bf16[512,1024]{1,0:T(8,128)(2,1)} %collective-permute-done.3.refs_4_), channel_id=1, source_target_pairs={{0,2},{1,3},{2,0},{3,1},{4,6},{5,7},{6,4},{7,5},{8,10},{9,11},{10,... | collective-permute-start | bytes 3145736 | tf_op jit(solution)/shard_map/ppermute | solution.py:293
  108.8 28.1 %collective-permute-start.16 = (bf16[512,1024]{1,0:T(8,128)(2,1)S(1)}, bf16[512,1024]{1,0:T(8,128)(2,1)S(1)}, u32[]{:S(2)}, u32[]{:S(2)}) collective-permute-start(bf16[512,1024]{1,0:T(8,128)(2,1)S(1)} %collective-permute-done.15.refs_10_), channel_id=1, source_target_pairs={{16,24},{20,28},{17,25},{21,29},{18,26},{22,30},{19,27},{23,31}} | collective-permute-start | bytes 3145736 | tf_op jit(solution)/shard_map/ppermute | solution.py:273
  127.1 24.4 %collective-permute-start.19 = (bf16[512,1024]{1,0:T(8,128)(2,1)S(1)}, bf16[512,1024]{1,0:T(8,128)(2,1)S(1)}, u32[]{:S(2)}, u32[]{:S(2)}) collective-permute-start(bf16[512,1024]{1,0:T(8,128)(2,1)S(1)} %collective-permute-done.18.refs_13_), channel_id=1, source_target_pairs={{8,0},{12,4},{9,1},{13,5},{10,2},{14,6},{11,3},{15,7}} | collective-permute-start | bytes 3145736 | tf_op jit(solution)/shard_map/ppermute | solution.py:274
  129.3 24.5 %collective-permute-start.4 = (bf16[512,1024]{1,0:T(8,128)(2,1)}, bf16[512,1024]{1,0:T(8,128)(2,1)}, u32[]{:S(2)}, u32[]{:S(2)}) collective-permute-start(bf16[512,1024]{1,0:T(8,128)(2,1)} %collective-permute-done.3.refs_4_), channel_id=1, source_target_pairs={{0,1},{1,0},{2,3},{3,2},{4,5},{5,4},{6,7},{7,6},{8,9},{9,8},{10,11... | collective-permute-start | bytes 3145736 | tf_op jit(solution)/shard_map/ppermute | solution.py:295
  130.3 25.2 %collective-permute-start.2 = (bf16[512,1024]{1,0:T(8,128)(2,1)}, bf16[512,1024]{1,0:T(8,128)(2,1)}, u32[]{:S(2)}, u32[]{:S(2)}) collective-permute-start(bf16[512,1024]{1,0:T(8,128)(2,1)} %collective-permute-done.1.refs_2_), channel_id=1, source_target_pairs={{0,1},{1,0},{2,3},{3,2},{4,5},{5,4},{6,7},{7,6},{8,9},{9,8},{10,11... | collective-permute-start | bytes 3145736 | tf_op jit(solution)/shard_map/ppermute | solution.py:294
  136.9 19.2 %collective-permute-start.6 = (bf16[512,1024]{1,0:T(8,128)(2,1)}, bf16[512,1024]{1,0:T(8,128)(2,1)}, u32[]{:S(2)}, u32[]{:S(2)}) collective-permute-start(bf16[512,1024]{1,0:T(8,128)(2,1)} %collective-permute-done.5.refs_6_), channel_id=1, source_target_pairs={{0,1},{1,0},{2,3},{3,2},{4,5},{5,4},{6,7},{7,6},{8,9},{9,8},{10,11... | collective-permute-start | bytes 3145736 | tf_op jit(solution)/shard_map/ppermute | solution.py:295
  138.0 33.9 %collective-permute-start.10 = (bf16[512,640]{1,0:T(8,128)(2,1)}, bf16[512,640]{1,0:T(8,128)(2,1)}, u32[]{:S(2)}, u32[]{:S(2)}) collective-permute-start(bf16[512,640]{1,0:T(8,128)(2,1)} %collective-permute-done.9.refs_10_), channel_id=1, source_target_pairs={{16,24},{20,28},{17,25},{21,29},{18,26},{22,30},{19,27},{23,31}} | collective-permute-start | bytes 1966088 | tf_op jit(solution)/shard_map/ppermute | solution.py:273
  152.4 19.4 %collective-permute-start.13 = (bf16[512,640]{1,0:T(8,128)(2,1)}, bf16[512,640]{1,0:T(8,128)(2,1)}, u32[]{:S(2)}, u32[]{:S(2)}) collective-permute-start(bf16[512,640]{1,0:T(8,128)(2,1)} %collective-permute-done.12.refs_13_), channel_id=1, source_target_pairs={{8,0},{12,4},{9,1},{13,5},{10,2},{14,6},{11,3},{15,7}} | collective-permute-start | bytes 1966088 | tf_op jit(solution)/shard_map/ppermute | solution.py:274
  153.9 26.1 %collective-permute-start.27 = (bf16[512,128]{1,0:T(8,128)(2,1)S(1)}, bf16[512,128]{1,0:T(8,128)(2,1)S(1)}, u32[]{:S(2)}, u32[]{:S(2)}) collective-permute-start(bf16[512,128]{1,0:T(8,128)(2,1)S(1)} %constant_dynamic-slice_fusion), channel_id=1, source_target_pairs={{0,4},{4,0},{8,12},{12,8},{16,20},{20,16},{24,28},{28,24},{1,5},{5... | collective-permute-start | bytes 393224 | tf_op jit(solution)/shard_map/ppermute | solution.py:289
  155.5 32.7 %collective-permute-start.22 = (bf16[512,256]{1,0:T(8,128)(2,1)}, bf16[512,256]{1,0:T(8,128)(2,1)S(1)}, u32[]{:S(2)}, u32[]{:S(2)}) collective-permute-start(bf16[512,256]{1,0:T(8,128)(2,1)} %copy-done.4), channel_id=1, source_target_pairs={{8,16},{12,20},{16,24},{20,28},{9,17},{13,21},{17,25},{21,29},{10,... | collective-permute-start | bytes 786440 | tf_op jit(solution)/shard_map/ppermute | solution.py:273
  156.1 32.7 %collective-permute-start.25 = (bf16[512,256]{1,0:T(8,128)(2,1)}, bf16[512,256]{1,0:T(8,128)(2,1)S(1)}, u32[]{:S(2)}, u32[]{:S(2)}) collective-permute-start(bf16[512,256]{1,0:T(8,128)(2,1)} %collective-permute-done.24.refs_12_), channel_id=1, source_target_pairs={{8,0},{12,4},{16,8},{20,12},{9,1},{13,5},{17,9},{21,13},{10,2},{14... | collective-permute-start | bytes 786440 | tf_op jit(solution)/shard_map/ppermute | solution.py:274
  179.4 40.6 %collective-permute-start.34 = (bf16[512,640]{1,0:T(8,128)(2,1)S(1)}, bf16[512,640]{1,0:T(8,128)(2,1)S(1)}, u32[]{:S(2)}, u32[]{:S(2)}) collective-permute-start(bf16[512,640]{1,0:T(8,128)(2,1)S(1)} %get-tuple-element.20), channel_id=1, source_target_pairs={{0,4},{4,0},{8,12},{12,8},{16,20},{20,16},{24,28},{28,24},{1,5},{5... | collective-permute-start | bytes 1966088 | tf_op jit(solution)/shard_map/ppermute | solution.py:301
  180.0 10.2 %collective-permute-start.28 = (bf16[512,128]{1,0:T(8,128)(2,1)S(1)}, bf16[512,128]{1,0:T(8,128)(2,1)S(1)}, u32[]{:S(2)}, u32[]{:S(2)}) collective-permute-start(bf16[512,128]{1,0:T(8,128)(2,1)S(1)} %collective-permute-done.27.refs_8_), channel_id=1, source_target_pairs={{0,8},{4,12},{8,16},{12,20},{16,24},{20,28},{1,9},{5,13},{9,17},{1... | collective-permute-start | bytes 393224 | tf_op jit(solution)/shard_map/ppermute | solution.py:273
  188.2 15.4 %collective-permute-start.23 = (bf16[512,256]{1,0:T(8,128)(2,1)S(1)}, bf16[512,256]{1,0:T(8,128)(2,1)S(1)}, u32[]{:S(2)}, u32[]{:S(2)}) collective-permute-start(bf16[512,256]{1,0:T(8,128)(2,1)S(1)} %collective-permute-done.22.refs_10_), channel_id=1, source_target_pairs={{16,24},{20,28},{17,25},{21,29},{18,26},{22,30},{19,27},{23,31}} | collective-permute-start | bytes 786440 | tf_op jit(solution)/shard_map/ppermute | solution.py:273
  188.9 14.8 %collective-permute-start.26 = (bf16[512,256]{1,0:T(8,128)(2,1)S(1)}, bf16[512,256]{1,0:T(8,128)(2,1)S(1)}, u32[]{:S(2)}, u32[]{:S(2)}) collective-permute-start(bf16[512,256]{1,0:T(8,128)(2,1)S(1)} %collective-permute-done.25.refs_13_), channel_id=1, source_target_pairs={{8,0},{12,4},{9,1},{13,5},{10,2},{14,6},{11,3},{15,7}} | collective-permute-start | bytes 786440 | tf_op jit(solution)/shard_map/ppermute | solution.py:274
  195.1 14.7 %collective-permute-start.30 = (bf16[512,128]{1,0:T(8,128)(2,1)S(1)}, bf16[512,128]{1,0:T(8,128)(2,1)S(1)}, u32[]{:S(2)}, u32[]{:S(2)}) collective-permute-start(bf16[512,128]{1,0:T(8,128)(2,1)S(1)} %collective-permute-done.29.refs_10_), channel_id=1, source_target_pairs={{16,24},{20,28},{17,25},{21,29},{18,26},{22,30},{19,27},{23,31}} | collective-permute-start | bytes 393224 | tf_op jit(solution)/shard_map/ppermute | solution.py:273
  208.2 11.8 %collective-permute-start.35 = (bf16[512,256]{1,0:T(8,128)(2,1)S(1)}, bf16[512,256]{1,0:T(8,128)(2,1)S(1)}, u32[]{:S(2)}, u32[]{:S(2)}) collective-permute-start(bf16[512,256]{1,0:T(8,128)(2,1)S(1)} %get-tuple-element.21), channel_id=1, source_target_pairs={{0,4},{4,0},{8,12},{12,8},{16,20},{20,16},{24,28},{28,24},{1,5},{5... | collective-permute-start | bytes 786440 | tf_op jit(solution)/shard_map/ppermute | solution.py:301
  (29 other events, 228.3 us)

commit v2 on v0

--- a/solution.py
+++ b/solution.py
@@ -96,9 +96,9 @@
             pltpu.VMEM((heads, 1, rows), jnp.float32),
             pltpu.VMEM((heads, HEAD_SIZE, rows), jnp.float32),
         ],
-        compiler_params=pltpu.CompilerParams(vmem_limit_bytes=40 << 20),
+        compiler_params=pltpu.CompilerParams(vmem_limit_bytes=16 << 20),
         cost_estimate=pl.CostEstimate(
-            flops=4 * rows * width * 16 * KEY_BLOCK_TOKENS,
+            flops=24 * rows * width * 16 * KEY_BLOCK_TOKENS,
             transcendentals=rows * heads * 16 * KEY_BLOCK_TOKENS,
             bytes_accessed=2 * (3 * rows * width + kv.size),
         ),
@@ -121,71 +121,238 @@
     )
 
 
-def ring_of(pb_size):
-    if pb_size == 8:
-        return [0, 2, 4, 6, 7, 5, 3, 1]
-    return list(range(pb_size))
-
-
-def project_ring(attn, wo):
-    pb_size = lax.axis_size("pb")
+def collect_copies(z, me, column, own_rows, other_rows, slabs, left, right, sems, start=0):
+    rows, depth = left.shape[0] // 2, left.shape[1] // 4
+
+    def left_copy(target, slot, side):
+        source = (own_rows, other_rows)[side][slot]
+        return pltpu.make_async_copy(
+            source.at[:, pl.ds(column, depth)],
+            left.at[pl.ds(side * rows, rows), pl.ds(target * depth, depth)],
+            sems.at[target, side],
+        )
+
+    def slab_copy(target, slot):
+        width = right.shape[1]
+        source = slabs[slot]
+        if source.shape[1] != width:
+            source = source.at[:, pl.ds(start, width)]
+        return pltpu.make_async_copy(
+            source, right.at[pl.ds(target * depth, depth), :], sems.at[target, 2]
+        )
+
+    for target in range(4):
+        if own_rows is not None:
+            slot_here = jnp.bitwise_xor(me, target)
+            for slot in range(4):
+
+                @pl.when(slot_here == slot)
+                def _(slot=slot):
+                    left_copy(target, slot, 0).start()
+                    left_copy(target, slot, 1).start()
+
+        if slabs is not None:
+            for position in range(4):
+
+                @pl.when(z == position)
+                def _(position=position):
+                    distance = target - position
+                    slab_copy(target, -distance if distance <= 0 else 3 + distance).start()
+
+    def wait():
+        for target in range(4):
+            if own_rows is not None:
+                left_copy(target, 0, 0).wait()
+                left_copy(target, 0, 1).wait()
+            if slabs is not None:
+                slab_copy(target, 0).wait()
+
+    return wait
+
+
+ROW_TILE = 256
+
+
+def first_kernel(chunks, place_ref, *refs):
+    z, y, me = place_ref[0], place_ref[1], place_ref[2]
+    own_rows, other_rows, slabs, refs = refs[:4], refs[4:8], refs[8:15], refs[15:]
+    outs, spare, left, right, sems, spare_sems = (
+        refs[: len(chunks)],
+        *refs[len(chunks) : len(chunks) + 5],
+    )
+    depth = right.shape[0] // 4
+    own_column = pl.multiple_of(y * depth, depth)
+    other_column = pl.multiple_of((1 - y) * depth, depth)
+    wait = collect_copies(z, me, own_column, own_rows, other_rows, slabs, left, right, sems)
+    wait_spare = collect_copies(
+        z, me, other_column, own_rows, other_rows, None, spare, None, spare_sems
+    )
+    wait()
+
+    def rows_tile(step, carry):
+        at = pl.ds(pl.multiple_of(step * ROW_TILE, ROW_TILE), ROW_TILE)
+        product = jnp.dot(left[at, :], right[...], preferred_element_type=jnp.float32)
+        start = 0
+        for out, chunk in zip(outs, chunks):
+            out[at, :] = product[:, start : start + chunk]
+            start += chunk
+        return carry
+
+    lax.fori_loop(0, left.shape[0] // ROW_TILE, rows_tile, 0)
+    wait_spare()
+
+
+def rest_kernel(start, place_ref, left, base_ref, *refs):
+    slabs, (own_out, other_out, right, sems) = refs[:7], refs[7:]
+    rows = own_out.shape[0]
+    wait = collect_copies(
+        place_ref[0], place_ref[2], 0, None, None, slabs, left, right, sems, start
+    )
+    wait()
+
+    def rows_tile(step, carry):
+        for out, offset in ((own_out, 0), (other_out, rows)):
+            at = pl.ds(pl.multiple_of(step * ROW_TILE + offset, ROW_TILE), ROW_TILE)
+            product = jnp.dot(left[at, :], right[...], preferred_element_type=jnp.float32)
+            out[pl.ds(pl.multiple_of(step * ROW_TILE, ROW_TILE), ROW_TILE), :] = (
+                product + base_ref[at, :]
+            ).astype(jnp.bfloat16)
+        return carry
+
+    lax.fori_loop(0, rows // ROW_TILE, rows_tile, 0)
+
+
+IN_HBM = pl.BlockSpec(memory_space=pltpu.HBM)
+IN_VMEM = pl.BlockSpec(memory_space=pltpu.VMEM)
+IN_SMEM = pl.BlockSpec(memory_space=pltpu.SMEM)
+
+
+def first_product(where, own_rows, other_rows, slabs, chunks):
+    rows = own_rows[0].shape[0]
+    depth, columns = slabs[0].shape
+    return pl.pallas_call(
+        functools.partial(first_kernel, chunks),
+        out_shape=[jax.ShapeDtypeStruct((2 * rows, chunk), jnp.float32) for chunk in chunks]
+        + [jax.ShapeDtypeStruct((2 * rows, 4 * depth), jnp.bfloat16)],
+        in_specs=[IN_SMEM] + [IN_HBM] * 15,
+        out_specs=[IN_VMEM] * (len(chunks) + 1),
+        scratch_shapes=[
+            pltpu.VMEM((2 * rows, 4 * depth), jnp.bfloat16),
+            pltpu.VMEM((4 * depth, columns), jnp.bfloat16),
+            pltpu.SemaphoreType.DMA((4, 3)),
+            pltpu.SemaphoreType.DMA((4, 2)),
+        ],
+        compiler_params=pltpu.CompilerParams(vmem_limit_bytes=14 << 20),
+        cost_estimate=pl.CostEstimate(
+            flops=2 * 2 * rows * 4 * depth * columns,
+            transcendentals=0,
+            bytes_accessed=2 * (4 * rows * 4 * depth + 4 * depth * columns) + 8 * rows * columns,
+        ),
+        name="first_product",
+    )(where, *own_rows, *other_rows, *slabs)
+
+
+def rest_product(where, left, base, slabs, start):
+    rows = left.shape[0] // 2
+    depth = slabs[0].shape[0]
+    columns = base.shape[1]
+    return pl.pallas_call(
+        functools.partial(rest_kernel, start),
+        out_shape=[jax.ShapeDtypeStruct((rows, columns), jnp.bfloat16)] * 2,
+        in_specs=[IN_SMEM, IN_VMEM, IN_VMEM] + [IN_HBM] * 7,
+        out_specs=[IN_VMEM] * 2,
+        scratch_shapes=[
+            pltpu.VMEM((4 * depth, columns), jnp.bfloat16),
+            pltpu.SemaphoreType.DMA((4, 3)),
+        ],
+        compiler_params=pltpu.CompilerParams(vmem_limit_bytes=8 << 20),
+        cost_estimate=pl.CostEstimate(
+            flops=2 * 2 * rows * 4 * depth * columns,
+            transcendentals=0,
+            bytes_accessed=2 * 4 * depth * columns + 8 * rows * columns,
+        ),
+        name="rest_product",
+    )(where, left, base, *slabs)
+
+
+UP = [[(i, i + 2) for i in range(2 * s, 6)] for s in range(3)]
+DOWN = [[(i + 2, i) for i in range(6 - 2 * s)] for s in range(3)]
+ACROSS_Y = [(i, i ^ 1) for i in range(8)]
+ACROSS_X = [(i, i ^ 2) for i in range(4)]
+ACROSS_CORE = [(i, i ^ 1) for i in range(4)]
+
+
+def project(where, wo, inputs, attend_with):
+    y = where[1]
     depth, columns = wo.shape
-    ring = ring_of(pb_size)
-    place_of = [ring.index(p) for p in range(pb_size)]
-    forward = [(ring[i], ring[(i + 1) % pb_size]) for i in range(pb_size)]
-    backward = [(b, a) for a, b in forward]
-    here = jnp.asarray(place_of, jnp.int32)[lax.axis_index("pb")]
-    order = jnp.asarray(ring, jnp.int32)
     half = columns // 2
-    far = pb_size // 2
-    slabs = [[(0, wo[:, :half])], [(0, wo[:, half:])]]
-    moving = [[slabs[0][0][1]] * 2, [slabs[1][0][1]] * 2]
-    for hop in range(1, far + 1):
-        for part in range(2):
-            if hop < far or part == 0:
-                moving[part][0] = lax.ppermute(moving[part][0], "pb", forward)
-                slabs[part].append((-hop, moving[part][0]))
-            if hop < far or part == 1:
-                moving[part][1] = lax.ppermute(moving[part][1], "pb", backward)
-                slabs[part].append((hop, moving[part][1]))
-    attn_blocks = attn
-    results = []
-    for part in range(2):
-        total = None
-        for offset, slab in slabs[part]:
-            source = order[(here + offset + pb_size) % pb_size]
-            left = attn_blocks(source)
-            term = jnp.dot(left, slab, preferred_element_type=jnp.float32)
-            total = term if total is None else total + term
-        results.append(total.astype(jnp.bfloat16))
-    return jnp.concatenate(results, axis=1)
+    chunks = (half * 5 // 8, half // 4, half // 8)
+    starts = (0, chunks[0], chunks[0] + chunks[1])
+
+    def up(piece, hop):
+        return lax.ppermute(piece, "pb", UP[hop])
+
+    def down(piece, hop):
+        return lax.ppermute(piece, "pb", DOWN[hop])
+
+    def other_core(piece):
+        return lax.ppermute(piece, "ka", ACROSS_CORE)
+
+    kept = lax.dynamic_slice(wo, (0, y * half), (depth, half))
+    given = lax.dynamic_slice(wo, (0, (1 - y) * half), (depth, half))
+    taken = lax.ppermute(given, "pb", ACROSS_Y)
+    kept_up, kept_down = [up(kept, 0)], [down(kept, 0)]
+    taken_up, taken_down = [up(taken, 0)], [down(taken, 0)]
+    kept_up.append(up(kept_up[0], 1))
+    kept_down.append(down(kept_down[0], 1))
+    inputs, taken_up[0], taken_down[0] = lax.optimization_barrier(
+        (inputs, taken_up[0], taken_down[0])
+    )
+    taken_up.append(up(taken_up[0], 1))
+    taken_down.append(down(taken_down[0], 1))
+    attn = attend_with(inputs)
+    attn, kept_up[1], kept_down[1] = lax.optimization_barrier((attn, kept_up[1], kept_down[1]))
+    kept_up.append(up(kept_up[1], 2))
+    kept_down.append(down(kept_down[1], 2))
+    across_y = lax.ppermute(attn, "pb", ACROSS_Y)
+    across_x = lax.ppermute(attn, "ka", ACROSS_X)
+    across_y, across_x, taken_up[1], taken_down[1] = lax.optimization_barrier(
+        (across_y, across_x, taken_up[1], taken_down[1])
+    )
+    last = []
+    for chunk, start in zip(chunks, starts):
+        piece = [taken_up[1][:, start : start + chunk], taken_down[1][:, start : start + chunk]]
+        last.append((up(piece[0], 2), down(piece[1], 2)))
+    corner = lax.ppermute(across_y, "ka", ACROSS_X)
+    own_rows = [attn, other_core(attn), across_x, other_core(across_x)]
+    other_rows = [across_y, other_core(across_y), corner, other_core(corner)]
+    *bases, left = first_product(
+        where, own_rows, other_rows, [kept] + kept_up + kept_down, chunks
+    )
+    own_out, received = [], []
+    for base, start, (last_up, last_down) in zip(bases, starts, last):
+        slabs = [taken] + taken_up + [last_up] + taken_down + [last_down]
+        own, other = rest_product(where, left, base, slabs, start)
+        own_out.append(own)
+        received.append(lax.ppermute(other, "pb", ACROSS_Y))
+    first_half = [jnp.where(y == 0, a, b) for a, b in zip(own_out, received)]
+    second_half = [jnp.where(y == 0, b, a) for a, b in zip(own_out, received)]
+    return jnp.concatenate(first_half + second_half, axis=1)
 
 
 def shards(queries, keys, values, block_ids, counts, refresh, cached_attn, wo):
     groups = lax.axis_size("ka")
     pb_size = lax.axis_size("pb")
     me = lax.axis_index("ka")
-    width = QUERY_HEAD_COUNT * HEAD_SIZE
-    depth = wo.shape[0]
     kv = own_head_keys_values(keys, values, groups)
     meta = jnp.concatenate([counts[0], refresh[0], block_ids[0, 0]])
-    attn = attend(meta, queries[0], kv, cached_attn[0])
+    inputs = (meta, queries[0], kv, cached_attn[0])
     if pb_size == 8 and groups == 4:
-        across = lax.ppermute(attn, "ka", [(i, i ^ 2) for i in range(4)])
-        beside = lax.ppermute(attn, "ka", [(i, i ^ 1) for i in range(4)])
-        corner = lax.ppermute(across, "ka", [(i, i ^ 1) for i in range(4)])
-        pieces = jnp.stack([attn, beside, across, corner])
-        per = attn.shape[1] // depth
-
-        def block(source):
-            slot = jnp.bitwise_xor(source // per, me)
-            return lax.dynamic_slice(
-                pieces, (slot, 0, (source % per) * depth), (1, attn.shape[0], depth)
-            )[0]
-
-        mixed = project_ring(block, wo)
+        pb = lax.axis_index("pb")
+        where = jnp.stack([pb // 2, pb % 2, me]).astype(jnp.int32)
+        mixed = project(where, wo, inputs, lambda values: attend(*values))
     else:
-        attn_full = lax.all_gather(attn, "ka", axis=1, tiled=True)
+        attn_full = lax.all_gather(attend(*inputs), "ka", axis=1, tiled=True)
         mixed = jnp.dot(
             attn_full, lax.all_gather(wo, "pb", axis=0, tiled=True), preferred_element_type=jnp.float32
         ).astype(jnp.bfloat16)

time: 193 us -> 214 us (1.11); the launches traced: 191 us -> 215 us
  Pallas kernels: 0.62 us -> 47 us
  between operations: 30 us -> 1.74 us
  matrix products: 24.8 us -> 0 us
  starting transfers between devices: 20.8 us -> 39.9 us
  local copies, waits for them, and re-layouts: 9.56 us -> 27.7 us
  waiting for transfers between devices: 100 us -> 95.4 us
    dot_general x16 -> x0, matrix products: 24.8 us -> none  [project_ring(): term = jnp.dot(left, slab, preferred_element_type=jnp.float32)]
    pallas_call x1, Pallas kernels: 0.62 us -> 25.4 us  [attend(): pl.pallas_call(functools.partial(attention_kernel, heads), out_shape=jax....]
    pallas_call x0 -> x4, Pallas kernels: none -> 21.7 us  [the longest x3 13 us: rest_product(): pl.pallas_call(functools.partial(rest_kernel, start), out_shape=[jax.Shap...]
    ppermute x17 -> x27, starting transfers between devices: 16.6 us -> 35.3 us  [the longest x8 15.1 us: up(): return lax.ppermute(piece, 'pb', UP[hop])]
    unnamed x16 -> x58, local copies, waits for them, and re-layouts: 3.96 us -> 19.8 us
    ppermute x17 -> x27, waiting for transfers between devices: 100 us -> 95.4 us  [the longest x8 24.4 us: down(): return lax.ppermute(piece, 'pb', DOWN[hop])]
    another operation x1, other arithmetic: 2.26 us -> 0.08 us  [shards(): where = jnp.stack([pb // 2, pb % 2, me]).astype(jnp.int32)]
    slice x1 -> x6, local copies, waits for them, and re-layouts: 2.71 us -> 4.68 us  [the longest x3 2.35 us: project(): taken_up[1][:, start:start + chunk]]
  transfers between devices with their start and end apart: 18 -> 28, of which waited for: 7 -> 13; matrix products, arithmetic and copies ran while one was open for 16% -> 3% of each run, Pallas kernels for 0% -> 19%
where the time goes in v2:
time: 214 us; the launch traced here: 215 us
  waiting for transfers between devices  95.4 us (45%)
  Pallas kernels  47 us (22%)
  starting transfers between devices  39.9 us (19%)
  local copies, waits for them, and re-layouts  27.7 us (13%)
  other arithmetic  3.44 us (2%)
    pallas_call x1, Pallas kernels, attend(): pl.pallas_call(functools.partial(attention_kernel, heads), out_shape=jax....  25.4 us
    ppermute x8, waiting for transfers between devices, down(): return lax.ppermute(piece, 'pb', DOWN[hop])  24.4 us
    unnamed x58, local copies, waits for them, and re-layouts  19.8 us
    ppermute x1, waiting for transfers between devices, project(): across_y = lax.ppermute(attn, 'pb', ACROSS_Y)  18.9 us
    ppermute x8, waiting for transfers between devices, up(): return lax.ppermute(piece, 'pb', UP[hop])  18.5 us
    ppermute x1, waiting for transfers between devices, project(): corner = lax.ppermute(across_y, 'ka', ACROSS_X)  17.5 us
    ppermute x8, starting transfers between devices, up(): return lax.ppermute(piece, 'pb', UP[hop])  15.1 us
    pallas_call x3, Pallas kernels, rest_product(): pl.pallas_call(functools.partial(rest_kernel, start), out_shape=[jax.Shap...  13 us
  transfers between devices with their start and end apart: 28, of which 13 were waited for; matrix products, arithmetic and copies ran while one was open for 3% of the time, Pallas kernels for 19%

profile of v2, /device:TPU:0, one launch (start us, length us, event | category | flops | bytes accessed | tf_op | source)
XLA Modules:
  0.0 215.2 jit_solution(4029076240690007824)
XLA Ops:
  0.0 2.8 %constant_dynamic-slice_fusion = (bf16[512,1024]{1,0:T(8,128)(2,1)}, bf16[512,1024]{1,0:T(8,128)(2,1)S(1)}) fusion(bf16[512,2048]{1,0:T(8,128)(2,1)} %param.15, s32[]{:T(128)S(6)} %select_n.57, s32[]{:T(128)S(6)} %select_n.56), kind=kLoop, calls=%fused_computation.11 | loop fusion | bytes 4194312 | tf_op jit(solution)/shard_map/dynamic_slice | solution.py:301
  2.8 3.0 %collective-permute-start = (bf16[512,1024]{1,0:T(8,128)(2,1)S(1)}, bf16[512,1024]{1,0:T(8,128)(2,1)S(1)}, u32[]{:S(2)}, u32[]{:S(2)}) collective-permute-start(bf16[512,1024]{1,0:T(8,128)(2,1)S(1)} %get-tuple-element.52), channel_id=1, source_target_pairs={{0,4},{4,0},{8,12},{12,8},{16,20},{20,16},{24,28},{28,24},{1,5},{5... | collective-permute-start | bytes 3145736 | tf_op jit(solution)/shard_map/ppermute | solution.py:303
  6.2 1.5 pad_maximum_fusion
  7.7 4.6 %all-to-all-start = ((bf16[1024,4,256]{2,0,1:T(8,128)(2,1)}), bf16[1024,4,256]{2,0,1:T(8,128)(2,1)}, u32[]{:S(2)}, u32[]{:S(2)}) async-start(bf16[1024,4,256]{2,0,1:T(8,128)(2,1)} %pad_maximum_fusion), calls=%async_computation | async-start | bytes 4194304 | tf_op jit(solution)/shard_map/all_to_all | solution.py:119
  12.3 4.5 %collective-permute-start.3 = (bf16[512,1024]{1,0:T(8,128)(2,1)}, bf16[512,1024]{1,0:T(8,128)(2,1)}, u32[]{:S(2)}, u32[]{:S(2)}) collective-permute-start(bf16[512,1024]{1,0:T(8,128)(2,1)} %get-tuple-element.51.refs_8_), channel_id=1, source_target_pairs={{0,8},{4,12},{8,16},{12,20},{16,24},{20,28},{1,9},{5,13},{9,17},{1... | collective-permute-start | bytes 3145736 | tf_op jit(solution)/shard_map/ppermute | solution.py:293
  18.1 10.9 %collective-permute-done.refs_0_ = bf16[512,1024]{1,0:T(8,128)(2,1)S(1)} collective-permute-done((bf16[512,1024]{1,0:T(8,128)(2,1)S(1)}, bf16[512,1024]{1,0:T(8,128)(2,1)S(1)}, u32[]{:S(2)}, u32[]{:S(2)}) %collective-permute-start) | collective-permute-done | bytes 1048608 | tf_op jit(solution)/shard_map/ppermute | solution.py:303
  29.0 4.7 %collective-permute-start.1 = (bf16[512,1024]{1,0:T(8,128)(2,1)S(1)}, bf16[512,1024]{1,0:T(8,128)(2,1)}, u32[]{:S(2)}, u32[]{:S(2)}) collective-permute-start(bf16[512,1024]{1,0:T(8,128)(2,1)S(1)} %collective-permute-done.refs_0_), channel_id=1, source_target_pairs={{0,8},{4,12},{8,16},{12,20},{16,24},{20,28},{1,9},{5,13},{9,17},{1... | collective-permute-start | bytes 3145736 | tf_op jit(solution)/shard_map/ppermute | solution.py:293
  36.4 3.3 %collective-permute-done.3.refs_9_ = bf16[512,1024]{1,0:T(8,128)(2,1)} collective-permute-done((bf16[512,1024]{1,0:T(8,128)(2,1)}, bf16[512,1024]{1,0:T(8,128)(2,1)}, u32[]{:S(2)}, u32[]{:S(2)}) %collective-permute-start.3) | collective-permute-done | bytes 1048608 | tf_op jit(solution)/shard_map/ppermute | solution.py:293
  39.6 1.6 collective-permute-start.4
  41.2 3.8 %collective-permute-done.5.refs_12_ = bf16[512,1024]{1,0:T(8,128)(2,1)} collective-permute-done((bf16[512,1024]{1,0:T(8,128)(2,1)}, bf16[512,1024]{1,0:T(8,128)(2,1)}, u32[]{:S(2)}, u32[]{:S(2)}) %collective-permute-start.5) | collective-permute-done | bytes 1048608 | tf_op jit(solution)/shard_map/ppermute | solution.py:296
  46.3 15.2 %collective-permute-done.1.refs_1_ = bf16[512,1024]{1,0:T(8,128)(2,1)} collective-permute-done((bf16[512,1024]{1,0:T(8,128)(2,1)S(1)}, bf16[512,1024]{1,0:T(8,128)(2,1)}, u32[]{:S(2)}, u32[]{:S(2)}) %collective-permute-start.1) | collective-permute-done | bytes 1048608 | tf_op jit(solution)/shard_map/ppermute | solution.py:293
  61.5 5.9 %collective-permute-done.2.refs_4_ = bf16[512,1024]{1,0:T(8,128)(2,1)S(1)} collective-permute-done((bf16[512,1024]{1,0:T(8,128)(2,1)S(1)}, bf16[512,1024]{1,0:T(8,128)(2,1)S(1)}, u32[]{:S(2)}, u32[]{:S(2)}) %collective-permute-start.2) | collective-permute-done | bytes 1048608 | tf_op jit(solution)/shard_map/ppermute | solution.py:296
  67.4 1.6 copy-done.16
  70.2 25.4 %attend.1.refs_0_ = bf16[512,1024]{1,0:T(8,128)(2,1)S(1)} custom-call(s32[18]{0:T(128)S(1)} %pad_add_fusion.1.meta_ref, bf16[512,1024]{1,0:T(8,128)(2,1)S(1)} %bitcast.24, bf16[4096,256]{1,0:T(8,128)(2,1)} %bitcast.8.kv_ref, bf16[512,1024]{1,0:T(8,128)(2,1)S(1)} %bitcast.25), custom_call_target="tpu_custom_call" | custom-call | flops 25769803776 | bytes 5242880 | tf_op jit(solution)/shard_map/attend/pallas_call | solution.py:89
  95.7 2.1 collective-permute-start.9
  100.5 18.9 %collective-permute-done.8.refs_4_ = bf16[512,1024]{1,0:T(8,128)(2,1)} collective-permute-done((bf16[512,1024]{1,0:T(8,128)(2,1)S(1)}, bf16[512,1024]{1,0:T(8,128)(2,1)}, u32[]{:S(2)}, u32[]{:S(2)}) %collective-permute-start.8) | collective-permute-done | bytes 1048608 | tf_op jit(solution)/shard_map/ppermute | solution.py:317
  119.5 3.8 %collective-permute-done.11.refs_5_ = bf16[512,1024]{1,0:T(8,128)(2,1)S(1)} collective-permute-done((bf16[512,1024]{1,0:T(8,128)(2,1)}, bf16[512,1024]{1,0:T(8,128)(2,1)S(1)}, u32[]{:S(2)}, u32[]{:S(2)}) %collective-permute-start.11) | collective-permute-done | bytes 1048608 | tf_op jit(solution)/shard_map/ppermute | solution.py:296
  127.8 17.5 %collective-permute-done.14.refs_6_ = bf16[512,1024]{1,0:T(8,128)(2,1)} collective-permute-done((bf16[512,1024]{1,0:T(8,128)(2,1)}, bf16[512,1024]{1,0:T(8,128)(2,1)}, u32[]{:S(2)}, u32[]{:S(2)}) %collective-permute-start.14) | collective-permute-done | bytes 1048608 | tf_op jit(solution)/shard_map/ppermute | solution.py:326
  149.2 1.5 collective-permute-start.18
  153.2 1.4 copy-done.19
  158.2 8.6 %first_product.1 = (f32[1024,640]{1,0:T(8,128)S(1)}, f32[1024,256]{1,0:T(8,128)S(1)}, f32[1024,128]{1,0:T(8,128)S(1)}, bf16[1024,2048]{1,0:T(8,128)(2,1)S(1)}) custom-call(s32[3]{0:T(128)S(1)} %pad_add_fusion.place_ref, bf16[512,1024]{1,0:T(8,128)(2,1)S(1)} %copy-done.19, bf16[512,1024]{1,0:T(8,128)(2,1)S(1)} %copy-done.25, ...), custom_call_target="tpu_custom_call" | custom-call | flops 4294967296 | bytes 16777216 | tf_op jit(solution)/shard_map/first_product/pallas_call | solution.py:233
  166.9 3.2 %collective-permute-done.19.refs_6_ = bf16[512,640]{1,0:T(8,128)(2,1)} collective-permute-done((bf16[512,640]{1,0:T(8,128)(2,1)}, bf16[512,640]{1,0:T(8,128)(2,1)}, u32[]{:S(2)}, u32[]{:S(2)}) %collective-permute-start.19) | collective-permute-done | bytes 655392 | tf_op jit(solution)/shard_map/ppermute | solution.py:296
  170.1 6.5 %rest_product.3 = (bf16[512,640]{1,0:T(8,128)(2,1)S(1)}, bf16[512,640]{1,0:T(8,128)(2,1)}) custom-call(s32[3]{0:T(128)S(1)} %pad_add_fusion.place_ref, bf16[1024,2048]{1,0:T(8,128)(2,1)S(1)} %get-tuple-element.39.left, f32[1024,640]{1,0:T(8,128)S(1)} %get-tuple-element.40.base_ref, bf16[512,1024]{1,0:T(8,128)(2,1)S(1)} %copy-done.5, ...), custom_call_target="tpu_custom_call" | custom-call | flops 2684354560 | bytes 5242880 | tf_op jit(solution)/shard_map/rest_product/pallas_call | solution.py:259
  177.5 1.4 collective-permute-start.20
  185.7 6.8 %collective-permute-done.25.refs_6_ = bf16[512,128]{1,0:T(8,128)(2,1)} collective-permute-done((bf16[512,128]{1,0:T(8,128)(2,1)}, bf16[512,128]{1,0:T(8,128)(2,1)}, u32[]{:S(2)}, u32[]{:S(2)}) %collective-permute-start.25) | collective-permute-done | bytes 131104 | tf_op jit(solution)/shard_map/ppermute | solution.py:296
  192.5 2.2 %copy-done.2 = bf16[1024,2048]{1,0:T(8,128)(2,1)S(1)} copy-done((bf16[1024,2048]{1,0:T(8,128)(2,1)S(1)}, bf16[1024,2048]{1,0:T(8,128)(2,1)}, u32[]{:S(2)}) %copy-start.2) | copy-done | bytes 4194328
  198.2 3.4 %rest_product.5 = (bf16[512,128]{1,0:T(8,128)(2,1)S(1)}, bf16[512,128]{1,0:T(8,128)(2,1)S(1)}) custom-call(s32[3]{0:T(128)S(1)} %pad_add_fusion.place_ref, bf16[1024,2048]{1,0:T(8,128)(2,1)S(1)} %copy-done.2, f32[1024,128]{1,0:T(8,128)S(1)} %copy-done.15, bf16[512,1024]{1,0:T(8,128)(2,1)S(1)} %copy-done.6, bf16[512,1024]{1,0:T(8,128)(2,1)} %collective-permute-done.1.refs_1_, ...), custom_call_target="tpu_custom_call" | custom-call | flops 536870912 | bytes 1048576 | tf_op jit(solution)/shard_map/rest_product/pallas_call | solution.py:259
  202.4 3.2 %rest_product.4 = (bf16[512,256]{1,0:T(8,128)(2,1)S(1)}, bf16[512,256]{1,0:T(8,128)(2,1)S(1)}) custom-call(s32[3]{0:T(128)S(1)} %pad_add_fusion.place_ref, bf16[1024,2048]{1,0:T(8,128)(2,1)S(1)} %copy-done.3, f32[1024,256]{1,0:T(8,128)S(1)} %copy-done.13, bf16[512,1024]{1,0:T(8,128)(2,1)S(1)} %copy-done.6, bf16[512,1024]{1,0:T(8,128)(2,1)} %collective-permute-done.1.refs_1_, ...), custom_call_target="tpu_custom_call" | custom-call | flops 1073741824 | bytes 2097152 | tf_op jit(solution)/shard_map/rest_product/pallas_call | solution.py:259
  205.5 1.4 collective-permute-start.23
  207.2 5.1 %collective-permute-done.23 = bf16[512,256]{1,0:T(8,128)(2,1)S(1)} collective-permute-done((bf16[512,256]{1,0:T(8,128)(2,1)S(1)}, bf16[512,256]{1,0:T(8,128)(2,1)S(1)}, u32[]{:S(2)}, u32[]{:S(2)}) %collective-permute-start.23) | collective-permute-done | bytes 262176 | tf_op jit(solution)/shard_map/ppermute | solution.py:337
  212.4 1.3 select_dynamic-update-slice_fusion
  213.9 1.3 copy-done.27
  (104 shorter events, 35.2 us)
Async XLA Ops:
  2.8 26.1 %collective-permute-start = (bf16[512,1024]{1,0:T(8,128)(2,1)S(1)}, bf16[512,1024]{1,0:T(8,128)(2,1)S(1)}, u32[]{:S(2)}, u32[]{:S(2)}) collective-permute-start(bf16[512,1024]{1,0:T(8,128)(2,1)S(1)} %get-tuple-element.52), channel_id=1, source_target_pairs={{0,4},{4,0},{8,12},{12,8},{16,20},{20,16},{24,28},{28,24},{1,5},{5... | collective-permute-start | bytes 3145736 | tf_op jit(solution)/shard_map/ppermute | solution.py:303
  7.7 28.5 %copy-start.28 = (s32[1,1,16]{2,1,0:T(1,128)S(1)}, s32[1,1,16]{2,1,0:T(1,128)}, u32[]{:S(2)}) copy-start(s32[1,1,16]{2,1,0:T(1,128)} %param.11) | copy-start | bytes 196
  7.7 38.6 %all-to-all-start = ((bf16[1024,4,256]{2,0,1:T(8,128)(2,1)}), bf16[1024,4,256]{2,0,1:T(8,128)(2,1)}, u32[]{:S(2)}, u32[]{:S(2)}) async-start(bf16[1024,4,256]{2,0,1:T(8,128)(2,1)} %pad_maximum_fusion), calls=%async_computation | async-start | bytes 4194304 | tf_op jit(solution)/shard_map/all_to_all | solution.py:119
  12.3 27.3 %collective-permute-start.3 = (bf16[512,1024]{1,0:T(8,128)(2,1)}, bf16[512,1024]{1,0:T(8,128)(2,1)}, u32[]{:S(2)}, u32[]{:S(2)}) collective-permute-start(bf16[512,1024]{1,0:T(8,128)(2,1)} %get-tuple-element.51.refs_8_), channel_id=1, source_target_pairs={{0,8},{4,12},{8,16},{12,20},{16,24},{20,28},{1,9},{5,13},{9,17},{1... | collective-permute-start | bytes 3145736 | tf_op jit(solution)/shard_map/ppermute | solution.py:293
  16.8 28.2 %collective-permute-start.5 = (bf16[512,1024]{1,0:T(8,128)(2,1)}, bf16[512,1024]{1,0:T(8,128)(2,1)}, u32[]{:S(2)}, u32[]{:S(2)}) collective-permute-start(bf16[512,1024]{1,0:T(8,128)(2,1)} %get-tuple-element.51.refs_8_), channel_id=1, source_target_pairs={{8,0},{12,4},{16,8},{20,12},{24,16},{28,20},{9,1},{13,5},{17,9},{2... | collective-permute-start | bytes 3145736 | tf_op jit(solution)/shard_map/ppermute | solution.py:296
  29.0 66.6 %copy-start.4 = (bf16[512,1024]{1,0:T(8,128)(2,1)}, bf16[512,1024]{1,0:T(8,128)(2,1)S(1)}, u32[]{:S(2)}) copy-start(bf16[512,1024]{1,0:T(8,128)(2,1)S(1)} %collective-permute-done.refs_0_) | copy-start | bytes 3145732
  29.0 32.6 %collective-permute-start.1 = (bf16[512,1024]{1,0:T(8,128)(2,1)S(1)}, bf16[512,1024]{1,0:T(8,128)(2,1)}, u32[]{:S(2)}, u32[]{:S(2)}) collective-permute-start(bf16[512,1024]{1,0:T(8,128)(2,1)S(1)} %collective-permute-done.refs_0_), channel_id=1, source_target_pairs={{0,8},{4,12},{8,16},{12,20},{16,24},{20,28},{1,9},{5,13},{9,17},{1... | collective-permute-start | bytes 3145736 | tf_op jit(solution)/shard_map/ppermute | solution.py:293
  33.7 33.7 %collective-permute-start.2 = (bf16[512,1024]{1,0:T(8,128)(2,1)S(1)}, bf16[512,1024]{1,0:T(8,128)(2,1)S(1)}, u32[]{:S(2)}, u32[]{:S(2)}) collective-permute-start(bf16[512,1024]{1,0:T(8,128)(2,1)S(1)} %collective-permute-done.refs_0_), channel_id=1, source_target_pairs={{8,0},{12,4},{16,8},{20,12},{24,16},{28,20},{9,1},{13,5},{17,9},{2... | collective-permute-start | bytes 3145736 | tf_op jit(solution)/shard_map/ppermute | solution.py:296
  39.6 56.0 %collective-permute-start.4 = (bf16[512,1024]{1,0:T(8,128)(2,1)}, bf16[512,1024]{1,0:T(8,128)(2,1)}, u32[]{:S(2)}, u32[]{:S(2)}) collective-permute-start(bf16[512,1024]{1,0:T(8,128)(2,1)} %collective-permute-done.3.refs_9_), channel_id=1, source_target_pairs={{8,16},{12,20},{16,24},{20,28},{9,17},{13,21},{17,25},{21,29},{10,... | collective-permute-start | bytes 3145736 | tf_op jit(solution)/shard_map/ppermute | solution.py:293
  45.0 50.6 %collective-permute-start.6 = (bf16[512,1024]{1,0:T(8,128)(2,1)}, bf16[512,1024]{1,0:T(8,128)(2,1)}, u32[]{:S(2)}, u32[]{:S(2)}) collective-permute-start(bf16[512,1024]{1,0:T(8,128)(2,1)} %collective-permute-done.5.refs_12_), channel_id=1, source_target_pairs={{8,0},{12,4},{16,8},{20,12},{9,1},{13,5},{17,9},{21,13},{10,2},{14... | collective-permute-start | bytes 3145736 | tf_op jit(solution)/shard_map/ppermute | solution.py:296
  67.4 28.2 %copy-start.7 = (bf16[512,1024]{1,0:T(8,128)(2,1)}, bf16[512,1024]{1,0:T(8,128)(2,1)S(1)}, u32[]{:S(2)}) copy-start(bf16[512,1024]{1,0:T(8,128)(2,1)S(1)} %collective-permute-done.2.refs_4_) | copy-start | bytes 3145732
  95.6 23.8 %collective-permute-start.8 = (bf16[512,1024]{1,0:T(8,128)(2,1)S(1)}, bf16[512,1024]{1,0:T(8,128)(2,1)}, u32[]{:S(2)}, u32[]{:S(2)}) collective-permute-start(bf16[512,1024]{1,0:T(8,128)(2,1)S(1)} %attend.1.refs_0_), channel_id=1, source_target_pairs={{0,4},{4,0},{8,12},{12,8},{16,20},{20,16},{24,28},{28,24},{1,5},{5... | collective-permute-start | bytes 3145736 | tf_op jit(solution)/shard_map/ppermute | solution.py:317
  95.7 23.8 %collective-permute-start.9 = (bf16[512,1024]{1,0:T(8,128)(2,1)S(1)}, bf16[512,1024]{1,0:T(8,128)(2,1)}, u32[]{:S(2)}, u32[]{:S(2)}) collective-permute-start(bf16[512,1024]{1,0:T(8,128)(2,1)S(1)} %attend.1.refs_0_), channel_id=1, source_target_pairs={{0,2},{1,3},{2,0},{3,1},{4,6},{5,7},{6,4},{7,5},{8,10},{9,11},{10,... | collective-permute-start | bytes 3145736 | tf_op jit(solution)/shard_map/ppermute | solution.py:318
  97.8 21.7 %collective-permute-start.10 = (bf16[512,1024]{1,0:T(8,128)(2,1)}, bf16[512,1024]{1,0:T(8,128)(2,1)S(1)}, u32[]{:S(2)}, u32[]{:S(2)}) collective-permute-start(bf16[512,1024]{1,0:T(8,128)(2,1)} %collective-permute-done.1.refs_1_), channel_id=1, source_target_pairs={{8,16},{12,20},{16,24},{20,28},{9,17},{13,21},{17,25},{21,29},{10,... | collective-permute-start | bytes 3145736 | tf_op jit(solution)/shard_map/ppermute | solution.py:293
  98.5 24.8 %collective-permute-start.11 = (bf16[512,1024]{1,0:T(8,128)(2,1)}, bf16[512,1024]{1,0:T(8,128)(2,1)S(1)}, u32[]{:S(2)}, u32[]{:S(2)}) collective-permute-start(bf16[512,1024]{1,0:T(8,128)(2,1)} %copy-done.7), channel_id=1, source_target_pairs={{8,0},{12,4},{16,8},{20,12},{9,1},{13,5},{17,9},{21,13},{10,2},{14... | collective-permute-start | bytes 3145736 | tf_op jit(solution)/shard_map/ppermute | solution.py:296
  99.8 27.0 %collective-permute-start.16 = (bf16[512,1024]{1,0:T(8,128)(2,1)}, bf16[512,1024]{1,0:T(8,128)(2,1)S(1)}, u32[]{:S(2)}, u32[]{:S(2)}) collective-permute-start(bf16[512,1024]{1,0:T(8,128)(2,1)} %collective-permute-done.4.refs_10_), channel_id=1, source_target_pairs={{16,24},{20,28},{17,25},{21,29},{18,26},{22,30},{19,27},{23,31}} | collective-permute-start | bytes 3145736 | tf_op jit(solution)/shard_map/ppermute | solution.py:293
  123.3 22.1 %collective-permute-start.14 = (bf16[512,1024]{1,0:T(8,128)(2,1)}, bf16[512,1024]{1,0:T(8,128)(2,1)}, u32[]{:S(2)}, u32[]{:S(2)}) collective-permute-start(bf16[512,1024]{1,0:T(8,128)(2,1)} %collective-permute-done.8.refs_4_), channel_id=1, source_target_pairs={{0,2},{1,3},{2,0},{3,1},{4,6},{5,7},{6,4},{7,5},{8,10},{9,11},{10,... | collective-permute-start | bytes 3145736 | tf_op jit(solution)/shard_map/ppermute | solution.py:326
  124.0 24.2 %collective-permute-start.17 = (bf16[512,1024]{1,0:T(8,128)(2,1)}, bf16[512,1024]{1,0:T(8,128)(2,1)S(1)}, u32[]{:S(2)}, u32[]{:S(2)}) collective-permute-start(bf16[512,1024]{1,0:T(8,128)(2,1)} %collective-permute-done.6.refs_13_), channel_id=1, source_target_pairs={{8,0},{12,4},{9,1},{13,5},{10,2},{14,6},{11,3},{15,7}} | collective-permute-start | bytes 3145736 | tf_op jit(solution)/shard_map/ppermute | solution.py:296
  125.3 25.5 %collective-permute-start.7 = (bf16[512,1024]{1,0:T(8,128)(2,1)S(1)}, bf16[512,1024]{1,0:T(8,128)(2,1)S(1)}, u32[]{:S(2)}, u32[]{:S(2)}) collective-permute-start(bf16[512,1024]{1,0:T(8,128)(2,1)S(1)} %attend.1.refs_0_), channel_id=1, source_target_pairs={{0,1},{1,0},{2,3},{3,2},{4,5},{5,4},{6,7},{7,6},{8,9},{9,8},{10,11... | collective-permute-start | bytes 3145736 | tf_op jit(solution)/shard_map/ppermute | solution.py:299
  126.3 26.8 %collective-permute-start.13 = (bf16[512,1024]{1,0:T(8,128)(2,1)}, bf16[512,1024]{1,0:T(8,128)(2,1)}, u32[]{:S(2)}, u32[]{:S(2)}) collective-permute-start(bf16[512,1024]{1,0:T(8,128)(2,1)} %collective-permute-done.8.refs_4_), channel_id=1, source_target_pairs={{0,1},{1,0},{2,3},{3,2},{4,5},{5,4},{6,7},{7,6},{8,9},{9,8},{10,11... | collective-permute-start | bytes 3145736 | tf_op jit(solution)/shard_map/ppermute | solution.py:299
  127.8 25.3 %collective-permute-start.12 = (bf16[512,1024]{1,0:T(8,128)(2,1)}, bf16[512,1024]{1,0:T(8,128)(2,1)}, u32[]{:S(2)}, u32[]{:S(2)}) collective-permute-start(bf16[512,1024]{1,0:T(8,128)(2,1)} %collective-permute-done.9.refs_2_), channel_id=1, source_target_pairs={{0,1},{1,0},{2,3},{3,2},{4,5},{5,4},{6,7},{7,6},{8,9},{9,8},{10,11... | collective-permute-start | bytes 3145736 | tf_op jit(solution)/shard_map/ppermute | solution.py:299
  145.3 7.8 %collective-permute-start.15 = (bf16[512,1024]{1,0:T(8,128)(2,1)}, bf16[512,1024]{1,0:T(8,128)(2,1)}, u32[]{:S(2)}, u32[]{:S(2)}) collective-permute-start(bf16[512,1024]{1,0:T(8,128)(2,1)} %collective-permute-done.14.refs_6_), channel_id=1, source_target_pairs={{0,1},{1,0},{2,3},{3,2},{4,5},{5,4},{6,7},{7,6},{8,9},{9,8},{10,11... | collective-permute-start | bytes 3145736 | tf_op jit(solution)/shard_map/ppermute | solution.py:299
  149.2 17.7 %collective-permute-start.18 = (bf16[512,640]{1,0:T(8,128)(2,1)}, bf16[512,640]{1,0:T(8,128)(2,1)}, u32[]{:S(2)}, u32[]{:S(2)}) collective-permute-start(bf16[512,640]{1,0:T(8,128)(2,1)} %slice.18), channel_id=1, source_target_pairs={{16,24},{20,28},{17,25},{21,29},{18,26},{22,30},{19,27},{23,31}} | collective-permute-start | bytes 1966088 | tf_op jit(solution)/shard_map/ppermute | solution.py:293
  151.7 18.3 %collective-permute-start.19 = (bf16[512,640]{1,0:T(8,128)(2,1)}, bf16[512,640]{1,0:T(8,128)(2,1)}, u32[]{:S(2)}, u32[]{:S(2)}) collective-permute-start(bf16[512,640]{1,0:T(8,128)(2,1)} %slice.19), channel_id=1, source_target_pairs={{8,0},{12,4},{9,1},{13,5},{10,2},{14,6},{11,3},{15,7}} | collective-permute-start | bytes 1966088 | tf_op jit(solution)/shard_map/ppermute | solution.py:296
  153.1 16.9 %copy-start.8 = (bf16[512,1024]{1,0:T(8,128)(2,1)S(1)}, bf16[512,1024]{1,0:T(8,128)(2,1)}, u32[]{:S(2)}) copy-start(bf16[512,1024]{1,0:T(8,128)(2,1)} %copy-done.7) | copy-start | bytes 3145732
  177.5 29.5 %collective-permute-start.20 = (bf16[512,640]{1,0:T(8,128)(2,1)}, bf16[512,640]{1,0:T(8,128)(2,1)}, u32[]{:S(2)}, u32[]{:S(2)}) collective-permute-start(bf16[512,640]{1,0:T(8,128)(2,1)} %get-tuple-element.44), channel_id=1, source_target_pairs={{0,4},{4,0},{8,12},{12,8},{16,20},{20,16},{24,28},{28,24},{1,5},{5... | collective-permute-start | bytes 1966088 | tf_op jit(solution)/shard_map/ppermute | solution.py:337
  180.4 22.0 %collective-permute-start.21 = (bf16[512,256]{1,0:T(8,128)(2,1)}, bf16[512,256]{1,0:T(8,128)(2,1)S(1)}, u32[]{:S(2)}, u32[]{:S(2)}) collective-permute-start(bf16[512,256]{1,0:T(8,128)(2,1)} %slice.20), channel_id=1, source_target_pairs={{16,24},{20,28},{17,25},{21,29},{18,26},{22,30},{19,27},{23,31}} | collective-permute-start | bytes 786440 | tf_op jit(solution)/shard_map/ppermute | solution.py:293
  181.0 21.3 %collective-permute-start.22 = (bf16[512,256]{1,0:T(8,128)(2,1)}, bf16[512,256]{1,0:T(8,128)(2,1)}, u32[]{:S(2)}, u32[]{:S(2)}) collective-permute-start(bf16[512,256]{1,0:T(8,128)(2,1)} %slice.21), channel_id=1, source_target_pairs={{8,0},{12,4},{9,1},{13,5},{10,2},{14,6},{11,3},{15,7}} | collective-permute-start | bytes 786440 | tf_op jit(solution)/shard_map/ppermute | solution.py:296
  183.7 2.0 collective-permute-start.24
  184.4 8.2 %collective-permute-start.25 = (bf16[512,128]{1,0:T(8,128)(2,1)}, bf16[512,128]{1,0:T(8,128)(2,1)}, u32[]{:S(2)}, u32[]{:S(2)}) collective-permute-start(bf16[512,128]{1,0:T(8,128)(2,1)} %slice.23), channel_id=1, source_target_pairs={{8,0},{12,4},{9,1},{13,5},{10,2},{14,6},{11,3},{15,7}} | collective-permute-start | bytes 393224 | tf_op jit(solution)/shard_map/ppermute | solution.py:296
  201.6 10.7 %collective-permute-start.26 = (bf16[512,128]{1,0:T(8,128)(2,1)S(1)}, bf16[512,128]{1,0:T(8,128)(2,1)S(1)}, u32[]{:S(2)}, u32[]{:S(2)}) collective-permute-start(bf16[512,128]{1,0:T(8,128)(2,1)S(1)} %get-tuple-element.50), channel_id=1, source_target_pairs={{0,4},{4,0},{8,12},{12,8},{16,20},{20,16},{24,28},{28,24},{1,5},{5... | collective-permute-start | bytes 393224 | tf_op jit(solution)/shard_map/ppermute | solution.py:337
  205.5 6.7 %collective-permute-start.23 = (bf16[512,256]{1,0:T(8,128)(2,1)S(1)}, bf16[512,256]{1,0:T(8,128)(2,1)S(1)}, u32[]{:S(2)}, u32[]{:S(2)}) collective-permute-start(bf16[512,256]{1,0:T(8,128)(2,1)S(1)} %get-tuple-element.47), channel_id=1, source_target_pairs={{0,4},{4,0},{8,12},{12,8},{16,20},{20,16},{24,28},{28,24},{1,5},{5... | collective-permute-start | bytes 786440 | tf_op jit(solution)/shard_map/ppermute | solution.py:337
  (25 other events, 90.3 us)

commit v3 on v2

--- a/solution.py
+++ b/solution.py
@@ -18,6 +18,9 @@
 EXP2_SCALE = math.log2(math.e) / math.sqrt(HEAD_SIZE)
 
 
+GROUP = 4
+
+
 def attention_kernel(heads, meta_ref, q_ref, kv_ref, old_ref, out_ref, peak_ref, denom_ref, acc_ref):
     live = meta_ref[0]
     flag = meta_ref[1]
@@ -32,51 +35,52 @@
         denom_ref[...] = jnp.zeros_like(denom_ref)
         acc_ref[...] = jnp.zeros_like(acc_ref)
 
-        def pair(step, carry):
-            second = 2 * step + 1 < live
-            first_row = pl.multiple_of(meta_ref[2 + 2 * step] * KEY_BLOCK_TOKENS, KEY_BLOCK_TOKENS)
-            second_block = jnp.where(
-                second, meta_ref[jnp.minimum(3 + 2 * step, meta_ref.shape[0] - 1)], 0
+        def group(step, carry):
+            tiles, biases = [], []
+            for member in range(GROUP):
+                slot = step * GROUP + member
+                if member > 0:
+                    present = slot < live
+                    block = jnp.where(
+                        present, meta_ref[2 + jnp.minimum(slot, meta_ref.shape[0] - 3)], 0
+                    )
+                    biases.append(jnp.where(present, 0.0, LOWEST).astype(jnp.float32))
+                else:
+                    block = meta_ref[2 + slot]
+                    biases.append(None)
+                row = pl.multiple_of(block * KEY_BLOCK_TOKENS, KEY_BLOCK_TOKENS)
+                tiles.append(kv_ref[pl.ds(row, KEY_BLOCK_TOKENS), :])
+            tile = jnp.concatenate(tiles, axis=0)
+            key_tile = tile[:, :HEAD_SIZE]
+            value_tile = tile[:, HEAD_SIZE:].T
+            value_tile = jnp.concatenate(
+                [value_tile, jnp.ones((16, value_tile.shape[1]), jnp.bfloat16)], axis=0
             )
-            second_row = pl.multiple_of(second_block * KEY_BLOCK_TOKENS, KEY_BLOCK_TOKENS)
-            bias = jnp.where(second, 0.0, LOWEST).astype(jnp.float32)
-            tile = jnp.concatenate(
-                [
-                    kv_ref[pl.ds(first_row, KEY_BLOCK_TOKENS), :],
-                    kv_ref[pl.ds(second_row, KEY_BLOCK_TOKENS), :],
-                ],
-                axis=0,
-            )
-            key_tile = tile[:, :HEAD_SIZE]
-            value_tile = tile[:, HEAD_SIZE:]
             for head in range(heads):
                 query = q_ref[:, head * HEAD_SIZE : (head + 1) * HEAD_SIZE]
                 scores = lax.dot_general(
                     key_tile, query, (((1,), (1,)), ((), ())), preferred_element_type=jnp.float32
                 )
-                upper = scores[:KEY_BLOCK_TOKENS]
-                lower = scores[KEY_BLOCK_TOKENS:] + bias
+                parts = [
+                    scores[member * KEY_BLOCK_TOKENS : (member + 1) * KEY_BLOCK_TOKENS]
+                    for member in range(GROUP)
+                ]
+                parts = [p if b is None else p + b for p, b in zip(parts, biases)]
+                top = functools.reduce(jnp.maximum, parts)
                 old_peak = peak_ref[head]
-                peak = jnp.maximum(
-                    old_peak, jnp.max(jnp.maximum(upper, lower), axis=0, keepdims=True)
+                peak = jnp.maximum(old_peak, jnp.max(top, axis=0, keepdims=True))
+                decay = jnp.exp2((old_peak - peak) * EXP2_SCALE)
+                parts = [jnp.exp2((p - peak) * EXP2_SCALE) for p in parts]
+                peak_ref[head] = peak
+                weights = jnp.concatenate([p.astype(jnp.bfloat16) for p in parts], axis=0)
+                update = lax.dot_general(
+                    value_tile, weights, (((1,), (0,)), ((), ())), preferred_element_type=jnp.float32
                 )
-                decay = jnp.exp2((old_peak - peak) * EXP2_SCALE)
-                upper = jnp.exp2((upper - peak) * EXP2_SCALE)
-                lower = jnp.exp2((lower - peak) * EXP2_SCALE)
-                peak_ref[head] = peak
-                denom_ref[head] = denom_ref[head] * decay + jnp.sum(
-                    upper + lower, axis=0, keepdims=True
-                )
-                weights = jnp.concatenate(
-                    [upper.astype(jnp.bfloat16), lower.astype(jnp.bfloat16)], axis=0
-                )
-                update = lax.dot_general(
-                    value_tile, weights, (((0,), (0,)), ((), ())), preferred_element_type=jnp.float32
-                )
-                acc_ref[head] = acc_ref[head] * decay + update
+                denom_ref[head] = denom_ref[head] * decay + update[HEAD_SIZE : HEAD_SIZE + 1]
+                acc_ref[head] = acc_ref[head] * decay + update[:HEAD_SIZE]
             return carry
 
-        lax.fori_loop(0, (live + 1) // 2, pair, 0)
+        lax.fori_loop(0, (live + GROUP - 1) // GROUP, group, 0)
         for head in range(heads):
             result = acc_ref[head] / denom_ref[head]
             out_ref[:, head * HEAD_SIZE : (head + 1) * HEAD_SIZE] = result.T.astype(jnp.bfloat16)
@@ -98,7 +102,7 @@
         ],
         compiler_params=pltpu.CompilerParams(vmem_limit_bytes=16 << 20),
         cost_estimate=pl.CostEstimate(
-            flops=24 * rows * width * 16 * KEY_BLOCK_TOKENS,
+            flops=4 * rows * width * 16 * KEY_BLOCK_TOKENS,
             transcendentals=rows * heads * 16 * KEY_BLOCK_TOKENS,
             bytes_accessed=2 * (3 * rows * width + kv.size),
         ),
@@ -202,12 +206,15 @@
     wait_spare()
 
 
-def rest_kernel(start, place_ref, left, base_ref, *refs):
-    slabs, (own_out, other_out, right, sems) = refs[:7], refs[7:]
+def rest_kernel(start, place_ref, left_ref, base_ref, *refs):
+    slabs, (own_out, other_out, left, right, sems, left_sem) = refs[:7], refs[7:]
     rows = own_out.shape[0]
+    left_copy = pltpu.make_async_copy(left_ref, left, left_sem)
+    left_copy.start()
     wait = collect_copies(
         place_ref[0], place_ref[2], 0, None, None, slabs, left, right, sems, start
     )
+    left_copy.wait()
     wait()
 
     def rows_tile(step, carry):
@@ -225,6 +232,9 @@
 IN_HBM = pl.BlockSpec(memory_space=pltpu.HBM)
 IN_VMEM = pl.BlockSpec(memory_space=pltpu.VMEM)
 IN_SMEM = pl.BlockSpec(memory_space=pltpu.SMEM)
+
+
+SMALL_COST = pl.CostEstimate(flops=1 << 20, transcendentals=0, bytes_accessed=1 << 20)
 
 
 def first_product(where, own_rows, other_rows, slabs, chunks):
@@ -243,13 +253,9 @@
             pltpu.SemaphoreType.DMA((4, 2)),
         ],
         compiler_params=pltpu.CompilerParams(vmem_limit_bytes=14 << 20),
-        cost_estimate=pl.CostEstimate(
-            flops=2 * 2 * rows * 4 * depth * columns,
-            transcendentals=0,
-            bytes_accessed=2 * (4 * rows * 4 * depth + 4 * depth * columns) + 8 * rows * columns,
-        ),
+        cost_estimate=SMALL_COST,
         name="first_product",
-    )(where, *own_rows, *other_rows, *slabs)
+    )(where, *[pltpu.with_memory_space_constraint(x, pltpu.HBM) for x in (*own_rows, *other_rows, *slabs)])
 
 
 def rest_product(where, left, base, slabs, start):
@@ -259,26 +265,25 @@
     return pl.pallas_call(
         functools.partial(rest_kernel, start),
         out_shape=[jax.ShapeDtypeStruct((rows, columns), jnp.bfloat16)] * 2,
-        in_specs=[IN_SMEM, IN_VMEM, IN_VMEM] + [IN_HBM] * 7,
+        in_specs=[IN_SMEM, IN_HBM, IN_VMEM] + [IN_HBM] * 7,
         out_specs=[IN_VMEM] * 2,
         scratch_shapes=[
+            pltpu.VMEM((2 * rows, 4 * depth), jnp.bfloat16),
             pltpu.VMEM((4 * depth, columns), jnp.bfloat16),
             pltpu.SemaphoreType.DMA((4, 3)),
+            pltpu.SemaphoreType.DMA,
         ],
-        compiler_params=pltpu.CompilerParams(vmem_limit_bytes=8 << 20),
-        cost_estimate=pl.CostEstimate(
-            flops=2 * 2 * rows * 4 * depth * columns,
-            transcendentals=0,
-            bytes_accessed=2 * 4 * depth * columns + 8 * rows * columns,
-        ),
+        compiler_params=pltpu.CompilerParams(vmem_limit_bytes=10 << 20),
+        cost_estimate=SMALL_COST,
         name="rest_product",
-    )(where, left, base, *slabs)
+    )(where, pltpu.with_memory_space_constraint(left, pltpu.HBM), base, *[pltpu.with_memory_space_constraint(x, pltpu.HBM) for x in slabs])
 
 
 UP = [[(i, i + 2) for i in range(2 * s, 6)] for s in range(3)]
 DOWN = [[(i + 2, i) for i in range(6 - 2 * s)] for s in range(3)]
 ACROSS_Y = [(i, i ^ 1) for i in range(8)]
 ACROSS_X = [(i, i ^ 2) for i in range(4)]
+ACROSS_BOTH = [(i, i ^ 6) for i in range(32)]
 ACROSS_CORE = [(i, i ^ 1) for i in range(4)]
 
 
@@ -286,7 +291,7 @@
     y = where[1]
     depth, columns = wo.shape
     half = columns // 2
-    chunks = (half * 5 // 8, half // 4, half // 8)
+    chunks = (half * 3 // 8, half * 3 // 8, half // 4)
     starts = (0, chunks[0], chunks[0] + chunks[1])
 
     def up(piece, hop):
@@ -303,36 +308,31 @@
     taken = lax.ppermute(given, "pb", ACROSS_Y)
     kept_up, kept_down = [up(kept, 0)], [down(kept, 0)]
     taken_up, taken_down = [up(taken, 0)], [down(taken, 0)]
-    kept_up.append(up(kept_up[0], 1))
-    kept_down.append(down(kept_down[0], 1))
-    inputs, taken_up[0], taken_down[0] = lax.optimization_barrier(
-        (inputs, taken_up[0], taken_down[0])
-    )
+    for hop in (1, 2):
+        kept_up.append(up(kept_up[-1], hop))
+        kept_down.append(down(kept_down[-1], hop))
     taken_up.append(up(taken_up[0], 1))
     taken_down.append(down(taken_down[0], 1))
-    attn = attend_with(inputs)
-    attn, kept_up[1], kept_down[1] = lax.optimization_barrier((attn, kept_up[1], kept_down[1]))
-    kept_up.append(up(kept_up[1], 2))
-    kept_down.append(down(kept_down[1], 2))
-    across_y = lax.ppermute(attn, "pb", ACROSS_Y)
-    across_x = lax.ppermute(attn, "ka", ACROSS_X)
-    across_y, across_x, taken_up[1], taken_down[1] = lax.optimization_barrier(
-        (across_y, across_x, taken_up[1], taken_down[1])
-    )
     last = []
     for chunk, start in zip(chunks, starts):
         piece = [taken_up[1][:, start : start + chunk], taken_down[1][:, start : start + chunk]]
         last.append((up(piece[0], 2), down(piece[1], 2)))
-    corner = lax.ppermute(across_y, "ka", ACROSS_X)
+    attn = attend_with(inputs)
+    across_y = lax.ppermute(attn, "pb", ACROSS_Y)
+    across_x = lax.ppermute(attn, "ka", ACROSS_X)
+    corner = lax.ppermute(attn, ("pb", "ka"), ACROSS_BOTH)
     own_rows = [attn, other_core(attn), across_x, other_core(across_x)]
     other_rows = [across_y, other_core(across_y), corner, other_core(corner)]
     *bases, left = first_product(
         where, own_rows, other_rows, [kept] + kept_up + kept_down, chunks
     )
     own_out, received = [], []
-    for base, start, (last_up, last_down) in zip(bases, starts, last):
+    for index, (base, start) in enumerate(zip(bases, starts)):
+        last_up, last_down = last[index]
         slabs = [taken] + taken_up + [last_up] + taken_down + [last_down]
         own, other = rest_product(where, left, base, slabs, start)
+        if not own_out:
+            other, last[1], last[2] = lax.optimization_barrier((other, last[1], last[2]))
         own_out.append(own)
         received.append(lax.ppermute(other, "pb", ACROSS_Y))
     first_half = [jnp.where(y == 0, a, b) for a, b in zip(own_out, received)]

time: 214 us -> 207 us (0.967)
  the two profiles are of different devices: /device:TPU:0 before, /device:TPU:16 now
where the time goes in v3:
time: 207 us
  waiting for transfers between devices  78.8 us (38%)
  starting transfers between devices  73.1 us (35%)
  Pallas kernels  32.4 us (16%)
  local copies, waits for them, and re-layouts  16.1 us (8%)
  other arithmetic  4.35 us (2%)
    ppermute x8, waiting for transfers between devices, down(): return lax.ppermute(piece, 'pb', DOWN[hop])  38.6 us
    ppermute x8, starting transfers between devices, down(): return lax.ppermute(piece, 'pb', DOWN[hop])  37.8 us
    ppermute x8, waiting for transfers between devices, up(): return lax.ppermute(piece, 'pb', UP[hop])  33.6 us
    ppermute x8, starting transfers between devices, up(): return lax.ppermute(piece, 'pb', UP[hop])  19.7 us
    pallas_call x3, Pallas kernels, rest_product(): pl.pallas_call(functools.partial(rest_kernel, start), out_shape=[jax.Shap...  17.1 us
    pallas_call x1, Pallas kernels, first_product(): pl.pallas_call(functools.partial(first_kernel, chunks), out_shape=[jax.Sh...  10.2 us
    unnamed x46, local copies, waits for them, and re-layouts  9.5 us
    ppermute x3, waiting for transfers between devices, project(): received.append(lax.ppermute(other, 'pb', ACROSS_Y))  6.63 us
  transfers between devices with their start and end apart: 28, of which 8 were waited for; matrix products, arithmetic and copies ran while one was open for 3% of the time, Pallas kernels for 16%

profile of v3, /device:TPU:16, one launch (start us, length us, event | category | flops | bytes accessed | tf_op | source)
XLA Modules:
  0.0 206.6 jit_solution(10853823724833786679)
XLA Ops:
  1.2 1.6 copy_bitcast_fusion
  2.9 1.5 pad_maximum_fusion
  4.4 3.6 %all-to-all-start = ((bf16[1024,4,256]{2,0,1:T(8,128)(2,1)}), bf16[1024,4,256]{2,0,1:T(8,128)(2,1)S(1)}, u32[]{:S(2)}, u32[]{:S(2)}) async-start(bf16[1024,4,256]{2,0,1:T(8,128)(2,1)} %pad_maximum_fusion), calls=%async_computation | async-start | bytes 4194304 | tf_op jit(solution)/shard_map/all_to_all | solution.py:123
  8.1 1.7 constant_dynamic-slice_fusion
  9.8 2.4 %collective-permute-start.10 = (bf16[512,1024]{1,0:T(8,128)(2,1)S(1)}, bf16[512,1024]{1,0:T(8,128)(2,1)}, u32[]{:S(2)}, u32[]{:S(2)}) collective-permute-start(bf16[512,1024]{1,0:T(8,128)(2,1)S(1)} %get-tuple-element.36.refs_8_), channel_id=1, source_target_pairs={{8,0},{12,4},{16,8},{20,12},{24,16},{28,20},{9,1},{13,5},{17,9},{2... | collective-permute-start | bytes 3145736 | tf_op jit(solution)/shard_map/ppermute | solution.py:301
  12.2 1.6 collective-permute-start.13
  13.7 4.4 %collective-permute-start.7 = (bf16[512,1024]{1,0:T(8,128)(2,1)S(1)}, bf16[512,1024]{1,0:T(8,128)(2,1)}, u32[]{:S(2)}, u32[]{:S(2)}) collective-permute-start(bf16[512,1024]{1,0:T(8,128)(2,1)S(1)} %get-tuple-element.36.refs_8_), channel_id=1, source_target_pairs={{0,8},{4,12},{8,16},{12,20},{16,24},{20,28},{1,9},{5,13},{9,17},{1... | collective-permute-start | bytes 3145736 | tf_op jit(solution)/shard_map/ppermute | solution.py:298
  18.1 19.2 %collective-permute-done.10.refs_12_ = bf16[512,1024]{1,0:T(8,128)(2,1)} collective-permute-done((bf16[512,1024]{1,0:T(8,128)(2,1)S(1)}, bf16[512,1024]{1,0:T(8,128)(2,1)}, u32[]{:S(2)}, u32[]{:S(2)}) %collective-permute-start.10) | collective-permute-done | bytes 1048608 | tf_op jit(solution)/shard_map/ppermute | solution.py:301
  37.3 3.3 %collective-permute-start.11 = (bf16[512,1024]{1,0:T(8,128)(2,1)}, bf16[512,1024]{1,0:T(8,128)(2,1)}, u32[]{:S(2)}, u32[]{:S(2)}) collective-permute-start(bf16[512,1024]{1,0:T(8,128)(2,1)} %collective-permute-done.10.refs_12_), channel_id=1, source_target_pairs={{8,0},{12,4},{16,8},{20,12},{9,1},{13,5},{17,9},{21,13},{10,2},{14... | collective-permute-start | bytes 3145736 | tf_op jit(solution)/shard_map/ppermute | solution.py:301
  42.0 1.9 collective-permute-start.14
  43.9 3.9 %collective-permute-start.17 = (bf16[512,1024]{1,0:T(8,128)(2,1)}, bf16[512,1024]{1,0:T(8,128)(2,1)}, u32[]{:S(2)}, u32[]{:S(2)}) collective-permute-start(bf16[512,1024]{1,0:T(8,128)(2,1)} %collective-permute-done.13.refs_0_), channel_id=1, source_target_pairs={{8,0},{12,4},{16,8},{20,12},{24,16},{28,20},{9,1},{13,5},{17,9},{2... | collective-permute-start | bytes 3145736 | tf_op jit(solution)/shard_map/ppermute | solution.py:301
  47.9 2.9 %collective-permute-start.8 = (bf16[512,1024]{1,0:T(8,128)(2,1)}, bf16[512,1024]{1,0:T(8,128)(2,1)}, u32[]{:S(2)}, u32[]{:S(2)}) collective-permute-start(bf16[512,1024]{1,0:T(8,128)(2,1)} %collective-permute-done.7.refs_9_), channel_id=1, source_target_pairs={{8,16},{12,20},{16,24},{20,28},{9,17},{13,21},{17,25},{21,29},{10,... | collective-permute-start | bytes 3145736 | tf_op jit(solution)/shard_map/ppermute | solution.py:298
  53.2 5.0 %attend.1.refs_0_ = bf16[512,1024]{1,0:T(8,128)(2,1)S(1)} custom-call(s32[18]{0:T(128)S(1)} %pad_add_fusion.1.meta_ref, bf16[512,1024]{1,0:T(8,128)(2,1)S(1)} %bitcast.25, bf16[4096,256]{1,0:T(8,128)(2,1)S(1)} %bitcast.24, bf16[512,1024]{1,0:T(8,128)(2,1)S(1)} %bitcast.26), custom_call_target="tpu_custom_call" | custom-call | flops 4294967296 | bytes 5242880 | tf_op jit(solution)/shard_map/attend/pallas_call | solution.py:93
  58.3 1.7 collective-permute-start.1
  60.0 3.5 %collective-permute-done.11.refs_13_ = bf16[512,1024]{1,0:T(8,128)(2,1)} collective-permute-done((bf16[512,1024]{1,0:T(8,128)(2,1)}, bf16[512,1024]{1,0:T(8,128)(2,1)}, u32[]{:S(2)}, u32[]{:S(2)}) %collective-permute-start.11) | collective-permute-done | bytes 1048608 | tf_op jit(solution)/shard_map/ppermute | solution.py:301
  63.5 1.5 collective-permute-start.3
  65.1 26.0 %collective-permute-done.8.refs_10_ = bf16[512,1024]{1,0:T(8,128)(2,1)} collective-permute-done((bf16[512,1024]{1,0:T(8,128)(2,1)}, bf16[512,1024]{1,0:T(8,128)(2,1)}, u32[]{:S(2)}, u32[]{:S(2)}) %collective-permute-start.8) | collective-permute-done | bytes 1048608 | tf_op jit(solution)/shard_map/ppermute | solution.py:298
  91.1 2.3 %collective-permute-start.5 = (bf16[512,1024]{1,0:T(8,128)(2,1)S(1)}, bf16[512,1024]{1,0:T(8,128)(2,1)S(1)}, u32[]{:S(2)}, u32[]{:S(2)}) collective-permute-start(bf16[512,1024]{1,0:T(8,128)(2,1)S(1)} %attend.1.refs_0_), channel_id=1, source_target_pairs={{0,6},{1,7},{2,4},{3,5},{4,2},{5,3},{6,0},{7,1},{8,14},{9,15},{10,... | collective-permute-start | bytes 3145736 | tf_op jit(solution)/shard_map/ppermute | solution.py:323
  94.2 2.2 %collective-permute-start.15 = (bf16[512,1024]{1,0:T(8,128)(2,1)}, bf16[512,1024]{1,0:T(8,128)(2,1)S(1)}, u32[]{:S(2)}, u32[]{:S(2)}) collective-permute-start(bf16[512,1024]{1,0:T(8,128)(2,1)} %collective-permute-done.14.refs_1_), channel_id=1, source_target_pairs={{8,16},{12,20},{16,24},{20,28},{9,17},{13,21},{17,25},{21,29},{10,... | collective-permute-start | bytes 3145736 | tf_op jit(solution)/shard_map/ppermute | solution.py:298
  96.4 24.0 %collective-permute-start.18 = (bf16[512,1024]{1,0:T(8,128)(2,1)}, bf16[512,1024]{1,0:T(8,128)(2,1)S(1)}, u32[]{:S(2)}, u32[]{:S(2)}) collective-permute-start(bf16[512,1024]{1,0:T(8,128)(2,1)} %collective-permute-done.17.refs_4_), channel_id=1, source_target_pairs={{8,0},{12,4},{16,8},{20,12},{9,1},{13,5},{17,9},{21,13},{10,2},{14... | collective-permute-start | bytes 3145736 | tf_op jit(solution)/shard_map/ppermute | solution.py:301
  124.3 15.8 %collective-permute-done.18.refs_5_ = bf16[512,1024]{1,0:T(8,128)(2,1)S(1)} collective-permute-done((bf16[512,1024]{1,0:T(8,128)(2,1)}, bf16[512,1024]{1,0:T(8,128)(2,1)S(1)}, u32[]{:S(2)}, u32[]{:S(2)}) %collective-permute-start.18) | collective-permute-done | bytes 1048608 | tf_op jit(solution)/shard_map/ppermute | solution.py:301
  142.3 3.3 %collective-permute-done.9.refs_11_ = bf16[512,1024]{1,0:T(8,128)(2,1)S(1)} collective-permute-done((bf16[512,1024]{1,0:T(8,128)(2,1)}, bf16[512,1024]{1,0:T(8,128)(2,1)S(1)}, u32[]{:S(2)}, u32[]{:S(2)}) %collective-permute-start.9) | collective-permute-done | bytes 1048608 | tf_op jit(solution)/shard_map/ppermute | solution.py:298
  146.3 4.2 %collective-permute-done.16.refs_3_ = bf16[512,384]{1,0:T(8,128)(2,1)S(1)} collective-permute-done((bf16[512,384]{1,0:T(8,128)(2,1)S(1)}, bf16[512,384]{1,0:T(8,128)(2,1)S(1)}, u32[]{:S(2)}, u32[]{:S(2)}) %collective-permute-start.16) | collective-permute-done | bytes 393248 | tf_op jit(solution)/shard_map/ppermute | solution.py:298
  150.5 4.4 %collective-permute-start.20 = (bf16[512,384]{1,0:T(8,128)(2,1)}, bf16[512,384]{1,0:T(8,128)(2,1)S(1)}, u32[]{:S(2)}, u32[]{:S(2)}) collective-permute-start(bf16[512,384]{1,0:T(8,128)(2,1)} %get-tuple-element.39), channel_id=1, source_target_pairs={{16,24},{20,28},{17,25},{21,29},{18,26},{22,30},{19,27},{23,31}} | collective-permute-start | bytes 1179656 | tf_op jit(solution)/shard_map/ppermute | solution.py:298
  161.7 10.2 %first_product.1 = (f32[1024,384]{1,0:T(8,128)S(1)}, f32[1024,384]{1,0:T(8,128)S(1)}, f32[1024,256]{1,0:T(8,128)S(1)}, bf16[1024,2048]{1,0:T(8,128)(2,1)S(1)}) custom-call(s32[3]{0:T(128)S(1)} %pad_add_fusion.place_ref, bf16[512,1024]{1,0:T(8,128)(2,1)} %copy-done.2, bf16[512,1024]{1,0:T(8,128)(2,1)} %copy-done.11, bf16[512,1024]{1,0:T(8,128)(2,1)} %copy-done.8, ...), custom_call_target="tpu_custom_call" | custom-call | flops 1048576 | bytes 1048576 | tf_op jit(solution)/shard_map/first_product/pallas_call | solution.py:243
  171.9 2.0 copy-done.1
  174.6 5.9 %rest_product.3 = (bf16[512,384]{1,0:T(8,128)(2,1)S(1)}, bf16[512,384]{1,0:T(8,128)(2,1)S(1)}) custom-call(s32[3]{0:T(128)S(1)} %pad_add_fusion.place_ref, bf16[1024,2048]{1,0:T(8,128)(2,1)} %copy-done.1, f32[1024,384]{1,0:T(8,128)S(1)} %get-tuple-element.21.base_ref, bf16[512,1024]{1,0:T(8,128)(2,1)} %collective-permute-done.13.refs_0_, ...), custom_call_target="tpu_custom_call" | custom-call | flops 1048576 | bytes 1048576 | tf_op jit(solution)/shard_map/rest_product/pallas_call | solution.py:265
  180.6 1.9 collective-permute-start.24
  182.5 6.6 %rest_product.4 = (bf16[512,384]{1,0:T(8,128)(2,1)S(1)}, bf16[512,384]{1,0:T(8,128)(2,1)}) custom-call(s32[3]{0:T(128)S(1)} %pad_add_fusion.place_ref, bf16[1024,2048]{1,0:T(8,128)(2,1)} %copy-done.1, f32[1024,384]{1,0:T(8,128)S(1)} %get-tuple-element.25.base_ref, bf16[512,1024]{1,0:T(8,128)(2,1)} %collective-permute-done.13.refs_0_, ...), custom_call_target="tpu_custom_call" | custom-call | flops 1048576 | bytes 1048576 | tf_op jit(solution)/shard_map/rest_product/pallas_call | solution.py:265
  189.9 4.6 %rest_product.5 = (bf16[512,256]{1,0:T(8,128)(2,1)S(1)}, bf16[512,256]{1,0:T(8,128)(2,1)S(1)}) custom-call(s32[3]{0:T(128)S(1)} %pad_add_fusion.place_ref, bf16[1024,2048]{1,0:T(8,128)(2,1)} %copy-done.1, f32[1024,256]{1,0:T(8,128)S(1)} %get-tuple-element.30.base_ref, bf16[512,1024]{1,0:T(8,128)(2,1)} %collective-permute-done.13.refs_0_, ...), custom_call_target="tpu_custom_call" | custom-call | flops 1048576 | bytes 1048576 | tf_op jit(solution)/shard_map/rest_product/pallas_call | solution.py:265
  196.0 4.1 %collective-permute-done.25 = bf16[512,384]{1,0:T(8,128)(2,1)} collective-permute-done((bf16[512,384]{1,0:T(8,128)(2,1)}, bf16[512,384]{1,0:T(8,128)(2,1)}, u32[]{:S(2)}, u32[]{:S(2)}) %collective-permute-start.25) | collective-permute-done | bytes 393248 | tf_op jit(solution)/shard_map/ppermute | solution.py:337
  200.2 2.6 %collective-permute-done.26 = bf16[512,256]{1,0:T(8,128)(2,1)S(1)} collective-permute-done((bf16[512,256]{1,0:T(8,128)(2,1)S(1)}, bf16[512,256]{1,0:T(8,128)(2,1)S(1)}, u32[]{:S(2)}, u32[]{:S(2)}) %collective-permute-start.26) | collective-permute-done | bytes 262176 | tf_op jit(solution)/shard_map/ppermute | solution.py:337
  (90 shorter events, 24.8 us)
Async XLA Ops:
  4.4 46.3 %all-to-all-start = ((bf16[1024,4,256]{2,0,1:T(8,128)(2,1)}), bf16[1024,4,256]{2,0,1:T(8,128)(2,1)S(1)}, u32[]{:S(2)}, u32[]{:S(2)}) async-start(bf16[1024,4,256]{2,0,1:T(8,128)(2,1)} %pad_maximum_fusion), calls=%async_computation | async-start | bytes 4194304 | tf_op jit(solution)/shard_map/all_to_all | solution.py:123
  9.8 27.5 %collective-permute-start.10 = (bf16[512,1024]{1,0:T(8,128)(2,1)S(1)}, bf16[512,1024]{1,0:T(8,128)(2,1)}, u32[]{:S(2)}, u32[]{:S(2)}) collective-permute-start(bf16[512,1024]{1,0:T(8,128)(2,1)S(1)} %get-tuple-element.36.refs_8_), channel_id=1, source_target_pairs={{8,0},{12,4},{16,8},{20,12},{24,16},{28,20},{9,1},{13,5},{17,9},{2... | collective-permute-start | bytes 3145736 | tf_op jit(solution)/shard_map/ppermute | solution.py:301
  12.2 29.8 %collective-permute-start.13 = (bf16[512,1024]{1,0:T(8,128)(2,1)S(1)}, bf16[512,1024]{1,0:T(8,128)(2,1)}, u32[]{:S(2)}, u32[]{:S(2)}) collective-permute-start(bf16[512,1024]{1,0:T(8,128)(2,1)S(1)} %get-tuple-element.35), channel_id=1, source_target_pairs={{0,4},{4,0},{8,12},{12,8},{16,20},{20,16},{24,28},{28,24},{1,5},{5... | collective-permute-start | bytes 3145736 | tf_op jit(solution)/shard_map/ppermute | solution.py:308
  13.7 34.1 %collective-permute-start.7 = (bf16[512,1024]{1,0:T(8,128)(2,1)S(1)}, bf16[512,1024]{1,0:T(8,128)(2,1)}, u32[]{:S(2)}, u32[]{:S(2)}) collective-permute-start(bf16[512,1024]{1,0:T(8,128)(2,1)S(1)} %get-tuple-element.36.refs_8_), channel_id=1, source_target_pairs={{0,8},{4,12},{8,16},{12,20},{16,24},{20,28},{1,9},{5,13},{9,17},{1... | collective-permute-start | bytes 3145736 | tf_op jit(solution)/shard_map/ppermute | solution.py:298
  37.3 26.2 %collective-permute-start.11 = (bf16[512,1024]{1,0:T(8,128)(2,1)}, bf16[512,1024]{1,0:T(8,128)(2,1)}, u32[]{:S(2)}, u32[]{:S(2)}) collective-permute-start(bf16[512,1024]{1,0:T(8,128)(2,1)} %collective-permute-done.10.refs_12_), channel_id=1, source_target_pairs={{8,0},{12,4},{16,8},{20,12},{9,1},{13,5},{17,9},{21,13},{10,2},{14... | collective-permute-start | bytes 3145736 | tf_op jit(solution)/shard_map/ppermute | solution.py:301
  42.0 51.4 %collective-permute-start.14 = (bf16[512,1024]{1,0:T(8,128)(2,1)}, bf16[512,1024]{1,0:T(8,128)(2,1)}, u32[]{:S(2)}, u32[]{:S(2)}) collective-permute-start(bf16[512,1024]{1,0:T(8,128)(2,1)} %collective-permute-done.13.refs_0_), channel_id=1, source_target_pairs={{0,8},{4,12},{8,16},{12,20},{16,24},{20,28},{1,9},{5,13},{9,17},{1... | collective-permute-start | bytes 3145736 | tf_op jit(solution)/shard_map/ppermute | solution.py:298
  43.9 49.5 %collective-permute-start.17 = (bf16[512,1024]{1,0:T(8,128)(2,1)}, bf16[512,1024]{1,0:T(8,128)(2,1)}, u32[]{:S(2)}, u32[]{:S(2)}) collective-permute-start(bf16[512,1024]{1,0:T(8,128)(2,1)} %collective-permute-done.13.refs_0_), channel_id=1, source_target_pairs={{8,0},{12,4},{16,8},{20,12},{24,16},{28,20},{9,1},{13,5},{17,9},{2... | collective-permute-start | bytes 3145736 | tf_op jit(solution)/shard_map/ppermute | solution.py:301
  47.9 43.2 %collective-permute-start.8 = (bf16[512,1024]{1,0:T(8,128)(2,1)}, bf16[512,1024]{1,0:T(8,128)(2,1)}, u32[]{:S(2)}, u32[]{:S(2)}) collective-permute-start(bf16[512,1024]{1,0:T(8,128)(2,1)} %collective-permute-done.7.refs_9_), channel_id=1, source_target_pairs={{8,16},{12,20},{16,24},{20,28},{9,17},{13,21},{17,25},{21,29},{10,... | collective-permute-start | bytes 3145736 | tf_op jit(solution)/shard_map/ppermute | solution.py:298
  58.2 99.6 %copy-start.2 = (bf16[512,1024]{1,0:T(8,128)(2,1)}, bf16[512,1024]{1,0:T(8,128)(2,1)S(1)}, u32[]{:S(2)}) copy-start(bf16[512,1024]{1,0:T(8,128)(2,1)S(1)} %attend.1.refs_0_) | copy-start | bytes 3145732
  58.3 35.9 %collective-permute-start.1 = (bf16[512,1024]{1,0:T(8,128)(2,1)S(1)}, bf16[512,1024]{1,0:T(8,128)(2,1)S(1)}, u32[]{:S(2)}, u32[]{:S(2)}) collective-permute-start(bf16[512,1024]{1,0:T(8,128)(2,1)S(1)} %attend.1.refs_0_), channel_id=1, source_target_pairs={{0,2},{1,3},{2,0},{3,1},{4,6},{5,7},{6,4},{7,5},{8,10},{9,11},{10,... | collective-permute-start | bytes 3145736 | tf_op jit(solution)/shard_map/ppermute | solution.py:322
  63.5 32.8 %collective-permute-start.3 = (bf16[512,1024]{1,0:T(8,128)(2,1)S(1)}, bf16[512,1024]{1,0:T(8,128)(2,1)S(1)}, u32[]{:S(2)}, u32[]{:S(2)}) collective-permute-start(bf16[512,1024]{1,0:T(8,128)(2,1)S(1)} %attend.1.refs_0_), channel_id=1, source_target_pairs={{0,4},{4,0},{8,12},{12,8},{16,20},{20,16},{24,28},{28,24},{1,5},{5... | collective-permute-start | bytes 3145736 | tf_op jit(solution)/shard_map/ppermute | solution.py:321
  91.1 29.3 %collective-permute-start.5 = (bf16[512,1024]{1,0:T(8,128)(2,1)S(1)}, bf16[512,1024]{1,0:T(8,128)(2,1)S(1)}, u32[]{:S(2)}, u32[]{:S(2)}) collective-permute-start(bf16[512,1024]{1,0:T(8,128)(2,1)S(1)} %attend.1.refs_0_), channel_id=1, source_target_pairs={{0,6},{1,7},{2,4},{3,5},{4,2},{5,3},{6,0},{7,1},{8,14},{9,15},{10,... | collective-permute-start | bytes 3145736 | tf_op jit(solution)/shard_map/ppermute | solution.py:323
  93.4 28.4 %collective-permute-start = (bf16[512,1024]{1,0:T(8,128)(2,1)S(1)}, bf16[512,1024]{1,0:T(8,128)(2,1)S(1)}, u32[]{:S(2)}, u32[]{:S(2)}) collective-permute-start(bf16[512,1024]{1,0:T(8,128)(2,1)S(1)} %attend.1.refs_0_), channel_id=1, source_target_pairs={{0,1},{1,0},{2,3},{3,2},{4,5},{5,4},{6,7},{7,6},{8,9},{9,8},{10,11... | collective-permute-start | bytes 3145736 | tf_op jit(solution)/shard_map/ppermute | solution.py:304
  93.4 28.5 %collective-permute-start.12 = (bf16[512,1024]{1,0:T(8,128)(2,1)}, bf16[512,1024]{1,0:T(8,128)(2,1)S(1)}, u32[]{:S(2)}, u32[]{:S(2)}) collective-permute-start(bf16[512,1024]{1,0:T(8,128)(2,1)} %collective-permute-done.11.refs_13_), channel_id=1, source_target_pairs={{8,0},{12,4},{9,1},{13,5},{10,2},{14,6},{11,3},{15,7}} | collective-permute-start | bytes 3145736 | tf_op jit(solution)/shard_map/ppermute | solution.py:301
  94.2 63.7 %copy-start.8 = (bf16[512,1024]{1,0:T(8,128)(2,1)}, bf16[512,1024]{1,0:T(8,128)(2,1)S(1)}, u32[]{:S(2)}) copy-start(bf16[512,1024]{1,0:T(8,128)(2,1)S(1)} %collective-permute-done.1.refs_2_) | copy-start | bytes 3145732
  94.2 28.2 %collective-permute-start.15 = (bf16[512,1024]{1,0:T(8,128)(2,1)}, bf16[512,1024]{1,0:T(8,128)(2,1)S(1)}, u32[]{:S(2)}, u32[]{:S(2)}) collective-permute-start(bf16[512,1024]{1,0:T(8,128)(2,1)} %collective-permute-done.14.refs_1_), channel_id=1, source_target_pairs={{8,16},{12,20},{16,24},{20,28},{9,17},{13,21},{17,25},{21,29},{10,... | collective-permute-start | bytes 3145736 | tf_op jit(solution)/shard_map/ppermute | solution.py:298
  96.4 62.8 %copy-start.9 = (bf16[512,1024]{1,0:T(8,128)(2,1)}, bf16[512,1024]{1,0:T(8,128)(2,1)S(1)}, u32[]{:S(2)}) copy-start(bf16[512,1024]{1,0:T(8,128)(2,1)S(1)} %collective-permute-done.3.refs_4_) | copy-start | bytes 3145732
  96.4 43.8 %collective-permute-start.18 = (bf16[512,1024]{1,0:T(8,128)(2,1)}, bf16[512,1024]{1,0:T(8,128)(2,1)S(1)}, u32[]{:S(2)}, u32[]{:S(2)}) collective-permute-start(bf16[512,1024]{1,0:T(8,128)(2,1)} %collective-permute-done.17.refs_4_), channel_id=1, source_target_pairs={{8,0},{12,4},{16,8},{20,12},{9,1},{13,5},{17,9},{21,13},{10,2},{14... | collective-permute-start | bytes 3145736 | tf_op jit(solution)/shard_map/ppermute | solution.py:301
  120.4 38.8 %copy-start.10 = (bf16[512,1024]{1,0:T(8,128)(2,1)}, bf16[512,1024]{1,0:T(8,128)(2,1)S(1)}, u32[]{:S(2)}) copy-start(bf16[512,1024]{1,0:T(8,128)(2,1)S(1)} %collective-permute-done.5.refs_6_) | copy-start | bytes 3145732
  120.4 25.2 %collective-permute-start.9 = (bf16[512,1024]{1,0:T(8,128)(2,1)}, bf16[512,1024]{1,0:T(8,128)(2,1)S(1)}, u32[]{:S(2)}, u32[]{:S(2)}) collective-permute-start(bf16[512,1024]{1,0:T(8,128)(2,1)} %collective-permute-done.8.refs_10_), channel_id=1, source_target_pairs={{16,24},{20,28},{17,25},{21,29},{18,26},{22,30},{19,27},{23,31}} | collective-permute-start | bytes 3145736 | tf_op jit(solution)/shard_map/ppermute | solution.py:298
  121.8 33.2 %collective-permute-start.2 = (bf16[512,1024]{1,0:T(8,128)(2,1)S(1)}, bf16[512,1024]{1,0:T(8,128)(2,1)S(1)}, u32[]{:S(2)}, u32[]{:S(2)}) collective-permute-start(bf16[512,1024]{1,0:T(8,128)(2,1)S(1)} %collective-permute-done.1.refs_2_), channel_id=1, source_target_pairs={{0,1},{1,0},{2,3},{3,2},{4,5},{5,4},{6,7},{7,6},{8,9},{9,8},{10,11... | collective-permute-start | bytes 3145736 | tf_op jit(solution)/shard_map/ppermute | solution.py:304
  121.9 36.0 %collective-permute-start.4 = (bf16[512,1024]{1,0:T(8,128)(2,1)S(1)}, bf16[512,1024]{1,0:T(8,128)(2,1)S(1)}, u32[]{:S(2)}, u32[]{:S(2)}) collective-permute-start(bf16[512,1024]{1,0:T(8,128)(2,1)S(1)} %collective-permute-done.3.refs_4_), channel_id=1, source_target_pairs={{0,1},{1,0},{2,3},{3,2},{4,5},{5,4},{6,7},{7,6},{8,9},{9,8},{10,11... | collective-permute-start | bytes 3145736 | tf_op jit(solution)/shard_map/ppermute | solution.py:304
  123.1 36.1 %collective-permute-start.6 = (bf16[512,1024]{1,0:T(8,128)(2,1)S(1)}, bf16[512,1024]{1,0:T(8,128)(2,1)S(1)}, u32[]{:S(2)}, u32[]{:S(2)}) collective-permute-start(bf16[512,1024]{1,0:T(8,128)(2,1)S(1)} %collective-permute-done.5.refs_6_), channel_id=1, source_target_pairs={{0,1},{1,0},{2,3},{3,2},{4,5},{5,4},{6,7},{7,6},{8,9},{9,8},{10,11... | collective-permute-start | bytes 3145736 | tf_op jit(solution)/shard_map/ppermute | solution.py:304
  140.2 10.3 %collective-permute-start.16 = (bf16[512,384]{1,0:T(8,128)(2,1)S(1)}, bf16[512,384]{1,0:T(8,128)(2,1)S(1)}, u32[]{:S(2)}, u32[]{:S(2)}) collective-permute-start(bf16[512,384]{1,0:T(8,128)(2,1)S(1)} %get-tuple-element.40), channel_id=1, source_target_pairs={{16,24},{20,28},{17,25},{21,29},{18,26},{22,30},{19,27},{23,31}} | collective-permute-start | bytes 1179656 | tf_op jit(solution)/shard_map/ppermute | solution.py:298
  145.6 28.3 %collective-permute-start.19 = (bf16[512,384]{1,0:T(8,128)(2,1)S(1)}, bf16[512,384]{1,0:T(8,128)(2,1)S(1)}, u32[]{:S(2)}, u32[]{:S(2)}) collective-permute-start(bf16[512,384]{1,0:T(8,128)(2,1)S(1)} %get-tuple-element.38), channel_id=1, source_target_pairs={{8,0},{12,4},{9,1},{13,5},{10,2},{14,6},{11,3},{15,7}} | collective-permute-start | bytes 1179656 | tf_op jit(solution)/shard_map/ppermute | solution.py:301
  150.5 30.0 %collective-permute-start.20 = (bf16[512,384]{1,0:T(8,128)(2,1)}, bf16[512,384]{1,0:T(8,128)(2,1)S(1)}, u32[]{:S(2)}, u32[]{:S(2)}) collective-permute-start(bf16[512,384]{1,0:T(8,128)(2,1)} %get-tuple-element.39), channel_id=1, source_target_pairs={{16,24},{20,28},{17,25},{21,29},{18,26},{22,30},{19,27},{23,31}} | collective-permute-start | bytes 1179656 | tf_op jit(solution)/shard_map/ppermute | solution.py:298
  155.0 25.6 %collective-permute-start.21 = (bf16[512,384]{1,0:T(8,128)(2,1)}, bf16[512,384]{1,0:T(8,128)(2,1)}, u32[]{:S(2)}, u32[]{:S(2)}) collective-permute-start(bf16[512,384]{1,0:T(8,128)(2,1)} %get-tuple-element.37), channel_id=1, source_target_pairs={{8,0},{12,4},{9,1},{13,5},{10,2},{14,6},{11,3},{15,7}} | collective-permute-start | bytes 1179656 | tf_op jit(solution)/shard_map/ppermute | solution.py:301
  157.9 22.6 %collective-permute-start.22 = (bf16[512,256]{1,0:T(8,128)(2,1)}, bf16[512,256]{1,0:T(8,128)(2,1)S(1)}, u32[]{:S(2)}, u32[]{:S(2)}) collective-permute-start(bf16[512,256]{1,0:T(8,128)(2,1)} %slice.28), channel_id=1, source_target_pairs={{16,24},{20,28},{17,25},{21,29},{18,26},{22,30},{19,27},{23,31}} | collective-permute-start | bytes 786440 | tf_op jit(solution)/shard_map/ppermute | solution.py:298
  160.3 20.3 %collective-permute-start.23 = (bf16[512,256]{1,0:T(8,128)(2,1)}, bf16[512,256]{1,0:T(8,128)(2,1)}, u32[]{:S(2)}, u32[]{:S(2)}) collective-permute-start(bf16[512,256]{1,0:T(8,128)(2,1)} %slice.29), channel_id=1, source_target_pairs={{8,0},{12,4},{9,1},{13,5},{10,2},{14,6},{11,3},{15,7}} | collective-permute-start | bytes 786440 | tf_op jit(solution)/shard_map/ppermute | solution.py:301
  180.6 15.3 %collective-permute-start.24 = (bf16[512,384]{1,0:T(8,128)(2,1)S(1)}, bf16[512,384]{1,0:T(8,128)(2,1)}, u32[]{:S(2)}, u32[]{:S(2)}) collective-permute-start(bf16[512,384]{1,0:T(8,128)(2,1)S(1)} %get-tuple-element.24), channel_id=1, source_target_pairs={{0,4},{4,0},{8,12},{12,8},{16,20},{20,16},{24,28},{28,24},{1,5},{5... | collective-permute-start | bytes 1179656 | tf_op jit(solution)/shard_map/ppermute | solution.py:337
  189.1 11.0 %collective-permute-start.25 = (bf16[512,384]{1,0:T(8,128)(2,1)}, bf16[512,384]{1,0:T(8,128)(2,1)}, u32[]{:S(2)}, u32[]{:S(2)}) collective-permute-start(bf16[512,384]{1,0:T(8,128)(2,1)} %get-tuple-element.29), channel_id=1, source_target_pairs={{0,4},{4,0},{8,12},{12,8},{16,20},{20,16},{24,28},{28,24},{1,5},{5... | collective-permute-start | bytes 1179656 | tf_op jit(solution)/shard_map/ppermute | solution.py:337
  194.5 8.3 %collective-permute-start.26 = (bf16[512,256]{1,0:T(8,128)(2,1)S(1)}, bf16[512,256]{1,0:T(8,128)(2,1)S(1)}, u32[]{:S(2)}, u32[]{:S(2)}) collective-permute-start(bf16[512,256]{1,0:T(8,128)(2,1)S(1)} %get-tuple-element.34), channel_id=1, source_target_pairs={{0,4},{4,0},{8,12},{12,8},{16,20},{20,16},{24,28},{28,24},{1,5},{5... | collective-permute-start | bytes 786440 | tf_op jit(solution)/shard_map/ppermute | solution.py:337
  (19 other events, 174.6 us)

commit v4 on v0

v4 whole, which is shorter than its diff:
```python
import functools
import math

import jax
import jax.numpy as jnp
from jax import lax
from jax.experimental import pallas as pl
from jax.experimental.pallas import tpu as pltpu
from jax.sharding import PartitionSpec as P

HEAD_SIZE = 128
QUERY_HEAD_COUNT = 32
KEY_VALUE_HEADS = 4
QUERY_BLOCK_SIZE = 512
KEY_BLOCK_TOKENS = 128
RATIO = QUERY_HEAD_COUNT // KEY_VALUE_HEADS
LOWEST = -1e30
EXP2_SCALE = math.log2(math.e) / math.sqrt(HEAD_SIZE)


GROUP = 4


def attention_kernel(heads, slots, meta_ref, q_hbm, old_hbm, *refs):
    kv_parts, (out_ref, q_ref, kv_ref, peak_ref, denom_ref, acc_ref, sems) = refs[:-7], refs[-7:]
    live = meta_ref[0]
    flag = meta_ref[1]

    @pl.when(flag <= 0)
    def _():
        copy = pltpu.make_async_copy(old_hbm, out_ref, sems.at[0])
        copy.start()
        copy.wait()

    @pl.when(flag > 0)
    def _():
        copies = [pltpu.make_async_copy(q_hbm, q_ref, sems.at[0])]
        for index, part in enumerate(kv_parts):
            rows = part.shape[0]
            start = pl.multiple_of(meta_ref[2 + slots + index] * rows, rows)
            copies.append(
                pltpu.make_async_copy(part, kv_ref.at[pl.ds(start, rows), :], sems.at[1 + index])
            )
        for copy in copies:
            copy.start()
        peak_ref[...] = jnp.full_like(peak_ref, LOWEST)
        denom_ref[...] = jnp.zeros_like(denom_ref)
        acc_ref[...] = jnp.zeros_like(acc_ref)
        for copy in copies:
            copy.wait()

        def group(step, carry):
            tiles, biases = [], []
            for member in range(GROUP):
                slot = step * GROUP + member
                if member > 0:
                    present = slot < live
                    block = jnp.where(
                        present, meta_ref[2 + jnp.minimum(slot, slots - 1)], 0
                    )
                    biases.append(jnp.where(present, 0.0, LOWEST).astype(jnp.float32))
                else:
                    block = meta_ref[2 + slot]
                    biases.append(None)
                row = pl.multiple_of(block * KEY_BLOCK_TOKENS, KEY_BLOCK_TOKENS)
                tiles.append(kv_ref[pl.ds(row, KEY_BLOCK_TOKENS), :])
            tile = jnp.concatenate(tiles, axis=0)
            key_tile = tile[:, :HEAD_SIZE]
            value_tile = tile[:, HEAD_SIZE:].T
            value_tile = jnp.concatenate(
                [value_tile, jnp.ones((16, value_tile.shape[1]), jnp.bfloat16)], axis=0
            )
            for head in range(heads):
                query = q_ref[:, head * HEAD_SIZE : (head + 1) * HEAD_SIZE]
                scores = lax.dot_general(
                    key_tile, query, (((1,), (1,)), ((), ())), preferred_element_type=jnp.float32
                )
                parts = [
                    scores[member * KEY_BLOCK_TOKENS : (member + 1) * KEY_BLOCK_TOKENS]
                    for member in range(GROUP)
                ]
                parts = [p if b is None else p + b for p, b in zip(parts, biases)]
                top = functools.reduce(jnp.maximum, parts)
                old_peak = peak_ref[head]
                peak = jnp.maximum(old_peak, jnp.max(top, axis=0, keepdims=True))
                decay = jnp.exp2((old_peak - peak) * EXP2_SCALE)
                parts = [jnp.exp2((p - peak) * EXP2_SCALE) for p in parts]
                peak_ref[head] = peak
                weights = jnp.concatenate([p.astype(jnp.bfloat16) for p in parts], axis=0)
                update = lax.dot_general(
                    value_tile, weights, (((1,), (0,)), ((), ())), preferred_element_type=jnp.float32
                )
                denom_ref[head] = denom_ref[head] * decay + update[HEAD_SIZE : HEAD_SIZE + 1]
                acc_ref[head] = acc_ref[head] * decay + update[:HEAD_SIZE]
            return carry

        lax.fori_loop(0, (live + GROUP - 1) // GROUP, group, 0)
        for head in range(heads):
            result = acc_ref[head] / denom_ref[head]
            out_ref[:, head * HEAD_SIZE : (head + 1) * HEAD_SIZE] = result.T.astype(jnp.bfloat16)


def attend(block_list, live, flag, queries, old, kv_parts, places):
    rows, width = queries.shape
    heads = width // HEAD_SIZE
    slots = block_list.shape[0]
    meta = jnp.concatenate([live[None], flag[None], block_list, *[p[None] for p in places]])
    in_hbm = pl.BlockSpec(memory_space=pltpu.HBM)
    return pl.pallas_call(
        functools.partial(attention_kernel, heads, slots),
        out_shape=jax.ShapeDtypeStruct((rows, width), jnp.bfloat16),
        in_specs=[pl.BlockSpec(memory_space=pltpu.SMEM)] + [in_hbm] * (2 + len(kv_parts)),
        out_specs=pl.BlockSpec(memory_space=pltpu.VMEM),
        scratch_shapes=[
            pltpu.VMEM((rows, width), jnp.bfloat16),
            pltpu.VMEM((sum(p.shape[0] for p in kv_parts), 2 * HEAD_SIZE), jnp.bfloat16),
            pltpu.VMEM((heads, 1, rows), jnp.float32),
            pltpu.VMEM((heads, 1, rows), jnp.float32),
            pltpu.VMEM((heads, HEAD_SIZE, rows), jnp.float32),
            pltpu.SemaphoreType.DMA((1 + len(kv_parts),)),
        ],
        compiler_params=pltpu.CompilerParams(vmem_limit_bytes=24 << 20),
        cost_estimate=pl.CostEstimate(
            flops=1 << 20, transcendentals=0, bytes_accessed=1 << 20
        ),
        name="attend",
    )(
        meta,
        *[
            pltpu.with_memory_space_constraint(x, pltpu.HBM)
            for x in (queries, old, *kv_parts)
        ],
    )


def own_head_keys_values(keys, values):
    groups = lax.axis_size("ka")
    me = lax.axis_index("ka")
    rows = keys.shape[0]
    if groups == KEY_VALUE_HEADS:

        def head_of(device):
            start = (0, device * HEAD_SIZE)
            return jnp.concatenate(
                [lax.dynamic_slice(x, start, (rows, HEAD_SIZE)) for x in (keys, values)], axis=1
            )

        parts, places = [head_of(me)], [me]
        for step in range(1, groups):
            partner = jnp.bitwise_xor(me, step)
            parts.append(
                lax.ppermute(head_of(partner), "ka", [(i, i ^ step) for i in range(groups)])
            )
            places.append(partner)
        return parts, places
    both = jnp.concatenate(
        [
            keys.reshape(rows, KEY_VALUE_HEADS, HEAD_SIZE),
            values.reshape(rows, KEY_VALUE_HEADS, HEAD_SIZE),
        ],
        axis=2,
    )
    both = jnp.repeat(both, groups // KEY_VALUE_HEADS, axis=1)
    everything = lax.all_to_all(
        both.reshape(rows, groups * 2 * HEAD_SIZE), "ka", split_axis=1, concat_axis=0, tiled=True
    )
    return [everything], [jnp.int32(0)]


def ring_of(pb_size):
    if pb_size == 8:
        return [0, 2, 4, 6, 7, 5, 3, 1]
    return list(range(pb_size))


def project_ring(wo, inputs, attend_with):
    pb_size = lax.axis_size("pb")
    depth, columns = wo.shape
    ring = ring_of(pb_size)
    forward = [(ring[i], ring[(i + 1) % pb_size]) for i in range(pb_size)]
    backward = [(b, a) for a, b in forward]
    half = columns // 2
    far = pb_size // 2
    parts = [wo[:, :half], wo[:, half:]]
    inputs, parts[0], parts[1] = lax.optimization_barrier((inputs, parts[0], parts[1]))
    slabs = [[(0, part)] for part in parts]
    moving = [[part, part] for part in parts]
    for hop in range(1, far + 1):
        for part in range(2):
            if hop < far or part == 0:
                moving[part][0] = lax.ppermute(moving[part][0], "pb", forward)
                slabs[part].append((-hop, moving[part][0]))
            if hop < far or part == 1:
                moving[part][1] = lax.ppermute(moving[part][1], "pb", backward)
                slabs[part].append((hop, moving[part][1]))
    attn = attend_with(inputs)
    across = lax.ppermute(attn, "ka", [(i, i ^ 2) for i in range(4)])
    beside = lax.ppermute(attn, "ka", [(i, i ^ 1) for i in range(4)])
    corner = lax.ppermute(across, "ka", [(i, i ^ 1) for i in range(4)])
    pieces = jnp.stack([attn, beside, across, corner])
    per = attn.shape[1] // depth
    around = jnp.asarray(
        [[ring[(ring.index(p) + step) % pb_size] for step in range(pb_size)] for p in range(pb_size)],
        jnp.int32,
    )
    sources = lax.dynamic_slice(around, (lax.axis_index("pb"), 0), (1, pb_size))[0]
    slots = jnp.bitwise_xor(sources // per, lax.axis_index("ka"))
    shifts = (sources % per) * depth
    results = []
    for part in range(2):
        total = None
        for offset, slab in slabs[part]:
            at = offset % pb_size
            left = lax.dynamic_slice(
                pieces, (slots[at], 0, shifts[at]), (1, attn.shape[0], depth)
            )[0]
            term = jnp.dot(left, slab, preferred_element_type=jnp.float32)
            total = term if total is None else total + term
        results.append(total.astype(jnp.bfloat16))
    return jnp.concatenate(results, axis=1)


def shards(queries, keys, values, block_ids, counts, refresh, cached_attn, wo):
    groups = lax.axis_size("ka")

    def attend_with(inputs):
        queries, keys, values, old = inputs
        parts, places = own_head_keys_values(keys, values)
        return attend(block_ids[0, 0], counts[0, 0], refresh[0, 0], queries, old, parts, places)

    inputs = (queries[0], keys, values, cached_attn[0])
    if lax.axis_size("pb") == 8 and groups == 4:
        mixed = project_ring(wo, inputs, attend_with)
    else:
        attn_full = lax.all_gather(attend_with(inputs), "ka", axis=1, tiled=True)
        mixed = jnp.dot(
            attn_full, lax.all_gather(wo, "pb", axis=0, tiled=True), preferred_element_type=jnp.float32
        ).astype(jnp.bfloat16)
    return mixed[None]


def solution(mesh):
    placed = (
        P(None, "pb", "ka"),
        P("ka", None),
        P("ka", None),
        P(None, "pb", None),
        P(None, "pb"),
        P(None, "pb"),
        P(None, "pb", "ka"),
        P("pb", "ka"),
    )
    return jax.shard_map(
        shards, mesh=mesh, in_specs=placed, out_specs=P(None, "pb", "ka"), check_vma=False
    )
```

time: 193 us -> 188 us (0.974)
  Pallas kernels: 0.62 us -> 18.7 us
  waiting for transfers between devices: 100 us -> 85.8 us
  starting transfers between devices: 20.8 us -> 15.1 us
  local copies, waits for them, and re-layouts: 9.56 us -> 5.72 us
    ppermute x3 -> x6, waiting for transfers between devices: 0.01 us -> 38.8 us  [the longest x3 20.4 us: own_head_keys_values(): lax.ppermute(head_of(partner), 'ka', [(i, i ^ step) for i in range(groups)])]
    ppermute x7, waiting for transfers between devices: 53.8 us -> 21.1 us  [project_ring(): moving[part][1] = lax.ppermute(moving[part][1], 'pb', backward)]
    ppermute x7, waiting for transfers between devices: 46.4 us -> 25.9 us  [project_ring(): moving[part][0] = lax.ppermute(moving[part][0], 'pb', forward)]
    pallas_call x1, Pallas kernels: 0.62 us -> 18.7 us  [attend(): pl.pallas_call(functools.partial(attention_kernel, heads, slots), out_sha...]
    all_to_all x1 -> x0, starting transfers between devices: 4.21 us -> none  [own_head_keys_values(): lax.all_to_all(both.reshape(rows, groups * 2 * HEAD_SIZE), 'ka', split_ax...]
    ppermute x7, starting transfers between devices: 9.84 us -> 5.67 us  [project_ring(): moving[part][1] = lax.ppermute(moving[part][1], 'pb', backward)]
    unnamed x16 -> x8, local copies, waits for them, and re-layouts: 3.96 us -> 0.98 us
  transfers between devices with their start and end apart: 18 -> 20, of which waited for: 7 -> 9; matrix products, arithmetic and copies ran while one was open for 16% -> 17% of each run, Pallas kernels for 0% -> 10%
where the time goes in v4:
time: 188 us; the launch traced here: 187 us
  waiting for transfers between devices  85.8 us (46%)
  between operations  30.7 us (16%)
  matrix products  24.3 us (13%)
  Pallas kernels  18.7 us (10%)
  starting transfers between devices  15.1 us (8%)
  other arithmetic  6.96 us (4%)
  local copies, waits for them, and re-layouts  5.72 us (3%)
    ppermute x7, waiting for transfers between devices, project_ring(): moving[part][0] = lax.ppermute(moving[part][0], 'pb', forward)  25.9 us
    dot_general x16, matrix products, project_ring(): term = jnp.dot(left, slab, preferred_element_type=jnp.float32)  24.3 us
    ppermute x7, waiting for transfers between devices, project_ring(): moving[part][1] = lax.ppermute(moving[part][1], 'pb', backward)  21.1 us
    ppermute x3, waiting for transfers between devices, own_head_keys_values(): lax.ppermute(head_of(partner), 'ka', [(i, i ^ step) for i in range(groups)])  20.4 us
    pallas_call x1, Pallas kernels, attend(): pl.pallas_call(functools.partial(attention_kernel, heads, slots), out_sha...  18.7 us
    ppermute x1, waiting for transfers between devices, project_ring(): across = lax.ppermute(attn, 'ka', [(i, i ^ 2) for i in range(4)])  18.4 us
    ppermute x7, starting transfers between devices, project_ring(): moving[part][0] = lax.ppermute(moving[part][0], 'pb', forward)  6.49 us
    ppermute x7, starting transfers between devices, project_ring(): moving[part][1] = lax.ppermute(moving[part][1], 'pb', backward)  5.67 us
  transfers between devices with their start and end apart: 20, of which 9 were waited for; matrix products, arithmetic and copies ran while one was open for 17% of the time, Pallas kernels for 10%

profile of v4, /device:TPU:0, one launch (start us, length us, event | category | flops | bytes accessed | tf_op | source)
XLA Modules:
  0.0 187.2 jit_solution(11542217566208450924)
XLA Ops:
  0.0 1.8 fusion.65
  1.8 3.0 %collective-permute-start.7 = (bf16[512,1024]{1,0:T(8,128)(2,1)S(1)}, bf16[512,1024]{1,0:T(8,128)(2,1)}, u32[]{:S(2)}, u32[]{:S(2)}) collective-permute-start(bf16[512,1024]{1,0:T(8,128)(2,1)S(1)} %get-tuple-element.15), channel_id=1, source_target_pairs={{8,0},{16,8},{24,16},{28,24},{20,28},{12,20},{4,12},{0,4},{9,1},{1... | collective-permute-start | bytes 3145736 | tf_op jit(solution)/shard_map/ppermute | solution.py:194
  4.8 2.2 %constant_dynamic-slice_fusion.1 = (bf16[1024,128]{1,0:T(8,128)(2,1)S(1)}, bf16[1024,128]{1,0:T(8,128)(2,1)S(1)}, bf16[1024,128]{1,0:T(8,128)(2,1)S(1)}, bf16[10...) fusion(bf16[1024,512]{1,0:T(8,128)(2,1)S(1)} %copy-done, ...), kind=kLoop, calls=%fused_computation.71 | loop fusion | bytes 4194320 | tf_op jit(solution)/shard_map/dynamic_slice | solution.py:145
  12.4 0.9 pad_maximum_fusion.1.refs_0_
  13.2 9.1 %collective-permute-done.2.refs_3_ = bf16[1024,256]{1,0:T(8,128)(2,1)} collective-permute-done((bf16[1024,256]{1,0:T(8,128)(2,1)}, bf16[1024,256]{1,0:T(8,128)(2,1)}, u32[]{:S(2)}, u32[]{:S(2)}) %collective-permute-start.2) | collective-permute-done | bytes 524320 | tf_op jit(solution)/shard_map/ppermute | solution.py:152
  22.4 11.3 %collective-permute-done.1.refs_2_ = bf16[1024,256]{1,0:T(8,128)(2,1)} collective-permute-done((bf16[1024,256]{1,0:T(8,128)(2,1)}, bf16[1024,256]{1,0:T(8,128)(2,1)}, u32[]{:S(2)}, u32[]{:S(2)}) %collective-permute-start.1) | collective-permute-done | bytes 524320 | tf_op jit(solution)/shard_map/ppermute | solution.py:152
  33.6 1.6 collective-permute-start.14
  35.2 18.7 %attend.1 = bf16[512,1024]{1,0:T(8,128)(2,1)S(1)} custom-call(s32[22]{0:T(128)S(1)} %concatenate.18.meta_ref, bf16[512,1024]{1,0:T(8,128)(2,1)} %bitcast.100, bf16[512,1024]{1,0:T(8,128)(2,1)} %bitcast.101, bf16[1024,256]{1,0:T(8,128)(2,1)} %pad_maximum_fusion.1.refs_0_, bf16[1024,256]{1,0:T(8,128)(2,1)} %collective-permute-done.refs_1_, ...), custom_call_target="tpu_custom_call" | custom-call | flops 1048576 | bytes 1048576 | tf_op jit(solution)/shard_map/attend/pallas_call | solution.py:109
  53.9 1.0 collective-permute-start.4
  55.0 3.5 %collective-permute-done.13 = bf16[512,1024]{1,0:T(8,128)(2,1)} collective-permute-done((bf16[512,1024]{1,0:T(8,128)(2,1)S(1)}, bf16[512,1024]{1,0:T(8,128)(2,1)}, u32[]{:S(2)}, u32[]{:S(2)}) %collective-permute-start.13) | collective-permute-done | bytes 1048608 | tf_op jit(solution)/shard_map/ppermute | solution.py:191
  59.3 1.2 collective-permute-start.15
  60.5 18.4 %collective-permute-done.4 = bf16[512,1024]{1,0:T(8,128)(2,1)} collective-permute-done((bf16[512,1024]{1,0:T(8,128)(2,1)S(1)}, bf16[512,1024]{1,0:T(8,128)(2,1)}, u32[]{:S(2)}, u32[]{:S(2)}) %collective-permute-start.4) | collective-permute-done | bytes 1048608 | tf_op jit(solution)/shard_map/ppermute | solution.py:197
  78.9 1.0 copy-done.1
  110.6 2.1 %collective-permute-start.10 = (bf16[512,1024]{1,0:T(8,128)(2,1)}, bf16[512,1024]{1,0:T(8,128)(2,1)S(1)}, u32[]{:S(2)}, u32[]{:S(2)}) collective-permute-start(bf16[512,1024]{1,0:T(8,128)(2,1)} %collective-permute-done.8), channel_id=1, source_target_pairs={{0,8},{8,16},{16,24},{24,28},{28,20},{20,12},{12,4},{4,0},{1,9},{9... | collective-permute-start | bytes 3145736 | tf_op jit(solution)/shard_map/ppermute | solution.py:191
  112.7 2.0 %collective-permute-start.17 = (bf16[512,1024]{1,0:T(8,128)(2,1)}, bf16[512,1024]{1,0:T(8,128)(2,1)S(1)}, u32[]{:S(2)}, u32[]{:S(2)}) collective-permute-start(bf16[512,1024]{1,0:T(8,128)(2,1)} %collective-permute-done.15), channel_id=1, source_target_pairs={{0,8},{8,16},{16,24},{24,28},{28,20},{20,12},{12,4},{4,0},{1,9},{9... | collective-permute-start | bytes 3145736 | tf_op jit(solution)/shard_map/ppermute | solution.py:191
  114.7 2.1 %pad_maximum_fusion = bf16[4,512,1024]{2,1,0:T(8,128)(2,1)S(1)} fusion(bf16[1,512,1024]{2,1,0:T(8,128)(2,1)} %bitcast.12, bf16[1,512,1024]{2,1,0:T(8,128)(2,1)} %bitcast.11, bf16[1,512,1024]{2,1,0:T(8,128)(2,1)} %bitcast.102, bf16[1,512,1024]{2,1,0:T(8,128)(2,1)S(1)} %bitcast.99), kind=kLoop, calls=%fused_computation | loop fusion | flops 6291456 | bytes 8388608 | tf_op jit(solution)/shard_map/stack | solution.py:200
  118.4 2.0 %fusion.12 = f32[512,1024]{1,0:T(8,128)S(1)} fusion(bf16[512,1024]{1,0:T(8,128)(2,1)} %collective-permute-done.9, bf16[4,512,1024]{2,1,0:T(8,128)(2,1)S(1)} %pad_maximum_fusion, s32[]{:T(128)S(6)} %select_n.110, s32[]{:T(128)S(6)} %select_n.111), kind=kOutput, calls=%fused_computation.20 | convolution fusion | flops 536870912 | bytes 3670024 | tf_op jit(solution)/shard_map/dot_general | solution.py:217
  120.4 2.0 %fusion.10 = f32[512,1024]{1,0:T(8,128)S(1)} fusion(bf16[512,1024]{1,0:T(8,128)(2,1)} %collective-permute-done.16, bf16[4,512,1024]{2,1,0:T(8,128)(2,1)S(1)} %pad_maximum_fusion, s32[]{:T(128)S(6)} %select_n.110, s32[]{:T(128)S(6)} %select_n.111), kind=kOutput, calls=%fused_computation.18 | convolution fusion | flops 536870912 | bytes 3670024 | tf_op jit(solution)/shard_map/dot_general | solution.py:217
  122.4 2.0 %fusion.16 = f32[512,1024]{1,0:T(8,128)S(1)} fusion(bf16[512,1024]{1,0:T(8,128)(2,1)} %collective-permute-done.8, bf16[4,512,1024]{2,1,0:T(8,128)(2,1)S(1)} %pad_maximum_fusion, s32[]{:T(128)S(6)} %select_n.108, s32[]{:T(128)S(6)} %select_n.109), kind=kOutput, calls=%fused_computation.24 | convolution fusion | flops 536870912 | bytes 3670024 | tf_op jit(solution)/shard_map/dot_general | solution.py:217
  124.4 2.0 %fusion.14 = f32[512,1024]{1,0:T(8,128)S(1)} fusion(bf16[512,1024]{1,0:T(8,128)(2,1)} %collective-permute-done.15, bf16[4,512,1024]{2,1,0:T(8,128)(2,1)S(1)} %pad_maximum_fusion, s32[]{:T(128)S(6)} %select_n.108, s32[]{:T(128)S(6)} %select_n.109), kind=kOutput, calls=%fused_computation.22 | convolution fusion | flops 536870912 | bytes 3670024 | tf_op jit(solution)/shard_map/dot_general | solution.py:217
  126.4 2.0 %fusion.20 = f32[512,1024]{1,0:T(8,128)S(1)} fusion(bf16[512,1024]{1,0:T(8,128)(2,1)} %collective-permute-done.7, bf16[4,512,1024]{2,1,0:T(8,128)(2,1)S(1)} %pad_maximum_fusion, s32[]{:T(128)S(6)} %select_n.106, s32[]{:T(128)S(6)} %select_n.107), kind=kOutput, calls=%fused_computation.28 | convolution fusion | flops 536870912 | bytes 3670024 | tf_op jit(solution)/shard_map/dot_general | solution.py:217
  128.4 2.0 %fusion.18 = f32[512,1024]{1,0:T(8,128)S(1)} fusion(bf16[512,1024]{1,0:T(8,128)(2,1)} %collective-permute-done.14, bf16[4,512,1024]{2,1,0:T(8,128)(2,1)S(1)} %pad_maximum_fusion, s32[]{:T(128)S(6)} %select_n.106, s32[]{:T(128)S(6)} %select_n.107), kind=kOutput, calls=%fused_computation.26 | convolution fusion | flops 536870912 | bytes 3670024 | tf_op jit(solution)/shard_map/dot_general | solution.py:217
  130.4 2.0 %fusion.24 = f32[512,1024]{1,0:T(8,128)S(1)} fusion(bf16[512,1024]{1,0:T(8,128)(2,1)} %collective-permute-done.6, bf16[4,512,1024]{2,1,0:T(8,128)(2,1)S(1)} %pad_maximum_fusion, s32[]{:T(128)S(6)} %select_n.104, s32[]{:T(128)S(6)} %select_n.105), kind=kOutput, calls=%fused_computation.32 | convolution fusion | flops 536870912 | bytes 3670024 | tf_op jit(solution)/shard_map/dot_general | solution.py:217
  132.4 2.0 %fusion.22 = f32[512,1024]{1,0:T(8,128)S(1)} fusion(bf16[512,1024]{1,0:T(8,128)(2,1)} %collective-permute-done.13, bf16[4,512,1024]{2,1,0:T(8,128)(2,1)S(1)} %pad_maximum_fusion, s32[]{:T(128)S(6)} %select_n.104, s32[]{:T(128)S(6)} %select_n.105), kind=kOutput, calls=%fused_computation.30 | convolution fusion | flops 536870912 | bytes 3670024 | tf_op jit(solution)/shard_map/dot_general | solution.py:217
  134.4 3.9 %collective-permute-done.10 = bf16[512,1024]{1,0:T(8,128)(2,1)S(1)} collective-permute-done((bf16[512,1024]{1,0:T(8,128)(2,1)}, bf16[512,1024]{1,0:T(8,128)(2,1)S(1)}, u32[]{:S(2)}, u32[]{:S(2)}) %collective-permute-start.10) | collective-permute-done | bytes 1048608 | tf_op jit(solution)/shard_map/ppermute | solution.py:191
  138.8 20.4 %collective-permute-done.18 = bf16[512,1024]{1,0:T(8,128)(2,1)} collective-permute-done((bf16[512,1024]{1,0:T(8,128)(2,1)}, bf16[512,1024]{1,0:T(8,128)(2,1)}, u32[]{:S(2)}, u32[]{:S(2)}) %collective-permute-start.18) | collective-permute-done | bytes 1048608 | tf_op jit(solution)/shard_map/ppermute | solution.py:194
  159.2 0.9 collective-permute-start.19
  160.1 2.0 %fusion.2 = f32[512,1024]{1,0:T(8,128)S(1)} fusion(bf16[512,1024]{1,0:T(8,128)(2,1)} %collective-permute-done.18, bf16[4,512,1024]{2,1,0:T(8,128)(2,1)S(1)} %pad_maximum_fusion, s32[]{:T(128)S(6)} %select_n.114, s32[]{:T(128)S(6)} %select_n.115), kind=kOutput, calls=%fused_computation.10 | convolution fusion | flops 536870912 | bytes 3670024 | tf_op jit(solution)/shard_map/dot_general | solution.py:217
  164.5 18.5 %collective-permute-done.12 = bf16[512,1024]{1,0:T(8,128)(2,1)S(1)} collective-permute-done((bf16[512,1024]{1,0:T(8,128)(2,1)S(1)}, bf16[512,1024]{1,0:T(8,128)(2,1)S(1)}, u32[]{:S(2)}, u32[]{:S(2)}) %collective-permute-start.12) | collective-permute-done | bytes 1048608 | tf_op jit(solution)/shard_map/ppermute | solution.py:191
  182.9 1.2 add_convert_fusion.1
  184.4 1.3 add_convert_fusion
  185.7 1.5 maximum_bitcast_fusion
  (44 shorter events, 11.2 us)
Async XLA Ops:
  0.0 4.8 %copy-start = (bf16[1024,512]{1,0:T(8,128)(2,1)S(1)}, bf16[1024,512]{1,0:T(8,128)(2,1)}, u32[]{:S(2)}) copy-start(bf16[1024,512]{1,0:T(8,128)(2,1)} %param.11) | copy-start | bytes 3145732
  1.8 53.1 %collective-permute-start.7 = (bf16[512,1024]{1,0:T(8,128)(2,1)S(1)}, bf16[512,1024]{1,0:T(8,128)(2,1)}, u32[]{:S(2)}, u32[]{:S(2)}) collective-permute-start(bf16[512,1024]{1,0:T(8,128)(2,1)S(1)} %get-tuple-element.15), channel_id=1, source_target_pairs={{8,0},{16,8},{24,16},{28,24},{20,28},{12,20},{4,12},{0,4},{9,1},{1... | collective-permute-start | bytes 3145736 | tf_op jit(solution)/shard_map/ppermute | solution.py:194
  7.0 5.3 %copy-start.3 = (s32[1,1,16]{2,1,0:T(1,128)S(1)}, s32[1,1,16]{2,1,0:T(1,128)}, u32[]{:S(2)}) copy-start(s32[1,1,16]{2,1,0:T(1,128)} %param.12) | copy-start | bytes 196
  7.0 5.4 %copy-start.2 = (bf16[1024,128]{1,0:T(8,128)(2,1)S(1)}, bf16[1024,128]{1,0:T(8,128)(2,1)}, u32[]{:S(2)}) copy-start(bf16[1024,128]{1,0:T(8,128)(2,1)} %get-tuple-element.53) | copy-start | bytes 786436
  7.8 14.5 %collective-permute-start.2 = (bf16[1024,256]{1,0:T(8,128)(2,1)}, bf16[1024,256]{1,0:T(8,128)(2,1)}, u32[]{:S(2)}, u32[]{:S(2)}) collective-permute-start(bf16[1024,256]{1,0:T(8,128)(2,1)} %pad_maximum_fusion.4), channel_id=1, source_target_pairs={{0,3},{1,2},{2,1},{3,0},{4,7},{5,6},{6,5},{7,4},{8,11},{9,10},{10,... | collective-permute-start | bytes 1572872 | tf_op jit(solution)/shard_map/ppermute | solution.py:152
  9.3 24.3 %collective-permute-start.1 = (bf16[1024,256]{1,0:T(8,128)(2,1)}, bf16[1024,256]{1,0:T(8,128)(2,1)}, u32[]{:S(2)}, u32[]{:S(2)}) collective-permute-start(bf16[1024,256]{1,0:T(8,128)(2,1)} %pad_maximum_fusion.3), channel_id=1, source_target_pairs={{0,2},{1,3},{2,0},{3,1},{4,6},{5,7},{6,4},{7,5},{8,10},{9,11},{10,... | collective-permute-start | bytes 1572872 | tf_op jit(solution)/shard_map/ppermute | solution.py:152
  10.2 25.0 %collective-permute-start = (bf16[1024,256]{1,0:T(8,128)(2,1)S(1)}, bf16[1024,256]{1,0:T(8,128)(2,1)}, u32[]{:S(2)}, u32[]{:S(2)}) collective-permute-start(bf16[1024,256]{1,0:T(8,128)(2,1)S(1)} %pad_maximum_fusion.2), channel_id=1, source_target_pairs={{0,1},{1,0},{2,3},{3,2},{4,5},{5,4},{6,7},{7,6},{8,9},{9,8},{10,11... | collective-permute-start | bytes 1572872 | tf_op jit(solution)/shard_map/ppermute | solution.py:152
  10.7 44.2 %collective-permute-start.6 = (bf16[512,1024]{1,0:T(8,128)(2,1)S(1)}, bf16[512,1024]{1,0:T(8,128)(2,1)}, u32[]{:S(2)}, u32[]{:S(2)}) collective-permute-start(bf16[512,1024]{1,0:T(8,128)(2,1)S(1)} %get-tuple-element.15), channel_id=1, source_target_pairs={{0,8},{8,16},{16,24},{24,28},{28,20},{20,12},{12,4},{4,0},{1,9},{9... | collective-permute-start | bytes 3145736 | tf_op jit(solution)/shard_map/ppermute | solution.py:191
  22.4 36.1 %collective-permute-start.13 = (bf16[512,1024]{1,0:T(8,128)(2,1)S(1)}, bf16[512,1024]{1,0:T(8,128)(2,1)}, u32[]{:S(2)}, u32[]{:S(2)}) collective-permute-start(bf16[512,1024]{1,0:T(8,128)(2,1)S(1)} %get-tuple-element.16), channel_id=1, source_target_pairs={{0,8},{8,16},{16,24},{24,28},{28,20},{20,12},{12,4},{4,0},{1,9},{9... | collective-permute-start | bytes 3145736 | tf_op jit(solution)/shard_map/ppermute | solution.py:191
  33.6 25.7 %collective-permute-start.14 = (bf16[512,1024]{1,0:T(8,128)(2,1)S(1)}, bf16[512,1024]{1,0:T(8,128)(2,1)}, u32[]{:S(2)}, u32[]{:S(2)}) collective-permute-start(bf16[512,1024]{1,0:T(8,128)(2,1)S(1)} %get-tuple-element.16), channel_id=1, source_target_pairs={{8,0},{16,8},{24,16},{28,24},{20,28},{12,20},{4,12},{0,4},{9,1},{1... | collective-permute-start | bytes 3145736 | tf_op jit(solution)/shard_map/ppermute | solution.py:194
  53.9 25.0 %collective-permute-start.4 = (bf16[512,1024]{1,0:T(8,128)(2,1)S(1)}, bf16[512,1024]{1,0:T(8,128)(2,1)}, u32[]{:S(2)}, u32[]{:S(2)}) collective-permute-start(bf16[512,1024]{1,0:T(8,128)(2,1)S(1)} %attend.1), channel_id=1, source_target_pairs={{0,2},{1,3},{2,0},{3,1},{4,6},{5,7},{6,4},{7,5},{8,10},{9,11},{10,... | collective-permute-start | bytes 3145736 | tf_op jit(solution)/shard_map/ppermute | solution.py:197
  54.9 24.0 %collective-permute-start.3 = (bf16[512,1024]{1,0:T(8,128)(2,1)S(1)}, bf16[512,1024]{1,0:T(8,128)(2,1)S(1)}, u32[]{:S(2)}, u32[]{:S(2)}) collective-permute-start(bf16[512,1024]{1,0:T(8,128)(2,1)S(1)} %attend.1), channel_id=1, source_target_pairs={{0,1},{1,0},{2,3},{3,2},{4,5},{5,4},{6,7},{7,6},{8,9},{9,8},{10,11... | collective-permute-start | bytes 3145736 | tf_op jit(solution)/shard_map/ppermute | solution.py:198
  54.9 55.6 %collective-permute-start.9 = (bf16[512,1024]{1,0:T(8,128)(2,1)}, bf16[512,1024]{1,0:T(8,128)(2,1)}, u32[]{:S(2)}, u32[]{:S(2)}) collective-permute-start(bf16[512,1024]{1,0:T(8,128)(2,1)} %collective-permute-done.7), channel_id=1, source_target_pairs={{8,0},{16,8},{24,16},{28,24},{20,28},{12,20},{4,12},{0,4},{9,1},{1... | collective-permute-start | bytes 3145736 | tf_op jit(solution)/shard_map/ppermute | solution.py:194
  58.5 52.1 %collective-permute-start.8 = (bf16[512,1024]{1,0:T(8,128)(2,1)}, bf16[512,1024]{1,0:T(8,128)(2,1)}, u32[]{:S(2)}, u32[]{:S(2)}) collective-permute-start(bf16[512,1024]{1,0:T(8,128)(2,1)} %collective-permute-done.6), channel_id=1, source_target_pairs={{0,8},{8,16},{16,24},{24,28},{28,20},{20,12},{12,4},{4,0},{1,9},{9... | collective-permute-start | bytes 3145736 | tf_op jit(solution)/shard_map/ppermute | solution.py:191
  59.3 53.3 %collective-permute-start.15 = (bf16[512,1024]{1,0:T(8,128)(2,1)}, bf16[512,1024]{1,0:T(8,128)(2,1)}, u32[]{:S(2)}, u32[]{:S(2)}) collective-permute-start(bf16[512,1024]{1,0:T(8,128)(2,1)} %collective-permute-done.13), channel_id=1, source_target_pairs={{0,8},{8,16},{16,24},{24,28},{28,20},{20,12},{12,4},{4,0},{1,9},{9... | collective-permute-start | bytes 3145736 | tf_op jit(solution)/shard_map/ppermute | solution.py:191
  78.9 35.7 %collective-permute-start.16 = (bf16[512,1024]{1,0:T(8,128)(2,1)}, bf16[512,1024]{1,0:T(8,128)(2,1)}, u32[]{:S(2)}, u32[]{:S(2)}) collective-permute-start(bf16[512,1024]{1,0:T(8,128)(2,1)} %collective-permute-done.14), channel_id=1, source_target_pairs={{8,0},{16,8},{24,16},{28,24},{20,28},{12,20},{4,12},{0,4},{9,1},{1... | collective-permute-start | bytes 3145736 | tf_op jit(solution)/shard_map/ppermute | solution.py:194
  78.9 1.0 copy-start.1
  79.9 34.8 %collective-permute-start.5 = (bf16[512,1024]{1,0:T(8,128)(2,1)}, bf16[512,1024]{1,0:T(8,128)(2,1)}, u32[]{:S(2)}, u32[]{:S(2)}) collective-permute-start(bf16[512,1024]{1,0:T(8,128)(2,1)} %collective-permute-done.4), channel_id=1, source_target_pairs={{0,1},{1,0},{2,3},{3,2},{4,5},{5,4},{6,7},{7,6},{8,9},{9,8},{10,11... | collective-permute-start | bytes 3145736 | tf_op jit(solution)/shard_map/ppermute | solution.py:199
  110.5 51.6 %collective-permute-start.11 = (bf16[512,1024]{1,0:T(8,128)(2,1)}, bf16[512,1024]{1,0:T(8,128)(2,1)S(1)}, u32[]{:S(2)}, u32[]{:S(2)}) collective-permute-start(bf16[512,1024]{1,0:T(8,128)(2,1)} %collective-permute-done.9), channel_id=1, source_target_pairs={{8,0},{16,8},{24,16},{28,24},{20,28},{12,20},{4,12},{0,4},{9,1},{1... | collective-permute-start | bytes 3145736 | tf_op jit(solution)/shard_map/ppermute | solution.py:194
  110.6 27.8 %collective-permute-start.10 = (bf16[512,1024]{1,0:T(8,128)(2,1)}, bf16[512,1024]{1,0:T(8,128)(2,1)S(1)}, u32[]{:S(2)}, u32[]{:S(2)}) collective-permute-start(bf16[512,1024]{1,0:T(8,128)(2,1)} %collective-permute-done.8), channel_id=1, source_target_pairs={{0,8},{8,16},{16,24},{24,28},{28,20},{20,12},{12,4},{4,0},{1,9},{9... | collective-permute-start | bytes 3145736 | tf_op jit(solution)/shard_map/ppermute | solution.py:191
  112.7 51.0 %collective-permute-start.17 = (bf16[512,1024]{1,0:T(8,128)(2,1)}, bf16[512,1024]{1,0:T(8,128)(2,1)S(1)}, u32[]{:S(2)}, u32[]{:S(2)}) collective-permute-start(bf16[512,1024]{1,0:T(8,128)(2,1)} %collective-permute-done.15), channel_id=1, source_target_pairs={{0,8},{8,16},{16,24},{24,28},{28,20},{20,12},{12,4},{4,0},{1,9},{9... | collective-permute-start | bytes 3145736 | tf_op jit(solution)/shard_map/ppermute | solution.py:191
  114.6 44.6 %collective-permute-start.18 = (bf16[512,1024]{1,0:T(8,128)(2,1)}, bf16[512,1024]{1,0:T(8,128)(2,1)}, u32[]{:S(2)}, u32[]{:S(2)}) collective-permute-start(bf16[512,1024]{1,0:T(8,128)(2,1)} %collective-permute-done.16), channel_id=1, source_target_pairs={{8,0},{16,8},{24,16},{28,24},{20,28},{12,20},{4,12},{0,4},{9,1},{1... | collective-permute-start | bytes 3145736 | tf_op jit(solution)/shard_map/ppermute | solution.py:194
  138.4 44.6 %collective-permute-start.12 = (bf16[512,1024]{1,0:T(8,128)(2,1)S(1)}, bf16[512,1024]{1,0:T(8,128)(2,1)S(1)}, u32[]{:S(2)}, u32[]{:S(2)}) collective-permute-start(bf16[512,1024]{1,0:T(8,128)(2,1)S(1)} %collective-permute-done.10), channel_id=1, source_target_pairs={{0,8},{8,16},{16,24},{24,28},{28,20},{20,12},{12,4},{4,0},{1,9},{9... | collective-permute-start | bytes 3145736 | tf_op jit(solution)/shard_map/ppermute | solution.py:191
  159.2 25.2 %collective-permute-start.19 = (bf16[512,1024]{1,0:T(8,128)(2,1)}, bf16[512,1024]{1,0:T(8,128)(2,1)S(1)}, u32[]{:S(2)}, u32[]{:S(2)}) collective-permute-start(bf16[512,1024]{1,0:T(8,128)(2,1)} %collective-permute-done.18), channel_id=1, source_target_pairs={{8,0},{16,8},{24,16},{28,24},{20,28},{12,20},{4,12},{0,4},{9,1},{1... | collective-permute-start | bytes 3145736 | tf_op jit(solution)/shard_map/ppermute | solution.py:194

commit v5 on v4

--- a/solution.py
+++ b/solution.py
@@ -173,6 +173,117 @@
     return list(range(pb_size))
 
 
+ROW_TILE = 128
+
+
+def ring_product_kernel(steps, has_base, last, where_ref, *refs):
+    count = len(steps)
+    blocks, slabs, refs = refs[:4], (refs[4 : 4 + count], refs[4 + count : 4 + 2 * count]), refs[4 + 2 * count :]
+    if has_base:
+        base_ref, refs = refs[0], refs[1:]
+    out_ref, left, right, block_sems, slab_sems = refs[:5]
+    rows, depth = left.shape[0], right.shape[1] // count
+    per = blocks[0].shape[1] // depth
+    me = where_ref[where_ref.shape[0] - 1]
+
+    def block_copy(index, slot, shift):
+        return pltpu.make_async_copy(
+            blocks[slot].at[:, pl.ds(shift, depth)],
+            left.at[:, pl.ds(index * depth, depth)],
+            block_sems.at[index],
+        )
+
+    def slab_copy(half, index):
+        return pltpu.make_async_copy(
+            slabs[half][index],
+            right.at[half, pl.ds(index * depth, depth), :],
+            slab_sems.at[half, index],
+        )
+
+    for index, step in enumerate(steps):
+        source = where_ref[step]
+        slot_here = jnp.bitwise_xor(source // per, me)
+        shift = pl.multiple_of((source % per) * depth, depth)
+        for slot in range(4):
+
+            @pl.when(slot_here == slot)
+            def _(slot=slot):
+                block_copy(index, slot, shift).start()
+
+    for half in range(2):
+        for index in range(count):
+            slab_copy(half, index).start()
+    for index in range(count):
+        block_copy(index, 0, 0).wait()
+    half_columns = right.shape[2]
+    if last:
+        staged, out_sems = refs[5:]
+    for half in range(2):
+        columns = pl.ds(half * half_columns, half_columns)
+        for index in range(count):
+            slab_copy(half, index).wait()
+
+        def rows_tile(step, carry):
+            at = pl.ds(pl.multiple_of(step * ROW_TILE, ROW_TILE), ROW_TILE)
+            product = jnp.dot(left[at, :], right[half], preferred_element_type=jnp.float32)
+            if has_base:
+                product = product + base_ref[at, columns]
+            if last:
+                staged[at, columns] = product.astype(jnp.bfloat16)
+            else:
+                out_ref[at, columns] = product
+            return carry
+
+        lax.fori_loop(0, rows // ROW_TILE, rows_tile, 0)
+        if last:
+            pltpu.make_async_copy(
+                staged.at[:, columns], out_ref.at[:, columns], out_sems.at[half]
+            ).start()
+    if last:
+        for half in range(2):
+            columns = pl.ds(half * half_columns, half_columns)
+            pltpu.make_async_copy(
+                staged.at[:, columns], out_ref.at[:, columns], out_sems.at[half]
+            ).wait()
+
+
+def ring_product(where, blocks, steps, slabs, base, last):
+    count = len(steps)
+    rows = blocks[0].shape[0]
+    depth, half = slabs[0][0].shape
+    in_hbm = pl.BlockSpec(memory_space=pltpu.HBM)
+    in_vmem = pl.BlockSpec(memory_space=pltpu.VMEM)
+    scratch = [
+        pltpu.VMEM((rows, count * depth), jnp.bfloat16),
+        pltpu.VMEM((2, count * depth, half), jnp.bfloat16),
+        pltpu.SemaphoreType.DMA((count,)),
+        pltpu.SemaphoreType.DMA((2, count)),
+    ]
+    if last:
+        scratch += [pltpu.VMEM((rows, 2 * half), jnp.bfloat16), pltpu.SemaphoreType.DMA((2,))]
+    return pl.pallas_call(
+        functools.partial(ring_product_kernel, steps, base is not None, last),
+        out_shape=jax.ShapeDtypeStruct((rows, 2 * half), jnp.bfloat16 if last else jnp.float32),
+        in_specs=[pl.BlockSpec(memory_space=pltpu.SMEM)]
+        + [in_hbm] * (4 + 2 * count)
+        + [in_vmem] * (base is not None),
+        out_specs=in_hbm if last else in_vmem,
+        scratch_shapes=scratch,
+        compiler_params=pltpu.CompilerParams(vmem_limit_bytes=(8 + 4 * count) << 20),
+        cost_estimate=pl.CostEstimate(
+            flops=1 << 20, transcendentals=0, bytes_accessed=1 << 20
+        ),
+        name="ring_product",
+    )(
+        where,
+        *[
+            pltpu.with_memory_space_constraint(x, pltpu.HBM)
+            for x in (*blocks, *slabs[0], *slabs[1])
+        ],
+        *([] if base is None else [base]),
+    )
+
+
 def project_ring(wo, inputs, attend_with):
     pb_size = lax.axis_size("pb")
     depth, columns = wo.shape
@@ -197,27 +308,20 @@
     across = lax.ppermute(attn, "ka", [(i, i ^ 2) for i in range(4)])
     beside = lax.ppermute(attn, "ka", [(i, i ^ 1) for i in range(4)])
     corner = lax.ppermute(across, "ka", [(i, i ^ 1) for i in range(4)])
-    pieces = jnp.stack([attn, beside, across, corner])
-    per = attn.shape[1] // depth
     around = jnp.asarray(
         [[ring[(ring.index(p) + step) % pb_size] for step in range(pb_size)] for p in range(pb_size)],
         jnp.int32,
     )
-    sources = lax.dynamic_slice(around, (lax.axis_index("pb"), 0), (1, pb_size))[0]
-    slots = jnp.bitwise_xor(sources // per, lax.axis_index("ka"))
-    shifts = (sources % per) * depth
-    results = []
-    for part in range(2):
-        total = None
-        for offset, slab in slabs[part]:
-            at = offset % pb_size
-            left = lax.dynamic_slice(
-                pieces, (slots[at], 0, shifts[at]), (1, attn.shape[0], depth)
-            )[0]
-            term = jnp.dot(left, slab, preferred_element_type=jnp.float32)
-            total = term if total is None else total + term
-        results.append(total.astype(jnp.bfloat16))
-    return jnp.concatenate(results, axis=1)
+    mine = lax.dynamic_slice(around, (lax.axis_index("pb"), 0), (1, pb_size))[0]
+    where = jnp.concatenate([mine, lax.axis_index("ka")[None].astype(jnp.int32)])
+    blocks = [attn, beside, across, corner]
+    at_step = [{offset % pb_size: slab for offset, slab in slabs[part]} for part in range(2)]
+    total = None
+    for offsets in ((0, -1, 1, -2, 2), (-3, 3), (4,)):
+        chosen = [[at_step[part][offset % pb_size] for offset in offsets] for part in range(2)]
+        steps = tuple(offset % pb_size for offset in offsets)
+        total = ring_product(where, blocks, steps, chosen, total, offsets == (far,))
+    return total
 
 
 def shards(queries, keys, values, block_ids, counts, refresh, cached_attn, wo):

time: 188 us -> 176 us (0.936)
  starting transfers between devices: 15.1 us -> 51.2 us
  between operations: 30.7 us -> 1.4 us
  matrix products: 24.3 us -> 0 us
  Pallas kernels: 18.7 us -> 25.5 us
  waiting for transfers between devices: 85.8 us -> 92.2 us
  other arithmetic: 6.96 us -> 1.13 us
    ppermute x7, starting transfers between devices: 6.49 us -> 36.8 us  [project_ring(): moving[part][0] = lax.ppermute(moving[part][0], 'pb', forward)]
    dot_general x16 -> x0, matrix products: 24.3 us -> none  [project_ring(): term = jnp.dot(left, slab, preferred_element_type=jnp.float32)]
    pallas_call x0 -> x3, Pallas kernels: none -> 23.7 us  [ring_product(): pl.pallas_call(functools.partial(ring_product_kernel, steps, base is not...]
    ppermute x7, waiting for transfers between devices: 21.1 us -> 42 us  [project_ring(): moving[part][1] = lax.ppermute(moving[part][1], 'pb', backward)]
    ppermute x1, waiting for transfers between devices: 18.4 us -> 0.58 us  [project_ring(): across = lax.ppermute(attn, 'ka', [(i, i ^ 2) for i in range(4)])]
    pallas_call x1, Pallas kernels: 18.7 us -> 1.81 us  [attend(): pl.pallas_call(functools.partial(attention_kernel, heads, slots), out_sha...]
    ppermute x7, starting transfers between devices: 5.67 us -> 11.5 us  [project_ring(): moving[part][1] = lax.ppermute(moving[part][1], 'pb', backward)]
    ppermute x7, waiting for transfers between devices: 25.9 us -> 31 us  [project_ring(): moving[part][0] = lax.ppermute(moving[part][0], 'pb', forward)]
  transfers between devices with their start and end apart: 20 -> 20, of which waited for: 9 -> 14; matrix products, arithmetic and copies ran while one was open for 17% -> 2% of each run, Pallas kernels for 10% -> 11%
where the time goes in v5:
time: 176 us
  waiting for transfers between devices  92.2 us (52%)
  starting transfers between devices  51.2 us (29%)
  Pallas kernels  25.5 us (14%)
  local copies, waits for them, and re-layouts  4.71 us (3%)
    ppermute x7, waiting for transfers between devices, project_ring(): moving[part][1] = lax.ppermute(moving[part][1], 'pb', backward)  42 us
    ppermute x7, starting transfers between devices, project_ring(): moving[part][0] = lax.ppermute(moving[part][0], 'pb', forward)  36.8 us
    ppermute x7, waiting for transfers between devices, project_ring(): moving[part][0] = lax.ppermute(moving[part][0], 'pb', forward)  31 us
    pallas_call x3, Pallas kernels, ring_product(): pl.pallas_call(functools.partial(ring_product_kernel, steps, base is not...  23.7 us
    ppermute x3, waiting for transfers between devices, own_head_keys_values(): lax.ppermute(head_of(partner), 'ka', [(i, i ^ step) for i in range(groups)])  18.6 us
    ppermute x7, starting transfers between devices, project_ring(): moving[part][1] = lax.ppermute(moving[part][1], 'pb', backward)  11.5 us
  transfers between devices with their start and end apart: 20, of which 14 were waited for; matrix products, arithmetic and copies ran while one was open for 2% of the time, Pallas kernels for 11%

profile of v5, /device:TPU:0, one launch (start us, length us, event | category | flops | bytes accessed | tf_op | source)
XLA Modules:
  0.0 176.1 jit_solution(9983094610944720968)
XLA Ops:
  0.0 2.8 %fusion.1 = (bf16[512,1024]{1,0:T(8,128)(2,1)}, bf16[512,1024]{1,0:T(8,128)(2,1)S(1)}) fusion(bf16[512,2048]{1,0:T(8,128)(2,1)} %param.16), kind=kLoop, calls=%fused_computation.15 | loop fusion | bytes 4194304 | tf_op jit(solution)/shard_map/slice | solution.py:295
  2.8 3.0 %collective-permute-start.10 = (bf16[512,1024]{1,0:T(8,128)(2,1)}, bf16[512,1024]{1,0:T(8,128)(2,1)}, u32[]{:S(2)}, u32[]{:S(2)}) collective-permute-start(bf16[512,1024]{1,0:T(8,128)(2,1)} %get-tuple-element.16.refs_9_), channel_id=1, source_target_pairs={{8,0},{16,8},{24,16},{28,24},{20,28},{12,20},{4,12},{0,4},{9,1},{1... | collective-permute-start | bytes 3145736 | tf_op jit(solution)/shard_map/ppermute | solution.py:305
  5.9 1.1 constant_dynamic-slice_fusion
  7.0 0.9 collective-permute-start.2
  7.9 1.2 collective-permute-start.1
  11.7 9.3 %collective-permute-done.2.refs_3_ = bf16[1024,256]{1,0:T(8,128)(2,1)} collective-permute-done((bf16[1024,256]{1,0:T(8,128)(2,1)S(1)}, bf16[1024,256]{1,0:T(8,128)(2,1)}, u32[]{:S(2)}, u32[]{:S(2)}) %collective-permute-start.2) | collective-permute-done | bytes 524320 | tf_op jit(solution)/shard_map/ppermute | solution.py:152
  21.0 2.3 %collective-permute-start.14 = (bf16[512,1024]{1,0:T(8,128)(2,1)S(1)}, bf16[512,1024]{1,0:T(8,128)(2,1)S(1)}, u32[]{:S(2)}, u32[]{:S(2)}) collective-permute-start(bf16[512,1024]{1,0:T(8,128)(2,1)S(1)} %get-tuple-element.15.refs_4_), channel_id=1, source_target_pairs={{8,0},{16,8},{24,16},{28,24},{20,28},{12,20},{4,12},{0,4},{9,1},{1... | collective-permute-start | bytes 3145736 | tf_op jit(solution)/shard_map/ppermute | solution.py:305
  23.3 9.3 %collective-permute-done.1.refs_2_ = bf16[1024,256]{1,0:T(8,128)(2,1)} collective-permute-done((bf16[1024,256]{1,0:T(8,128)(2,1)S(1)}, bf16[1024,256]{1,0:T(8,128)(2,1)}, u32[]{:S(2)}, u32[]{:S(2)}) %collective-permute-start.1) | collective-permute-done | bytes 524320 | tf_op jit(solution)/shard_map/ppermute | solution.py:152
  32.6 2.0 %collective-permute-start.17 = (bf16[512,1024]{1,0:T(8,128)(2,1)}, bf16[512,1024]{1,0:T(8,128)(2,1)S(1)}, u32[]{:S(2)}, u32[]{:S(2)}) collective-permute-start(bf16[512,1024]{1,0:T(8,128)(2,1)} %get-tuple-element.16.refs_9_), channel_id=1, source_target_pairs={{0,8},{8,16},{16,24},{24,28},{28,20},{20,12},{12,4},{4,0},{1,9},{9... | collective-permute-start | bytes 3145736 | tf_op jit(solution)/shard_map/ppermute | solution.py:302
  34.7 1.8 %attend.1.refs_0_ = bf16[512,1024]{1,0:T(8,128)(2,1)S(1)} custom-call(s32[22]{0:T(128)S(1)} %concatenate.19.meta_ref, bf16[512,1024]{1,0:T(8,128)(2,1)} %bitcast.14, bf16[512,1024]{1,0:T(8,128)(2,1)} %bitcast.15, bf16[1024,256]{1,0:T(8,128)(2,1)} %pad_maximum_fusion.refs_0_, bf16[1024,256]{1,0:T(8,128)(2,1)} %collective-permute-done.refs_1_, ...), custom_call_target="tpu_custom_call" | custom-call | flops 1048576 | bytes 1048576 | tf_op jit(solution)/shard_map/attend/pallas_call | solution.py:109
  37.5 14.1 %collective-permute-start.7 = (bf16[512,1024]{1,0:T(8,128)(2,1)}, bf16[512,1024]{1,0:T(8,128)(2,1)S(1)}, u32[]{:S(2)}, u32[]{:S(2)}) collective-permute-start(bf16[512,1024]{1,0:T(8,128)(2,1)} %collective-permute-done.6.refs_5_), channel_id=1, source_target_pairs={{0,8},{8,16},{16,24},{24,28},{28,20},{20,12},{12,4},{4,0},{1,9},{9... | collective-permute-start | bytes 3145736 | tf_op jit(solution)/shard_map/ppermute | solution.py:302
  52.1 6.8 %collective-permute-done.17.refs_10_ = bf16[512,1024]{1,0:T(8,128)(2,1)S(1)} collective-permute-done((bf16[512,1024]{1,0:T(8,128)(2,1)}, bf16[512,1024]{1,0:T(8,128)(2,1)S(1)}, u32[]{:S(2)}, u32[]{:S(2)}) %collective-permute-start.17) | collective-permute-done | bytes 1048608 | tf_op jit(solution)/shard_map/ppermute | solution.py:302
  58.8 2.0 %collective-permute-start.15 = (bf16[512,1024]{1,0:T(8,128)(2,1)S(1)}, bf16[512,1024]{1,0:T(8,128)(2,1)}, u32[]{:S(2)}, u32[]{:S(2)}) collective-permute-start(bf16[512,1024]{1,0:T(8,128)(2,1)S(1)} %collective-permute-done.14.refs_6_), channel_id=1, source_target_pairs={{8,0},{16,8},{24,16},{28,24},{20,28},{12,20},{4,12},{0,4},{9,1},{1... | collective-permute-start | bytes 3145736 | tf_op jit(solution)/shard_map/ppermute | solution.py:305
  61.4 14.5 %collective-permute-start.18 = (bf16[512,1024]{1,0:T(8,128)(2,1)S(1)}, bf16[512,1024]{1,0:T(8,128)(2,1)}, u32[]{:S(2)}, u32[]{:S(2)}) collective-permute-start(bf16[512,1024]{1,0:T(8,128)(2,1)S(1)} %collective-permute-done.17.refs_10_), channel_id=1, source_target_pairs={{0,8},{8,16},{16,24},{24,28},{28,20},{20,12},{12,4},{4,0},{1,9},{9... | collective-permute-start | bytes 3145736 | tf_op jit(solution)/shard_map/ppermute | solution.py:302
  75.9 1.1 collective-permute-start.12
  77.0 4.3 %collective-permute-done.7.refs_7_ = bf16[512,1024]{1,0:T(8,128)(2,1)S(1)} collective-permute-done((bf16[512,1024]{1,0:T(8,128)(2,1)}, bf16[512,1024]{1,0:T(8,128)(2,1)S(1)}, u32[]{:S(2)}, u32[]{:S(2)}) %collective-permute-start.7) | collective-permute-done | bytes 1048608 | tf_op jit(solution)/shard_map/ppermute | solution.py:302
  81.3 2.1 %collective-permute-start.8 = (bf16[512,1024]{1,0:T(8,128)(2,1)S(1)}, bf16[512,1024]{1,0:T(8,128)(2,1)}, u32[]{:S(2)}, u32[]{:S(2)}) collective-permute-start(bf16[512,1024]{1,0:T(8,128)(2,1)S(1)} %collective-permute-done.7.refs_7_), channel_id=1, source_target_pairs={{0,8},{8,16},{16,24},{24,28},{28,20},{20,12},{12,4},{4,0},{1,9},{9... | collective-permute-start | bytes 3145736 | tf_op jit(solution)/shard_map/ppermute | solution.py:302
  83.4 14.8 %collective-permute-done.15.refs_8_ = bf16[512,1024]{1,0:T(8,128)(2,1)} collective-permute-done((bf16[512,1024]{1,0:T(8,128)(2,1)S(1)}, bf16[512,1024]{1,0:T(8,128)(2,1)}, u32[]{:S(2)}, u32[]{:S(2)}) %collective-permute-start.15) | collective-permute-done | bytes 1048608 | tf_op jit(solution)/shard_map/ppermute | solution.py:305
  98.2 1.3 collective-permute-start.16
  99.6 4.3 %collective-permute-done.18.refs_12_ = bf16[512,1024]{1,0:T(8,128)(2,1)} collective-permute-done((bf16[512,1024]{1,0:T(8,128)(2,1)S(1)}, bf16[512,1024]{1,0:T(8,128)(2,1)}, u32[]{:S(2)}, u32[]{:S(2)}) %collective-permute-start.18) | collective-permute-done | bytes 1048608 | tf_op jit(solution)/shard_map/ppermute | solution.py:302
  103.9 2.1 %collective-permute-start.19 = (bf16[512,1024]{1,0:T(8,128)(2,1)}, bf16[512,1024]{1,0:T(8,128)(2,1)}, u32[]{:S(2)}, u32[]{:S(2)}) collective-permute-start(bf16[512,1024]{1,0:T(8,128)(2,1)} %collective-permute-done.18.refs_12_), channel_id=1, source_target_pairs={{0,8},{8,16},{16,24},{24,28},{28,20},{20,12},{12,4},{4,0},{1,9},{9... | collective-permute-start | bytes 3145736 | tf_op jit(solution)/shard_map/ppermute | solution.py:302
  105.9 14.8 %collective-permute-done.12.refs_7_ = bf16[512,1024]{1,0:T(8,128)(2,1)} collective-permute-done((bf16[512,1024]{1,0:T(8,128)(2,1)S(1)}, bf16[512,1024]{1,0:T(8,128)(2,1)}, u32[]{:S(2)}, u32[]{:S(2)}) %collective-permute-start.12) | collective-permute-done | bytes 1048608 | tf_op jit(solution)/shard_map/ppermute | solution.py:305
  120.7 1.3 collective-permute-start.13
  122.1 4.3 %collective-permute-done.8.refs_4_ = bf16[512,1024]{1,0:T(8,128)(2,1)} collective-permute-done((bf16[512,1024]{1,0:T(8,128)(2,1)S(1)}, bf16[512,1024]{1,0:T(8,128)(2,1)}, u32[]{:S(2)}, u32[]{:S(2)}) %collective-permute-start.8) | collective-permute-done | bytes 1048608 | tf_op jit(solution)/shard_map/ppermute | solution.py:302
  126.3 2.1 %collective-permute-start.9 = (bf16[512,1024]{1,0:T(8,128)(2,1)}, bf16[512,1024]{1,0:T(8,128)(2,1)}, u32[]{:S(2)}, u32[]{:S(2)}) collective-permute-start(bf16[512,1024]{1,0:T(8,128)(2,1)} %collective-permute-done.8.refs_4_), channel_id=1, source_target_pairs={{0,8},{8,16},{16,24},{24,28},{28,20},{20,12},{12,4},{4,0},{1,9},{9... | collective-permute-start | bytes 3145736 | tf_op jit(solution)/shard_map/ppermute | solution.py:302
  129.2 11.7 %ring_product.3.refs_8_ = f32[512,2048]{1,0:T(8,128)S(1)} custom-call(s32[9]{0:T(128)S(1)} %pad_add_fusion.where_ref, bf16[512,1024]{1,0:T(8,128)(2,1)} %copy-done, bf16[512,1024]{1,0:T(8,128)(2,1)} %copy-done.2, bf16[512,1024]{1,0:T(8,128)(2,1)} %copy-done.1, bf16[512,1024]{1,0:T(8,128)(2,1)} %collective-permute-done.5.refs_3_, ...), custom_call_target="tpu_custom_call" | custom-call | flops 1048576 | bytes 1048576 | tf_op jit(solution)/shard_map/ring_product/pallas_call | solution.py:264
  140.9 2.3 %collective-permute-done.16.refs_5_ = bf16[512,1024]{1,0:T(8,128)(2,1)} collective-permute-done((bf16[512,1024]{1,0:T(8,128)(2,1)}, bf16[512,1024]{1,0:T(8,128)(2,1)}, u32[]{:S(2)}, u32[]{:S(2)}) %collective-permute-start.16) | collective-permute-done | bytes 1048608 | tf_op jit(solution)/shard_map/ppermute | solution.py:305
  143.2 5.6 %collective-permute-done.19.refs_6_ = bf16[512,1024]{1,0:T(8,128)(2,1)} collective-permute-done((bf16[512,1024]{1,0:T(8,128)(2,1)}, bf16[512,1024]{1,0:T(8,128)(2,1)}, u32[]{:S(2)}, u32[]{:S(2)}) %collective-permute-start.19) | collective-permute-done | bytes 1048608 | tf_op jit(solution)/shard_map/ppermute | solution.py:302
  148.8 6.4 %ring_product.4.refs_6_ = f32[512,2048]{1,0:T(8,128)S(1)} custom-call(s32[9]{0:T(128)S(1)} %pad_add_fusion.where_ref, bf16[512,1024]{1,0:T(8,128)(2,1)} %copy-done, bf16[512,1024]{1,0:T(8,128)(2,1)} %copy-done.2, bf16[512,1024]{1,0:T(8,128)(2,1)} %copy-done.1, bf16[512,1024]{1,0:T(8,128)(2,1)} %collective-permute-done.5.refs_3_, ...), custom_call_target="tpu_custom_call" | custom-call | flops 1048576 | bytes 1048576 | tf_op jit(solution)/shard_map/ring_product/pallas_call | solution.py:264
  155.3 9.7 %collective-permute-done.13.refs_5_ = bf16[512,1024]{1,0:T(8,128)(2,1)} collective-permute-done((bf16[512,1024]{1,0:T(8,128)(2,1)}, bf16[512,1024]{1,0:T(8,128)(2,1)}, u32[]{:S(2)}, u32[]{:S(2)}) %collective-permute-start.13) | collective-permute-done | bytes 1048608 | tf_op jit(solution)/shard_map/ppermute | solution.py:305
  165.0 5.7 %collective-permute-done.9.refs_4_ = bf16[512,1024]{1,0:T(8,128)(2,1)} collective-permute-done((bf16[512,1024]{1,0:T(8,128)(2,1)}, bf16[512,1024]{1,0:T(8,128)(2,1)}, u32[]{:S(2)}, u32[]{:S(2)}) %collective-permute-start.9) | collective-permute-done | bytes 1048608 | tf_op jit(solution)/shard_map/ppermute | solution.py:302
  170.7 5.5 %ring_product.5 = bf16[512,2048]{1,0:T(8,128)(2,1)} custom-call(s32[9]{0:T(128)S(1)} %pad_add_fusion.where_ref, bf16[512,1024]{1,0:T(8,128)(2,1)} %copy-done, bf16[512,1024]{1,0:T(8,128)(2,1)} %copy-done.2, bf16[512,1024]{1,0:T(8,128)(2,1)} %copy-done.1, bf16[512,1024]{1,0:T(8,128)(2,1)} %collective-permute-done.5.refs_3_, ...), custom_call_target="tpu_custom_call" | custom-call | flops 1048576 | bytes 1048576 | tf_op jit(solution)/shard_map/ring_product/pallas_call | solution.py:264
  (45 shorter events, 4.3 us)
Async XLA Ops:
  0.0 5.9 %copy-start.5 = (bf16[1024,512]{1,0:T(8,128)(2,1)S(1)}, bf16[1024,512]{1,0:T(8,128)(2,1)}, u32[]{:S(2)}) copy-start(bf16[1024,512]{1,0:T(8,128)(2,1)} %param.10) | copy-start | bytes 3145732
  0.0 5.9 %copy-start.4 = (bf16[1024,512]{1,0:T(8,128)(2,1)S(1)}, bf16[1024,512]{1,0:T(8,128)(2,1)}, u32[]{:S(2)}) copy-start(bf16[1024,512]{1,0:T(8,128)(2,1)} %param.11) | copy-start | bytes 3145732
  2.8 18.1 %copy-start.3 = (bf16[512,1024]{1,0:T(8,128)(2,1)}, bf16[512,1024]{1,0:T(8,128)(2,1)S(1)}, u32[]{:S(2)}) copy-start(bf16[512,1024]{1,0:T(8,128)(2,1)S(1)} %get-tuple-element.15.refs_4_) | copy-start | bytes 3145732
  2.8 34.2 %collective-permute-start.10 = (bf16[512,1024]{1,0:T(8,128)(2,1)}, bf16[512,1024]{1,0:T(8,128)(2,1)}, u32[]{:S(2)}, u32[]{:S(2)}) collective-permute-start(bf16[512,1024]{1,0:T(8,128)(2,1)} %get-tuple-element.16.refs_9_), channel_id=1, source_target_pairs={{8,0},{16,8},{24,16},{28,24},{20,28},{12,20},{4,12},{0,4},{9,1},{1... | collective-permute-start | bytes 3145736 | tf_op jit(solution)/shard_map/ppermute | solution.py:305
  5.8 31.7 %collective-permute-start.6 = (bf16[512,1024]{1,0:T(8,128)(2,1)S(1)}, bf16[512,1024]{1,0:T(8,128)(2,1)}, u32[]{:S(2)}, u32[]{:S(2)}) collective-permute-start(bf16[512,1024]{1,0:T(8,128)(2,1)S(1)} %get-tuple-element.15.refs_4_), channel_id=1, source_target_pairs={{0,8},{8,16},{16,24},{24,28},{28,20},{20,12},{12,4},{4,0},{1,9},{9... | collective-permute-start | bytes 3145736 | tf_op jit(solution)/shard_map/ppermute | solution.py:302
  6.9 3.8 %copy-start.11 = (s32[1,1,16]{2,1,0:T(1,128)S(1)}, s32[1,1,16]{2,1,0:T(1,128)}, u32[]{:S(2)}) copy-start(s32[1,1,16]{2,1,0:T(1,128)} %param.12) | copy-start | bytes 196
  6.9 3.8 %copy-start.6 = (bf16[1024,128]{1,0:T(8,128)(2,1)S(1)}, bf16[1024,128]{1,0:T(8,128)(2,1)}, u32[]{:S(2)}) copy-start(bf16[1024,128]{1,0:T(8,128)(2,1)} %get-tuple-element.27) | copy-start | bytes 786436
  7.0 14.0 %collective-permute-start.2 = (bf16[1024,256]{1,0:T(8,128)(2,1)S(1)}, bf16[1024,256]{1,0:T(8,128)(2,1)}, u32[]{:S(2)}, u32[]{:S(2)}) collective-permute-start(bf16[1024,256]{1,0:T(8,128)(2,1)S(1)} %pad_maximum_fusion.3), channel_id=1, source_target_pairs={{0,3},{1,2},{2,1},{3,0},{4,7},{5,6},{6,5},{7,4},{8,11},{9,10},{10,... | collective-permute-start | bytes 1572872 | tf_op jit(solution)/shard_map/ppermute | solution.py:152
  7.9 24.7 %collective-permute-start.1 = (bf16[1024,256]{1,0:T(8,128)(2,1)S(1)}, bf16[1024,256]{1,0:T(8,128)(2,1)}, u32[]{:S(2)}, u32[]{:S(2)}) collective-permute-start(bf16[1024,256]{1,0:T(8,128)(2,1)S(1)} %pad_maximum_fusion.2), channel_id=1, source_target_pairs={{0,2},{1,3},{2,0},{3,1},{4,6},{5,7},{6,4},{7,5},{8,10},{9,11},{10,... | collective-permute-start | bytes 1572872 | tf_op jit(solution)/shard_map/ppermute | solution.py:152
  9.2 25.4 %collective-permute-start = (bf16[1024,256]{1,0:T(8,128)(2,1)S(1)}, bf16[1024,256]{1,0:T(8,128)(2,1)}, u32[]{:S(2)}, u32[]{:S(2)}) collective-permute-start(bf16[1024,256]{1,0:T(8,128)(2,1)S(1)} %pad_maximum_fusion.1), channel_id=1, source_target_pairs={{0,1},{1,0},{2,3},{3,2},{4,5},{5,4},{6,7},{7,6},{8,9},{9,8},{10,11... | collective-permute-start | bytes 1572872 | tf_op jit(solution)/shard_map/ppermute | solution.py:152
  21.0 31.1 %collective-permute-start.14 = (bf16[512,1024]{1,0:T(8,128)(2,1)S(1)}, bf16[512,1024]{1,0:T(8,128)(2,1)S(1)}, u32[]{:S(2)}, u32[]{:S(2)}) collective-permute-start(bf16[512,1024]{1,0:T(8,128)(2,1)S(1)} %get-tuple-element.15.refs_4_), channel_id=1, source_target_pairs={{8,0},{16,8},{24,16},{28,24},{20,28},{12,20},{4,12},{0,4},{9,1},{1... | collective-permute-start | bytes 3145736 | tf_op jit(solution)/shard_map/ppermute | solution.py:305
  32.6 26.2 %collective-permute-start.17 = (bf16[512,1024]{1,0:T(8,128)(2,1)}, bf16[512,1024]{1,0:T(8,128)(2,1)S(1)}, u32[]{:S(2)}, u32[]{:S(2)}) collective-permute-start(bf16[512,1024]{1,0:T(8,128)(2,1)} %get-tuple-element.16.refs_9_), channel_id=1, source_target_pairs={{0,8},{8,16},{16,24},{24,28},{28,20},{20,12},{12,4},{4,0},{1,9},{9... | collective-permute-start | bytes 3145736 | tf_op jit(solution)/shard_map/ppermute | solution.py:302
  36.5 92.7 %copy-start = (bf16[512,1024]{1,0:T(8,128)(2,1)}, bf16[512,1024]{1,0:T(8,128)(2,1)S(1)}, u32[]{:S(2)}) copy-start(bf16[512,1024]{1,0:T(8,128)(2,1)S(1)} %attend.1.refs_0_) | copy-start | bytes 3145732
  36.5 24.9 %collective-permute-start.4 = (bf16[512,1024]{1,0:T(8,128)(2,1)S(1)}, bf16[512,1024]{1,0:T(8,128)(2,1)S(1)}, u32[]{:S(2)}, u32[]{:S(2)}) collective-permute-start(bf16[512,1024]{1,0:T(8,128)(2,1)S(1)} %attend.1.refs_0_), channel_id=1, source_target_pairs={{0,2},{1,3},{2,0},{3,1},{4,6},{5,7},{6,4},{7,5},{8,10},{9,11},{10,... | collective-permute-start | bytes 3145736 | tf_op jit(solution)/shard_map/ppermute | solution.py:308
  37.0 38.9 %collective-permute-start.11 = (bf16[512,1024]{1,0:T(8,128)(2,1)}, bf16[512,1024]{1,0:T(8,128)(2,1)S(1)}, u32[]{:S(2)}, u32[]{:S(2)}) collective-permute-start(bf16[512,1024]{1,0:T(8,128)(2,1)} %collective-permute-done.10.refs_11_), channel_id=1, source_target_pairs={{8,0},{16,8},{24,16},{28,24},{20,28},{12,20},{4,12},{0,4},{9,1},{1... | collective-permute-start | bytes 3145736 | tf_op jit(solution)/shard_map/ppermute | solution.py:305
  37.5 43.8 %collective-permute-start.7 = (bf16[512,1024]{1,0:T(8,128)(2,1)}, bf16[512,1024]{1,0:T(8,128)(2,1)S(1)}, u32[]{:S(2)}, u32[]{:S(2)}) collective-permute-start(bf16[512,1024]{1,0:T(8,128)(2,1)} %collective-permute-done.6.refs_5_), channel_id=1, source_target_pairs={{0,8},{8,16},{16,24},{24,28},{28,20},{20,12},{12,4},{4,0},{1,9},{9... | collective-permute-start | bytes 3145736 | tf_op jit(solution)/shard_map/ppermute | solution.py:302
  52.0 31.3 %copy-start.7 = (bf16[512,1024]{1,0:T(8,128)(2,1)}, bf16[512,1024]{1,0:T(8,128)(2,1)S(1)}, u32[]{:S(2)}) copy-start(bf16[512,1024]{1,0:T(8,128)(2,1)S(1)} %collective-permute-done.14.refs_6_) | copy-start | bytes 3145732
  52.1 31.3 %collective-permute-start.3 = (bf16[512,1024]{1,0:T(8,128)(2,1)S(1)}, bf16[512,1024]{1,0:T(8,128)(2,1)S(1)}, u32[]{:S(2)}, u32[]{:S(2)}) collective-permute-start(bf16[512,1024]{1,0:T(8,128)(2,1)S(1)} %attend.1.refs_0_), channel_id=1, source_target_pairs={{0,1},{1,0},{2,3},{3,2},{4,5},{5,4},{6,7},{7,6},{8,9},{9,8},{10,11... | collective-permute-start | bytes 3145736 | tf_op jit(solution)/shard_map/ppermute | solution.py:309
  58.8 39.4 %copy-start.8 = (bf16[512,1024]{1,0:T(8,128)(2,1)}, bf16[512,1024]{1,0:T(8,128)(2,1)S(1)}, u32[]{:S(2)}) copy-start(bf16[512,1024]{1,0:T(8,128)(2,1)S(1)} %collective-permute-done.17.refs_10_) | copy-start | bytes 3145732
  58.8 39.4 %collective-permute-start.15 = (bf16[512,1024]{1,0:T(8,128)(2,1)S(1)}, bf16[512,1024]{1,0:T(8,128)(2,1)}, u32[]{:S(2)}, u32[]{:S(2)}) collective-permute-start(bf16[512,1024]{1,0:T(8,128)(2,1)S(1)} %collective-permute-done.14.refs_6_), channel_id=1, source_target_pairs={{8,0},{16,8},{24,16},{28,24},{20,28},{12,20},{4,12},{0,4},{9,1},{1... | collective-permute-start | bytes 3145736 | tf_op jit(solution)/shard_map/ppermute | solution.py:305
  61.4 67.8 %copy-start.1 = (bf16[512,1024]{1,0:T(8,128)(2,1)}, bf16[512,1024]{1,0:T(8,128)(2,1)S(1)}, u32[]{:S(2)}) copy-start(bf16[512,1024]{1,0:T(8,128)(2,1)S(1)} %collective-permute-done.4.refs_2_) | copy-start | bytes 3145732
  61.4 42.5 %collective-permute-start.18 = (bf16[512,1024]{1,0:T(8,128)(2,1)S(1)}, bf16[512,1024]{1,0:T(8,128)(2,1)}, u32[]{:S(2)}, u32[]{:S(2)}) collective-permute-start(bf16[512,1024]{1,0:T(8,128)(2,1)S(1)} %collective-permute-done.17.refs_10_), channel_id=1, source_target_pairs={{0,8},{8,16},{16,24},{24,28},{28,20},{20,12},{12,4},{4,0},{1,9},{9... | collective-permute-start | bytes 3145736 | tf_op jit(solution)/shard_map/ppermute | solution.py:302
  75.9 28.0 %copy-start.9 = (bf16[512,1024]{1,0:T(8,128)(2,1)}, bf16[512,1024]{1,0:T(8,128)(2,1)S(1)}, u32[]{:S(2)}) copy-start(bf16[512,1024]{1,0:T(8,128)(2,1)S(1)} %collective-permute-done.11.refs_13_) | copy-start | bytes 3145732
  75.9 44.8 %collective-permute-start.12 = (bf16[512,1024]{1,0:T(8,128)(2,1)S(1)}, bf16[512,1024]{1,0:T(8,128)(2,1)}, u32[]{:S(2)}, u32[]{:S(2)}) collective-permute-start(bf16[512,1024]{1,0:T(8,128)(2,1)S(1)} %collective-permute-done.11.refs_13_), channel_id=1, source_target_pairs={{8,0},{16,8},{24,16},{28,24},{20,28},{12,20},{4,12},{0,4},{9,1},{1... | collective-permute-start | bytes 3145736 | tf_op jit(solution)/shard_map/ppermute | solution.py:305
  81.3 39.4 %copy-start.10 = (bf16[512,1024]{1,0:T(8,128)(2,1)}, bf16[512,1024]{1,0:T(8,128)(2,1)S(1)}, u32[]{:S(2)}) copy-start(bf16[512,1024]{1,0:T(8,128)(2,1)S(1)} %collective-permute-done.7.refs_7_) | copy-start | bytes 3145732
  81.3 45.0 %collective-permute-start.8 = (bf16[512,1024]{1,0:T(8,128)(2,1)S(1)}, bf16[512,1024]{1,0:T(8,128)(2,1)}, u32[]{:S(2)}, u32[]{:S(2)}) collective-permute-start(bf16[512,1024]{1,0:T(8,128)(2,1)S(1)} %collective-permute-done.7.refs_7_), channel_id=1, source_target_pairs={{0,8},{8,16},{16,24},{24,28},{28,20},{20,12},{12,4},{4,0},{1,9},{9... | collective-permute-start | bytes 3145736 | tf_op jit(solution)/shard_map/ppermute | solution.py:302
  83.4 45.8 %copy-start.2 = (bf16[512,1024]{1,0:T(8,128)(2,1)}, bf16[512,1024]{1,0:T(8,128)(2,1)S(1)}, u32[]{:S(2)}) copy-start(bf16[512,1024]{1,0:T(8,128)(2,1)S(1)} %collective-permute-done.3.refs_1_) | copy-start | bytes 3145732
  83.4 45.8 %collective-permute-start.5 = (bf16[512,1024]{1,0:T(8,128)(2,1)S(1)}, bf16[512,1024]{1,0:T(8,128)(2,1)}, u32[]{:S(2)}, u32[]{:S(2)}) collective-permute-start(bf16[512,1024]{1,0:T(8,128)(2,1)S(1)} %collective-permute-done.4.refs_2_), channel_id=1, source_target_pairs={{0,1},{1,0},{2,3},{3,2},{4,5},{5,4},{6,7},{7,6},{8,9},{9,8},{10,11... | collective-permute-start | bytes 3145736 | tf_op jit(solution)/shard_map/ppermute | solution.py:310
  98.2 44.9 %collective-permute-start.16 = (bf16[512,1024]{1,0:T(8,128)(2,1)}, bf16[512,1024]{1,0:T(8,128)(2,1)}, u32[]{:S(2)}, u32[]{:S(2)}) collective-permute-start(bf16[512,1024]{1,0:T(8,128)(2,1)} %collective-permute-done.15.refs_8_), channel_id=1, source_target_pairs={{8,0},{16,8},{24,16},{28,24},{20,28},{12,20},{4,12},{0,4},{9,1},{1... | collective-permute-start | bytes 3145736 | tf_op jit(solution)/shard_map/ppermute | solution.py:305
  103.9 44.9 %collective-permute-start.19 = (bf16[512,1024]{1,0:T(8,128)(2,1)}, bf16[512,1024]{1,0:T(8,128)(2,1)}, u32[]{:S(2)}, u32[]{:S(2)}) collective-permute-start(bf16[512,1024]{1,0:T(8,128)(2,1)} %collective-permute-done.18.refs_12_), channel_id=1, source_target_pairs={{0,8},{8,16},{16,24},{24,28},{28,20},{20,12},{12,4},{4,0},{1,9},{9... | collective-permute-start | bytes 3145736 | tf_op jit(solution)/shard_map/ppermute | solution.py:302
  120.7 44.2 %collective-permute-start.13 = (bf16[512,1024]{1,0:T(8,128)(2,1)}, bf16[512,1024]{1,0:T(8,128)(2,1)}, u32[]{:S(2)}, u32[]{:S(2)}) collective-permute-start(bf16[512,1024]{1,0:T(8,128)(2,1)} %collective-permute-done.12.refs_7_), channel_id=1, source_target_pairs={{8,0},{16,8},{24,16},{28,24},{20,28},{12,20},{4,12},{0,4},{9,1},{1... | collective-permute-start | bytes 3145736 | tf_op jit(solution)/shard_map/ppermute | solution.py:305
  126.3 44.3 %collective-permute-start.9 = (bf16[512,1024]{1,0:T(8,128)(2,1)}, bf16[512,1024]{1,0:T(8,128)(2,1)}, u32[]{:S(2)}, u32[]{:S(2)}) collective-permute-start(bf16[512,1024]{1,0:T(8,128)(2,1)} %collective-permute-done.8.refs_4_), channel_id=1, source_target_pairs={{0,8},{8,16},{16,24},{24,28},{28,20},{20,12},{12,4},{4,0},{1,9},{9... | collective-permute-start | bytes 3145736 | tf_op jit(solution)/shard_map/ppermute | solution.py:302

commit v6 on v4

--- a/solution.py
+++ b/solution.py
@@ -167,72 +167,266 @@
     return [everything], [jnp.int32(0)]
 
 
-def ring_of(pb_size):
-    if pb_size == 8:
-        return [0, 2, 4, 6, 7, 5, 3, 1]
-    return list(range(pb_size))
-
-
-def project_ring(wo, inputs, attend_with):
-    pb_size = lax.axis_size("pb")
+ROW_TILE = 256
+IN_HBM = pl.BlockSpec(memory_space=pltpu.HBM)
+IN_VMEM = pl.BlockSpec(memory_space=pltpu.VMEM)
+IN_SMEM = pl.BlockSpec(memory_space=pltpu.SMEM)
+SMALL_COST = pl.CostEstimate(flops=1 << 20, transcendentals=0, bytes_accessed=1 << 20)
+
+
+def in_hbm(values):
+    return [pltpu.with_memory_space_constraint(x, pltpu.HBM) for x in values]
+
+
+def in_vmem(values):
+    return [pltpu.with_memory_space_constraint(x, pltpu.VMEM) for x in values]
+
+
+def slab_product_kernel(kind, distances, start, has_base, out_count, where_ref, *refs):
+    z, y, me = where_ref[0], where_ref[1], where_ref[2]
+    own_rows, other_rows, slabs, refs = refs[:4], refs[4:8], refs[8 : 8 + len(distances)], refs[8 + len(distances) :]
+    if has_base:
+        base_ref, refs = refs[0], refs[1:]
+    outs, (left, right, sems) = refs[:out_count], refs[out_count:]
+    rows = own_rows[0].shape[0]
+    depth, width = slabs[0].shape[0], right.shape[1]
+    if kind == "kept":
+        targets = [jnp.int32(i) for i in range(4)]
+    elif kind == "near":
+        targets = [(4 - z + i) % 4 for i in range(3)]
+    else:
+        targets = [3 - z]
+    column = pl.multiple_of((y if kind == "kept" else 1 - y) * depth, depth)
+
+    def left_copy(index, slot, side):
+        source = (own_rows, other_rows)[side][slot]
+        return pltpu.make_async_copy(
+            source.at[:, pl.ds(column, depth)],
+            left.at[pl.ds(side * rows, rows), pl.ds(index * depth, depth)],
+            sems.at[index, side],
+        )
+
+    def slab_copy(index, slab):
+        source = slabs[slab]
+        if source.shape[1] != width:
+            source = source.at[:, pl.ds(start, width)]
+        return pltpu.make_async_copy(
+            source, right.at[pl.ds(index * depth, depth), :], sems.at[index, 2]
+        )
+
+    for index, target in enumerate(targets):
+        slot_here = jnp.bitwise_xor(me, target)
+        for slot in range(4):
+
+            @pl.when(slot_here == slot)
+            def _(slot=slot):
+                left_copy(index, slot, 0).start()
+                left_copy(index, slot, 1).start()
+
+        away = target - z
+        for slab, distance in enumerate(distances):
+            here = away == distance
+            if distance == 3:
+                here = here | (away == -3)
+
+            @pl.when(here)
+            def _(slab=slab):
+                slab_copy(index, slab).start()
+
+    for index in range(len(targets)):
+        left_copy(index, 0, 0).wait()
+        left_copy(index, 0, 1).wait()
+        slab_copy(index, 0).wait()
+
+    def rows_tile(step, carry):
+        for side in range(2):
+            at = pl.ds(pl.multiple_of(step * ROW_TILE + side * rows, ROW_TILE), ROW_TILE)
+            product = jnp.dot(left[at, :], right[...], preferred_element_type=jnp.float32)
+            if has_base:
+                product = product + base_ref[at, :]
+            if kind == "far":
+                within = pl.ds(pl.multiple_of(step * ROW_TILE, ROW_TILE), ROW_TILE)
+                outs[side][within, :] = product.astype(jnp.bfloat16)
+            else:
+                first = 0
+                for out in outs:
+                    out[at, :] = product[:, first : first + out.shape[1]]
+                    first += out.shape[1]
+        return carry
+
+    lax.fori_loop(0, rows // ROW_TILE, rows_tile, 0)
+
+
+def slab_product(kind, where, own_rows, other_rows, slabs, base, widths, start=0):
+    rows = own_rows[0].shape[0]
+    depth = slabs[0][1].shape[0]
+    count = {"kept": 4, "near": 3, "far": 1}[kind]
+    if kind == "far":
+        out_shape = [jax.ShapeDtypeStruct((rows, widths[0]), jnp.bfloat16)] * 2
+    else:
+        out_shape = [jax.ShapeDtypeStruct((2 * rows, width), jnp.float32) for width in widths]
+    return pl.pallas_call(
+        functools.partial(
+            slab_product_kernel,
+            kind,
+            tuple(distance for distance, _ in slabs),
+            start,
+            base is not None,
+            len(out_shape),
+        ),
+        out_shape=out_shape,
+        in_specs=[IN_SMEM] + [IN_HBM] * (8 + len(slabs)) + [IN_VMEM] * (base is not None),
+        out_specs=[IN_VMEM] * len(out_shape),
+        scratch_shapes=[
+            pltpu.VMEM((2 * rows, count * depth), jnp.bfloat16),
+            pltpu.VMEM((count * depth, sum(widths)), jnp.bfloat16),
+            pltpu.SemaphoreType.DMA((count, 3)),
+        ],
+        compiler_params=pltpu.CompilerParams(vmem_limit_bytes=(4 + 3 * count) << 20),
+        cost_estimate=SMALL_COST,
+        name="product_" + kind,
+    )(
+        where,
+        *in_hbm([*own_rows, *other_rows, *[slab for _, slab in slabs]]),
+        *([] if base is None else in_vmem([base])),
+    )
+
+
+def finish_kernel(widths, where_ref, *refs):
+    count = len(widths)
+    out_ref, sems = refs[2 * count :]
+    half = sum(widths)
+    copies = []
+    for side in range(2):
+        start = 0
+        for index, width in enumerate(widths):
+            place = jnp.bitwise_xor(where_ref[1], side) * half + start
+            copies.append(
+                pltpu.make_async_copy(
+                    refs[side * count + index],
+                    out_ref.at[:, pl.ds(pl.multiple_of(place, HEAD_SIZE), width)],
+                    sems.at[side, index],
+                )
+            )
+            start += width
+    for copy in copies:
+        copy.start()
+    for copy in copies:
+        copy.wait()
+
+
+def finish(where, own, received):
+    widths = tuple(piece.shape[1] for piece in own)
+    return pl.pallas_call(
+        functools.partial(finish_kernel, widths),
+        out_shape=jax.ShapeDtypeStruct((own[0].shape[0], 2 * sum(widths)), jnp.bfloat16),
+        in_specs=[IN_SMEM] + [IN_VMEM] * (2 * len(widths)),
+        out_specs=IN_HBM,
+        scratch_shapes=[pltpu.SemaphoreType.DMA((2, len(widths)))],
+        cost_estimate=SMALL_COST,
+        name="finish",
+    )(where, *in_vmem([*own, *received]))
+
+
+UP = [[(i, i + 2) for i in range(2 * s, 6)] for s in range(2)]
+DOWN = [[(i + 2, i) for i in range(6 - 2 * s)] for s in range(2)]
+OUTWARD = [(2, 0), (3, 1), (4, 6), (5, 7)]
+ACROSS_Y = [(i, i ^ 1) for i in range(8)]
+ACROSS_X = [(i, i ^ 2) for i in range(4)]
+ACROSS_CORE = [(i, i ^ 1) for i in range(4)]
+
+
+def project(wo, inputs, attend_with):
+    pb = lax.axis_index("pb")
+    y = pb % 2
+    where = jnp.stack([pb // 2, y, lax.axis_index("ka")]).astype(jnp.int32)
     depth, columns = wo.shape
-    ring = ring_of(pb_size)
-    forward = [(ring[i], ring[(i + 1) % pb_size]) for i in range(pb_size)]
-    backward = [(b, a) for a, b in forward]
     half = columns // 2
-    far = pb_size // 2
-    parts = [wo[:, :half], wo[:, half:]]
-    inputs, parts[0], parts[1] = lax.optimization_barrier((inputs, parts[0], parts[1]))
-    slabs = [[(0, part)] for part in parts]
-    moving = [[part, part] for part in parts]
-    for hop in range(1, far + 1):
-        for part in range(2):
-            if hop < far or part == 0:
-                moving[part][0] = lax.ppermute(moving[part][0], "pb", forward)
-                slabs[part].append((-hop, moving[part][0]))
-            if hop < far or part == 1:
-                moving[part][1] = lax.ppermute(moving[part][1], "pb", backward)
-                slabs[part].append((hop, moving[part][1]))
-    attn = attend_with(inputs)
-    across = lax.ppermute(attn, "ka", [(i, i ^ 2) for i in range(4)])
-    beside = lax.ppermute(attn, "ka", [(i, i ^ 1) for i in range(4)])
-    corner = lax.ppermute(across, "ka", [(i, i ^ 1) for i in range(4)])
-    pieces = jnp.stack([attn, beside, across, corner])
-    per = attn.shape[1] // depth
-    around = jnp.asarray(
-        [[ring[(ring.index(p) + step) % pb_size] for step in range(pb_size)] for p in range(pb_size)],
-        jnp.int32,
-    )
-    sources = lax.dynamic_slice(around, (lax.axis_index("pb"), 0), (1, pb_size))[0]
-    slots = jnp.bitwise_xor(sources // per, lax.axis_index("ka"))
-    shifts = (sources % per) * depth
-    results = []
-    for part in range(2):
-        total = None
-        for offset, slab in slabs[part]:
-            at = offset % pb_size
-            left = lax.dynamic_slice(
-                pieces, (slots[at], 0, shifts[at]), (1, attn.shape[0], depth)
-            )[0]
-            term = jnp.dot(left, slab, preferred_element_type=jnp.float32)
-            total = term if total is None else total + term
-        results.append(total.astype(jnp.bfloat16))
-    return jnp.concatenate(results, axis=1)
+    widths = (half * 3 // 8, half * 3 // 8, half // 4)
+    kept = lax.dynamic_slice(wo, (0, y * half), (depth, half))
+    given = lax.dynamic_slice(wo, (0, (1 - y) * half), (depth, half))
+    inputs, kept, given = lax.optimization_barrier((inputs, kept, given))
+
+    def hop(up, down, step):
+        up = up + [lax.ppermute(up[-1], "pb", UP[step])]
+        down = down + [lax.ppermute(down[-1], "pb", DOWN[step])]
+        return (up[1:], down[1:]) if step == 0 else (up, down)
+
+    def other_core(piece):
+        return lax.ppermute(piece, "ka", ACROSS_CORE)
+
+    tie = lax.optimization_barrier
+    kept_up, kept_down = hop([kept], [kept], 0)
+    taken = lax.ppermute(given, "pb", ACROSS_Y)
+    queries, keys, values, old = inputs
+    parts, places = own_head_keys_values(keys, values)
+    parts, kept_up[0], kept_down[0], taken = tie((parts, kept_up[0], kept_down[0], taken))
+    kept_up, kept_down = hop(kept_up, kept_down, 1)
+    taken_up, taken_down = hop([taken], [taken], 0)
+    attn = attend_with(queries, old, parts, places)
+    attn, kept_up[1], kept_down[1] = tie((attn, kept_up[1], kept_down[1]))
+    kept_end = lax.ppermute(kept_up[1] + kept_down[1], "pb", OUTWARD)
+    across_y = lax.ppermute(attn, "pb", ACROSS_Y)
+    across_x = lax.ppermute(attn, "ka", ACROSS_X)
+    across_y, across_x, taken_up[0], taken_down[0] = tie(
+        (across_y, across_x, taken_up[0], taken_down[0])
+    )
+    taken_up, taken_down = hop(taken_up, taken_down, 1)
+    ends = []
+    start = 0
+    for width in widths:
+        piece = taken_up[1][:, start : start + width] + taken_down[1][:, start : start + width]
+        ends.append(lax.ppermute(piece, "pb", OUTWARD))
+        start += width
+    corner = lax.ppermute(across_y, "ka", ACROSS_X)
+    own_rows = [attn, other_core(attn), across_x, other_core(across_x)]
+    other_rows = [across_y, other_core(across_y), corner, other_core(corner)]
+
+    def near_slabs(piece, up, down):
+        return [(0, piece), (-1, up[0]), (-2, up[1]), (1, down[0]), (2, down[1])]
+
+    (base,) = slab_product(
+        "kept",
+        where,
+        own_rows,
+        other_rows,
+        near_slabs(kept, kept_up, kept_down) + [(3, kept_end)],
+        None,
+        (half,),
+    )
+    bases = slab_product(
+        "near", where, own_rows, other_rows, near_slabs(taken, taken_up, taken_down), base, widths
+    )
+    own_out, received = [], []
+    start = 0
+    for base, width, end in zip(bases, widths, ends):
+        own, other = slab_product(
+            "far",
+            where,
+            own_rows,
+            other_rows,
+            [(3, end), (-1, taken_up[0]), (1, taken_down[0])],
+            base,
+            (width,),
+            start,
+        )
+        own_out.append(own)
+        received.append(lax.ppermute(other, "pb", ACROSS_Y))
+        start += width
+    return finish(where, own_out, received)
 
 
 def shards(queries, keys, values, block_ids, counts, refresh, cached_attn, wo):
     groups = lax.axis_size("ka")
 
-    def attend_with(inputs):
-        queries, keys, values, old = inputs
-        parts, places = own_head_keys_values(keys, values)
+    def attend_with(queries, old, parts, places):
         return attend(block_ids[0, 0], counts[0, 0], refresh[0, 0], queries, old, parts, places)
 
-    inputs = (queries[0], keys, values, cached_attn[0])
     if lax.axis_size("pb") == 8 and groups == 4:
-        mixed = project_ring(wo, inputs, attend_with)
+        mixed = project(wo, (queries[0], keys, values, cached_attn[0]), attend_with)
     else:
-        attn_full = lax.all_gather(attend_with(inputs), "ka", axis=1, tiled=True)
+        attn = attend_with(queries[0], cached_attn[0], *own_head_keys_values(keys, values))
+        attn_full = lax.all_gather(attn, "ka", axis=1, tiled=True)
         mixed = jnp.dot(
             attn_full, lax.all_gather(wo, "pb", axis=0, tiled=True), preferred_element_type=jnp.float32
         ).astype(jnp.bfloat16)

time: 188 us -> 191 us (1.016)
  waiting for transfers between devices: 85.8 us -> 116 us
  between operations: 30.7 us -> 1.89 us
  matrix products: 24.3 us -> 0 us
  starting transfers between devices: 15.1 us -> 37.1 us
  Pallas kernels: 18.7 us -> 27.7 us
  other arithmetic: 6.96 us -> 3.26 us
    ppermute x17 -> x23, waiting for transfers between devices: 65.4 us -> 102 us  [the longest x4 68.1 us: hop(): down = down + [lax.ppermute(down[-1], 'pb', DOWN[step])]]
    pallas_call x0 -> x6, Pallas kernels: none -> 25.9 us  [the longest x5 23.8 us: slab_product(): pl.pallas_call(functools.partial(slab_product_kernel, kind, tuple((distan...]
    dot_general x16 -> x0, matrix products: 24.3 us -> none  [project_ring(): term = jnp.dot(left, slab, preferred_element_type=jnp.float32)]
    ppermute x17 -> x23, starting transfers between devices: 13.2 us -> 32.8 us  [the longest x4 12.1 us: hop(): up = up + [lax.ppermute(up[-1], 'pb', UP[step])]]
    pallas_call x1, Pallas kernels: 18.7 us -> 1.82 us  [attend(): pl.pallas_call(functools.partial(attention_kernel, heads, slots), out_sha...]
    ppermute x3, waiting for transfers between devices: 20.4 us -> 14.4 us  [own_head_keys_values(): lax.ppermute(head_of(partner), 'ka', [(i, i ^ step) for i in range(groups)])]
    slice x2 -> x0, local copies, waits for them, and re-layouts: 2.5 us -> none  [the longest x1 1.8 us: project_ring(): parts = [wo[:, :half], wo[:, half:]]]
    ppermute x3, starting transfers between devices: 1.93 us -> 4.31 us  [own_head_keys_values(): lax.ppermute(head_of(partner), 'ka', [(i, i ^ step) for i in range(groups)])]
  transfers between devices with their start and end apart: 20 -> 26, of which waited for: 9 -> 10; matrix products, arithmetic and copies ran while one was open for 17% -> 2% of each run, Pallas kernels for 10% -> 13%
where the time goes in v6:
time: 191 us
  waiting for transfers between devices  116 us (61%)
  starting transfers between devices  37.1 us (19%)
  Pallas kernels  27.7 us (15%)
  local copies, waits for them, and re-layouts  5.55 us (3%)
  other arithmetic  3.26 us (2%)
    ppermute x4, waiting for transfers between devices, hop(): down = down + [lax.ppermute(down[-1], 'pb', DOWN[step])]  68.1 us
    pallas_call x5, Pallas kernels, slab_product(): pl.pallas_call(functools.partial(slab_product_kernel, kind, tuple((distan...  23.8 us
    ppermute x1, waiting for transfers between devices, project(): kept_end = lax.ppermute(kept_up[1] + kept_down[1], 'pb', OUTWARD)  17.1 us
    ppermute x3, waiting for transfers between devices, own_head_keys_values(): lax.ppermute(head_of(partner), 'ka', [(i, i ^ step) for i in range(groups)])  14.4 us
    ppermute x3, waiting for transfers between devices, project(): received.append(lax.ppermute(other, 'pb', ACROSS_Y))  12.2 us
    ppermute x4, starting transfers between devices, hop(): up = up + [lax.ppermute(up[-1], 'pb', UP[step])]  12.1 us
    ppermute x4, starting transfers between devices, hop(): down = down + [lax.ppermute(down[-1], 'pb', DOWN[step])]  5.17 us
    ppermute x3, starting transfers between devices, own_head_keys_values(): lax.ppermute(head_of(partner), 'ka', [(i, i ^ step) for i in range(groups)])  4.31 us
  transfers between devices with their start and end apart: 26, of which 10 were waited for; matrix products, arithmetic and copies ran while one was open for 2% of the time, Pallas kernels for 13%

profile of v6, /device:TPU:0, one launch (start us, length us, event | category | flops | bytes accessed | tf_op | source)
XLA Modules:
  0.0 191.4 jit_solution(16716090944320367001)
XLA Ops:
  0.0 1.8 constant_dynamic-slice_fusion.8
  1.9 1.8 constant_dynamic-slice_fusion
  3.8 2.4 %collective-permute-start.2 = (bf16[1024,256]{1,0:T(8,128)(2,1)S(1)}, bf16[1024,256]{1,0:T(8,128)(2,1)S(1)}, u32[]{:S(2)}, u32[]{:S(2)}) collective-permute-start(bf16[1024,256]{1,0:T(8,128)(2,1)S(1)} %pad_maximum_fusion.3), channel_id=1, source_target_pairs={{0,3},{1,2},{2,1},{3,0},{4,7},{5,6},{6,5},{7,4},{8,11},{9,10},{10,... | collective-permute-start | bytes 1572872 | tf_op jit(solution)/shard_map/ppermute | solution.py:152
  6.2 3.5 %collective-permute-start.3 = (bf16[512,1024]{1,0:T(8,128)(2,1)S(1)}, bf16[512,1024]{1,0:T(8,128)(2,1)S(1)}, u32[]{:S(2)}, u32[]{:S(2)}) collective-permute-start(bf16[512,1024]{1,0:T(8,128)(2,1)S(1)} %get-tuple-element.38.refs_8_), channel_id=1, source_target_pairs={{0,8},{4,12},{8,16},{12,20},{16,24},{20,28},{1,9},{5,13},{9,17},{1... | collective-permute-start | bytes 3145736 | tf_op jit(solution)/shard_map/ppermute | solution.py:351
  9.8 1.3 collective-permute-start.4
  11.1 1.6 collective-permute-start.5
  13.4 5.1 %collective-permute-done.2.refs_3_ = bf16[1024,256]{1,0:T(8,128)(2,1)S(1)} collective-permute-done((bf16[1024,256]{1,0:T(8,128)(2,1)S(1)}, bf16[1024,256]{1,0:T(8,128)(2,1)S(1)}, u32[]{:S(2)}, u32[]{:S(2)}) %collective-permute-start.2) | collective-permute-done | bytes 524320 | tf_op jit(solution)/shard_map/ppermute | solution.py:152
  20.6 9.3 %collective-permute-done.1.refs_2_ = bf16[1024,256]{1,0:T(8,128)(2,1)S(1)} collective-permute-done((bf16[1024,256]{1,0:T(8,128)(2,1)S(1)}, bf16[1024,256]{1,0:T(8,128)(2,1)S(1)}, u32[]{:S(2)}, u32[]{:S(2)}) %collective-permute-start.1) | collective-permute-done | bytes 524320 | tf_op jit(solution)/shard_map/ppermute | solution.py:152
  29.9 3.0 %collective-permute-done.3.refs_9_ = bf16[512,1024]{1,0:T(8,128)(2,1)S(1)} collective-permute-done((bf16[512,1024]{1,0:T(8,128)(2,1)S(1)}, bf16[512,1024]{1,0:T(8,128)(2,1)S(1)}, u32[]{:S(2)}, u32[]{:S(2)}) %collective-permute-start.3) | collective-permute-done | bytes 1048608 | tf_op jit(solution)/shard_map/ppermute | solution.py:351
  32.9 4.3 %collective-permute-done.4.refs_11_ = bf16[512,1024]{1,0:T(8,128)(2,1)} collective-permute-done((bf16[512,1024]{1,0:T(8,128)(2,1)S(1)}, bf16[512,1024]{1,0:T(8,128)(2,1)}, u32[]{:S(2)}, u32[]{:S(2)}) %collective-permute-start.4) | collective-permute-done | bytes 1048608 | tf_op jit(solution)/shard_map/ppermute | solution.py:352
  38.0 1.3 collective-permute-start.7
  40.7 7.2 %collective-permute-start.11 = (bf16[512,1024]{1,0:T(8,128)(2,1)}, bf16[512,1024]{1,0:T(8,128)(2,1)S(1)}, u32[]{:S(2)}, u32[]{:S(2)}) collective-permute-start(bf16[512,1024]{1,0:T(8,128)(2,1)} %collective-permute-done.5.refs_8_), channel_id=1, source_target_pairs={{0,8},{4,12},{8,16},{12,20},{16,24},{20,28},{1,9},{5,13},{9,17},{1... | collective-permute-start | bytes 3145736 | tf_op jit(solution)/shard_map/ppermute | solution.py:351
  47.9 1.3 collective-permute-start.12
  49.2 1.8 attend.1.refs_0_
  51.0 17.7 %collective-permute-done.7.refs_12_ = bf16[512,1024]{1,0:T(8,128)(2,1)S(1)} collective-permute-done((bf16[512,1024]{1,0:T(8,128)(2,1)}, bf16[512,1024]{1,0:T(8,128)(2,1)S(1)}, u32[]{:S(2)}, u32[]{:S(2)}) %collective-permute-start.7) | collective-permute-done | bytes 1048608 | tf_op jit(solution)/shard_map/ppermute | solution.py:352
  69.3 1.5 collective-permute-start.9
  70.8 18.8 %collective-permute-done.12.refs_11_.refs_10_ = bf16[512,1024]{1,0:T(8,128)(2,1)S(1)} collective-permute-done((bf16[512,1024]{1,0:T(8,128)(2,1)}, bf16[512,1024]{1,0:T(8,128)(2,1)S(1)}, u32[]{:S(2)}, u32[]{:S(2)}) %collective-permute-start.12) | collective-permute-done | bytes 1048608 | tf_op jit(solution)/shard_map/ppermute | solution.py:352
  91.4 1.3 collective-permute-start.18
  92.7 1.8 collective-permute-start.15
  96.8 27.3 %collective-permute-done.18.refs_12_ = bf16[512,1024]{1,0:T(8,128)(2,1)S(1)} collective-permute-done((bf16[512,1024]{1,0:T(8,128)(2,1)S(1)}, bf16[512,1024]{1,0:T(8,128)(2,1)S(1)}, u32[]{:S(2)}, u32[]{:S(2)}) %collective-permute-start.18) | collective-permute-done | bytes 1048608 | tf_op jit(solution)/shard_map/ppermute | solution.py:352
  125.6 17.1 %collective-permute-done.20.refs_13_ = bf16[512,1024]{1,0:T(8,128)(2,1)S(1)} collective-permute-done((bf16[512,1024]{1,0:T(8,128)(2,1)S(1)}, bf16[512,1024]{1,0:T(8,128)(2,1)S(1)}, u32[]{:S(2)}, u32[]{:S(2)}) %collective-permute-start.20) | collective-permute-done | bytes 1048608 | tf_op jit(solution)/shard_map/ppermute | solution.py:368
  144.0 1.3 collective-permute-start.19
  147.1 1.5 collective-permute-start.22
  148.7 8.7 %product_kept.1.refs_13_ = f32[1024,1024]{1,0:T(8,128)S(1)} custom-call(s32[3]{0:T(128)S(1)} %pad_add_fusion.where_ref, bf16[512,1024]{1,0:T(8,128)(2,1)} %copy-done, bf16[512,1024]{1,0:T(8,128)(2,1)} %copy-done.4, bf16[512,1024]{1,0:T(8,128)(2,1)} %copy-done.2, bf16[512,1024]{1,0:T(8,128)(2,1)} %copy-done.5, bf16[512,1024]{1,0:T(8,128)(2,1)} %copy-done.3, ...), custom_call_target="tpu_custom_call" | custom-call | flops 1048576 | bytes 1048576 | tf_op jit(solution)/shard_map/product_kept/pallas_call | solution.py:268
  157.4 7.1 %product_near.1 = (f32[1024,384]{1,0:T(8,128)S(1)}, f32[1024,384]{1,0:T(8,128)S(1)}, f32[1024,256]{1,0:T(8,128)S(1)}) custom-call(s32[3]{0:T(128)S(1)} %pad_add_fusion.where_ref, bf16[512,1024]{1,0:T(8,128)(2,1)} %copy-done, bf16[512,1024]{1,0:T(8,128)(2,1)} %copy-done.4, bf16[512,1024]{1,0:T(8,128)(2,1)} %copy-done.2, bf16[512,1024]{1,0:T(8,128)(2,1)} %copy-done.5, ...), custom_call_target="tpu_custom_call" | custom-call | flops 1048576 | bytes 1048576 | tf_op jit(solution)/shard_map/product_near/pallas_call | solution.py:268
  164.6 2.8 %product_far.4 = (bf16[512,384]{1,0:T(8,128)(2,1)S(1)}, bf16[512,384]{1,0:T(8,128)(2,1)S(1)}) custom-call(s32[3]{0:T(128)S(1)} %pad_add_fusion.where_ref, bf16[512,1024]{1,0:T(8,128)(2,1)} %copy-done, bf16[512,1024]{1,0:T(8,128)(2,1)} %copy-done.4, bf16[512,1024]{1,0:T(8,128)(2,1)} %copy-done.2, bf16[512,1024]{1,0:T(8,128)(2,1)} %copy-done.5, ...), custom_call_target="tpu_custom_call" | custom-call | flops 1048576 | bytes 1048576 | tf_op jit(solution)/shard_map/product_far/pallas_call | solution.py:268
  167.4 1.6 collective-permute-start.24
  169.7 2.7 %product_far.3 = (bf16[512,384]{1,0:T(8,128)(2,1)S(1)}, bf16[512,384]{1,0:T(8,128)(2,1)S(1)}) custom-call(s32[3]{0:T(128)S(1)} %pad_add_fusion.where_ref, bf16[512,1024]{1,0:T(8,128)(2,1)} %copy-done, bf16[512,1024]{1,0:T(8,128)(2,1)} %copy-done.4, bf16[512,1024]{1,0:T(8,128)(2,1)} %copy-done.2, bf16[512,1024]{1,0:T(8,128)(2,1)} %copy-done.5, ...), custom_call_target="tpu_custom_call" | custom-call | flops 1048576 | bytes 1048576 | tf_op jit(solution)/shard_map/product_far/pallas_call | solution.py:268
  173.1 2.4 %product_far.5 = (bf16[512,256]{1,0:T(8,128)(2,1)S(1)}, bf16[512,256]{1,0:T(8,128)(2,1)S(1)}) custom-call(s32[3]{0:T(128)S(1)} %pad_add_fusion.where_ref, bf16[512,1024]{1,0:T(8,128)(2,1)} %copy-done, bf16[512,1024]{1,0:T(8,128)(2,1)} %copy-done.4, bf16[512,1024]{1,0:T(8,128)(2,1)} %copy-done.2, bf16[512,1024]{1,0:T(8,128)(2,1)} %copy-done.5, ...), custom_call_target="tpu_custom_call" | custom-call | flops 1048576 | bytes 1048576 | tf_op jit(solution)/shard_map/product_far/pallas_call | solution.py:268
  175.5 1.6 collective-permute-start.25
  177.1 12.1 %collective-permute-done.25.refs_5_ = bf16[512,256]{1,0:T(8,128)(2,1)S(1)} collective-permute-done((bf16[512,256]{1,0:T(8,128)(2,1)S(1)}, bf16[512,256]{1,0:T(8,128)(2,1)S(1)}, u32[]{:S(2)}, u32[]{:S(2)}) %collective-permute-start.25) | collective-permute-done | bytes 262176 | tf_op jit(solution)/shard_map/ppermute | solution.py:414
  189.2 2.0 %finish.1 = bf16[512,2048]{1,0:T(8,128)(2,1)} custom-call(s32[3]{0:T(128)} %copy-done.1, bf16[512,384]{1,0:T(8,128)(2,1)S(1)} %get-tuple-element.55.refs_0_, bf16[512,384]{1,0:T(8,128)(2,1)S(1)} %get-tuple-element.57.refs_1_, bf16[512,256]{1,0:T(8,128)(2,1)S(1)} %get-tuple-element.59.refs_2_, bf16[512,384]{1,0:T(8,128)(2,1)S(1)} %collective-permute-done.23.refs_3_, ...), custom_call_target="tpu_custom_call" | custom-call | flops 1048576 | bytes 1048576 | tf_op jit(solution)/shard_map/finish/pallas_call | solution.py:320
  (80 shorter events, 14.4 us)
Async XLA Ops:
  3.7 36.9 %copy-start.20 = (s32[1,1,16]{2,1,0:T(1,128)S(1)}, s32[1,1,16]{2,1,0:T(1,128)}, u32[]{:S(2)}) copy-start(s32[1,1,16]{2,1,0:T(1,128)} %param.11) | copy-start | bytes 196
  3.8 14.8 %collective-permute-start.2 = (bf16[1024,256]{1,0:T(8,128)(2,1)S(1)}, bf16[1024,256]{1,0:T(8,128)(2,1)S(1)}, u32[]{:S(2)}, u32[]{:S(2)}) collective-permute-start(bf16[1024,256]{1,0:T(8,128)(2,1)S(1)} %pad_maximum_fusion.3), channel_id=1, source_target_pairs={{0,3},{1,2},{2,1},{3,0},{4,7},{5,6},{6,5},{7,4},{8,11},{9,10},{10,... | collective-permute-start | bytes 1572872 | tf_op jit(solution)/shard_map/ppermute | solution.py:152
  6.2 26.7 %collective-permute-start.3 = (bf16[512,1024]{1,0:T(8,128)(2,1)S(1)}, bf16[512,1024]{1,0:T(8,128)(2,1)S(1)}, u32[]{:S(2)}, u32[]{:S(2)}) collective-permute-start(bf16[512,1024]{1,0:T(8,128)(2,1)S(1)} %get-tuple-element.38.refs_8_), channel_id=1, source_target_pairs={{0,8},{4,12},{8,16},{12,20},{16,24},{20,28},{1,9},{5,13},{9,17},{1... | collective-permute-start | bytes 3145736 | tf_op jit(solution)/shard_map/ppermute | solution.py:351
  9.8 27.5 %collective-permute-start.4 = (bf16[512,1024]{1,0:T(8,128)(2,1)S(1)}, bf16[512,1024]{1,0:T(8,128)(2,1)}, u32[]{:S(2)}, u32[]{:S(2)}) collective-permute-start(bf16[512,1024]{1,0:T(8,128)(2,1)S(1)} %get-tuple-element.38.refs_8_), channel_id=1, source_target_pairs={{8,0},{12,4},{16,8},{20,12},{24,16},{28,20},{9,1},{13,5},{17,9},{2... | collective-permute-start | bytes 3145736 | tf_op jit(solution)/shard_map/ppermute | solution.py:352
  11.1 26.2 %collective-permute-start.5 = (bf16[512,1024]{1,0:T(8,128)(2,1)S(1)}, bf16[512,1024]{1,0:T(8,128)(2,1)}, u32[]{:S(2)}, u32[]{:S(2)}) collective-permute-start(bf16[512,1024]{1,0:T(8,128)(2,1)S(1)} %get-tuple-element.39), channel_id=1, source_target_pairs={{0,4},{4,0},{8,12},{12,8},{16,20},{20,16},{24,28},{28,24},{1,5},{5... | collective-permute-start | bytes 3145736 | tf_op jit(solution)/shard_map/ppermute | solution.py:360
  12.7 17.2 %collective-permute-start.1 = (bf16[1024,256]{1,0:T(8,128)(2,1)S(1)}, bf16[1024,256]{1,0:T(8,128)(2,1)S(1)}, u32[]{:S(2)}, u32[]{:S(2)}) collective-permute-start(bf16[1024,256]{1,0:T(8,128)(2,1)S(1)} %pad_maximum_fusion.2), channel_id=1, source_target_pairs={{0,2},{1,3},{2,0},{3,1},{4,6},{5,7},{6,4},{7,5},{8,10},{9,11},{10,... | collective-permute-start | bytes 1572872 | tf_op jit(solution)/shard_map/ppermute | solution.py:152
  18.5 11.4 %collective-permute-start = (bf16[1024,256]{1,0:T(8,128)(2,1)S(1)}, bf16[1024,256]{1,0:T(8,128)(2,1)S(1)}, u32[]{:S(2)}, u32[]{:S(2)}) collective-permute-start(bf16[1024,256]{1,0:T(8,128)(2,1)S(1)} %pad_maximum_fusion.1), channel_id=1, source_target_pairs={{0,1},{1,0},{2,3},{3,2},{4,5},{5,4},{6,7},{7,6},{8,9},{9,8},{10,11... | collective-permute-start | bytes 1572872 | tf_op jit(solution)/shard_map/ppermute | solution.py:152
  37.2 13.8 %collective-permute-start.6 = (bf16[512,1024]{1,0:T(8,128)(2,1)S(1)}, bf16[512,1024]{1,0:T(8,128)(2,1)S(1)}, u32[]{:S(2)}, u32[]{:S(2)}) collective-permute-start(bf16[512,1024]{1,0:T(8,128)(2,1)S(1)} %collective-permute-done.3.refs_9_), channel_id=1, source_target_pairs={{8,16},{12,20},{16,24},{20,28},{9,17},{13,21},{17,25},{21,29},{10,... | collective-permute-start | bytes 3145736 | tf_op jit(solution)/shard_map/ppermute | solution.py:351
  38.0 30.8 %collective-permute-start.7 = (bf16[512,1024]{1,0:T(8,128)(2,1)}, bf16[512,1024]{1,0:T(8,128)(2,1)S(1)}, u32[]{:S(2)}, u32[]{:S(2)}) collective-permute-start(bf16[512,1024]{1,0:T(8,128)(2,1)} %collective-permute-done.4.refs_11_), channel_id=1, source_target_pairs={{8,0},{12,4},{16,8},{20,12},{9,1},{13,5},{17,9},{21,13},{10,2},{14... | collective-permute-start | bytes 3145736 | tf_op jit(solution)/shard_map/ppermute | solution.py:352
  40.7 30.1 %collective-permute-start.11 = (bf16[512,1024]{1,0:T(8,128)(2,1)}, bf16[512,1024]{1,0:T(8,128)(2,1)S(1)}, u32[]{:S(2)}, u32[]{:S(2)}) collective-permute-start(bf16[512,1024]{1,0:T(8,128)(2,1)} %collective-permute-done.5.refs_8_), channel_id=1, source_target_pairs={{0,8},{4,12},{8,16},{12,20},{16,24},{20,28},{1,9},{5,13},{9,17},{1... | collective-permute-start | bytes 3145736 | tf_op jit(solution)/shard_map/ppermute | solution.py:351
  47.9 41.7 %collective-permute-start.12 = (bf16[512,1024]{1,0:T(8,128)(2,1)}, bf16[512,1024]{1,0:T(8,128)(2,1)S(1)}, u32[]{:S(2)}, u32[]{:S(2)}) collective-permute-start(bf16[512,1024]{1,0:T(8,128)(2,1)} %collective-permute-done.5.refs_8_), channel_id=1, source_target_pairs={{8,0},{12,4},{16,8},{20,12},{24,16},{28,20},{9,1},{13,5},{17,9},{2... | collective-permute-start | bytes 3145736 | tf_op jit(solution)/shard_map/ppermute | solution.py:352
  51.0 74.6 %copy-start = (bf16[512,1024]{1,0:T(8,128)(2,1)}, bf16[512,1024]{1,0:T(8,128)(2,1)S(1)}, u32[]{:S(2)}) copy-start(bf16[512,1024]{1,0:T(8,128)(2,1)S(1)} %attend.1.refs_0_) | copy-start | bytes 3145732
  51.0 97.6 %copy-start.11 = (bf16[512,1024]{1,0:T(8,128)(2,1)}, bf16[512,1024]{1,0:T(8,128)(2,1)S(1)}, u32[]{:S(2)}) copy-start(bf16[512,1024]{1,0:T(8,128)(2,1)S(1)} %collective-permute-done.6.refs_10_) | copy-start | bytes 3145732
  68.7 79.9 %copy-start.12 = (bf16[512,1024]{1,0:T(8,128)(2,1)}, bf16[512,1024]{1,0:T(8,128)(2,1)S(1)}, u32[]{:S(2)}) copy-start(bf16[512,1024]{1,0:T(8,128)(2,1)S(1)} %collective-permute-done.7.refs_12_) | copy-start | bytes 3145732
  68.7 21.9 %collective-permute-start.10 = (bf16[512,1024]{1,0:T(8,128)(2,1)S(1)}, bf16[512,1024]{1,0:T(8,128)(2,1)S(1)}, u32[]{:S(2)}, u32[]{:S(2)}) collective-permute-start(bf16[512,1024]{1,0:T(8,128)(2,1)S(1)} %attend.1.refs_0_), channel_id=1, source_target_pairs={{0,2},{1,3},{2,0},{3,1},{4,6},{5,7},{6,4},{7,5},{8,10},{9,11},{10,... | collective-permute-start | bytes 3145736 | tf_op jit(solution)/shard_map/ppermute | solution.py:370
  69.3 21.4 %collective-permute-start.9 = (bf16[512,1024]{1,0:T(8,128)(2,1)S(1)}, bf16[512,1024]{1,0:T(8,128)(2,1)S(1)}, u32[]{:S(2)}, u32[]{:S(2)}) collective-permute-start(bf16[512,1024]{1,0:T(8,128)(2,1)S(1)} %attend.1.refs_0_), channel_id=1, source_target_pairs={{0,4},{4,0},{8,12},{12,8},{16,20},{20,16},{24,28},{28,24},{1,5},{5... | collective-permute-start | bytes 3145736 | tf_op jit(solution)/shard_map/ppermute | solution.py:369
  70.8 54.8 %copy-start.6 = (bf16[512,1024]{1,0:T(8,128)(2,1)}, bf16[512,1024]{1,0:T(8,128)(2,1)S(1)}, u32[]{:S(2)}) copy-start(bf16[512,1024]{1,0:T(8,128)(2,1)S(1)} %collective-permute-done.11.refs_9_) | copy-start | bytes 3145732
  90.7 5.6 %collective-permute-start.17 = (bf16[512,1024]{1,0:T(8,128)(2,1)S(1)}, bf16[512,1024]{1,0:T(8,128)(2,1)S(1)}, u32[]{:S(2)}, u32[]{:S(2)}) collective-permute-start(bf16[512,1024]{1,0:T(8,128)(2,1)S(1)} %collective-permute-done.11.refs_9_), channel_id=1, source_target_pairs={{8,16},{12,20},{16,24},{20,28},{9,17},{13,21},{17,25},{21,29},{10,... | collective-permute-start | bytes 3145736 | tf_op jit(solution)/shard_map/ppermute | solution.py:351
  91.4 32.7 %collective-permute-start.18 = (bf16[512,1024]{1,0:T(8,128)(2,1)S(1)}, bf16[512,1024]{1,0:T(8,128)(2,1)S(1)}, u32[]{:S(2)}, u32[]{:S(2)}) collective-permute-start(bf16[512,1024]{1,0:T(8,128)(2,1)S(1)} %collective-permute-done.12.refs_11_.refs_10_), channel_id=1, source_target_pairs={{8,0},{12,4},{16,8},{20,12},{9,1},{13,5},{17,9},{21,13},{10,2},{14... | collective-permute-start | bytes 3145736 | tf_op jit(solution)/shard_map/ppermute | solution.py:352
  92.7 31.4 %collective-permute-start.15 = (bf16[512,1024]{1,0:T(8,128)(2,1)S(1)}, bf16[512,1024]{1,0:T(8,128)(2,1)}, u32[]{:S(2)}, u32[]{:S(2)}) collective-permute-start(bf16[512,1024]{1,0:T(8,128)(2,1)S(1)} %collective-permute-done.9.refs_4_), channel_id=1, source_target_pairs={{0,2},{1,3},{2,0},{3,1},{4,6},{5,7},{6,4},{7,5},{8,10},{9,11},{10,... | collective-permute-start | bytes 3145736 | tf_op jit(solution)/shard_map/ppermute | solution.py:381
  94.9 47.8 %collective-permute-start.20 = (bf16[512,1024]{1,0:T(8,128)(2,1)S(1)}, bf16[512,1024]{1,0:T(8,128)(2,1)S(1)}, u32[]{:S(2)}, u32[]{:S(2)}) collective-permute-start(bf16[512,1024]{1,0:T(8,128)(2,1)S(1)} %add.47), channel_id=1, source_target_pairs={{8,0},{12,4},{16,24},{20,28},{9,1},{13,5},{17,25},{21,29},{10,2},{... | collective-permute-start | bytes 3145736 | tf_op jit(solution)/shard_map/ppermute | solution.py:368
  96.2 47.8 %collective-permute-start.8 = (bf16[512,1024]{1,0:T(8,128)(2,1)S(1)}, bf16[512,1024]{1,0:T(8,128)(2,1)S(1)}, u32[]{:S(2)}, u32[]{:S(2)}) collective-permute-start(bf16[512,1024]{1,0:T(8,128)(2,1)S(1)} %attend.1.refs_0_), channel_id=1, source_target_pairs={{0,1},{1,0},{2,3},{3,2},{4,5},{5,4},{6,7},{7,6},{8,9},{9,8},{10,11... | collective-permute-start | bytes 3145736 | tf_op jit(solution)/shard_map/ppermute | solution.py:356
  96.3 49.8 %copy-start.8 = (bf16[512,1024]{1,0:T(8,128)(2,1)}, bf16[512,1024]{1,0:T(8,128)(2,1)S(1)}, u32[]{:S(2)}) copy-start(bf16[512,1024]{1,0:T(8,128)(2,1)S(1)} %collective-permute-done.17.refs_10_) | copy-start | bytes 3145732
  96.3 49.8 %collective-permute-start.13 = (bf16[512,1024]{1,0:T(8,128)(2,1)S(1)}, bf16[512,1024]{1,0:T(8,128)(2,1)S(1)}, u32[]{:S(2)}, u32[]{:S(2)}) collective-permute-start(bf16[512,1024]{1,0:T(8,128)(2,1)S(1)} %collective-permute-done.10.refs_2_), channel_id=1, source_target_pairs={{0,1},{1,0},{2,3},{3,2},{4,5},{5,4},{6,7},{7,6},{8,9},{9,8},{10,11... | collective-permute-start | bytes 3145736 | tf_op jit(solution)/shard_map/ppermute | solution.py:356
  124.1 24.6 %collective-permute-start.14 = (bf16[512,1024]{1,0:T(8,128)(2,1)S(1)}, bf16[512,1024]{1,0:T(8,128)(2,1)}, u32[]{:S(2)}, u32[]{:S(2)}) collective-permute-start(bf16[512,1024]{1,0:T(8,128)(2,1)S(1)} %collective-permute-done.9.refs_4_), channel_id=1, source_target_pairs={{0,1},{1,0},{2,3},{3,2},{4,5},{5,4},{6,7},{7,6},{8,9},{9,8},{10,11... | collective-permute-start | bytes 3145736 | tf_op jit(solution)/shard_map/ppermute | solution.py:356
  124.1 24.6 %collective-permute-start.16 = (bf16[512,1024]{1,0:T(8,128)(2,1)}, bf16[512,1024]{1,0:T(8,128)(2,1)}, u32[]{:S(2)}, u32[]{:S(2)}) collective-permute-start(bf16[512,1024]{1,0:T(8,128)(2,1)} %collective-permute-done.15.refs_6_), channel_id=1, source_target_pairs={{0,1},{1,0},{2,3},{3,2},{4,5},{5,4},{6,7},{7,6},{8,9},{9,8},{10,11... | collective-permute-start | bytes 3145736 | tf_op jit(solution)/shard_map/ppermute | solution.py:356
  142.7 21.9 %collective-permute-start.21 = (bf16[512,384]{1,0:T(8,128)(2,1)}, bf16[512,384]{1,0:T(8,128)(2,1)}, u32[]{:S(2)}, u32[]{:S(2)}) collective-permute-start(bf16[512,384]{1,0:T(8,128)(2,1)} %get-tuple-element.63), channel_id=1, source_target_pairs={{8,0},{12,4},{16,24},{20,28},{9,1},{13,5},{17,25},{21,29},{10,2},{... | collective-permute-start | bytes 1179656 | tf_op jit(solution)/shard_map/ppermute | solution.py:379
  144.0 24.9 %collective-permute-start.19 = (bf16[512,384]{1,0:T(8,128)(2,1)}, bf16[512,384]{1,0:T(8,128)(2,1)S(1)}, u32[]{:S(2)}, u32[]{:S(2)}) collective-permute-start(bf16[512,384]{1,0:T(8,128)(2,1)} %get-tuple-element.64), channel_id=1, source_target_pairs={{8,0},{12,4},{16,24},{20,28},{9,1},{13,5},{17,25},{21,29},{10,2},{... | collective-permute-start | bytes 1179656 | tf_op jit(solution)/shard_map/ppermute | solution.py:379
  147.1 26.0 %collective-permute-start.22 = (bf16[512,256]{1,0:T(8,128)(2,1)}, bf16[512,256]{1,0:T(8,128)(2,1)}, u32[]{:S(2)}, u32[]{:S(2)}) collective-permute-start(bf16[512,256]{1,0:T(8,128)(2,1)} %slice_add_fusion.2), channel_id=1, source_target_pairs={{8,0},{12,4},{16,24},{20,28},{9,1},{13,5},{17,25},{21,29},{10,2},{... | collective-permute-start | bytes 786440 | tf_op jit(solution)/shard_map/ppermute | solution.py:379
  167.4 21.9 %collective-permute-start.24 = (bf16[512,384]{1,0:T(8,128)(2,1)S(1)}, bf16[512,384]{1,0:T(8,128)(2,1)S(1)}, u32[]{:S(2)}, u32[]{:S(2)}) collective-permute-start(bf16[512,384]{1,0:T(8,128)(2,1)S(1)} %get-tuple-element.61), channel_id=1, source_target_pairs={{0,4},{4,0},{8,12},{12,8},{16,20},{20,16},{24,28},{28,24},{1,5},{5... | collective-permute-start | bytes 1179656 | tf_op jit(solution)/shard_map/ppermute | solution.py:414
  172.5 16.8 %collective-permute-start.23 = (bf16[512,384]{1,0:T(8,128)(2,1)S(1)}, bf16[512,384]{1,0:T(8,128)(2,1)S(1)}, u32[]{:S(2)}, u32[]{:S(2)}) collective-permute-start(bf16[512,384]{1,0:T(8,128)(2,1)S(1)} %get-tuple-element.60), channel_id=1, source_target_pairs={{0,4},{4,0},{8,12},{12,8},{16,20},{20,16},{24,28},{28,24},{1,5},{5... | collective-permute-start | bytes 1179656 | tf_op jit(solution)/shard_map/ppermute | solution.py:414
  175.5 13.7 %collective-permute-start.25 = (bf16[512,256]{1,0:T(8,128)(2,1)S(1)}, bf16[512,256]{1,0:T(8,128)(2,1)S(1)}, u32[]{:S(2)}, u32[]{:S(2)}) collective-permute-start(bf16[512,256]{1,0:T(8,128)(2,1)S(1)} %get-tuple-element.62), channel_id=1, source_target_pairs={{0,4},{4,0},{8,12},{12,8},{16,20},{20,16},{24,28},{28,24},{1,5},{5... | collective-permute-start | bytes 786440 | tf_op jit(solution)/shard_map/ppermute | solution.py:414
  (15 other events, 230.8 us)

commit v7 on v5

--- a/solution.py
+++ b/solution.py
@@ -21,7 +21,7 @@
 GROUP = 4
 
 
-def attention_kernel(heads, slots, meta_ref, q_hbm, old_hbm, *refs):
+def attention_kernel(heads, slots, row_starts, meta_ref, q_hbm, old_hbm, *refs):
     kv_parts, (out_ref, q_ref, kv_ref, peak_ref, denom_ref, acc_ref, sems) = refs[:-7], refs[-7:]
     live = meta_ref[0]
     flag = meta_ref[1]
@@ -35,12 +35,26 @@
     @pl.when(flag > 0)
     def _():
         copies = [pltpu.make_async_copy(q_hbm, q_ref, sems.at[0])]
+        rows = kv_ref.shape[0] // len(kv_parts)
+        pick = pl.multiple_of(meta_ref[2 + slots + len(kv_parts)] * HEAD_SIZE, HEAD_SIZE)
         for index, part in enumerate(kv_parts):
-            rows = part.shape[0]
             start = pl.multiple_of(meta_ref[2 + slots + index] * rows, rows)
-            copies.append(
-                pltpu.make_async_copy(part, kv_ref.at[pl.ds(start, rows), :], sems.at[1 + index])
-            )
+            source_rows, target_rows = pl.ds(row_starts[index], rows), pl.ds(start, rows)
+            if part.shape[1] == 2 * HEAD_SIZE:
+                pairs = [(pl.ds(0, 2 * HEAD_SIZE), pl.ds(0, 2 * HEAD_SIZE))]
+            else:
+                pairs = [
+                    (pl.ds(pick, HEAD_SIZE), pl.ds(0, HEAD_SIZE)),
+                    (pl.ds(part.shape[1] // 2 + pick, HEAD_SIZE), pl.ds(HEAD_SIZE, HEAD_SIZE)),
+                ]
+            for side, (source_columns, target_columns) in enumerate(pairs):
+                copies.append(
+                    pltpu.make_async_copy(
+                        part.at[source_rows, source_columns],
+                        kv_ref.at[target_rows, target_columns],
+                        sems.at[1 + 2 * index + side],
+                    )
+                )
         for copy in copies:
             copy.start()
         peak_ref[...] = jnp.full_like(peak_ref, LOWEST)
@@ -100,24 +114,28 @@
             out_ref[:, head * HEAD_SIZE : (head + 1) * HEAD_SIZE] = result.T.astype(jnp.bfloat16)
 
 
-def attend(block_list, live, flag, queries, old, kv_parts, places):
+def attend(block_list, live, flag, queries, old, key_values):
+    arrays, row_starts, places, pick = key_values
     rows, width = queries.shape
     heads = width // HEAD_SIZE
     slots = block_list.shape[0]
-    meta = jnp.concatenate([live[None], flag[None], block_list, *[p[None] for p in places]])
+    part_rows = min(x.shape[0] for x in arrays)
+    meta = jnp.concatenate(
+        [live[None], flag[None], block_list, *[p[None] for p in places], pick[None]]
+    )
     in_hbm = pl.BlockSpec(memory_space=pltpu.HBM)
     return pl.pallas_call(
-        functools.partial(attention_kernel, heads, slots),
+        functools.partial(attention_kernel, heads, slots, tuple(row_starts)),
         out_shape=jax.ShapeDtypeStruct((rows, width), jnp.bfloat16),
-        in_specs=[pl.BlockSpec(memory_space=pltpu.SMEM)] + [in_hbm] * (2 + len(kv_parts)),
+        in_specs=[pl.BlockSpec(memory_space=pltpu.SMEM)] + [in_hbm] * (2 + len(arrays)),
         out_specs=pl.BlockSpec(memory_space=pltpu.VMEM),
         scratch_shapes=[
             pltpu.VMEM((rows, width), jnp.bfloat16),
-            pltpu.VMEM((sum(p.shape[0] for p in kv_parts), 2 * HEAD_SIZE), jnp.bfloat16),
+            pltpu.VMEM((part_rows * len(arrays), 2 * HEAD_SIZE), jnp.bfloat16),
             pltpu.VMEM((heads, 1, rows), jnp.float32),
             pltpu.VMEM((heads, 1, rows), jnp.float32),
             pltpu.VMEM((heads, HEAD_SIZE, rows), jnp.float32),
-            pltpu.SemaphoreType.DMA((1 + len(kv_parts),)),
+            pltpu.SemaphoreType.DMA((1 + 2 * len(arrays),)),
         ],
         compiler_params=pltpu.CompilerParams(vmem_limit_bytes=24 << 20),
         cost_estimate=pl.CostEstimate(
@@ -128,7 +146,7 @@
         meta,
         *[
             pltpu.with_memory_space_constraint(x, pltpu.HBM)
-            for x in (queries, old, *kv_parts)
+            for x in (queries, old, *arrays)
         ],
     )
 
@@ -137,22 +155,31 @@
     groups = lax.axis_size("ka")
     me = lax.axis_index("ka")
     rows = keys.shape[0]
-    if groups == KEY_VALUE_HEADS:
-
-        def head_of(device):
-            start = (0, device * HEAD_SIZE)
+    if groups == KEY_VALUE_HEADS == 4:
+        x, core = me // 2, me % 2
+        pair = 2 * HEAD_SIZE
+
+        def heads_of(chip):
             return jnp.concatenate(
-                [lax.dynamic_slice(x, start, (rows, HEAD_SIZE)) for x in (keys, values)], axis=1
+                [lax.dynamic_slice(a, (0, chip * pair), (rows, pair)) for a in (keys, values)], axis=1
             )
 
-        parts, places = [head_of(me)], [me]
-        for step in range(1, groups):
-            partner = jnp.bitwise_xor(me, step)
-            parts.append(
-                lax.ppermute(head_of(partner), "ka", [(i, i ^ step) for i in range(groups)])
-            )
-            places.append(partner)
-        return parts, places
+        def head_of(both):
+            picked = [
+                lax.dynamic_slice(both, (0, side * pair + (1 - core) * HEAD_SIZE), (rows, HEAD_SIZE))
+                for side in range(2)
+            ]
+            return jnp.concatenate(picked, axis=1)
+
+        across = lax.ppermute(heads_of(1 - x), "ka", [(i, i ^ 2) for i in range(4)])
+        mine = heads_of(x)
+        beside = lax.ppermute(
+            jnp.concatenate([head_of(mine), head_of(across)], axis=0),
+            "ka",
+            [(i, i ^ 1) for i in range(4)],
+        )
+        places = [jnp.bitwise_xor(me, step) for step in (0, 2, 1, 3)]
+        return [mine, across, beside, beside], [0, 0, 0, rows], places, core
     both = jnp.concatenate(
         [
             keys.reshape(rows, KEY_VALUE_HEADS, HEAD_SIZE),
@@ -164,7 +191,7 @@
     everything = lax.all_to_all(
         both.reshape(rows, groups * 2 * HEAD_SIZE), "ka", split_axis=1, concat_axis=0, tiled=True
     )
-    return [everything], [jnp.int32(0)]
+    return [everything], [0], [jnp.int32(0)], jnp.int32(0)
 
 
 def ring_of(pb_size):
@@ -329,8 +356,9 @@
 
     def attend_with(inputs):
         queries, keys, values, old = inputs
-        parts, places = own_head_keys_values(keys, values)
-        return attend(block_ids[0, 0], counts[0, 0], refresh[0, 0], queries, old, parts, places)
+        return attend(
+            block_ids[0, 0], counts[0, 0], refresh[0, 0], queries, old, own_head_keys_values(keys, values)
+        )
 
     inputs = (queries[0], keys, values, cached_attn[0])
     if lax.axis_size("pb") == 8 and groups == 4:

time: 176 us -> 178 us (1.011)
  starting transfers between devices: 51.2 us -> 21.5 us
  Pallas kernels: 25.5 us -> 42.4 us
  waiting for transfers between devices: 92.2 us -> 101 us
  local copies, waits for them, and re-layouts: 4.71 us -> 7.3 us
  other arithmetic: 1.13 us -> 3.5 us
    ppermute x7, waiting for transfers between devices: 42 us -> 73.6 us  [project_ring(): moving[part][1] = lax.ppermute(moving[part][1], 'pb', backward)]
    ppermute x7, starting transfers between devices: 36.8 us -> 9.06 us  [project_ring(): moving[part][0] = lax.ppermute(moving[part][0], 'pb', forward)]
    ppermute x7, waiting for transfers between devices: 31 us -> 7.81 us  [project_ring(): moving[part][0] = lax.ppermute(moving[part][0], 'pb', forward)]
    pallas_call x1, Pallas kernels: 1.81 us -> 18.7 us  [attend(): pl.pallas_call(functools.partial(attention_kernel, heads, slots, tuple(ro...]
    concatenate x4, other arithmetic: 1.05 us -> 3.42 us  [the longest x3 2.32 us: heads_of(): jnp.concatenate([lax.dynamic_slice(a, (0, chip * pair), (rows, pair)) for...]
    ppermute x7, starting transfers between devices: 11.5 us -> 9.34 us  [project_ring(): moving[part][1] = lax.ppermute(moving[part][1], 'pb', backward)]
    unnamed x24 -> x16, local copies, waits for them, and re-layouts: 0.04 us -> 1.93 us
    ppermute x3 -> x2, waiting for transfers between devices: 18.6 us -> 19.6 us  [the longest x1 19.6 us: own_head_keys_values(): across = lax.ppermute(heads_of(1 - x), 'ka', [(i, i ^ 2) for i in range(4)])]
  transfers between devices with their start and end apart: 20 -> 19, of which waited for: 14 -> 11; matrix products, arithmetic and copies ran while one was open for 2% -> 2% of each run, Pallas kernels for 11% -> 21%
where the time goes in v7:
time: 178 us
  waiting for transfers between devices  101 us (57%)
  Pallas kernels  42.4 us (24%)
  starting transfers between devices  21.5 us (12%)
  local copies, waits for them, and re-layouts  7.3 us (4%)
  other arithmetic  3.5 us (2%)
    ppermute x7, waiting for transfers between devices, project_ring(): moving[part][1] = lax.ppermute(moving[part][1], 'pb', backward)  73.6 us
    pallas_call x3, Pallas kernels, ring_product(): pl.pallas_call(functools.partial(ring_product_kernel, steps, base is not...  23.6 us
    ppermute x1, waiting for transfers between devices, own_head_keys_values(): across = lax.ppermute(heads_of(1 - x), 'ka', [(i, i ^ 2) for i in range(4)])  19.6 us
    pallas_call x1, Pallas kernels, attend(): pl.pallas_call(functools.partial(attention_kernel, heads, slots, tuple(ro...  18.7 us
    ppermute x7, starting transfers between devices, project_ring(): moving[part][1] = lax.ppermute(moving[part][1], 'pb', backward)  9.34 us
    ppermute x7, starting transfers between devices, project_ring(): moving[part][0] = lax.ppermute(moving[part][0], 'pb', forward)  9.06 us
    ppermute x7, waiting for transfers between devices, project_ring(): moving[part][0] = lax.ppermute(moving[part][0], 'pb', forward)  7.81 us
  transfers between devices with their start and end apart: 19, of which 11 were waited for; matrix products, arithmetic and copies ran while one was open for 2% of the time, Pallas kernels for 21%

profile of v7, /device:TPU:0, one launch (start us, length us, event | category | flops | bytes accessed | tf_op | source)
XLA Modules:
  0.0 177.5 jit_solution(11643616960833702799)
XLA Ops:
  0.0 2.8 %fusion.3 = (bf16[512,1024]{1,0:T(8,128)(2,1)S(1)}, bf16[512,1024]{1,0:T(8,128)(2,1)}) fusion(bf16[512,2048]{1,0:T(8,128)(2,1)} %param.16), kind=kLoop, calls=%fused_computation.18 | loop fusion | bytes 4194304 | tf_op jit(solution)/shard_map/slice | solution.py:322
  2.8 1.7 constant_dynamic-slice_fusion.2
  4.5 1.1 pad_maximum_fusion.1
  5.6 2.9 %collective-permute-start = (bf16[1024,512]{1,0:T(8,128)(2,1)}, bf16[1024,512]{1,0:T(8,128)(2,1)S(1)}, u32[]{:S(2)}, u32[]{:S(2)}) collective-permute-start(bf16[1024,512]{1,0:T(8,128)(2,1)} %pad_maximum_fusion.1), channel_id=1, source_target_pairs={{0,2},{1,3},{2,0},{3,1},{4,6},{5,7},{6,4},{7,5},{8,10},{9,11},{10,... | collective-permute-start | bytes 3145736 | tf_op jit(solution)/shard_map/ppermute | solution.py:174
  8.5 1.5 collective-permute-start.9
  10.0 1.6 collective-permute-start.13
  12.3 19.6 %collective-permute-done.refs_1_ = bf16[1024,512]{1,0:T(8,128)(2,1)S(1)} collective-permute-done((bf16[1024,512]{1,0:T(8,128)(2,1)}, bf16[1024,512]{1,0:T(8,128)(2,1)S(1)}, u32[]{:S(2)}, u32[]{:S(2)}) %collective-permute-start) | collective-permute-done | bytes 1048608 | tf_op jit(solution)/shard_map/ppermute | solution.py:174
  31.9 0.9 copy-done.5
  32.9 1.1 maximum_maximum_fusion
  34.0 1.9 %collective-permute-start.16 = (bf16[512,1024]{1,0:T(8,128)(2,1)S(1)}, bf16[512,1024]{1,0:T(8,128)(2,1)}, u32[]{:S(2)}, u32[]{:S(2)}) collective-permute-start(bf16[512,1024]{1,0:T(8,128)(2,1)S(1)} %get-tuple-element.16.refs_9_), channel_id=1, source_target_pairs={{0,8},{8,16},{16,24},{24,28},{28,20},{20,12},{12,4},{4,0},{1,9},{9... | collective-permute-start | bytes 3145736 | tf_op jit(solution)/shard_map/ppermute | solution.py:329
  36.2 20.9 %collective-permute-done.13.refs_6_ = bf16[512,1024]{1,0:T(8,128)(2,1)} collective-permute-done((bf16[512,1024]{1,0:T(8,128)(2,1)}, bf16[512,1024]{1,0:T(8,128)(2,1)}, u32[]{:S(2)}, u32[]{:S(2)}) %collective-permute-start.13) | collective-permute-done | bytes 1048608 | tf_op jit(solution)/shard_map/ppermute | solution.py:332
  57.2 1.5 collective-permute-start.14
  60.6 1.1 pad_maximum_fusion.refs_0_
  61.6 1.0 copy-done.3
  62.6 18.7 %attend.1.refs_0_ = bf16[512,1024]{1,0:T(8,128)(2,1)S(1)} custom-call(s32[23]{0:T(128)S(1)} %concatenate.22.meta_ref, bf16[512,1024]{1,0:T(8,128)(2,1)} %bitcast.15, bf16[512,1024]{1,0:T(8,128)(2,1)} %bitcast.16, bf16[1024,512]{1,0:T(8,128)(2,1)} %pad_maximum_fusion.refs_0_, bf16[1024,512]{1,0:T(8,128)(2,1)} %copy-done.5, bf16[2048,256]{1,0:T(8,128)(2,1)} %copy-done.3, ...), custom_call_target="tpu_custom_call" | custom-call | flops 1048576 | bytes 1048576 | tf_op jit(solution)/shard_map/attend/pallas_call | solution.py:127
  81.6 2.0 %collective-permute-start.17 = (bf16[512,1024]{1,0:T(8,128)(2,1)}, bf16[512,1024]{1,0:T(8,128)(2,1)}, u32[]{:S(2)}, u32[]{:S(2)}) collective-permute-start(bf16[512,1024]{1,0:T(8,128)(2,1)} %collective-permute-done.16.refs_10_), channel_id=1, source_target_pairs={{0,8},{8,16},{16,24},{24,28},{28,20},{20,12},{12,4},{4,0},{1,9},{9... | collective-permute-start | bytes 3145736 | tf_op jit(solution)/shard_map/ppermute | solution.py:329
  83.6 17.0 %collective-permute-done.14.refs_8_ = bf16[512,1024]{1,0:T(8,128)(2,1)} collective-permute-done((bf16[512,1024]{1,0:T(8,128)(2,1)}, bf16[512,1024]{1,0:T(8,128)(2,1)}, u32[]{:S(2)}, u32[]{:S(2)}) %collective-permute-start.14) | collective-permute-done | bytes 1048608 | tf_op jit(solution)/shard_map/ppermute | solution.py:332
  100.6 1.5 collective-permute-start.11
  103.2 3.2 %collective-permute-done.17.refs_12_ = bf16[512,1024]{1,0:T(8,128)(2,1)} collective-permute-done((bf16[512,1024]{1,0:T(8,128)(2,1)}, bf16[512,1024]{1,0:T(8,128)(2,1)}, u32[]{:S(2)}, u32[]{:S(2)}) %collective-permute-start.17) | collective-permute-done | bytes 1048608 | tf_op jit(solution)/shard_map/ppermute | solution.py:329
  106.4 1.3 collective-permute-start.15
  107.7 1.2 collective-permute-start.18
  108.9 18.1 %collective-permute-done.11.refs_7_ = bf16[512,1024]{1,0:T(8,128)(2,1)} collective-permute-done((bf16[512,1024]{1,0:T(8,128)(2,1)}, bf16[512,1024]{1,0:T(8,128)(2,1)}, u32[]{:S(2)}, u32[]{:S(2)}) %collective-permute-start.11) | collective-permute-done | bytes 1048608 | tf_op jit(solution)/shard_map/ppermute | solution.py:332
  127.1 1.5 collective-permute-start.12
  128.9 2.5 %collective-permute-start.8 = (bf16[512,1024]{1,0:T(8,128)(2,1)}, bf16[512,1024]{1,0:T(8,128)(2,1)}, u32[]{:S(2)}, u32[]{:S(2)}) collective-permute-start(bf16[512,1024]{1,0:T(8,128)(2,1)} %collective-permute-done.7.refs_4_), channel_id=1, source_target_pairs={{0,8},{8,16},{16,24},{24,28},{28,20},{20,12},{12,4},{4,0},{1,9},{9... | collective-permute-start | bytes 3145736 | tf_op jit(solution)/shard_map/ppermute | solution.py:329
  131.3 0.7 fusion.2
  132.1 11.7 %ring_product.3.refs_8_ = f32[512,2048]{1,0:T(8,128)S(1)} custom-call(s32[9]{0:T(128)S(1)} %pad_add_fusion.where_ref, bf16[512,1024]{1,0:T(8,128)(2,1)} %copy-done, bf16[512,1024]{1,0:T(8,128)(2,1)} %copy-done.2, bf16[512,1024]{1,0:T(8,128)(2,1)} %copy-done.1, bf16[512,1024]{1,0:T(8,128)(2,1)} %collective-permute-done.4.refs_3_, ...), custom_call_target="tpu_custom_call" | custom-call | flops 1048576 | bytes 1048576 | tf_op jit(solution)/shard_map/ring_product/pallas_call | solution.py:291
  143.9 5.6 %collective-permute-done.15.refs_5_ = bf16[512,1024]{1,0:T(8,128)(2,1)} collective-permute-done((bf16[512,1024]{1,0:T(8,128)(2,1)}, bf16[512,1024]{1,0:T(8,128)(2,1)}, u32[]{:S(2)}, u32[]{:S(2)}) %collective-permute-start.15) | collective-permute-done | bytes 1048608 | tf_op jit(solution)/shard_map/ppermute | solution.py:332
  149.5 1.8 %collective-permute-done.18.refs_6_ = bf16[512,1024]{1,0:T(8,128)(2,1)} collective-permute-done((bf16[512,1024]{1,0:T(8,128)(2,1)}, bf16[512,1024]{1,0:T(8,128)(2,1)}, u32[]{:S(2)}, u32[]{:S(2)}) %collective-permute-start.18) | collective-permute-done | bytes 1048608 | tf_op jit(solution)/shard_map/ppermute | solution.py:329
  151.3 6.4 %ring_product.4.refs_6_ = f32[512,2048]{1,0:T(8,128)S(1)} custom-call(s32[9]{0:T(128)S(1)} %pad_add_fusion.where_ref, bf16[512,1024]{1,0:T(8,128)(2,1)} %copy-done, bf16[512,1024]{1,0:T(8,128)(2,1)} %copy-done.2, bf16[512,1024]{1,0:T(8,128)(2,1)} %copy-done.1, bf16[512,1024]{1,0:T(8,128)(2,1)} %collective-permute-done.4.refs_3_, ...), custom_call_target="tpu_custom_call" | custom-call | flops 1048576 | bytes 1048576 | tf_op jit(solution)/shard_map/ring_product/pallas_call | solution.py:291
  157.8 11.8 %collective-permute-done.12.refs_5_ = bf16[512,1024]{1,0:T(8,128)(2,1)} collective-permute-done((bf16[512,1024]{1,0:T(8,128)(2,1)}, bf16[512,1024]{1,0:T(8,128)(2,1)}, u32[]{:S(2)}, u32[]{:S(2)}) %collective-permute-start.12) | collective-permute-done | bytes 1048608 | tf_op jit(solution)/shard_map/ppermute | solution.py:332
  169.6 2.5 %collective-permute-done.8.refs_4_ = bf16[512,1024]{1,0:T(8,128)(2,1)} collective-permute-done((bf16[512,1024]{1,0:T(8,128)(2,1)}, bf16[512,1024]{1,0:T(8,128)(2,1)}, u32[]{:S(2)}, u32[]{:S(2)}) %collective-permute-start.8) | collective-permute-done | bytes 1048608 | tf_op jit(solution)/shard_map/ppermute | solution.py:329
  172.1 5.5 %ring_product.5 = bf16[512,2048]{1,0:T(8,128)(2,1)} custom-call(s32[9]{0:T(128)S(1)} %pad_add_fusion.where_ref, bf16[512,1024]{1,0:T(8,128)(2,1)} %copy-done, bf16[512,1024]{1,0:T(8,128)(2,1)} %copy-done.2, bf16[512,1024]{1,0:T(8,128)(2,1)} %copy-done.1, bf16[512,1024]{1,0:T(8,128)(2,1)} %collective-permute-done.4.refs_3_, ...), custom_call_target="tpu_custom_call" | custom-call | flops 1048576 | bytes 1048576 | tf_op jit(solution)/shard_map/ring_product/pallas_call | solution.py:291
  (36 shorter events, 3.3 us)
Async XLA Ops:
  0.0 2.8 %copy-start.6 = (bf16[1024,512]{1,0:T(8,128)(2,1)S(1)}, bf16[1024,512]{1,0:T(8,128)(2,1)}, u32[]{:S(2)}) copy-start(bf16[1024,512]{1,0:T(8,128)(2,1)} %param.11) | copy-start | bytes 3145732
  2.8 31.2 %copy-start.4 = (bf16[512,1024]{1,0:T(8,128)(2,1)}, bf16[512,1024]{1,0:T(8,128)(2,1)S(1)}, u32[]{:S(2)}) copy-start(bf16[512,1024]{1,0:T(8,128)(2,1)S(1)} %get-tuple-element.16.refs_9_) | copy-start | bytes 3145732
  5.6 26.3 %collective-permute-start = (bf16[1024,512]{1,0:T(8,128)(2,1)}, bf16[1024,512]{1,0:T(8,128)(2,1)S(1)}, u32[]{:S(2)}, u32[]{:S(2)}) collective-permute-start(bf16[1024,512]{1,0:T(8,128)(2,1)} %pad_maximum_fusion.1), channel_id=1, source_target_pairs={{0,2},{1,3},{2,0},{3,1},{4,6},{5,7},{6,4},{7,5},{8,10},{9,11},{10,... | collective-permute-start | bytes 3145736 | tf_op jit(solution)/shard_map/ppermute | solution.py:174
  8.5 27.3 %collective-permute-start.9 = (bf16[512,1024]{1,0:T(8,128)(2,1)S(1)}, bf16[512,1024]{1,0:T(8,128)(2,1)}, u32[]{:S(2)}, u32[]{:S(2)}) collective-permute-start(bf16[512,1024]{1,0:T(8,128)(2,1)S(1)} %get-tuple-element.16.refs_9_), channel_id=1, source_target_pairs={{8,0},{16,8},{24,16},{28,24},{20,28},{12,20},{4,12},{0,4},{9,1},{1... | collective-permute-start | bytes 3145736 | tf_op jit(solution)/shard_map/ppermute | solution.py:332
  10.0 47.1 %collective-permute-start.13 = (bf16[512,1024]{1,0:T(8,128)(2,1)}, bf16[512,1024]{1,0:T(8,128)(2,1)}, u32[]{:S(2)}, u32[]{:S(2)}) collective-permute-start(bf16[512,1024]{1,0:T(8,128)(2,1)} %get-tuple-element.15.refs_4_), channel_id=1, source_target_pairs={{8,0},{16,8},{24,16},{28,24},{20,28},{12,20},{4,12},{0,4},{9,1},{1... | collective-permute-start | bytes 3145736 | tf_op jit(solution)/shard_map/ppermute | solution.py:332
  11.6 47.1 %collective-permute-start.5 = (bf16[512,1024]{1,0:T(8,128)(2,1)}, bf16[512,1024]{1,0:T(8,128)(2,1)}, u32[]{:S(2)}, u32[]{:S(2)}) collective-permute-start(bf16[512,1024]{1,0:T(8,128)(2,1)} %get-tuple-element.15.refs_4_), channel_id=1, source_target_pairs={{0,8},{8,16},{16,24},{24,28},{28,20},{20,12},{12,4},{4,0},{1,9},{9... | collective-permute-start | bytes 3145736 | tf_op jit(solution)/shard_map/ppermute | solution.py:329
  12.1 48.4 %copy-start.7 = (s32[1,1,16]{2,1,0:T(1,128)S(1)}, s32[1,1,16]{2,1,0:T(1,128)}, u32[]{:S(2)}) copy-start(s32[1,1,16]{2,1,0:T(1,128)} %param.12) | copy-start | bytes 196
  31.9 1.0 copy-start.5
  34.0 27.7 %collective-permute-start.1 = (bf16[2048,256]{1,0:T(8,128)(2,1)}, bf16[2048,256]{1,0:T(8,128)(2,1)S(1)}, u32[]{:S(2)}, u32[]{:S(2)}) collective-permute-start(bf16[2048,256]{1,0:T(8,128)(2,1)} %maximum_maximum_fusion), channel_id=1, source_target_pairs={{0,1},{1,0},{2,3},{3,2},{4,5},{5,4},{6,7},{7,6},{8,9},{9,8},{10,11... | collective-permute-start | bytes 3145736 | tf_op jit(solution)/shard_map/ppermute | solution.py:176
  34.0 47.6 %collective-permute-start.16 = (bf16[512,1024]{1,0:T(8,128)(2,1)S(1)}, bf16[512,1024]{1,0:T(8,128)(2,1)}, u32[]{:S(2)}, u32[]{:S(2)}) collective-permute-start(bf16[512,1024]{1,0:T(8,128)(2,1)S(1)} %get-tuple-element.16.refs_9_), channel_id=1, source_target_pairs={{0,8},{8,16},{16,24},{24,28},{28,20},{20,12},{12,4},{4,0},{1,9},{9... | collective-permute-start | bytes 3145736 | tf_op jit(solution)/shard_map/ppermute | solution.py:329
  35.8 47.8 %collective-permute-start.10 = (bf16[512,1024]{1,0:T(8,128)(2,1)}, bf16[512,1024]{1,0:T(8,128)(2,1)}, u32[]{:S(2)}, u32[]{:S(2)}) collective-permute-start(bf16[512,1024]{1,0:T(8,128)(2,1)} %collective-permute-done.9.refs_11_), channel_id=1, source_target_pairs={{8,0},{16,8},{24,16},{28,24},{20,28},{12,20},{4,12},{0,4},{9,1},{1... | collective-permute-start | bytes 3145736 | tf_op jit(solution)/shard_map/ppermute | solution.py:332
  57.2 43.5 %collective-permute-start.14 = (bf16[512,1024]{1,0:T(8,128)(2,1)}, bf16[512,1024]{1,0:T(8,128)(2,1)}, u32[]{:S(2)}, u32[]{:S(2)}) collective-permute-start(bf16[512,1024]{1,0:T(8,128)(2,1)} %collective-permute-done.13.refs_6_), channel_id=1, source_target_pairs={{8,0},{16,8},{24,16},{28,24},{20,28},{12,20},{4,12},{0,4},{9,1},{1... | collective-permute-start | bytes 3145736 | tf_op jit(solution)/shard_map/ppermute | solution.py:332
  58.7 43.5 %collective-permute-start.6 = (bf16[512,1024]{1,0:T(8,128)(2,1)}, bf16[512,1024]{1,0:T(8,128)(2,1)}, u32[]{:S(2)}, u32[]{:S(2)}) collective-permute-start(bf16[512,1024]{1,0:T(8,128)(2,1)} %collective-permute-done.5.refs_5_), channel_id=1, source_target_pairs={{0,8},{8,16},{16,24},{24,28},{28,20},{20,12},{12,4},{4,0},{1,9},{9... | collective-permute-start | bytes 3145736 | tf_op jit(solution)/shard_map/ppermute | solution.py:329
  61.6 1.0 copy-start.3
  81.4 50.8 %copy-start = (bf16[512,1024]{1,0:T(8,128)(2,1)}, bf16[512,1024]{1,0:T(8,128)(2,1)S(1)}, u32[]{:S(2)}) copy-start(bf16[512,1024]{1,0:T(8,128)(2,1)S(1)} %attend.1.refs_0_) | copy-start | bytes 3145732
  81.4 21.8 %collective-permute-start.3 = (bf16[512,1024]{1,0:T(8,128)(2,1)S(1)}, bf16[512,1024]{1,0:T(8,128)(2,1)S(1)}, u32[]{:S(2)}, u32[]{:S(2)}) collective-permute-start(bf16[512,1024]{1,0:T(8,128)(2,1)S(1)} %attend.1.refs_0_), channel_id=1, source_target_pairs={{0,2},{1,3},{2,0},{3,1},{4,6},{5,7},{6,4},{7,5},{8,10},{9,11},{10,... | collective-permute-start | bytes 3145736 | tf_op jit(solution)/shard_map/ppermute | solution.py:335
  81.6 24.8 %collective-permute-start.17 = (bf16[512,1024]{1,0:T(8,128)(2,1)}, bf16[512,1024]{1,0:T(8,128)(2,1)}, u32[]{:S(2)}, u32[]{:S(2)}) collective-permute-start(bf16[512,1024]{1,0:T(8,128)(2,1)} %collective-permute-done.16.refs_10_), channel_id=1, source_target_pairs={{0,8},{8,16},{16,24},{24,28},{28,20},{20,12},{12,4},{4,0},{1,9},{9... | collective-permute-start | bytes 3145736 | tf_op jit(solution)/shard_map/ppermute | solution.py:329
  83.6 24.1 %collective-permute-start.2 = (bf16[512,1024]{1,0:T(8,128)(2,1)S(1)}, bf16[512,1024]{1,0:T(8,128)(2,1)S(1)}, u32[]{:S(2)}, u32[]{:S(2)}) collective-permute-start(bf16[512,1024]{1,0:T(8,128)(2,1)S(1)} %attend.1.refs_0_), channel_id=1, source_target_pairs={{0,1},{1,0},{2,3},{3,2},{4,5},{5,4},{6,7},{7,6},{8,9},{9,8},{10,11... | collective-permute-start | bytes 3145736 | tf_op jit(solution)/shard_map/ppermute | solution.py:336
  100.6 26.4 %collective-permute-start.11 = (bf16[512,1024]{1,0:T(8,128)(2,1)}, bf16[512,1024]{1,0:T(8,128)(2,1)}, u32[]{:S(2)}, u32[]{:S(2)}) collective-permute-start(bf16[512,1024]{1,0:T(8,128)(2,1)} %collective-permute-done.10.refs_13_), channel_id=1, source_target_pairs={{8,0},{16,8},{24,16},{28,24},{20,28},{12,20},{4,12},{0,4},{9,1},{1... | collective-permute-start | bytes 3145736 | tf_op jit(solution)/shard_map/ppermute | solution.py:332
  102.2 26.7 %collective-permute-start.7 = (bf16[512,1024]{1,0:T(8,128)(2,1)}, bf16[512,1024]{1,0:T(8,128)(2,1)}, u32[]{:S(2)}, u32[]{:S(2)}) collective-permute-start(bf16[512,1024]{1,0:T(8,128)(2,1)} %collective-permute-done.6.refs_7_), channel_id=1, source_target_pairs={{0,8},{8,16},{16,24},{24,28},{28,20},{20,12},{12,4},{4,0},{1,9},{9... | collective-permute-start | bytes 3145736 | tf_op jit(solution)/shard_map/ppermute | solution.py:329
  103.1 29.0 %copy-start.1 = (bf16[512,1024]{1,0:T(8,128)(2,1)}, bf16[512,1024]{1,0:T(8,128)(2,1)S(1)}, u32[]{:S(2)}) copy-start(bf16[512,1024]{1,0:T(8,128)(2,1)S(1)} %collective-permute-done.3.refs_2_) | copy-start | bytes 3145732
  103.1 29.0 %collective-permute-start.4 = (bf16[512,1024]{1,0:T(8,128)(2,1)S(1)}, bf16[512,1024]{1,0:T(8,128)(2,1)}, u32[]{:S(2)}, u32[]{:S(2)}) collective-permute-start(bf16[512,1024]{1,0:T(8,128)(2,1)S(1)} %collective-permute-done.3.refs_2_), channel_id=1, source_target_pairs={{0,1},{1,0},{2,3},{3,2},{4,5},{5,4},{6,7},{7,6},{8,9},{9,8},{10,11... | collective-permute-start | bytes 3145736 | tf_op jit(solution)/shard_map/ppermute | solution.py:337
  106.4 43.1 %collective-permute-start.15 = (bf16[512,1024]{1,0:T(8,128)(2,1)}, bf16[512,1024]{1,0:T(8,128)(2,1)}, u32[]{:S(2)}, u32[]{:S(2)}) collective-permute-start(bf16[512,1024]{1,0:T(8,128)(2,1)} %collective-permute-done.14.refs_8_), channel_id=1, source_target_pairs={{8,0},{16,8},{24,16},{28,24},{20,28},{12,20},{4,12},{0,4},{9,1},{1... | collective-permute-start | bytes 3145736 | tf_op jit(solution)/shard_map/ppermute | solution.py:332
  107.7 24.4 %copy-start.2 = (bf16[512,1024]{1,0:T(8,128)(2,1)}, bf16[512,1024]{1,0:T(8,128)(2,1)S(1)}, u32[]{:S(2)}) copy-start(bf16[512,1024]{1,0:T(8,128)(2,1)S(1)} %collective-permute-done.2.refs_1_) | copy-start | bytes 3145732
  107.7 43.6 %collective-permute-start.18 = (bf16[512,1024]{1,0:T(8,128)(2,1)}, bf16[512,1024]{1,0:T(8,128)(2,1)}, u32[]{:S(2)}, u32[]{:S(2)}) collective-permute-start(bf16[512,1024]{1,0:T(8,128)(2,1)} %collective-permute-done.17.refs_12_), channel_id=1, source_target_pairs={{0,8},{8,16},{16,24},{24,28},{28,20},{20,12},{12,4},{4,0},{1,9},{9... | collective-permute-start | bytes 3145736 | tf_op jit(solution)/shard_map/ppermute | solution.py:329
  127.1 42.6 %collective-permute-start.12 = (bf16[512,1024]{1,0:T(8,128)(2,1)}, bf16[512,1024]{1,0:T(8,128)(2,1)}, u32[]{:S(2)}, u32[]{:S(2)}) collective-permute-start(bf16[512,1024]{1,0:T(8,128)(2,1)} %collective-permute-done.11.refs_7_), channel_id=1, source_target_pairs={{8,0},{16,8},{24,16},{28,24},{20,28},{12,20},{4,12},{0,4},{9,1},{1... | collective-permute-start | bytes 3145736 | tf_op jit(solution)/shard_map/ppermute | solution.py:332
  128.9 43.2 %collective-permute-start.8 = (bf16[512,1024]{1,0:T(8,128)(2,1)}, bf16[512,1024]{1,0:T(8,128)(2,1)}, u32[]{:S(2)}, u32[]{:S(2)}) collective-permute-start(bf16[512,1024]{1,0:T(8,128)(2,1)} %collective-permute-done.7.refs_4_), channel_id=1, source_target_pairs={{0,8},{8,16},{16,24},{24,28},{28,20},{20,12},{12,4},{4,0},{1,9},{9... | collective-permute-start | bytes 3145736 | tf_op jit(solution)/shard_map/ppermute | solution.py:329

commit v8 on v5

--- a/solution.py
+++ b/solution.py
@@ -21,7 +21,9 @@
 GROUP = 4
 
 
-def attention_kernel(heads, slots, meta_ref, q_hbm, old_hbm, *refs):
+def attention_kernel(
+    heads, slots, part_rows, first_rows, targets, meta_ref, q_hbm, old_hbm, *refs
+):
     kv_parts, (out_ref, q_ref, kv_ref, peak_ref, denom_ref, acc_ref, sems) = refs[:-7], refs[-7:]
     live = meta_ref[0]
     flag = meta_ref[1]
@@ -35,11 +37,15 @@
     @pl.when(flag > 0)
     def _():
         copies = [pltpu.make_async_copy(q_hbm, q_ref, sems.at[0])]
-        for index, part in enumerate(kv_parts):
-            rows = part.shape[0]
-            start = pl.multiple_of(meta_ref[2 + slots + index] * rows, rows)
+        for index, (part, first_row, target) in enumerate(zip(kv_parts, first_rows, targets)):
+            column = pl.multiple_of(meta_ref[2 + slots + 2 * index] * HEAD_SIZE, HEAD_SIZE)
+            start = pl.multiple_of(meta_ref[3 + slots + 2 * index] * part_rows, part_rows)
             copies.append(
-                pltpu.make_async_copy(part, kv_ref.at[pl.ds(start, rows), :], sems.at[1 + index])
+                pltpu.make_async_copy(
+                    part.at[pl.ds(first_row, part_rows), pl.ds(column, HEAD_SIZE)],
+                    kv_ref.at[pl.ds(start, part_rows), pl.ds(target * HEAD_SIZE, HEAD_SIZE)],
+                    sems.at[1 + index],
+                )
             )
         for copy in copies:
             copy.start()
@@ -100,24 +106,27 @@
             out_ref[:, head * HEAD_SIZE : (head + 1) * HEAD_SIZE] = result.T.astype(jnp.bfloat16)
 
 
-def attend(block_list, live, flag, queries, old, kv_parts, places):
+def attend(block_list, live, flag, queries, old, key_values):
+    part_rows, sources = key_values
+    arrays, first_rows, heads_at, targets, places = zip(*sources)
     rows, width = queries.shape
     heads = width // HEAD_SIZE
     slots = block_list.shape[0]
-    meta = jnp.concatenate([live[None], flag[None], block_list, *[p[None] for p in places]])
+    spots = [value[None] for pair in zip(heads_at, places) for value in pair]
+    meta = jnp.concatenate([live[None], flag[None], block_list, *spots])
     in_hbm = pl.BlockSpec(memory_space=pltpu.HBM)
     return pl.pallas_call(
-        functools.partial(attention_kernel, heads, slots),
+        functools.partial(attention_kernel, heads, slots, part_rows, first_rows, targets),
         out_shape=jax.ShapeDtypeStruct((rows, width), jnp.bfloat16),
-        in_specs=[pl.BlockSpec(memory_space=pltpu.SMEM)] + [in_hbm] * (2 + len(kv_parts)),
+        in_specs=[pl.BlockSpec(memory_space=pltpu.SMEM)] + [in_hbm] * (2 + len(arrays)),
         out_specs=pl.BlockSpec(memory_space=pltpu.VMEM),
         scratch_shapes=[
             pltpu.VMEM((rows, width), jnp.bfloat16),
-            pltpu.VMEM((sum(p.shape[0] for p in kv_parts), 2 * HEAD_SIZE), jnp.bfloat16),
+            pltpu.VMEM((part_rows * len(arrays) // 2, 2 * HEAD_SIZE), jnp.bfloat16),
             pltpu.VMEM((heads, 1, rows), jnp.float32),
             pltpu.VMEM((heads, 1, rows), jnp.float32),
             pltpu.VMEM((heads, HEAD_SIZE, rows), jnp.float32),
-            pltpu.SemaphoreType.DMA((1 + len(kv_parts),)),
+            pltpu.SemaphoreType.DMA((1 + len(arrays),)),
         ],
         compiler_params=pltpu.CompilerParams(vmem_limit_bytes=24 << 20),
         cost_estimate=pl.CostEstimate(
@@ -128,31 +137,52 @@
         meta,
         *[
             pltpu.with_memory_space_constraint(x, pltpu.HBM)
-            for x in (queries, old, *kv_parts)
+            for x in (queries, old, *arrays)
         ],
     )
 
 
-def own_head_keys_values(keys, values):
+def own_head_keys_values(keys, values, gate=lambda x: x):
     groups = lax.axis_size("ka")
     me = lax.axis_index("ka")
     rows = keys.shape[0]
-    if groups == KEY_VALUE_HEADS:
-
-        def head_of(device):
-            start = (0, device * HEAD_SIZE)
-            return jnp.concatenate(
-                [lax.dynamic_slice(x, start, (rows, HEAD_SIZE)) for x in (keys, values)], axis=1
-            )
-
-        parts, places = [head_of(me)], [me]
-        for step in range(1, groups):
-            partner = jnp.bitwise_xor(me, step)
-            parts.append(
-                lax.ppermute(head_of(partner), "ka", [(i, i ^ step) for i in range(groups)])
-            )
-            places.append(partner)
-        return parts, places
+    if groups == KEY_VALUE_HEADS == 4:
+        x, core = me // 2, me % 2
+        pair = 2 * HEAD_SIZE
+
+        def heads_of(array, chip):
+            return lax.dynamic_slice(array, (0, chip * pair), (rows, pair))
+
+        def head_of(array, head):
+            return lax.dynamic_slice(array, (0, head * HEAD_SIZE), (rows, HEAD_SIZE))
+
+        across = [
+            lax.ppermute(heads_of(a, 1 - x), "ka", [(i, i ^ 2) for i in range(4)])
+            for a in (keys, values)
+        ]
+        across = gate(across)
+        beside = lax.ppermute(
+            jnp.concatenate(
+                [
+                    jnp.concatenate([head_of(a, 2 * x + 1 - core) for a in (keys, values)], axis=1),
+                    jnp.concatenate([head_of(a, 1 - core) for a in across], axis=1),
+                ],
+                axis=0,
+            ),
+            "ka",
+            [(i, i ^ 1) for i in range(4)],
+        )
+        near, far = jnp.bitwise_xor(me, 1), jnp.bitwise_xor(me, 3)
+        sources = [
+            (keys, 0, me, 0, me),
+            (values, 0, me, 1, me),
+            (across[0], 0, core, 0, jnp.bitwise_xor(me, 2)),
+            (across[1], 0, core, 1, jnp.bitwise_xor(me, 2)),
+        ]
+        for side in range(2):
+            for row, place in ((0, near), (rows, far)):
+                sources.append((beside, row, jnp.int32(side), side, place))
+        return rows, sources
     both = jnp.concatenate(
         [
             keys.reshape(rows, KEY_VALUE_HEADS, HEAD_SIZE),
@@ -164,7 +194,8 @@
     everything = lax.all_to_all(
         both.reshape(rows, groups * 2 * HEAD_SIZE), "ka", split_axis=1, concat_axis=0, tiled=True
     )
-    return [everything], [jnp.int32(0)]
+    first = jnp.int32(0)
+    return everything.shape[0], [(everything, 0, jnp.int32(side), side, first) for side in range(2)]
 
 
 def ring_of(pb_size):
@@ -296,18 +327,36 @@
     inputs, parts[0], parts[1] = lax.optimization_barrier((inputs, parts[0], parts[1]))
     slabs = [[(0, part)] for part in parts]
     moving = [[part, part] for part in parts]
-    for hop in range(1, far + 1):
+
+    def travel(hop):
         for part in range(2):
             if hop < far or part == 0:
                 moving[part][0] = lax.ppermute(moving[part][0], "pb", forward)
+            if hop < far or part == 1:
+                moving[part][1] = lax.ppermute(moving[part][1], "pb", backward)
+
+    def keep(hop):
+        for part in range(2):
+            if hop < far or part == 0:
                 slabs[part].append((-hop, moving[part][0]))
             if hop < far or part == 1:
-                moving[part][1] = lax.ppermute(moving[part][1], "pb", backward)
                 slabs[part].append((hop, moving[part][1]))
-    attn = attend_with(inputs)
+
+    def gate(value):
+        value, moving[0][0], moving[0][1] = lax.optimization_barrier(
+            (value, moving[0][0], moving[0][1])
+        )
+        return value
+
+    travel(1)
+    attn = attend_with(inputs, gate)
+    keep(1)
+    for hop in range(2, far + 1):
+        travel(hop)
+        keep(hop)
     across = lax.ppermute(attn, "ka", [(i, i ^ 2) for i in range(4)])
     beside = lax.ppermute(attn, "ka", [(i, i ^ 1) for i in range(4)])
-    corner = lax.ppermute(across, "ka", [(i, i ^ 1) for i in range(4)])
+    corner = lax.ppermute(attn, "ka", [(i, i ^ 3) for i in range(4)])
     around = jnp.asarray(
         [[ring[(ring.index(p) + step) % pb_size] for step in range(pb_size)] for p in range(pb_size)],
         jnp.int32,
@@ -327,10 +376,11 @@
 def shards(queries, keys, values, block_ids, counts, refresh, cached_attn, wo):
     groups = lax.axis_size("ka")
 
-    def attend_with(inputs):
+    def attend_with(inputs, gate=lambda x: x):
         queries, keys, values, old = inputs
-        parts, places = own_head_keys_values(keys, values)
-        return attend(block_ids[0, 0], counts[0, 0], refresh[0, 0], queries, old, parts, places)
+        return attend(
+            block_ids[0, 0], counts[0, 0], refresh[0, 0], queries, old, own_head_keys_values(keys, values, gate)
+        )
 
     inputs = (queries[0], keys, values, cached_attn[0])
     if lax.axis_size("pb") == 8 and groups == 4:

time: 176 us -> 172 us (0.977)
  starting transfers between devices: 51.2 us -> 19.7 us
  waiting for transfers between devices: 92.2 us -> 116 us
  local copies, waits for them, and re-layouts: 4.71 us -> 8.36 us
    ppermute x18, starting transfers between devices: 50.6 us -> 18.2 us  [the longest x7 10.1 us: travel(): moving[part][0] = lax.ppermute(moving[part][0], 'pb', forward)]
    ppermute x18, waiting for transfers between devices: 91.7 us -> 116 us  [the longest x7 66.3 us: travel(): moving[part][1] = lax.ppermute(moving[part][1], 'pb', backward)]
    dynamic_slice x1 -> x4, local copies, waits for them, and re-layouts: 1.07 us -> 4.77 us  [the longest x2 2.7 us: heads_of(): return lax.dynamic_slice(array, (0, chip * pair), (rows, pair))]
  transfers between devices with their start and end apart: 20 -> 20, of which waited for: 14 -> 10; matrix products, arithmetic and copies ran while one was open for 2% -> 3% of each run, Pallas kernels for 11% -> 12%
where the time goes in v8:
time: 172 us; the launch traced here: 171 us
  waiting for transfers between devices  116 us (67%)
  Pallas kernels  25.5 us (15%)
  starting transfers between devices  19.7 us (11%)
  local copies, waits for them, and re-layouts  8.36 us (5%)
    ppermute x7, waiting for transfers between devices, travel(): moving[part][1] = lax.ppermute(moving[part][1], 'pb', backward)  66.3 us
    ppermute x7, waiting for transfers between devices, travel(): moving[part][0] = lax.ppermute(moving[part][0], 'pb', forward)  29.5 us
    pallas_call x3, Pallas kernels, ring_product(): pl.pallas_call(functools.partial(ring_product_kernel, steps, base is not...  23.7 us
    ppermute x2, waiting for transfers between devices, own_head_keys_values(): lax.ppermute(heads_of(a, 1 - x), 'ka', [(i, i ^ 2) for i in range(4)])  20.4 us
    ppermute x7, starting transfers between devices, travel(): moving[part][0] = lax.ppermute(moving[part][0], 'pb', forward)  10.1 us
    ppermute x7, starting transfers between devices, travel(): moving[part][1] = lax.ppermute(moving[part][1], 'pb', backward)  5.91 us
  transfers between devices with their start and end apart: 20, of which 10 were waited for; matrix products, arithmetic and copies ran while one was open for 3% of the time, Pallas kernels for 12%

profile of v8, /device:TPU:0, one launch (start us, length us, event | category | flops | bytes accessed | tf_op | source)
XLA Modules:
  0.0 171.5 jit_solution(1991717989090953343)
XLA Ops:
  0.0 1.8 %fusion.1 = (bf16[512,1024]{1,0:T(8,128)(2,1)S(1)}, bf16[512,1024]{1,0:T(8,128)(2,1)S(1)}) fusion(bf16[512,2048]{1,0:T(8,128)(2,1)} %param.16), kind=kLoop, calls=%fused_computation.10 | loop fusion | bytes 4194304 | tf_op jit(solution)/shard_map/slice | solution.py:326
  1.8 3.1 %collective-permute-start.2 = (bf16[512,1024]{1,0:T(8,128)(2,1)S(1)}, bf16[512,1024]{1,0:T(8,128)(2,1)}, u32[]{:S(2)}, u32[]{:S(2)}) collective-permute-start(bf16[512,1024]{1,0:T(8,128)(2,1)S(1)} %get-tuple-element.19.refs_4_), channel_id=1, source_target_pairs={{0,8},{8,16},{16,24},{24,28},{28,20},{20,12},{12,4},{4,0},{1,9},{9... | collective-permute-start | bytes 3145736 | tf_op jit(solution)/shard_map/ppermute | solution.py:334
  4.9 2.0 %collective-permute-start.11 = (bf16[512,1024]{1,0:T(8,128)(2,1)S(1)}, bf16[512,1024]{1,0:T(8,128)(2,1)}, u32[]{:S(2)}, u32[]{:S(2)}) collective-permute-start(bf16[512,1024]{1,0:T(8,128)(2,1)S(1)} %get-tuple-element.23.refs_9_), channel_id=1, source_target_pairs={{8,0},{16,8},{24,16},{28,24},{20,28},{12,20},{4,12},{0,4},{9,1},{1... | collective-permute-start | bytes 3145736 | tf_op jit(solution)/shard_map/ppermute | solution.py:336
  6.9 1.9 %constant_dynamic-slice_fusion.4 = bf16[1024,256]{1,0:T(8,128)(2,1)} fusion(bf16[1024,512]{1,0:T(8,128)(2,1)} %refs_1_, s32[]{:T(128)S(6)} %select_n.29), kind=kLoop, calls=%fused_computation.5 | loop fusion | bytes 1048580 | tf_op jit(solution)/shard_map/dynamic_slice | solution.py:154
  8.7 1.5 collective-permute-start.1
  10.2 0.8 constant_dynamic-slice_fusion.5
  11.1 0.5 collective-permute-start
  11.6 1.0 constant_dynamic-slice_fusion.2
  12.6 11.3 %collective-permute-done.1.refs_3_ = bf16[1024,256]{1,0:T(8,128)(2,1)} collective-permute-done((bf16[1024,256]{1,0:T(8,128)(2,1)}, bf16[1024,256]{1,0:T(8,128)(2,1)}, u32[]{:S(2)}, u32[]{:S(2)}) %collective-permute-start.1) | collective-permute-done | bytes 524320 | tf_op jit(solution)/shard_map/ppermute | solution.py:160
  24.0 9.1 %collective-permute-done.refs_2_ = bf16[1024,256]{1,0:T(8,128)(2,1)} collective-permute-done((bf16[1024,256]{1,0:T(8,128)(2,1)}, bf16[1024,256]{1,0:T(8,128)(2,1)}, u32[]{:S(2)}, u32[]{:S(2)}) %collective-permute-start) | collective-permute-done | bytes 524320 | tf_op jit(solution)/shard_map/ppermute | solution.py:160
  33.1 1.1 constant_dynamic-slice_fusion
  34.4 1.6 collective-permute-start.15
  36.5 17.1 %collective-permute-done.11.refs_11_ = bf16[512,1024]{1,0:T(8,128)(2,1)} collective-permute-done((bf16[512,1024]{1,0:T(8,128)(2,1)S(1)}, bf16[512,1024]{1,0:T(8,128)(2,1)}, u32[]{:S(2)}, u32[]{:S(2)}) %collective-permute-start.11) | collective-permute-done | bytes 1048608 | tf_op jit(solution)/shard_map/ppermute | solution.py:336
  55.0 2.1 %collective-permute-start.18 = (bf16[512,1024]{1,0:T(8,128)(2,1)}, bf16[512,1024]{1,0:T(8,128)(2,1)}, u32[]{:S(2)}, u32[]{:S(2)}) collective-permute-start(bf16[512,1024]{1,0:T(8,128)(2,1)} %collective-permute-done.17.refs_10_), channel_id=1, source_target_pairs={{0,8},{8,16},{16,24},{24,28},{28,20},{20,12},{12,4},{4,0},{1,9},{9... | collective-permute-start | bytes 3145736 | tf_op jit(solution)/shard_map/ppermute | solution.py:334
  57.1 1.0 copy-done.1
  58.0 1.8 %attend.1.refs_0_ = bf16[512,1024]{1,0:T(8,128)(2,1)S(1)} custom-call(s32[34]{0:T(128)S(1)} %concatenate.16.meta_ref, bf16[512,1024]{1,0:T(8,128)(2,1)} %bitcast.15, bf16[512,1024]{1,0:T(8,128)(2,1)} %bitcast.16, bf16[1024,512]{1,0:T(8,128)(2,1)} %refs_0_, bf16[1024,512]{1,0:T(8,128)(2,1)} %refs_1_, bf16[1024,256]{1,0:T(8,128)(2,1)} %collective-permute-done.refs_2_, ...), custom_call_target="tpu_custom_call" | custom-call | flops 1048576 | bytes 1048576 | tf_op jit(solution)/shard_map/attend/pallas_call | solution.py:118
  60.0 16.1 %collective-permute-done.15.refs_8_ = bf16[512,1024]{1,0:T(8,128)(2,1)} collective-permute-done((bf16[512,1024]{1,0:T(8,128)(2,1)}, bf16[512,1024]{1,0:T(8,128)(2,1)}, u32[]{:S(2)}, u32[]{:S(2)}) %collective-permute-start.15) | collective-permute-done | bytes 1048608 | tf_op jit(solution)/shard_map/ppermute | solution.py:336
  76.0 1.5 collective-permute-start.6
  77.5 1.6 collective-permute-start.9
  79.1 17.9 %collective-permute-done.12.refs_13_ = bf16[512,1024]{1,0:T(8,128)(2,1)} collective-permute-done((bf16[512,1024]{1,0:T(8,128)(2,1)}, bf16[512,1024]{1,0:T(8,128)(2,1)}, u32[]{:S(2)}, u32[]{:S(2)}) %collective-permute-start.12) | collective-permute-done | bytes 1048608 | tf_op jit(solution)/shard_map/ppermute | solution.py:336
  97.4 1.7 %collective-permute-start.16 = (bf16[512,1024]{1,0:T(8,128)(2,1)}, bf16[512,1024]{1,0:T(8,128)(2,1)}, u32[]{:S(2)}, u32[]{:S(2)}) collective-permute-start(bf16[512,1024]{1,0:T(8,128)(2,1)} %collective-permute-done.15.refs_8_), channel_id=1, source_target_pairs={{8,0},{16,8},{24,16},{28,24},{20,28},{12,20},{4,12},{0,4},{9,1},{1... | collective-permute-start | bytes 3145736 | tf_op jit(solution)/shard_map/ppermute | solution.py:336
  99.1 0.8 collective-permute-start.19
  99.9 19.0 %collective-permute-done.9.refs_4_ = bf16[512,1024]{1,0:T(8,128)(2,1)} collective-permute-done((bf16[512,1024]{1,0:T(8,128)(2,1)}, bf16[512,1024]{1,0:T(8,128)(2,1)}, u32[]{:S(2)}, u32[]{:S(2)}) %collective-permute-start.9) | collective-permute-done | bytes 1048608 | tf_op jit(solution)/shard_map/ppermute | solution.py:334
  118.8 2.1 %collective-permute-start.10 = (bf16[512,1024]{1,0:T(8,128)(2,1)}, bf16[512,1024]{1,0:T(8,128)(2,1)}, u32[]{:S(2)}, u32[]{:S(2)}) collective-permute-start(bf16[512,1024]{1,0:T(8,128)(2,1)} %collective-permute-done.9.refs_4_), channel_id=1, source_target_pairs={{0,8},{8,16},{16,24},{24,28},{28,20},{20,12},{12,4},{4,0},{1,9},{9... | collective-permute-start | bytes 3145736 | tf_op jit(solution)/shard_map/ppermute | solution.py:334
  120.9 2.5 %collective-permute-done.13.refs_7_ = bf16[512,1024]{1,0:T(8,128)(2,1)} collective-permute-done((bf16[512,1024]{1,0:T(8,128)(2,1)}, bf16[512,1024]{1,0:T(8,128)(2,1)}, u32[]{:S(2)}, u32[]{:S(2)}) %collective-permute-start.13) | collective-permute-done | bytes 1048608 | tf_op jit(solution)/shard_map/ppermute | solution.py:336
  123.7 0.7 fusion
  124.5 11.7 %ring_product.3.refs_8_ = f32[512,2048]{1,0:T(8,128)S(1)} custom-call(s32[9]{0:T(128)S(1)} %pad_add_fusion.where_ref, bf16[512,1024]{1,0:T(8,128)(2,1)} %copy-done, bf16[512,1024]{1,0:T(8,128)(2,1)} %copy-done.2, bf16[512,1024]{1,0:T(8,128)(2,1)} %copy-done.3, bf16[512,1024]{1,0:T(8,128)(2,1)} %collective-permute-done.7.refs_3_, ...), custom_call_target="tpu_custom_call" | custom-call | flops 1048576 | bytes 1048576 | tf_op jit(solution)/shard_map/ring_product/pallas_call | solution.py:295
  136.3 9.6 %collective-permute-done.16.refs_5_ = bf16[512,1024]{1,0:T(8,128)(2,1)} collective-permute-done((bf16[512,1024]{1,0:T(8,128)(2,1)}, bf16[512,1024]{1,0:T(8,128)(2,1)}, u32[]{:S(2)}, u32[]{:S(2)}) %collective-permute-start.16) | collective-permute-done | bytes 1048608 | tf_op jit(solution)/shard_map/ppermute | solution.py:336
  145.9 6.4 %ring_product.4.refs_6_ = f32[512,2048]{1,0:T(8,128)S(1)} custom-call(s32[9]{0:T(128)S(1)} %pad_add_fusion.where_ref, bf16[512,1024]{1,0:T(8,128)(2,1)} %copy-done, bf16[512,1024]{1,0:T(8,128)(2,1)} %copy-done.2, bf16[512,1024]{1,0:T(8,128)(2,1)} %copy-done.3, bf16[512,1024]{1,0:T(8,128)(2,1)} %collective-permute-done.7.refs_3_, ...), custom_call_target="tpu_custom_call" | custom-call | flops 1048576 | bytes 1048576 | tf_op jit(solution)/shard_map/ring_product/pallas_call | solution.py:295
  152.4 10.6 %collective-permute-done.10.refs_4_ = bf16[512,1024]{1,0:T(8,128)(2,1)} collective-permute-done((bf16[512,1024]{1,0:T(8,128)(2,1)}, bf16[512,1024]{1,0:T(8,128)(2,1)}, u32[]{:S(2)}, u32[]{:S(2)}) %collective-permute-start.10) | collective-permute-done | bytes 1048608 | tf_op jit(solution)/shard_map/ppermute | solution.py:334
  162.9 3.1 %collective-permute-done.14.refs_5_ = bf16[512,1024]{1,0:T(8,128)(2,1)} collective-permute-done((bf16[512,1024]{1,0:T(8,128)(2,1)}, bf16[512,1024]{1,0:T(8,128)(2,1)}, u32[]{:S(2)}, u32[]{:S(2)}) %collective-permute-start.14) | collective-permute-done | bytes 1048608 | tf_op jit(solution)/shard_map/ppermute | solution.py:336
  166.0 5.5 %ring_product.5 = bf16[512,2048]{1,0:T(8,128)(2,1)} custom-call(s32[9]{0:T(128)S(1)} %pad_add_fusion.where_ref, bf16[512,1024]{1,0:T(8,128)(2,1)} %copy-done, bf16[512,1024]{1,0:T(8,128)(2,1)} %copy-done.2, bf16[512,1024]{1,0:T(8,128)(2,1)} %copy-done.3, bf16[512,1024]{1,0:T(8,128)(2,1)} %collective-permute-done.7.refs_3_, ...), custom_call_target="tpu_custom_call" | custom-call | flops 1048576 | bytes 1048576 | tf_op jit(solution)/shard_map/ring_product/pallas_call | solution.py:295
  (37 shorter events, 1.6 us)
Async XLA Ops:
  0.0 10.2 %copy-start.6 = (bf16[1024,512]{1,0:T(8,128)(2,1)S(1)}, bf16[1024,512]{1,0:T(8,128)(2,1)}, u32[]{:S(2)}) copy-start(bf16[1024,512]{1,0:T(8,128)(2,1)} %refs_0_) | copy-start | bytes 3145732
  1.8 32.4 %copy-start.4 = (bf16[512,1024]{1,0:T(8,128)(2,1)}, bf16[512,1024]{1,0:T(8,128)(2,1)S(1)}, u32[]{:S(2)}) copy-start(bf16[512,1024]{1,0:T(8,128)(2,1)S(1)} %get-tuple-element.23.refs_9_) | copy-start | bytes 3145732
  1.8 32.4 %copy-start.5 = (bf16[512,1024]{1,0:T(8,128)(2,1)}, bf16[512,1024]{1,0:T(8,128)(2,1)S(1)}, u32[]{:S(2)}) copy-start(bf16[512,1024]{1,0:T(8,128)(2,1)S(1)} %get-tuple-element.19.refs_4_) | copy-start | bytes 3145732
  1.8 31.3 %collective-permute-start.2 = (bf16[512,1024]{1,0:T(8,128)(2,1)S(1)}, bf16[512,1024]{1,0:T(8,128)(2,1)}, u32[]{:S(2)}, u32[]{:S(2)}) collective-permute-start(bf16[512,1024]{1,0:T(8,128)(2,1)S(1)} %get-tuple-element.19.refs_4_), channel_id=1, source_target_pairs={{0,8},{8,16},{16,24},{24,28},{28,20},{20,12},{12,4},{4,0},{1,9},{9... | collective-permute-start | bytes 3145736 | tf_op jit(solution)/shard_map/ppermute | solution.py:334
  4.9 28.2 %collective-permute-start.3 = (bf16[512,1024]{1,0:T(8,128)(2,1)S(1)}, bf16[512,1024]{1,0:T(8,128)(2,1)}, u32[]{:S(2)}, u32[]{:S(2)}) collective-permute-start(bf16[512,1024]{1,0:T(8,128)(2,1)S(1)} %get-tuple-element.19.refs_4_), channel_id=1, source_target_pairs={{8,0},{16,8},{24,16},{28,24},{20,28},{12,20},{4,12},{0,4},{9,1},{1... | collective-permute-start | bytes 3145736 | tf_op jit(solution)/shard_map/ppermute | solution.py:336
  4.9 48.6 %collective-permute-start.11 = (bf16[512,1024]{1,0:T(8,128)(2,1)S(1)}, bf16[512,1024]{1,0:T(8,128)(2,1)}, u32[]{:S(2)}, u32[]{:S(2)}) collective-permute-start(bf16[512,1024]{1,0:T(8,128)(2,1)S(1)} %get-tuple-element.23.refs_9_), channel_id=1, source_target_pairs={{8,0},{16,8},{24,16},{28,24},{20,28},{12,20},{4,12},{0,4},{9,1},{1... | collective-permute-start | bytes 3145736 | tf_op jit(solution)/shard_map/ppermute | solution.py:336
  8.7 15.2 %collective-permute-start.1 = (bf16[1024,256]{1,0:T(8,128)(2,1)}, bf16[1024,256]{1,0:T(8,128)(2,1)}, u32[]{:S(2)}, u32[]{:S(2)}) collective-permute-start(bf16[1024,256]{1,0:T(8,128)(2,1)} %constant_dynamic-slice_fusion.4), channel_id=1, source_target_pairs={{0,2},{1,3},{2,0},{3,1},{4,6},{5,7},{6,4},{7,5},{8,10},{9,11},{10,... | collective-permute-start | bytes 1572872 | tf_op jit(solution)/shard_map/ppermute | solution.py:160
  11.1 22.1 %collective-permute-start = (bf16[1024,256]{1,0:T(8,128)(2,1)}, bf16[1024,256]{1,0:T(8,128)(2,1)}, u32[]{:S(2)}, u32[]{:S(2)}) collective-permute-start(bf16[1024,256]{1,0:T(8,128)(2,1)} %constant_dynamic-slice_fusion.5), channel_id=1, source_target_pairs={{0,2},{1,3},{2,0},{3,1},{4,6},{5,7},{6,4},{7,5},{8,10},{9,11},{10,... | collective-permute-start | bytes 1572872 | tf_op jit(solution)/shard_map/ppermute | solution.py:160
  11.6 43.3 %copy-start.7 = (s32[1,1,16]{2,1,0:T(1,128)S(1)}, s32[1,1,16]{2,1,0:T(1,128)}, u32[]{:S(2)}) copy-start(s32[1,1,16]{2,1,0:T(1,128)} %param.12) | copy-start | bytes 196
  23.9 31.1 %collective-permute-start.17 = (bf16[512,1024]{1,0:T(8,128)(2,1)S(1)}, bf16[512,1024]{1,0:T(8,128)(2,1)}, u32[]{:S(2)}, u32[]{:S(2)}) collective-permute-start(bf16[512,1024]{1,0:T(8,128)(2,1)S(1)} %get-tuple-element.23.refs_9_), channel_id=1, source_target_pairs={{0,8},{8,16},{16,24},{24,28},{28,20},{20,12},{12,4},{4,0},{1,9},{9... | collective-permute-start | bytes 3145736 | tf_op jit(solution)/shard_map/ppermute | solution.py:334
  34.3 22.7 %collective-permute-start.4 = (bf16[2048,256]{1,0:T(8,128)(2,1)S(1)}, bf16[2048,256]{1,0:T(8,128)(2,1)S(1)}, u32[]{:S(2)}, u32[]{:S(2)}) collective-permute-start(bf16[2048,256]{1,0:T(8,128)(2,1)S(1)} %maximum_maximum_fusion), channel_id=1, source_target_pairs={{0,1},{1,0},{2,3},{3,2},{4,5},{5,4},{6,7},{7,6},{8,9},{9,8},{10,11... | collective-permute-start | bytes 3145736 | tf_op jit(solution)/shard_map/ppermute | solution.py:164
  34.4 41.6 %collective-permute-start.15 = (bf16[512,1024]{1,0:T(8,128)(2,1)}, bf16[512,1024]{1,0:T(8,128)(2,1)}, u32[]{:S(2)}, u32[]{:S(2)}) collective-permute-start(bf16[512,1024]{1,0:T(8,128)(2,1)} %collective-permute-done.3.refs_6_), channel_id=1, source_target_pairs={{8,0},{16,8},{24,16},{28,24},{20,28},{12,20},{4,12},{0,4},{9,1},{1... | collective-permute-start | bytes 3145736 | tf_op jit(solution)/shard_map/ppermute | solution.py:336
  36.0 41.5 %collective-permute-start.8 = (bf16[512,1024]{1,0:T(8,128)(2,1)}, bf16[512,1024]{1,0:T(8,128)(2,1)}, u32[]{:S(2)}, u32[]{:S(2)}) collective-permute-start(bf16[512,1024]{1,0:T(8,128)(2,1)} %collective-permute-done.2.refs_5_), channel_id=1, source_target_pairs={{0,8},{8,16},{16,24},{24,28},{28,20},{20,12},{12,4},{4,0},{1,9},{9... | collective-permute-start | bytes 3145736 | tf_op jit(solution)/shard_map/ppermute | solution.py:334
  53.6 43.5 %collective-permute-start.12 = (bf16[512,1024]{1,0:T(8,128)(2,1)}, bf16[512,1024]{1,0:T(8,128)(2,1)}, u32[]{:S(2)}, u32[]{:S(2)}) collective-permute-start(bf16[512,1024]{1,0:T(8,128)(2,1)} %collective-permute-done.11.refs_11_), channel_id=1, source_target_pairs={{8,0},{16,8},{24,16},{28,24},{20,28},{12,20},{4,12},{0,4},{9,1},{1... | collective-permute-start | bytes 3145736 | tf_op jit(solution)/shard_map/ppermute | solution.py:336
  55.0 42.3 %collective-permute-start.18 = (bf16[512,1024]{1,0:T(8,128)(2,1)}, bf16[512,1024]{1,0:T(8,128)(2,1)}, u32[]{:S(2)}, u32[]{:S(2)}) collective-permute-start(bf16[512,1024]{1,0:T(8,128)(2,1)} %collective-permute-done.17.refs_10_), channel_id=1, source_target_pairs={{0,8},{8,16},{16,24},{24,28},{28,20},{20,12},{12,4},{4,0},{1,9},{9... | collective-permute-start | bytes 3145736 | tf_op jit(solution)/shard_map/ppermute | solution.py:334
  57.1 1.0 copy-start.1
  59.9 64.6 %copy-start = (bf16[512,1024]{1,0:T(8,128)(2,1)}, bf16[512,1024]{1,0:T(8,128)(2,1)S(1)}, u32[]{:S(2)}) copy-start(bf16[512,1024]{1,0:T(8,128)(2,1)S(1)} %attend.1.refs_0_) | copy-start | bytes 3145732
  59.9 37.4 %collective-permute-start.5 = (bf16[512,1024]{1,0:T(8,128)(2,1)S(1)}, bf16[512,1024]{1,0:T(8,128)(2,1)S(1)}, u32[]{:S(2)}, u32[]{:S(2)}) collective-permute-start(bf16[512,1024]{1,0:T(8,128)(2,1)S(1)} %attend.1.refs_0_), channel_id=1, source_target_pairs={{0,1},{1,0},{2,3},{3,2},{4,5},{5,4},{6,7},{7,6},{8,9},{9,8},{10,11... | collective-permute-start | bytes 3145736 | tf_op jit(solution)/shard_map/ppermute | solution.py:358
  76.0 23.1 %collective-permute-start.6 = (bf16[512,1024]{1,0:T(8,128)(2,1)S(1)}, bf16[512,1024]{1,0:T(8,128)(2,1)S(1)}, u32[]{:S(2)}, u32[]{:S(2)}) collective-permute-start(bf16[512,1024]{1,0:T(8,128)(2,1)S(1)} %attend.1.refs_0_), channel_id=1, source_target_pairs={{0,2},{1,3},{2,0},{3,1},{4,6},{5,7},{6,4},{7,5},{8,10},{9,11},{10,... | collective-permute-start | bytes 3145736 | tf_op jit(solution)/shard_map/ppermute | solution.py:357
  77.5 41.3 %collective-permute-start.9 = (bf16[512,1024]{1,0:T(8,128)(2,1)}, bf16[512,1024]{1,0:T(8,128)(2,1)}, u32[]{:S(2)}, u32[]{:S(2)}) collective-permute-start(bf16[512,1024]{1,0:T(8,128)(2,1)} %collective-permute-done.8.refs_7_), channel_id=1, source_target_pairs={{0,8},{8,16},{16,24},{24,28},{28,20},{20,12},{12,4},{4,0},{1,9},{9... | collective-permute-start | bytes 3145736 | tf_op jit(solution)/shard_map/ppermute | solution.py:334
  97.0 26.4 %collective-permute-start.13 = (bf16[512,1024]{1,0:T(8,128)(2,1)}, bf16[512,1024]{1,0:T(8,128)(2,1)}, u32[]{:S(2)}, u32[]{:S(2)}) collective-permute-start(bf16[512,1024]{1,0:T(8,128)(2,1)} %collective-permute-done.12.refs_13_), channel_id=1, source_target_pairs={{8,0},{16,8},{24,16},{28,24},{20,28},{12,20},{4,12},{0,4},{9,1},{1... | collective-permute-start | bytes 3145736 | tf_op jit(solution)/shard_map/ppermute | solution.py:336
  97.3 27.2 %collective-permute-start.7 = (bf16[512,1024]{1,0:T(8,128)(2,1)S(1)}, bf16[512,1024]{1,0:T(8,128)(2,1)}, u32[]{:S(2)}, u32[]{:S(2)}) collective-permute-start(bf16[512,1024]{1,0:T(8,128)(2,1)S(1)} %attend.1.refs_0_), channel_id=1, source_target_pairs={{0,3},{1,2},{2,1},{3,0},{4,7},{5,6},{6,5},{7,4},{8,11},{9,10},{10,... | collective-permute-start | bytes 3145736 | tf_op jit(solution)/shard_map/ppermute | solution.py:359
  97.3 27.2 %copy-start.2 = (bf16[512,1024]{1,0:T(8,128)(2,1)}, bf16[512,1024]{1,0:T(8,128)(2,1)S(1)}, u32[]{:S(2)}) copy-start(bf16[512,1024]{1,0:T(8,128)(2,1)S(1)} %collective-permute-done.5.refs_1_) | copy-start | bytes 3145732
  97.4 48.6 %collective-permute-start.16 = (bf16[512,1024]{1,0:T(8,128)(2,1)}, bf16[512,1024]{1,0:T(8,128)(2,1)}, u32[]{:S(2)}, u32[]{:S(2)}) collective-permute-start(bf16[512,1024]{1,0:T(8,128)(2,1)} %collective-permute-done.15.refs_8_), channel_id=1, source_target_pairs={{8,0},{16,8},{24,16},{28,24},{20,28},{12,20},{4,12},{0,4},{9,1},{1... | collective-permute-start | bytes 3145736 | tf_op jit(solution)/shard_map/ppermute | solution.py:336
  99.1 25.4 %copy-start.3 = (bf16[512,1024]{1,0:T(8,128)(2,1)}, bf16[512,1024]{1,0:T(8,128)(2,1)S(1)}, u32[]{:S(2)}) copy-start(bf16[512,1024]{1,0:T(8,128)(2,1)S(1)} %collective-permute-done.6.refs_2_) | copy-start | bytes 3145732
  99.1 46.8 %collective-permute-start.19 = (bf16[512,1024]{1,0:T(8,128)(2,1)}, bf16[512,1024]{1,0:T(8,128)(2,1)}, u32[]{:S(2)}, u32[]{:S(2)}) collective-permute-start(bf16[512,1024]{1,0:T(8,128)(2,1)} %collective-permute-done.18.refs_12_), channel_id=1, source_target_pairs={{0,8},{8,16},{16,24},{24,28},{28,20},{20,12},{12,4},{4,0},{1,9},{9... | collective-permute-start | bytes 3145736 | tf_op jit(solution)/shard_map/ppermute | solution.py:334
  118.8 44.1 %collective-permute-start.10 = (bf16[512,1024]{1,0:T(8,128)(2,1)}, bf16[512,1024]{1,0:T(8,128)(2,1)}, u32[]{:S(2)}, u32[]{:S(2)}) collective-permute-start(bf16[512,1024]{1,0:T(8,128)(2,1)} %collective-permute-done.9.refs_4_), channel_id=1, source_target_pairs={{0,8},{8,16},{16,24},{24,28},{28,20},{20,12},{12,4},{4,0},{1,9},{9... | collective-permute-start | bytes 3145736 | tf_op jit(solution)/shard_map/ppermute | solution.py:334
  123.5 42.6 %collective-permute-start.14 = (bf16[512,1024]{1,0:T(8,128)(2,1)}, bf16[512,1024]{1,0:T(8,128)(2,1)}, u32[]{:S(2)}, u32[]{:S(2)}) collective-permute-start(bf16[512,1024]{1,0:T(8,128)(2,1)} %collective-permute-done.13.refs_7_), channel_id=1, source_target_pairs={{8,0},{16,8},{24,16},{28,24},{20,28},{12,20},{4,12},{0,4},{9,1},{1... | collective-permute-start | bytes 3145736 | tf_op jit(solution)/shard_map/ppermute | solution.py:336

commit v9 on v8

--- a/solution.py
+++ b/solution.py
@@ -205,23 +205,33 @@
 
 
 ROW_TILE = 128
-
-
-def ring_product_kernel(steps, has_base, last, where_ref, *refs):
+IN_HBM = pl.BlockSpec(memory_space=pltpu.HBM)
+IN_VMEM = pl.BlockSpec(memory_space=pltpu.VMEM)
+IN_SMEM = pl.BlockSpec(memory_space=pltpu.SMEM)
+SMALL_COST = pl.CostEstimate(flops=1 << 20, transcendentals=0, bytes_accessed=1 << 20)
+
+
+def pinned(values, space):
+    return [pltpu.with_memory_space_constraint(x, space) for x in values]
+
+
+def ring_product_kernel(steps, spare_step, where_ref, *refs):
     count = len(steps)
     blocks, slabs, refs = refs[:4], (refs[4 : 4 + count], refs[4 + count : 4 + 2 * count]), refs[4 + 2 * count :]
-    if has_base:
-        base_ref, refs = refs[0], refs[1:]
-    out_ref, left, right, block_sems, slab_sems = refs[:5]
+    if spare_step is not None:
+        base_ref, out_ref, spare_ref = refs[:3]
+        refs = refs[3:]
+    else:
+        out_ref, refs = refs[0], refs[1:]
+    left, right, block_sems, slab_sems = refs
     rows, depth = left.shape[0], right.shape[1] // count
     per = blocks[0].shape[1] // depth
     me = where_ref[where_ref.shape[0] - 1]
 
     def block_copy(index, slot, shift):
+        target = spare_ref if index == count else left.at[:, pl.ds(index * depth, depth)]
         return pltpu.make_async_copy(
-            blocks[slot].at[:, pl.ds(shift, depth)],
-            left.at[:, pl.ds(index * depth, depth)],
-            block_sems.at[index],
+            blocks[slot].at[:, pl.ds(shift, depth)], target, block_sems.at[index]
         )
 
     def slab_copy(half, index):
@@ -231,7 +241,8 @@
             slab_sems.at[half, index],
         )
 
-    for index, step in enumerate(steps):
+    all_steps = steps if spare_step is None else (*steps, spare_step)
+    for index, step in enumerate(all_steps):
         source = where_ref[step]
         slot_here = jnp.bitwise_xor(source // per, me)
         shift = pl.multiple_of((source % per) * depth, depth)
@@ -244,11 +255,9 @@
     for half in range(2):
         for index in range(count):
             slab_copy(half, index).start()
-    for index in range(count):
+    for index in range(len(all_steps)):
         block_copy(index, 0, 0).wait()
     half_columns = right.shape[2]
-    if last:
-        staged, out_sems = refs[5:]
     for half in range(2):
         columns = pl.ds(half * half_columns, half_columns)
         for index in range(count):
@@ -257,62 +266,77 @@
         def rows_tile(step, carry):
             at = pl.ds(pl.multiple_of(step * ROW_TILE, ROW_TILE), ROW_TILE)
             product = jnp.dot(left[at, :], right[half], preferred_element_type=jnp.float32)
-            if has_base:
+            if spare_step is not None:
                 product = product + base_ref[at, columns]
-            if last:
-                staged[at, columns] = product.astype(jnp.bfloat16)
-            else:
-                out_ref[at, columns] = product
+            out_ref[at, columns] = product
             return carry
 
         lax.fori_loop(0, rows // ROW_TILE, rows_tile, 0)
-        if last:
-            pltpu.make_async_copy(
-                staged.at[:, columns], out_ref.at[:, columns], out_sems.at[half]
-            ).start()
-    if last:
-        for half in range(2):
-            columns = pl.ds(half * half_columns, half_columns)
-            pltpu.make_async_copy(
-                staged.at[:, columns], out_ref.at[:, columns], out_sems.at[half]
-            ).wait()
-
-
-def ring_product(where, blocks, steps, slabs, base, last):
+
+
+def ring_product(where, blocks, steps, slabs, base=None, spare_step=None):
     count = len(steps)
     rows = blocks[0].shape[0]
     depth, half = slabs[0][0].shape
-    in_hbm = pl.BlockSpec(memory_space=pltpu.HBM)
-    in_vmem = pl.BlockSpec(memory_space=pltpu.VMEM)
-    scratch = [
-        pltpu.VMEM((rows, count * depth), jnp.bfloat16),
-        pltpu.VMEM((2, count * depth, half), jnp.bfloat16),
-        pltpu.SemaphoreType.DMA((count,)),
-        pltpu.SemaphoreType.DMA((2, count)),
-    ]
-    if last:
-        scratch += [pltpu.VMEM((rows, 2 * half), jnp.bfloat16), pltpu.SemaphoreType.DMA((2,))]
+    spare = spare_step is not None
+    out_shape = [jax.ShapeDtypeStruct((rows, 2 * half), jnp.float32)]
+    if spare:
+        out_shape.append(jax.ShapeDtypeStruct((rows, depth), jnp.bfloat16))
     return pl.pallas_call(
-        functools.partial(ring_product_kernel, steps, base is not None, last),
-        out_shape=jax.ShapeDtypeStruct((rows, 2 * half), jnp.bfloat16 if last else jnp.float32),
-        in_specs=[pl.BlockSpec(memory_space=pltpu.SMEM)]
-        + [in_hbm] * (4 + 2 * count)
-        + [in_vmem] * (base is not None),
-        out_specs=in_hbm if last else in_vmem,
-        scratch_shapes=scratch,
-        compiler_params=pltpu.CompilerParams(vmem_limit_bytes=(8 + 4 * count) << 20),
-        cost_estimate=pl.CostEstimate(
-            flops=1 << 20, transcendentals=0, bytes_accessed=1 << 20
-        ),
+        functools.partial(ring_product_kernel, steps, spare_step),
+        out_shape=out_shape,
+        in_specs=[IN_SMEM] + [IN_HBM] * (4 + 2 * count) + [IN_VMEM] * spare,
+        out_specs=[IN_VMEM] * len(out_shape),
+        scratch_shapes=[
+            pltpu.VMEM((rows, count * depth), jnp.bfloat16),
+            pltpu.VMEM((2, count * depth, half), jnp.bfloat16),
+            pltpu.SemaphoreType.DMA((count + spare,)),
+            pltpu.SemaphoreType.DMA((2, count)),
+        ],
+        compiler_params=pltpu.CompilerParams(vmem_limit_bytes=(6 + 4 * count) << 20),
+        cost_estimate=SMALL_COST,
         name="ring_product",
     )(
         where,
-        *[
-            pltpu.with_memory_space_constraint(x, pltpu.HBM)
-            for x in (*blocks, *slabs[0], *slabs[1])
+        *pinned([*blocks, *slabs[0], *slabs[1]], pltpu.HBM),
+        *(pinned([base], pltpu.VMEM) if spare else []),
+    )
+
+
+def last_product_kernel(block_ref, left_slab, right_slab, base_ref, out_ref, staged, sems):
+    half = left_slab.shape[1]
+
+    def tile_copy(tile):
+        at = pl.ds(tile * ROW_TILE, ROW_TILE)
+        return pltpu.make_async_copy(staged.at[at, :], out_ref.at[at, :], sems.at[tile])
+
+    tiles = block_ref.shape[0] // ROW_TILE
+    for tile in range(tiles):
+        at = pl.ds(tile * ROW_TILE, ROW_TILE)
+        for slab, start in ((left_slab, 0), (right_slab, half)):
+            columns = pl.ds(start, half)
+            product = jnp.dot(block_ref[at, :], slab[...], preferred_element_type=jnp.float32)
+            staged[at, columns] = (product + base_ref[at, columns]).astype(jnp.bfloat16)
+        tile_copy(tile).start()
+    for tile in range(tiles):
+        tile_copy(tile).wait()
+
+
+def last_product(block, left_slab, right_slab, base):
+    rows, columns = base.shape
+    return pl.pallas_call(
+        last_product_kernel,
+        out_shape=jax.ShapeDtypeStruct((rows, columns), jnp.bfloat16),
+        in_specs=[IN_VMEM] * 4,
+        out_specs=IN_HBM,
+        scratch_shapes=[
+            pltpu.VMEM((rows, columns), jnp.bfloat16),
+            pltpu.SemaphoreType.DMA((rows // ROW_TILE,)),
         ],
-        *([] if base is None else [base]),
-    )
+        compiler_params=pltpu.CompilerParams(vmem_limit_bytes=8 << 20),
+        cost_estimate=SMALL_COST,
+        name="last_product",
+    )(*pinned([block, left_slab, right_slab, base], pltpu.VMEM))
 
 
 def project_ring(wo, inputs, attend_with):
@@ -365,12 +389,17 @@
     where = jnp.concatenate([mine, lax.axis_index("ka")[None].astype(jnp.int32)])
     blocks = [attn, beside, across, corner]
     at_step = [{offset % pb_size: slab for offset, slab in slabs[part]} for part in range(2)]
-    total = None
-    for offsets in ((0, -1, 1, -2, 2), (-3, 3), (4,)):
-        chosen = [[at_step[part][offset % pb_size] for offset in offsets] for part in range(2)]
-        steps = tuple(offset % pb_size for offset in offsets)
-        total = ring_product(where, blocks, steps, chosen, total, offsets == (far,))
-    return total
+
+    def chosen(offsets):
+        return [[at_step[part][offset % pb_size] for offset in offsets] for part in range(2)]
+
+    def steps(offsets):
+        return tuple(offset % pb_size for offset in offsets)
+
+    early, late = (0, -1, 1, -2, 2), (-3, 3)
+    (base,) = ring_product(where, blocks, steps(early), chosen(early))
+    base, block = ring_product(where, blocks, steps(late), chosen(late), base, far)
+    return last_product(block, at_step[0][far], at_step[1][far], base)
 
 
 def shards(queries, keys, values, block_ids, counts, refresh, cached_attn, wo):

time: 172 us -> 168 us (0.977)
  waiting for transfers between devices: 116 us -> 98.2 us
  Pallas kernels: 25.5 us -> 39.2 us
    ppermute x7, waiting for transfers between devices: 66.3 us -> 49.3 us  [travel(): moving[part][1] = lax.ppermute(moving[part][1], 'pb', backward)]
    pallas_call x1, Pallas kernels: 1.85 us -> 18.7 us  [attend(): pl.pallas_call(functools.partial(attention_kernel, heads, slots, part_row...]
    ppermute x7, waiting for transfers between devices: 29.5 us -> 24.6 us  [travel(): moving[part][0] = lax.ppermute(moving[part][0], 'pb', forward)]
    ppermute x1, waiting for transfers between devices: 0.01 us -> 3.79 us  [project_ring(): across = lax.ppermute(attn, 'ka', [(i, i ^ 2) for i in range(4)])]
    pallas_call x3, Pallas kernels: 23.7 us -> 20.5 us  [the longest x2 18.4 us: ring_product(): pl.pallas_call(functools.partial(ring_product_kernel, steps, spare_step),...]
  transfers between devices with their start and end apart: 20 -> 20, of which waited for: 10 -> 10; matrix products, arithmetic and copies ran while one was open for 3% -> 3% of each run, Pallas kernels for 12% -> 22%
where the time goes in v9:
time: 168 us
  waiting for transfers between devices  98.2 us (58%)
  Pallas kernels  39.2 us (23%)
  starting transfers between devices  20.6 us (12%)
  local copies, waits for them, and re-layouts  8.37 us (5%)
    ppermute x7, waiting for transfers between devices, travel(): moving[part][1] = lax.ppermute(moving[part][1], 'pb', backward)  49.3 us
    ppermute x7, waiting for transfers between devices, travel(): moving[part][0] = lax.ppermute(moving[part][0], 'pb', forward)  24.6 us
    ppermute x2, waiting for transfers between devices, own_head_keys_values(): lax.ppermute(heads_of(a, 1 - x), 'ka', [(i, i ^ 2) for i in range(4)])  20.4 us
    pallas_call x1, Pallas kernels, attend(): pl.pallas_call(functools.partial(attention_kernel, heads, slots, part_row...  18.7 us
    pallas_call x2, Pallas kernels, ring_product(): pl.pallas_call(functools.partial(ring_product_kernel, steps, spare_step),...  18.4 us
    ppermute x7, starting transfers between devices, travel(): moving[part][0] = lax.ppermute(moving[part][0], 'pb', forward)  11 us
    ppermute x7, starting transfers between devices, travel(): moving[part][1] = lax.ppermute(moving[part][1], 'pb', backward)  5.91 us
    ppermute x1, waiting for transfers between devices, project_ring(): across = lax.ppermute(attn, 'ka', [(i, i ^ 2) for i in range(4)])  3.79 us
  transfers between devices with their start and end apart: 20, of which 10 were waited for; matrix products, arithmetic and copies ran while one was open for 3% of the time, Pallas kernels for 22%

profile of v9, /device:TPU:0, one launch (start us, length us, event | category | flops | bytes accessed | tf_op | source)
XLA Modules:
  0.0 168.0 jit_solution(17804123950352903342)
XLA Ops:
  0.0 1.8 %fusion.1 = (bf16[512,1024]{1,0:T(8,128)(2,1)S(1)}, bf16[512,1024]{1,0:T(8,128)(2,1)S(1)}) fusion(bf16[512,2048]{1,0:T(8,128)(2,1)} %param.16), kind=kLoop, calls=%fused_computation.10 | loop fusion | bytes 4194304 | tf_op jit(solution)/shard_map/slice | solution.py:350
  1.8 3.1 %collective-permute-start.2 = (bf16[512,1024]{1,0:T(8,128)(2,1)S(1)}, bf16[512,1024]{1,0:T(8,128)(2,1)}, u32[]{:S(2)}, u32[]{:S(2)}) collective-permute-start(bf16[512,1024]{1,0:T(8,128)(2,1)S(1)} %get-tuple-element.21.refs_4_), channel_id=1, source_target_pairs={{0,8},{8,16},{16,24},{24,28},{28,20},{20,12},{12,4},{4,0},{1,9},{9... | collective-permute-start | bytes 3145736 | tf_op jit(solution)/shard_map/ppermute | solution.py:358
  4.9 2.0 %collective-permute-start.15 = (bf16[512,1024]{1,0:T(8,128)(2,1)S(1)}, bf16[512,1024]{1,0:T(8,128)(2,1)}, u32[]{:S(2)}, u32[]{:S(2)}) collective-permute-start(bf16[512,1024]{1,0:T(8,128)(2,1)S(1)} %get-tuple-element.26.refs_9_), channel_id=1, source_target_pairs={{8,0},{16,8},{24,16},{28,24},{20,28},{12,20},{4,12},{0,4},{9,1},{1... | collective-permute-start | bytes 3145736 | tf_op jit(solution)/shard_map/ppermute | solution.py:360
  6.9 1.9 %constant_dynamic-slice_fusion.4 = bf16[1024,256]{1,0:T(8,128)(2,1)} fusion(bf16[1024,512]{1,0:T(8,128)(2,1)} %refs_1_, s32[]{:T(128)S(6)} %select_n.29), kind=kLoop, calls=%fused_computation.5 | loop fusion | bytes 1048580 | tf_op jit(solution)/shard_map/dynamic_slice | solution.py:154
  8.8 1.5 collective-permute-start.1
  10.3 0.8 constant_dynamic-slice_fusion.5
  11.1 0.5 collective-permute-start
  11.6 1.0 constant_dynamic-slice_fusion.2
  12.6 11.3 %collective-permute-done.1.refs_3_ = bf16[1024,256]{1,0:T(8,128)(2,1)} collective-permute-done((bf16[1024,256]{1,0:T(8,128)(2,1)}, bf16[1024,256]{1,0:T(8,128)(2,1)}, u32[]{:S(2)}, u32[]{:S(2)}) %collective-permute-start.1) | collective-permute-done | bytes 524320 | tf_op jit(solution)/shard_map/ppermute | solution.py:160
  24.0 9.1 %collective-permute-done.refs_2_ = bf16[1024,256]{1,0:T(8,128)(2,1)} collective-permute-done((bf16[1024,256]{1,0:T(8,128)(2,1)}, bf16[1024,256]{1,0:T(8,128)(2,1)}, u32[]{:S(2)}, u32[]{:S(2)}) %collective-permute-start) | collective-permute-done | bytes 524320 | tf_op jit(solution)/shard_map/ppermute | solution.py:160
  33.1 1.1 constant_dynamic-slice_fusion
  34.4 1.6 collective-permute-start.10
  36.5 17.1 %collective-permute-done.15.refs_11_ = bf16[512,1024]{1,0:T(8,128)(2,1)} collective-permute-done((bf16[512,1024]{1,0:T(8,128)(2,1)S(1)}, bf16[512,1024]{1,0:T(8,128)(2,1)}, u32[]{:S(2)}, u32[]{:S(2)}) %collective-permute-start.15) | collective-permute-done | bytes 1048608 | tf_op jit(solution)/shard_map/ppermute | solution.py:360
  55.0 2.1 %collective-permute-start.13 = (bf16[512,1024]{1,0:T(8,128)(2,1)}, bf16[512,1024]{1,0:T(8,128)(2,1)}, u32[]{:S(2)}, u32[]{:S(2)}) collective-permute-start(bf16[512,1024]{1,0:T(8,128)(2,1)} %collective-permute-done.12.refs_10_), channel_id=1, source_target_pairs={{0,8},{8,16},{16,24},{24,28},{28,20},{20,12},{12,4},{4,0},{1,9},{9... | collective-permute-start | bytes 3145736 | tf_op jit(solution)/shard_map/ppermute | solution.py:358
  57.1 1.0 copy-done.1
  58.0 18.7 %attend.1.refs_0_ = bf16[512,1024]{1,0:T(8,128)(2,1)S(1)} custom-call(s32[34]{0:T(128)S(1)} %concatenate.16.meta_ref, bf16[512,1024]{1,0:T(8,128)(2,1)} %bitcast.15, bf16[512,1024]{1,0:T(8,128)(2,1)} %bitcast.16, bf16[1024,512]{1,0:T(8,128)(2,1)} %refs_0_, bf16[1024,512]{1,0:T(8,128)(2,1)} %refs_1_, bf16[1024,256]{1,0:T(8,128)(2,1)} %collective-permute-done.refs_2_, ...), custom_call_target="tpu_custom_call" | custom-call | flops 1048576 | bytes 1048576 | tf_op jit(solution)/shard_map/attend/pallas_call | solution.py:118
  76.8 1.6 collective-permute-start.6
  78.4 1.6 collective-permute-start.9
  80.0 17.0 %collective-permute-done.16.refs_13_ = bf16[512,1024]{1,0:T(8,128)(2,1)} collective-permute-done((bf16[512,1024]{1,0:T(8,128)(2,1)}, bf16[512,1024]{1,0:T(8,128)(2,1)}, u32[]{:S(2)}, u32[]{:S(2)}) %collective-permute-start.16) | collective-permute-done | bytes 1048608 | tf_op jit(solution)/shard_map/ppermute | solution.py:360
  97.4 1.7 %collective-permute-start.11 = (bf16[512,1024]{1,0:T(8,128)(2,1)}, bf16[512,1024]{1,0:T(8,128)(2,1)}, u32[]{:S(2)}, u32[]{:S(2)}) collective-permute-start(bf16[512,1024]{1,0:T(8,128)(2,1)} %collective-permute-done.10.refs_8_), channel_id=1, source_target_pairs={{8,0},{16,8},{24,16},{28,24},{20,28},{12,20},{4,12},{0,4},{9,1},{1... | collective-permute-start | bytes 3145736 | tf_op jit(solution)/shard_map/ppermute | solution.py:360
  99.1 3.8 %collective-permute-done.6.refs_2_ = bf16[512,1024]{1,0:T(8,128)(2,1)S(1)} collective-permute-done((bf16[512,1024]{1,0:T(8,128)(2,1)S(1)}, bf16[512,1024]{1,0:T(8,128)(2,1)S(1)}, u32[]{:S(2)}, u32[]{:S(2)}) %collective-permute-start.6) | collective-permute-done | bytes 1048608 | tf_op jit(solution)/shard_map/ppermute | solution.py:381
  102.9 1.6 collective-permute-start.14
  104.5 14.4 %collective-permute-done.9.refs_4_ = bf16[512,1024]{1,0:T(8,128)(2,1)} collective-permute-done((bf16[512,1024]{1,0:T(8,128)(2,1)}, bf16[512,1024]{1,0:T(8,128)(2,1)}, u32[]{:S(2)}, u32[]{:S(2)}) %collective-permute-start.9) | collective-permute-done | bytes 1048608 | tf_op jit(solution)/shard_map/ppermute | solution.py:358
  118.8 2.1 %collective-permute-start.18 = (bf16[512,1024]{1,0:T(8,128)(2,1)}, bf16[512,1024]{1,0:T(8,128)(2,1)S(1)}, u32[]{:S(2)}, u32[]{:S(2)}) collective-permute-start(bf16[512,1024]{1,0:T(8,128)(2,1)} %collective-permute-done.9.refs_4_), channel_id=1, source_target_pairs={{0,8},{8,16},{16,24},{24,28},{28,20},{20,12},{12,4},{4,0},{1,9},{9... | collective-permute-start | bytes 3145736 | tf_op jit(solution)/shard_map/ppermute | solution.py:358
  120.9 2.5 %collective-permute-done.17.refs_7_ = bf16[512,1024]{1,0:T(8,128)(2,1)} collective-permute-done((bf16[512,1024]{1,0:T(8,128)(2,1)}, bf16[512,1024]{1,0:T(8,128)(2,1)}, u32[]{:S(2)}, u32[]{:S(2)}) %collective-permute-start.17) | collective-permute-done | bytes 1048608 | tf_op jit(solution)/shard_map/ppermute | solution.py:360
  123.7 0.7 fusion
  124.5 11.7 %ring_product.2.refs_8_ = f32[512,2048]{1,0:T(8,128)S(1)} custom-call(s32[9]{0:T(128)S(1)} %pad_add_fusion.where_ref, bf16[512,1024]{1,0:T(8,128)(2,1)} %copy-done, bf16[512,1024]{1,0:T(8,128)(2,1)} %copy-done.2, bf16[512,1024]{1,0:T(8,128)(2,1)} %copy-done.3, bf16[512,1024]{1,0:T(8,128)(2,1)} %collective-permute-done.7.refs_3_, ...), custom_call_target="tpu_custom_call" | custom-call | flops 1048576 | bytes 1048576 | tf_op jit(solution)/shard_map/ring_product/pallas_call | solution.py:285
  136.3 9.7 %collective-permute-done.11.refs_5_ = bf16[512,1024]{1,0:T(8,128)(2,1)} collective-permute-done((bf16[512,1024]{1,0:T(8,128)(2,1)}, bf16[512,1024]{1,0:T(8,128)(2,1)}, u32[]{:S(2)}, u32[]{:S(2)}) %collective-permute-start.11) | collective-permute-done | bytes 1048608 | tf_op jit(solution)/shard_map/ppermute | solution.py:360
  145.9 6.6 %ring_product.3 = (f32[512,2048]{1,0:T(8,128)S(1)}, bf16[512,512]{1,0:T(8,128)(2,1)S(1)}) custom-call(s32[9]{0:T(128)S(1)} %pad_add_fusion.where_ref, bf16[512,1024]{1,0:T(8,128)(2,1)} %copy-done, bf16[512,1024]{1,0:T(8,128)(2,1)} %copy-done.2, bf16[512,1024]{1,0:T(8,128)(2,1)} %copy-done.3, bf16[512,1024]{1,0:T(8,128)(2,1)} %collective-permute-done.7.refs_3_, ...), custom_call_target="tpu_custom_call" | custom-call | flops 1048576 | bytes 1048576 | tf_op jit(solution)/shard_map/ring_product/pallas_call | solution.py:285
  152.6 10.3 %collective-permute-done.18.left_slab = bf16[512,1024]{1,0:T(8,128)(2,1)S(1)} collective-permute-done((bf16[512,1024]{1,0:T(8,128)(2,1)}, bf16[512,1024]{1,0:T(8,128)(2,1)S(1)}, u32[]{:S(2)}, u32[]{:S(2)}) %collective-permute-start.18) | collective-permute-done | bytes 1048608 | tf_op jit(solution)/shard_map/ppermute | solution.py:358
  162.8 3.1 %collective-permute-done.19.right_slab = bf16[512,1024]{1,0:T(8,128)(2,1)S(1)} collective-permute-done((bf16[512,1024]{1,0:T(8,128)(2,1)}, bf16[512,1024]{1,0:T(8,128)(2,1)S(1)}, u32[]{:S(2)}, u32[]{:S(2)}) %collective-permute-start.19) | collective-permute-done | bytes 1048608 | tf_op jit(solution)/shard_map/ppermute | solution.py:360
  165.9 2.1 %last_product.1 = bf16[512,2048]{1,0:T(8,128)(2,1)} custom-call(bf16[512,512]{1,0:T(8,128)(2,1)S(1)} %get-tuple-element.27.block_ref, bf16[512,1024]{1,0:T(8,128)(2,1)S(1)} %collective-permute-done.18.left_slab, bf16[512,1024]{1,0:T(8,128)(2,1)S(1)} %collective-permute-done.19.right_slab, f32[512,2048]{1,0:T(8,128)S(1)} %get-tuple-element.28.base_ref), custom_call_target="tpu_custom_call" | custom-call | flops 1048576 | bytes 1048576 | tf_op jit(solution)/shard_map/last_product/pallas_call | solution.py:327
  (37 shorter events, 1.6 us)
Async XLA Ops:
  0.0 10.3 %copy-start.6 = (bf16[1024,512]{1,0:T(8,128)(2,1)S(1)}, bf16[1024,512]{1,0:T(8,128)(2,1)}, u32[]{:S(2)}) copy-start(bf16[1024,512]{1,0:T(8,128)(2,1)} %refs_0_) | copy-start | bytes 3145732
  1.8 32.4 %copy-start.4 = (bf16[512,1024]{1,0:T(8,128)(2,1)}, bf16[512,1024]{1,0:T(8,128)(2,1)S(1)}, u32[]{:S(2)}) copy-start(bf16[512,1024]{1,0:T(8,128)(2,1)S(1)} %get-tuple-element.26.refs_9_) | copy-start | bytes 3145732
  1.8 32.4 %copy-start.5 = (bf16[512,1024]{1,0:T(8,128)(2,1)}, bf16[512,1024]{1,0:T(8,128)(2,1)S(1)}, u32[]{:S(2)}) copy-start(bf16[512,1024]{1,0:T(8,128)(2,1)S(1)} %get-tuple-element.21.refs_4_) | copy-start | bytes 3145732
  1.8 31.3 %collective-permute-start.2 = (bf16[512,1024]{1,0:T(8,128)(2,1)S(1)}, bf16[512,1024]{1,0:T(8,128)(2,1)}, u32[]{:S(2)}, u32[]{:S(2)}) collective-permute-start(bf16[512,1024]{1,0:T(8,128)(2,1)S(1)} %get-tuple-element.21.refs_4_), channel_id=1, source_target_pairs={{0,8},{8,16},{16,24},{24,28},{28,20},{20,12},{12,4},{4,0},{1,9},{9... | collective-permute-start | bytes 3145736 | tf_op jit(solution)/shard_map/ppermute | solution.py:358
  4.9 28.2 %collective-permute-start.3 = (bf16[512,1024]{1,0:T(8,128)(2,1)S(1)}, bf16[512,1024]{1,0:T(8,128)(2,1)}, u32[]{:S(2)}, u32[]{:S(2)}) collective-permute-start(bf16[512,1024]{1,0:T(8,128)(2,1)S(1)} %get-tuple-element.21.refs_4_), channel_id=1, source_target_pairs={{8,0},{16,8},{24,16},{28,24},{20,28},{12,20},{4,12},{0,4},{9,1},{1... | collective-permute-start | bytes 3145736 | tf_op jit(solution)/shard_map/ppermute | solution.py:360
  4.9 48.6 %collective-permute-start.15 = (bf16[512,1024]{1,0:T(8,128)(2,1)S(1)}, bf16[512,1024]{1,0:T(8,128)(2,1)}, u32[]{:S(2)}, u32[]{:S(2)}) collective-permute-start(bf16[512,1024]{1,0:T(8,128)(2,1)S(1)} %get-tuple-element.26.refs_9_), channel_id=1, source_target_pairs={{8,0},{16,8},{24,16},{28,24},{20,28},{12,20},{4,12},{0,4},{9,1},{1... | collective-permute-start | bytes 3145736 | tf_op jit(solution)/shard_map/ppermute | solution.py:360
  8.8 15.2 %collective-permute-start.1 = (bf16[1024,256]{1,0:T(8,128)(2,1)}, bf16[1024,256]{1,0:T(8,128)(2,1)}, u32[]{:S(2)}, u32[]{:S(2)}) collective-permute-start(bf16[1024,256]{1,0:T(8,128)(2,1)} %constant_dynamic-slice_fusion.4), channel_id=1, source_target_pairs={{0,2},{1,3},{2,0},{3,1},{4,6},{5,7},{6,4},{7,5},{8,10},{9,11},{10,... | collective-permute-start | bytes 1572872 | tf_op jit(solution)/shard_map/ppermute | solution.py:160
  11.1 22.1 %collective-permute-start = (bf16[1024,256]{1,0:T(8,128)(2,1)}, bf16[1024,256]{1,0:T(8,128)(2,1)}, u32[]{:S(2)}, u32[]{:S(2)}) collective-permute-start(bf16[1024,256]{1,0:T(8,128)(2,1)} %constant_dynamic-slice_fusion.5), channel_id=1, source_target_pairs={{0,2},{1,3},{2,0},{3,1},{4,6},{5,7},{6,4},{7,5},{8,10},{9,11},{10,... | collective-permute-start | bytes 1572872 | tf_op jit(solution)/shard_map/ppermute | solution.py:160
  11.6 43.3 %copy-start.7 = (s32[1,1,16]{2,1,0:T(1,128)S(1)}, s32[1,1,16]{2,1,0:T(1,128)}, u32[]{:S(2)}) copy-start(s32[1,1,16]{2,1,0:T(1,128)} %param.12) | copy-start | bytes 196
  23.9 31.0 %collective-permute-start.12 = (bf16[512,1024]{1,0:T(8,128)(2,1)S(1)}, bf16[512,1024]{1,0:T(8,128)(2,1)}, u32[]{:S(2)}, u32[]{:S(2)}) collective-permute-start(bf16[512,1024]{1,0:T(8,128)(2,1)S(1)} %get-tuple-element.26.refs_9_), channel_id=1, source_target_pairs={{0,8},{8,16},{16,24},{24,28},{28,20},{20,12},{12,4},{4,0},{1,9},{9... | collective-permute-start | bytes 3145736 | tf_op jit(solution)/shard_map/ppermute | solution.py:358
  34.4 22.7 %collective-permute-start.4 = (bf16[2048,256]{1,0:T(8,128)(2,1)S(1)}, bf16[2048,256]{1,0:T(8,128)(2,1)S(1)}, u32[]{:S(2)}, u32[]{:S(2)}) collective-permute-start(bf16[2048,256]{1,0:T(8,128)(2,1)S(1)} %maximum_maximum_fusion), channel_id=1, source_target_pairs={{0,1},{1,0},{2,3},{3,2},{4,5},{5,4},{6,7},{7,6},{8,9},{9,8},{10,11... | collective-permute-start | bytes 3145736 | tf_op jit(solution)/shard_map/ppermute | solution.py:164
  34.4 42.4 %collective-permute-start.10 = (bf16[512,1024]{1,0:T(8,128)(2,1)}, bf16[512,1024]{1,0:T(8,128)(2,1)}, u32[]{:S(2)}, u32[]{:S(2)}) collective-permute-start(bf16[512,1024]{1,0:T(8,128)(2,1)} %collective-permute-done.3.refs_6_), channel_id=1, source_target_pairs={{8,0},{16,8},{24,16},{28,24},{20,28},{12,20},{4,12},{0,4},{9,1},{1... | collective-permute-start | bytes 3145736 | tf_op jit(solution)/shard_map/ppermute | solution.py:360
  36.1 42.4 %collective-permute-start.8 = (bf16[512,1024]{1,0:T(8,128)(2,1)}, bf16[512,1024]{1,0:T(8,128)(2,1)}, u32[]{:S(2)}, u32[]{:S(2)}) collective-permute-start(bf16[512,1024]{1,0:T(8,128)(2,1)} %collective-permute-done.2.refs_5_), channel_id=1, source_target_pairs={{0,8},{8,16},{16,24},{24,28},{28,20},{20,12},{12,4},{4,0},{1,9},{9... | collective-permute-start | bytes 3145736 | tf_op jit(solution)/shard_map/ppermute | solution.py:358
  53.6 43.5 %collective-permute-start.16 = (bf16[512,1024]{1,0:T(8,128)(2,1)}, bf16[512,1024]{1,0:T(8,128)(2,1)}, u32[]{:S(2)}, u32[]{:S(2)}) collective-permute-start(bf16[512,1024]{1,0:T(8,128)(2,1)} %collective-permute-done.15.refs_11_), channel_id=1, source_target_pairs={{8,0},{16,8},{24,16},{28,24},{20,28},{12,20},{4,12},{0,4},{9,1},{1... | collective-permute-start | bytes 3145736 | tf_op jit(solution)/shard_map/ppermute | solution.py:360
  55.0 42.3 %collective-permute-start.13 = (bf16[512,1024]{1,0:T(8,128)(2,1)}, bf16[512,1024]{1,0:T(8,128)(2,1)}, u32[]{:S(2)}, u32[]{:S(2)}) collective-permute-start(bf16[512,1024]{1,0:T(8,128)(2,1)} %collective-permute-done.12.refs_10_), channel_id=1, source_target_pairs={{0,8},{8,16},{16,24},{24,28},{28,20},{20,12},{12,4},{4,0},{1,9},{9... | collective-permute-start | bytes 3145736 | tf_op jit(solution)/shard_map/ppermute | solution.py:358
  57.1 1.0 copy-start.1
  76.7 47.8 %copy-start = (bf16[512,1024]{1,0:T(8,128)(2,1)}, bf16[512,1024]{1,0:T(8,128)(2,1)S(1)}, u32[]{:S(2)}) copy-start(bf16[512,1024]{1,0:T(8,128)(2,1)S(1)} %attend.1.refs_0_) | copy-start | bytes 3145732
  76.8 20.6 %collective-permute-start.5 = (bf16[512,1024]{1,0:T(8,128)(2,1)S(1)}, bf16[512,1024]{1,0:T(8,128)(2,1)S(1)}, u32[]{:S(2)}, u32[]{:S(2)}) collective-permute-start(bf16[512,1024]{1,0:T(8,128)(2,1)S(1)} %attend.1.refs_0_), channel_id=1, source_target_pairs={{0,1},{1,0},{2,3},{3,2},{4,5},{5,4},{6,7},{7,6},{8,9},{9,8},{10,11... | collective-permute-start | bytes 3145736 | tf_op jit(solution)/shard_map/ppermute | solution.py:382
  76.8 26.0 %collective-permute-start.6 = (bf16[512,1024]{1,0:T(8,128)(2,1)S(1)}, bf16[512,1024]{1,0:T(8,128)(2,1)S(1)}, u32[]{:S(2)}, u32[]{:S(2)}) collective-permute-start(bf16[512,1024]{1,0:T(8,128)(2,1)S(1)} %attend.1.refs_0_), channel_id=1, source_target_pairs={{0,2},{1,3},{2,0},{3,1},{4,6},{5,7},{6,4},{7,5},{8,10},{9,11},{10,... | collective-permute-start | bytes 3145736 | tf_op jit(solution)/shard_map/ppermute | solution.py:381
  78.4 40.4 %collective-permute-start.9 = (bf16[512,1024]{1,0:T(8,128)(2,1)}, bf16[512,1024]{1,0:T(8,128)(2,1)}, u32[]{:S(2)}, u32[]{:S(2)}) collective-permute-start(bf16[512,1024]{1,0:T(8,128)(2,1)} %collective-permute-done.8.refs_7_), channel_id=1, source_target_pairs={{0,8},{8,16},{16,24},{24,28},{28,20},{20,12},{12,4},{4,0},{1,9},{9... | collective-permute-start | bytes 3145736 | tf_op jit(solution)/shard_map/ppermute | solution.py:358
  97.0 26.4 %collective-permute-start.17 = (bf16[512,1024]{1,0:T(8,128)(2,1)}, bf16[512,1024]{1,0:T(8,128)(2,1)}, u32[]{:S(2)}, u32[]{:S(2)}) collective-permute-start(bf16[512,1024]{1,0:T(8,128)(2,1)} %collective-permute-done.16.refs_13_), channel_id=1, source_target_pairs={{8,0},{16,8},{24,16},{28,24},{20,28},{12,20},{4,12},{0,4},{9,1},{1... | collective-permute-start | bytes 3145736 | tf_op jit(solution)/shard_map/ppermute | solution.py:360
  97.3 27.2 %collective-permute-start.7 = (bf16[512,1024]{1,0:T(8,128)(2,1)S(1)}, bf16[512,1024]{1,0:T(8,128)(2,1)}, u32[]{:S(2)}, u32[]{:S(2)}) collective-permute-start(bf16[512,1024]{1,0:T(8,128)(2,1)S(1)} %attend.1.refs_0_), channel_id=1, source_target_pairs={{0,3},{1,2},{2,1},{3,0},{4,7},{5,6},{6,5},{7,4},{8,11},{9,10},{10,... | collective-permute-start | bytes 3145736 | tf_op jit(solution)/shard_map/ppermute | solution.py:383
  97.3 23.6 %copy-start.2 = (bf16[512,1024]{1,0:T(8,128)(2,1)}, bf16[512,1024]{1,0:T(8,128)(2,1)S(1)}, u32[]{:S(2)}) copy-start(bf16[512,1024]{1,0:T(8,128)(2,1)S(1)} %collective-permute-done.5.refs_1_) | copy-start | bytes 3145732
  97.4 48.6 %collective-permute-start.11 = (bf16[512,1024]{1,0:T(8,128)(2,1)}, bf16[512,1024]{1,0:T(8,128)(2,1)}, u32[]{:S(2)}, u32[]{:S(2)}) collective-permute-start(bf16[512,1024]{1,0:T(8,128)(2,1)} %collective-permute-done.10.refs_8_), channel_id=1, source_target_pairs={{8,0},{16,8},{24,16},{28,24},{20,28},{12,20},{4,12},{0,4},{9,1},{1... | collective-permute-start | bytes 3145736 | tf_op jit(solution)/shard_map/ppermute | solution.py:360
  102.9 20.6 %copy-start.3 = (bf16[512,1024]{1,0:T(8,128)(2,1)}, bf16[512,1024]{1,0:T(8,128)(2,1)S(1)}, u32[]{:S(2)}) copy-start(bf16[512,1024]{1,0:T(8,128)(2,1)S(1)} %collective-permute-done.6.refs_2_) | copy-start | bytes 3145732
  102.9 43.0 %collective-permute-start.14 = (bf16[512,1024]{1,0:T(8,128)(2,1)}, bf16[512,1024]{1,0:T(8,128)(2,1)}, u32[]{:S(2)}, u32[]{:S(2)}) collective-permute-start(bf16[512,1024]{1,0:T(8,128)(2,1)} %collective-permute-done.13.refs_12_), channel_id=1, source_target_pairs={{0,8},{8,16},{16,24},{24,28},{28,20},{20,12},{12,4},{4,0},{1,9},{9... | collective-permute-start | bytes 3145736 | tf_op jit(solution)/shard_map/ppermute | solution.py:358
  118.8 44.0 %collective-permute-start.18 = (bf16[512,1024]{1,0:T(8,128)(2,1)}, bf16[512,1024]{1,0:T(8,128)(2,1)S(1)}, u32[]{:S(2)}, u32[]{:S(2)}) collective-permute-start(bf16[512,1024]{1,0:T(8,128)(2,1)} %collective-permute-done.9.refs_4_), channel_id=1, source_target_pairs={{0,8},{8,16},{16,24},{24,28},{28,20},{20,12},{12,4},{4,0},{1,9},{9... | collective-permute-start | bytes 3145736 | tf_op jit(solution)/shard_map/ppermute | solution.py:358
  123.5 42.4 %collective-permute-start.19 = (bf16[512,1024]{1,0:T(8,128)(2,1)}, bf16[512,1024]{1,0:T(8,128)(2,1)S(1)}, u32[]{:S(2)}, u32[]{:S(2)}) collective-permute-start(bf16[512,1024]{1,0:T(8,128)(2,1)} %collective-permute-done.17.refs_7_), channel_id=1, source_target_pairs={{8,0},{16,8},{24,16},{28,24},{20,28},{12,20},{4,12},{0,4},{9,1},{1... | collective-permute-start | bytes 3145736 | tf_op jit(solution)/shard_map/ppermute | solution.py:360

commit v10 on v9

--- a/solution.py
+++ b/solution.py
@@ -223,8 +223,8 @@
         refs = refs[3:]
     else:
         out_ref, refs = refs[0], refs[1:]
-    left, right, block_sems, slab_sems = refs
-    rows, depth = left.shape[0], right.shape[1] // count
+    left, block_sems = refs
+    depth = slabs[0][0].shape[0]
     per = blocks[0].shape[1] // depth
     me = where_ref[where_ref.shape[0] - 1]
 
@@ -232,13 +232,6 @@
         target = spare_ref if index == count else left.at[:, pl.ds(index * depth, depth)]
         return pltpu.make_async_copy(
             blocks[slot].at[:, pl.ds(shift, depth)], target, block_sems.at[index]
-        )
-
-    def slab_copy(half, index):
-        return pltpu.make_async_copy(
-            slabs[half][index],
-            right.at[half, pl.ds(index * depth, depth), :],
-            slab_sems.at[half, index],
         )
 
     all_steps = steps if spare_step is None else (*steps, spare_step)
@@ -252,26 +245,26 @@
             def _(slot=slot):
                 block_copy(index, slot, shift).start()
 
-    for half in range(2):
-        for index in range(count):
-            slab_copy(half, index).start()
     for index in range(len(all_steps)):
         block_copy(index, 0, 0).wait()
-    half_columns = right.shape[2]
+    half_columns = slabs[0][0].shape[1]
     for half in range(2):
         columns = pl.ds(half * half_columns, half_columns)
-        for index in range(count):
-            slab_copy(half, index).wait()
 
         def rows_tile(step, carry):
             at = pl.ds(pl.multiple_of(step * ROW_TILE, ROW_TILE), ROW_TILE)
-            product = jnp.dot(left[at, :], right[half], preferred_element_type=jnp.float32)
-            if spare_step is not None:
-                product = product + base_ref[at, columns]
-            out_ref[at, columns] = product
+            total = None if spare_step is None else base_ref[at, columns]
+            for index in range(count):
+                product = jnp.dot(
+                    left[at, index * depth : (index + 1) * depth],
+                    slabs[half][index][...],
+                    preferred_element_type=jnp.float32,
+                )
+                total = product if total is None else total + product
+            out_ref[at, columns] = total
             return carry
 
-        lax.fori_loop(0, rows // ROW_TILE, rows_tile, 0)
+        lax.fori_loop(0, left.shape[0] // ROW_TILE, rows_tile, 0)
 
 
 def ring_product(where, blocks, steps, slabs, base=None, spare_step=None):
@@ -285,21 +278,19 @@
     return pl.pallas_call(
         functools.partial(ring_product_kernel, steps, spare_step),
         out_shape=out_shape,
-        in_specs=[IN_SMEM] + [IN_HBM] * (4 + 2 * count) + [IN_VMEM] * spare,
+        in_specs=[IN_SMEM] + [IN_HBM] * 4 + [IN_VMEM] * (2 * count + spare),
         out_specs=[IN_VMEM] * len(out_shape),
         scratch_shapes=[
             pltpu.VMEM((rows, count * depth), jnp.bfloat16),
-            pltpu.VMEM((2, count * depth, half), jnp.bfloat16),
             pltpu.SemaphoreType.DMA((count + spare,)),
-            pltpu.SemaphoreType.DMA((2, count)),
         ],
-        compiler_params=pltpu.CompilerParams(vmem_limit_bytes=(6 + 4 * count) << 20),
+        compiler_params=pltpu.CompilerParams(vmem_limit_bytes=12 << 20),
         cost_estimate=SMALL_COST,
         name="ring_product",
     )(
         where,
-        *pinned([*blocks, *slabs[0], *slabs[1]], pltpu.HBM),
-        *(pinned([base], pltpu.VMEM) if spare else []),
+        *pinned(blocks, pltpu.HBM),
+        *pinned([*slabs[0], *slabs[1], *([base] if spare else [])], pltpu.VMEM),
     )
 
 

time: 168 us -> 170 us (1.012)
  waiting for transfers between devices: 98.2 us -> 116 us
  Pallas kernels: 39.2 us -> 24.7 us
    ppermute x7, waiting for transfers between devices: 49.3 us -> 67 us  [travel(): moving[part][1] = lax.ppermute(moving[part][1], 'pb', backward)]
    pallas_call x1, Pallas kernels: 18.7 us -> 1.85 us  [attend(): pl.pallas_call(functools.partial(attention_kernel, heads, slots, part_row...]
    ppermute x7, waiting for transfers between devices: 24.6 us -> 28.5 us  [travel(): moving[part][0] = lax.ppermute(moving[part][0], 'pb', forward)]
    ppermute x1, waiting for transfers between devices: 3.79 us -> 0.01 us  [project_ring(): across = lax.ppermute(attn, 'ka', [(i, i ^ 2) for i in range(4)])]
  transfers between devices with their start and end apart: 20 -> 20, of which waited for: 10 -> 10; matrix products, arithmetic and copies ran while one was open for 3% -> 3% of each run, Pallas kernels for 22% -> 12%
where the time goes in v10:
time: 170 us
  waiting for transfers between devices  116 us (68%)
  Pallas kernels  24.7 us (15%)
  starting transfers between devices  20 us (12%)
  local copies, waits for them, and re-layouts  7.39 us (4%)
    ppermute x7, waiting for transfers between devices, travel(): moving[part][1] = lax.ppermute(moving[part][1], 'pb', backward)  67 us
    ppermute x7, waiting for transfers between devices, travel(): moving[part][0] = lax.ppermute(moving[part][0], 'pb', forward)  28.5 us
    ppermute x2, waiting for transfers between devices, own_head_keys_values(): lax.ppermute(heads_of(a, 1 - x), 'ka', [(i, i ^ 2) for i in range(4)])  20.4 us
    pallas_call x2, Pallas kernels, ring_product(): pl.pallas_call(functools.partial(ring_product_kernel, steps, spare_step),...  19.2 us
    ppermute x7, starting transfers between devices, travel(): moving[part][0] = lax.ppermute(moving[part][0], 'pb', forward)  10.4 us
    ppermute x7, starting transfers between devices, travel(): moving[part][1] = lax.ppermute(moving[part][1], 'pb', backward)  5.91 us
    pallas_call x1, Pallas kernels, last_product(): pl.pallas_call(last_product_kernel, out_shape=jax.ShapeDtypeStruct((rows,...  3.65 us
  transfers between devices with their start and end apart: 20, of which 10 were waited for; matrix products, arithmetic and copies ran while one was open for 3% of the time, Pallas kernels for 12%

profile of v10, /device:TPU:0, one launch (start us, length us, event | category | flops | bytes accessed | tf_op | source)
XLA Modules:
  0.0 169.6 jit_solution(4466091624559219317)
XLA Ops:
  0.0 1.8 %fusion.1 = (bf16[512,1024]{1,0:T(8,128)(2,1)S(1)}, bf16[512,1024]{1,0:T(8,128)(2,1)S(1)}) fusion(bf16[512,2048]{1,0:T(8,128)(2,1)} %param.16), kind=kLoop, calls=%fused_computation.10 | loop fusion | bytes 4194304 | tf_op jit(solution)/shard_map/slice | solution.py:341
  1.8 3.1 %collective-permute-start.2 = (bf16[512,1024]{1,0:T(8,128)(2,1)S(1)}, bf16[512,1024]{1,0:T(8,128)(2,1)}, u32[]{:S(2)}, u32[]{:S(2)}) collective-permute-start(bf16[512,1024]{1,0:T(8,128)(2,1)S(1)} %get-tuple-element.21.refs_4_), channel_id=1, source_target_pairs={{0,8},{8,16},{16,24},{24,28},{28,20},{20,12},{12,4},{4,0},{1,9},{9... | collective-permute-start | bytes 3145736 | tf_op jit(solution)/shard_map/ppermute | solution.py:349
  4.9 2.0 %collective-permute-start.15 = (bf16[512,1024]{1,0:T(8,128)(2,1)S(1)}, bf16[512,1024]{1,0:T(8,128)(2,1)}, u32[]{:S(2)}, u32[]{:S(2)}) collective-permute-start(bf16[512,1024]{1,0:T(8,128)(2,1)S(1)} %get-tuple-element.26.refs_9_), channel_id=1, source_target_pairs={{8,0},{16,8},{24,16},{28,24},{20,28},{12,20},{4,12},{0,4},{9,1},{1... | collective-permute-start | bytes 3145736 | tf_op jit(solution)/shard_map/ppermute | solution.py:351
  6.9 1.9 %constant_dynamic-slice_fusion.4 = bf16[1024,256]{1,0:T(8,128)(2,1)} fusion(bf16[1024,512]{1,0:T(8,128)(2,1)} %refs_1_, s32[]{:T(128)S(6)} %select_n.29), kind=kLoop, calls=%fused_computation.5 | loop fusion | bytes 1048580 | tf_op jit(solution)/shard_map/dynamic_slice | solution.py:154
  8.7 1.5 collective-permute-start.1
  10.2 0.8 constant_dynamic-slice_fusion.5
  11.1 0.5 collective-permute-start
  11.6 1.0 constant_dynamic-slice_fusion.2
  12.6 11.3 %collective-permute-done.1.refs_3_ = bf16[1024,256]{1,0:T(8,128)(2,1)} collective-permute-done((bf16[1024,256]{1,0:T(8,128)(2,1)}, bf16[1024,256]{1,0:T(8,128)(2,1)}, u32[]{:S(2)}, u32[]{:S(2)}) %collective-permute-start.1) | collective-permute-done | bytes 524320 | tf_op jit(solution)/shard_map/ppermute | solution.py:160
  24.0 9.1 %collective-permute-done.refs_2_ = bf16[1024,256]{1,0:T(8,128)(2,1)} collective-permute-done((bf16[1024,256]{1,0:T(8,128)(2,1)}, bf16[1024,256]{1,0:T(8,128)(2,1)}, u32[]{:S(2)}, u32[]{:S(2)}) %collective-permute-start) | collective-permute-done | bytes 524320 | tf_op jit(solution)/shard_map/ppermute | solution.py:160
  33.1 1.1 constant_dynamic-slice_fusion
  34.4 1.6 collective-permute-start.10
  36.0 0.4 collective-permute-start.8
  36.5 17.1 %collective-permute-done.15.refs_11_ = bf16[512,1024]{1,0:T(8,128)(2,1)} collective-permute-done((bf16[512,1024]{1,0:T(8,128)(2,1)S(1)}, bf16[512,1024]{1,0:T(8,128)(2,1)}, u32[]{:S(2)}, u32[]{:S(2)}) %collective-permute-start.15) | collective-permute-done | bytes 1048608 | tf_op jit(solution)/shard_map/ppermute | solution.py:351
  55.0 2.1 %collective-permute-start.13 = (bf16[512,1024]{1,0:T(8,128)(2,1)}, bf16[512,1024]{1,0:T(8,128)(2,1)}, u32[]{:S(2)}, u32[]{:S(2)}) collective-permute-start(bf16[512,1024]{1,0:T(8,128)(2,1)} %collective-permute-done.12.refs_10_), channel_id=1, source_target_pairs={{0,8},{8,16},{16,24},{24,28},{28,20},{20,12},{12,4},{4,0},{1,9},{9... | collective-permute-start | bytes 3145736 | tf_op jit(solution)/shard_map/ppermute | solution.py:349
  57.0 1.8 %attend.1.refs_0_ = bf16[512,1024]{1,0:T(8,128)(2,1)S(1)} custom-call(s32[34]{0:T(128)S(1)} %concatenate.16.meta_ref, bf16[512,1024]{1,0:T(8,128)(2,1)} %bitcast.15, bf16[512,1024]{1,0:T(8,128)(2,1)} %bitcast.16, bf16[1024,512]{1,0:T(8,128)(2,1)} %refs_0_, bf16[1024,512]{1,0:T(8,128)(2,1)} %refs_1_, bf16[1024,256]{1,0:T(8,128)(2,1)} %collective-permute-done.refs_2_, ...), custom_call_target="tpu_custom_call" | custom-call | flops 1048576 | bytes 1048576 | tf_op jit(solution)/shard_map/attend/pallas_call | solution.py:118
  59.0 17.0 %collective-permute-done.10.refs_8_ = bf16[512,1024]{1,0:T(8,128)(2,1)} collective-permute-done((bf16[512,1024]{1,0:T(8,128)(2,1)}, bf16[512,1024]{1,0:T(8,128)(2,1)}, u32[]{:S(2)}, u32[]{:S(2)}) %collective-permute-start.10) | collective-permute-done | bytes 1048608 | tf_op jit(solution)/shard_map/ppermute | solution.py:351
  76.0 1.5 collective-permute-start.6
  77.5 1.6 collective-permute-start.9
  79.1 17.9 %collective-permute-done.16.refs_13_ = bf16[512,1024]{1,0:T(8,128)(2,1)} collective-permute-done((bf16[512,1024]{1,0:T(8,128)(2,1)}, bf16[512,1024]{1,0:T(8,128)(2,1)}, u32[]{:S(2)}, u32[]{:S(2)}) %collective-permute-start.16) | collective-permute-done | bytes 1048608 | tf_op jit(solution)/shard_map/ppermute | solution.py:351
  97.3 1.7 %collective-permute-start.11 = (bf16[512,1024]{1,0:T(8,128)(2,1)}, bf16[512,1024]{1,0:T(8,128)(2,1)}, u32[]{:S(2)}, u32[]{:S(2)}) collective-permute-start(bf16[512,1024]{1,0:T(8,128)(2,1)} %collective-permute-done.10.refs_8_), channel_id=1, source_target_pairs={{8,0},{16,8},{24,16},{28,24},{20,28},{12,20},{4,12},{0,4},{9,1},{1... | collective-permute-start | bytes 3145736 | tf_op jit(solution)/shard_map/ppermute | solution.py:351
  99.1 1.0 collective-permute-start.14
  100.1 18.7 %collective-permute-done.9.refs_4_ = bf16[512,1024]{1,0:T(8,128)(2,1)} collective-permute-done((bf16[512,1024]{1,0:T(8,128)(2,1)}, bf16[512,1024]{1,0:T(8,128)(2,1)}, u32[]{:S(2)}, u32[]{:S(2)}) %collective-permute-start.9) | collective-permute-done | bytes 1048608 | tf_op jit(solution)/shard_map/ppermute | solution.py:349
  118.8 2.1 %collective-permute-start.18 = (bf16[512,1024]{1,0:T(8,128)(2,1)}, bf16[512,1024]{1,0:T(8,128)(2,1)}, u32[]{:S(2)}, u32[]{:S(2)}) collective-permute-start(bf16[512,1024]{1,0:T(8,128)(2,1)} %collective-permute-done.9.refs_4_), channel_id=1, source_target_pairs={{0,8},{8,16},{16,24},{24,28},{28,20},{20,12},{12,4},{4,0},{1,9},{9... | collective-permute-start | bytes 3145736 | tf_op jit(solution)/shard_map/ppermute | solution.py:349
  120.9 2.5 %collective-permute-done.17.refs_7_ = bf16[512,1024]{1,0:T(8,128)(2,1)} collective-permute-done((bf16[512,1024]{1,0:T(8,128)(2,1)}, bf16[512,1024]{1,0:T(8,128)(2,1)}, u32[]{:S(2)}, u32[]{:S(2)}) %collective-permute-start.17) | collective-permute-done | bytes 1048608 | tf_op jit(solution)/shard_map/ppermute | solution.py:351
  123.7 0.7 fusion
  124.5 12.0 %ring_product.2.refs_8_ = f32[512,2048]{1,0:T(8,128)S(1)} custom-call(s32[9]{0:T(128)S(1)} %pad_add_fusion.where_ref, bf16[512,1024]{1,0:T(8,128)(2,1)} %copy-done, bf16[512,1024]{1,0:T(8,128)(2,1)} %copy-done.1, bf16[512,1024]{1,0:T(8,128)(2,1)} %copy-done.2, bf16[512,1024]{1,0:T(8,128)(2,1)} %collective-permute-done.7.refs_3_, ...), custom_call_target="tpu_custom_call" | custom-call | flops 1048576 | bytes 1048576 | tf_op jit(solution)/shard_map/ring_product/pallas_call | solution.py:278
  136.5 9.4 %collective-permute-done.11.refs_5_ = bf16[512,1024]{1,0:T(8,128)(2,1)} collective-permute-done((bf16[512,1024]{1,0:T(8,128)(2,1)}, bf16[512,1024]{1,0:T(8,128)(2,1)}, u32[]{:S(2)}, u32[]{:S(2)}) %collective-permute-start.11) | collective-permute-done | bytes 1048608 | tf_op jit(solution)/shard_map/ppermute | solution.py:351
  145.9 7.2 %ring_product.3 = (f32[512,2048]{1,0:T(8,128)S(1)}, bf16[512,512]{1,0:T(8,128)(2,1)S(1)}) custom-call(s32[9]{0:T(128)S(1)} %pad_add_fusion.where_ref, bf16[512,1024]{1,0:T(8,128)(2,1)} %copy-done, bf16[512,1024]{1,0:T(8,128)(2,1)} %copy-done.1, bf16[512,1024]{1,0:T(8,128)(2,1)} %copy-done.2, bf16[512,1024]{1,0:T(8,128)(2,1)} %collective-permute-done.7.refs_3_, ...), custom_call_target="tpu_custom_call" | custom-call | flops 1048576 | bytes 1048576 | tf_op jit(solution)/shard_map/ring_product/pallas_call | solution.py:278
  153.1 9.8 %collective-permute-done.18.left_slab = bf16[512,1024]{1,0:T(8,128)(2,1)} collective-permute-done((bf16[512,1024]{1,0:T(8,128)(2,1)}, bf16[512,1024]{1,0:T(8,128)(2,1)}, u32[]{:S(2)}, u32[]{:S(2)}) %collective-permute-start.18) | collective-permute-done | bytes 1048608 | tf_op jit(solution)/shard_map/ppermute | solution.py:349
  162.9 3.1 %collective-permute-done.19.right_slab = bf16[512,1024]{1,0:T(8,128)(2,1)} collective-permute-done((bf16[512,1024]{1,0:T(8,128)(2,1)}, bf16[512,1024]{1,0:T(8,128)(2,1)}, u32[]{:S(2)}, u32[]{:S(2)}) %collective-permute-start.19) | collective-permute-done | bytes 1048608 | tf_op jit(solution)/shard_map/ppermute | solution.py:351
  166.0 3.7 %last_product.1 = bf16[512,2048]{1,0:T(8,128)(2,1)} custom-call(bf16[512,512]{1,0:T(8,128)(2,1)S(1)} %get-tuple-element.27.block_ref, bf16[512,1024]{1,0:T(8,128)(2,1)} %collective-permute-done.18.left_slab, bf16[512,1024]{1,0:T(8,128)(2,1)} %collective-permute-done.19.right_slab, f32[512,2048]{1,0:T(8,128)S(1)} %get-tuple-element.28.base_ref), custom_call_target="tpu_custom_call" | custom-call | flops 1048576 | bytes 1048576 | tf_op jit(solution)/shard_map/last_product/pallas_call | solution.py:318
  (31 shorter events, 1.2 us)
Async XLA Ops:
  0.0 10.2 %copy-start.3 = (bf16[1024,512]{1,0:T(8,128)(2,1)S(1)}, bf16[1024,512]{1,0:T(8,128)(2,1)}, u32[]{:S(2)}) copy-start(bf16[1024,512]{1,0:T(8,128)(2,1)} %refs_0_) | copy-start | bytes 3145732
  1.8 31.3 %collective-permute-start.2 = (bf16[512,1024]{1,0:T(8,128)(2,1)S(1)}, bf16[512,1024]{1,0:T(8,128)(2,1)}, u32[]{:S(2)}, u32[]{:S(2)}) collective-permute-start(bf16[512,1024]{1,0:T(8,128)(2,1)S(1)} %get-tuple-element.21.refs_4_), channel_id=1, source_target_pairs={{0,8},{8,16},{16,24},{24,28},{28,20},{20,12},{12,4},{4,0},{1,9},{9... | collective-permute-start | bytes 3145736 | tf_op jit(solution)/shard_map/ppermute | solution.py:349
  4.9 28.2 %collective-permute-start.3 = (bf16[512,1024]{1,0:T(8,128)(2,1)S(1)}, bf16[512,1024]{1,0:T(8,128)(2,1)}, u32[]{:S(2)}, u32[]{:S(2)}) collective-permute-start(bf16[512,1024]{1,0:T(8,128)(2,1)S(1)} %get-tuple-element.21.refs_4_), channel_id=1, source_target_pairs={{8,0},{16,8},{24,16},{28,24},{20,28},{12,20},{4,12},{0,4},{9,1},{1... | collective-permute-start | bytes 3145736 | tf_op jit(solution)/shard_map/ppermute | solution.py:351
  4.9 48.6 %collective-permute-start.15 = (bf16[512,1024]{1,0:T(8,128)(2,1)S(1)}, bf16[512,1024]{1,0:T(8,128)(2,1)}, u32[]{:S(2)}, u32[]{:S(2)}) collective-permute-start(bf16[512,1024]{1,0:T(8,128)(2,1)S(1)} %get-tuple-element.26.refs_9_), channel_id=1, source_target_pairs={{8,0},{16,8},{24,16},{28,24},{20,28},{12,20},{4,12},{0,4},{9,1},{1... | collective-permute-start | bytes 3145736 | tf_op jit(solution)/shard_map/ppermute | solution.py:351
  8.7 15.2 %collective-permute-start.1 = (bf16[1024,256]{1,0:T(8,128)(2,1)}, bf16[1024,256]{1,0:T(8,128)(2,1)}, u32[]{:S(2)}, u32[]{:S(2)}) collective-permute-start(bf16[1024,256]{1,0:T(8,128)(2,1)} %constant_dynamic-slice_fusion.4), channel_id=1, source_target_pairs={{0,2},{1,3},{2,0},{3,1},{4,6},{5,7},{6,4},{7,5},{8,10},{9,11},{10,... | collective-permute-start | bytes 1572872 | tf_op jit(solution)/shard_map/ppermute | solution.py:160
  11.1 22.1 %collective-permute-start = (bf16[1024,256]{1,0:T(8,128)(2,1)}, bf16[1024,256]{1,0:T(8,128)(2,1)}, u32[]{:S(2)}, u32[]{:S(2)}) collective-permute-start(bf16[1024,256]{1,0:T(8,128)(2,1)} %constant_dynamic-slice_fusion.5), channel_id=1, source_target_pairs={{0,2},{1,3},{2,0},{3,1},{4,6},{5,7},{6,4},{7,5},{8,10},{9,11},{10,... | collective-permute-start | bytes 1572872 | tf_op jit(solution)/shard_map/ppermute | solution.py:160
  11.6 43.3 %copy-start.4 = (s32[1,1,16]{2,1,0:T(1,128)S(1)}, s32[1,1,16]{2,1,0:T(1,128)}, u32[]{:S(2)}) copy-start(s32[1,1,16]{2,1,0:T(1,128)} %param.12) | copy-start | bytes 196
  23.9 31.0 %collective-permute-start.12 = (bf16[512,1024]{1,0:T(8,128)(2,1)S(1)}, bf16[512,1024]{1,0:T(8,128)(2,1)}, u32[]{:S(2)}, u32[]{:S(2)}) collective-permute-start(bf16[512,1024]{1,0:T(8,128)(2,1)S(1)} %get-tuple-element.26.refs_9_), channel_id=1, source_target_pairs={{0,8},{8,16},{16,24},{24,28},{28,20},{20,12},{12,4},{4,0},{1,9},{9... | collective-permute-start | bytes 3145736 | tf_op jit(solution)/shard_map/ppermute | solution.py:349
  34.3 22.7 %collective-permute-start.4 = (bf16[2048,256]{1,0:T(8,128)(2,1)S(1)}, bf16[2048,256]{1,0:T(8,128)(2,1)}, u32[]{:S(2)}, u32[]{:S(2)}) collective-permute-start(bf16[2048,256]{1,0:T(8,128)(2,1)S(1)} %maximum_maximum_fusion), channel_id=1, source_target_pairs={{0,1},{1,0},{2,3},{3,2},{4,5},{5,4},{6,7},{7,6},{8,9},{9,8},{10,11... | collective-permute-start | bytes 3145736 | tf_op jit(solution)/shard_map/ppermute | solution.py:164
  34.4 41.6 %collective-permute-start.10 = (bf16[512,1024]{1,0:T(8,128)(2,1)}, bf16[512,1024]{1,0:T(8,128)(2,1)}, u32[]{:S(2)}, u32[]{:S(2)}) collective-permute-start(bf16[512,1024]{1,0:T(8,128)(2,1)} %collective-permute-done.3.refs_6_), channel_id=1, source_target_pairs={{8,0},{16,8},{24,16},{28,24},{20,28},{12,20},{4,12},{0,4},{9,1},{1... | collective-permute-start | bytes 3145736 | tf_op jit(solution)/shard_map/ppermute | solution.py:351
  36.0 41.5 %collective-permute-start.8 = (bf16[512,1024]{1,0:T(8,128)(2,1)}, bf16[512,1024]{1,0:T(8,128)(2,1)}, u32[]{:S(2)}, u32[]{:S(2)}) collective-permute-start(bf16[512,1024]{1,0:T(8,128)(2,1)} %collective-permute-done.2.refs_5_), channel_id=1, source_target_pairs={{0,8},{8,16},{16,24},{24,28},{28,20},{20,12},{12,4},{4,0},{1,9},{9... | collective-permute-start | bytes 3145736 | tf_op jit(solution)/shard_map/ppermute | solution.py:349
  53.5 43.5 %collective-permute-start.16 = (bf16[512,1024]{1,0:T(8,128)(2,1)}, bf16[512,1024]{1,0:T(8,128)(2,1)}, u32[]{:S(2)}, u32[]{:S(2)}) collective-permute-start(bf16[512,1024]{1,0:T(8,128)(2,1)} %collective-permute-done.15.refs_11_), channel_id=1, source_target_pairs={{8,0},{16,8},{24,16},{28,24},{20,28},{12,20},{4,12},{0,4},{9,1},{1... | collective-permute-start | bytes 3145736 | tf_op jit(solution)/shard_map/ppermute | solution.py:351
  55.0 42.3 %collective-permute-start.13 = (bf16[512,1024]{1,0:T(8,128)(2,1)}, bf16[512,1024]{1,0:T(8,128)(2,1)}, u32[]{:S(2)}, u32[]{:S(2)}) collective-permute-start(bf16[512,1024]{1,0:T(8,128)(2,1)} %collective-permute-done.12.refs_10_), channel_id=1, source_target_pairs={{0,8},{8,16},{16,24},{24,28},{28,20},{20,12},{12,4},{4,0},{1,9},{9... | collective-permute-start | bytes 3145736 | tf_op jit(solution)/shard_map/ppermute | solution.py:349
  58.9 65.6 %copy-start = (bf16[512,1024]{1,0:T(8,128)(2,1)}, bf16[512,1024]{1,0:T(8,128)(2,1)S(1)}, u32[]{:S(2)}) copy-start(bf16[512,1024]{1,0:T(8,128)(2,1)S(1)} %attend.1.refs_0_) | copy-start | bytes 3145732
  58.9 38.4 %collective-permute-start.5 = (bf16[512,1024]{1,0:T(8,128)(2,1)S(1)}, bf16[512,1024]{1,0:T(8,128)(2,1)S(1)}, u32[]{:S(2)}, u32[]{:S(2)}) collective-permute-start(bf16[512,1024]{1,0:T(8,128)(2,1)S(1)} %attend.1.refs_0_), channel_id=1, source_target_pairs={{0,1},{1,0},{2,3},{3,2},{4,5},{5,4},{6,7},{7,6},{8,9},{9,8},{10,11... | collective-permute-start | bytes 3145736 | tf_op jit(solution)/shard_map/ppermute | solution.py:373
  76.0 23.1 %collective-permute-start.6 = (bf16[512,1024]{1,0:T(8,128)(2,1)S(1)}, bf16[512,1024]{1,0:T(8,128)(2,1)S(1)}, u32[]{:S(2)}, u32[]{:S(2)}) collective-permute-start(bf16[512,1024]{1,0:T(8,128)(2,1)S(1)} %attend.1.refs_0_), channel_id=1, source_target_pairs={{0,2},{1,3},{2,0},{3,1},{4,6},{5,7},{6,4},{7,5},{8,10},{9,11},{10,... | collective-permute-start | bytes 3145736 | tf_op jit(solution)/shard_map/ppermute | solution.py:372
  77.5 41.3 %collective-permute-start.9 = (bf16[512,1024]{1,0:T(8,128)(2,1)}, bf16[512,1024]{1,0:T(8,128)(2,1)}, u32[]{:S(2)}, u32[]{:S(2)}) collective-permute-start(bf16[512,1024]{1,0:T(8,128)(2,1)} %collective-permute-done.8.refs_7_), channel_id=1, source_target_pairs={{0,8},{8,16},{16,24},{24,28},{28,20},{20,12},{12,4},{4,0},{1,9},{9... | collective-permute-start | bytes 3145736 | tf_op jit(solution)/shard_map/ppermute | solution.py:349
  97.0 26.4 %collective-permute-start.17 = (bf16[512,1024]{1,0:T(8,128)(2,1)}, bf16[512,1024]{1,0:T(8,128)(2,1)}, u32[]{:S(2)}, u32[]{:S(2)}) collective-permute-start(bf16[512,1024]{1,0:T(8,128)(2,1)} %collective-permute-done.16.refs_13_), channel_id=1, source_target_pairs={{8,0},{16,8},{24,16},{28,24},{20,28},{12,20},{4,12},{0,4},{9,1},{1... | collective-permute-start | bytes 3145736 | tf_op jit(solution)/shard_map/ppermute | solution.py:351
  97.3 27.2 %collective-permute-start.7 = (bf16[512,1024]{1,0:T(8,128)(2,1)S(1)}, bf16[512,1024]{1,0:T(8,128)(2,1)}, u32[]{:S(2)}, u32[]{:S(2)}) collective-permute-start(bf16[512,1024]{1,0:T(8,128)(2,1)S(1)} %attend.1.refs_0_), channel_id=1, source_target_pairs={{0,3},{1,2},{2,1},{3,0},{4,7},{5,6},{6,5},{7,4},{8,11},{9,10},{10,... | collective-permute-start | bytes 3145736 | tf_op jit(solution)/shard_map/ppermute | solution.py:374
  97.3 1.7 %copy-start.1 = (bf16[512,1024]{1,0:T(8,128)(2,1)}, bf16[512,1024]{1,0:T(8,128)(2,1)S(1)}, u32[]{:S(2)}) copy-start(bf16[512,1024]{1,0:T(8,128)(2,1)S(1)} %collective-permute-done.5.refs_1_) | copy-start | bytes 3145732
  97.3 48.6 %collective-permute-start.11 = (bf16[512,1024]{1,0:T(8,128)(2,1)}, bf16[512,1024]{1,0:T(8,128)(2,1)}, u32[]{:S(2)}, u32[]{:S(2)}) collective-permute-start(bf16[512,1024]{1,0:T(8,128)(2,1)} %collective-permute-done.10.refs_8_), channel_id=1, source_target_pairs={{8,0},{16,8},{24,16},{28,24},{20,28},{12,20},{4,12},{0,4},{9,1},{1... | collective-permute-start | bytes 3145736 | tf_op jit(solution)/shard_map/ppermute | solution.py:351
  99.1 1.0 copy-start.2
  99.1 46.8 %collective-permute-start.14 = (bf16[512,1024]{1,0:T(8,128)(2,1)}, bf16[512,1024]{1,0:T(8,128)(2,1)}, u32[]{:S(2)}, u32[]{:S(2)}) collective-permute-start(bf16[512,1024]{1,0:T(8,128)(2,1)} %collective-permute-done.13.refs_12_), channel_id=1, source_target_pairs={{0,8},{8,16},{16,24},{24,28},{28,20},{20,12},{12,4},{4,0},{1,9},{9... | collective-permute-start | bytes 3145736 | tf_op jit(solution)/shard_map/ppermute | solution.py:349
  118.8 44.1 %collective-permute-start.18 = (bf16[512,1024]{1,0:T(8,128)(2,1)}, bf16[512,1024]{1,0:T(8,128)(2,1)}, u32[]{:S(2)}, u32[]{:S(2)}) collective-permute-start(bf16[512,1024]{1,0:T(8,128)(2,1)} %collective-permute-done.9.refs_4_), channel_id=1, source_target_pairs={{0,8},{8,16},{16,24},{24,28},{28,20},{20,12},{12,4},{4,0},{1,9},{9... | collective-permute-start | bytes 3145736 | tf_op jit(solution)/shard_map/ppermute | solution.py:349
  123.4 42.6 %collective-permute-start.19 = (bf16[512,1024]{1,0:T(8,128)(2,1)}, bf16[512,1024]{1,0:T(8,128)(2,1)}, u32[]{:S(2)}, u32[]{:S(2)}) collective-permute-start(bf16[512,1024]{1,0:T(8,128)(2,1)} %collective-permute-done.17.refs_7_), channel_id=1, source_target_pairs={{8,0},{16,8},{24,16},{28,24},{20,28},{12,20},{4,12},{0,4},{9,1},{1... | collective-permute-start | bytes 3145736 | tf_op jit(solution)/shard_map/ppermute | solution.py:351

commit v11 on v6

--- a/solution.py
+++ b/solution.py
@@ -21,7 +21,9 @@
 GROUP = 4
 
 
-def attention_kernel(heads, slots, meta_ref, q_hbm, old_hbm, *refs):
+def attention_kernel(
+    heads, slots, part_rows, first_rows, targets, meta_ref, q_hbm, old_hbm, *refs
+):
     kv_parts, (out_ref, q_ref, kv_ref, peak_ref, denom_ref, acc_ref, sems) = refs[:-7], refs[-7:]
     live = meta_ref[0]
     flag = meta_ref[1]
@@ -35,11 +37,15 @@
     @pl.when(flag > 0)
     def _():
         copies = [pltpu.make_async_copy(q_hbm, q_ref, sems.at[0])]
-        for index, part in enumerate(kv_parts):
-            rows = part.shape[0]
-            start = pl.multiple_of(meta_ref[2 + slots + index] * rows, rows)
+        for index, (part, first_row, target) in enumerate(zip(kv_parts, first_rows, targets)):
+            column = pl.multiple_of(meta_ref[2 + slots + 2 * index] * HEAD_SIZE, HEAD_SIZE)
+            start = pl.multiple_of(meta_ref[3 + slots + 2 * index] * part_rows, part_rows)
             copies.append(
-                pltpu.make_async_copy(part, kv_ref.at[pl.ds(start, rows), :], sems.at[1 + index])
+                pltpu.make_async_copy(
+                    part.at[pl.ds(first_row, part_rows), pl.ds(column, HEAD_SIZE)],
+                    kv_ref.at[pl.ds(start, part_rows), pl.ds(target * HEAD_SIZE, HEAD_SIZE)],
+                    sems.at[1 + index],
+                )
             )
         for copy in copies:
             copy.start()
@@ -100,24 +106,27 @@
             out_ref[:, head * HEAD_SIZE : (head + 1) * HEAD_SIZE] = result.T.astype(jnp.bfloat16)
 
 
-def attend(block_list, live, flag, queries, old, kv_parts, places):
+def attend(block_list, live, flag, queries, old, key_values):
+    part_rows, sources = key_values
+    arrays, first_rows, heads_at, targets, places = zip(*sources)
     rows, width = queries.shape
     heads = width // HEAD_SIZE
     slots = block_list.shape[0]
-    meta = jnp.concatenate([live[None], flag[None], block_list, *[p[None] for p in places]])
+    spots = [value[None] for pair in zip(heads_at, places) for value in pair]
+    meta = jnp.concatenate([live[None], flag[None], block_list, *spots])
     in_hbm = pl.BlockSpec(memory_space=pltpu.HBM)
     return pl.pallas_call(
-        functools.partial(attention_kernel, heads, slots),
+        functools.partial(attention_kernel, heads, slots, part_rows, first_rows, targets),
         out_shape=jax.ShapeDtypeStruct((rows, width), jnp.bfloat16),
-        in_specs=[pl.BlockSpec(memory_space=pltpu.SMEM)] + [in_hbm] * (2 + len(kv_parts)),
+        in_specs=[pl.BlockSpec(memory_space=pltpu.SMEM)] + [in_hbm] * (2 + len(arrays)),
         out_specs=pl.BlockSpec(memory_space=pltpu.VMEM),
         scratch_shapes=[
             pltpu.VMEM((rows, width), jnp.bfloat16),
-            pltpu.VMEM((sum(p.shape[0] for p in kv_parts), 2 * HEAD_SIZE), jnp.bfloat16),
+            pltpu.VMEM((part_rows * len(arrays) // 2, 2 * HEAD_SIZE), jnp.bfloat16),
             pltpu.VMEM((heads, 1, rows), jnp.float32),
             pltpu.VMEM((heads, 1, rows), jnp.float32),
             pltpu.VMEM((heads, HEAD_SIZE, rows), jnp.float32),
-            pltpu.SemaphoreType.DMA((1 + len(kv_parts),)),
+            pltpu.SemaphoreType.DMA((1 + len(arrays),)),
         ],
         compiler_params=pltpu.CompilerParams(vmem_limit_bytes=24 << 20),
         cost_estimate=pl.CostEstimate(
@@ -128,31 +137,52 @@
         meta,
         *[
             pltpu.with_memory_space_constraint(x, pltpu.HBM)
-            for x in (queries, old, *kv_parts)
+            for x in (queries, old, *arrays)
         ],
     )
 
 
-def own_head_keys_values(keys, values):
+def own_head_keys_values(keys, values, gate=lambda x: x):
     groups = lax.axis_size("ka")
     me = lax.axis_index("ka")
     rows = keys.shape[0]
-    if groups == KEY_VALUE_HEADS:
-
-        def head_of(device):
-            start = (0, device * HEAD_SIZE)
-            return jnp.concatenate(
-                [lax.dynamic_slice(x, start, (rows, HEAD_SIZE)) for x in (keys, values)], axis=1
-            )
-
-        parts, places = [head_of(me)], [me]
-        for step in range(1, groups):
-            partner = jnp.bitwise_xor(me, step)
-            parts.append(
-                lax.ppermute(head_of(partner), "ka", [(i, i ^ step) for i in range(groups)])
-            )
-            places.append(partner)
-        return parts, places
+    if groups == KEY_VALUE_HEADS == 4:
+        x, core = me // 2, me % 2
+        pair = 2 * HEAD_SIZE
+
+        def heads_of(array, chip):
+            return lax.dynamic_slice(array, (0, chip * pair), (rows, pair))
+
+        def head_of(array, head):
+            return lax.dynamic_slice(array, (0, head * HEAD_SIZE), (rows, HEAD_SIZE))
+
+        across = [
+            lax.ppermute(heads_of(a, 1 - x), "ka", [(i, i ^ 2) for i in range(4)])
+            for a in (keys, values)
+        ]
+        across = gate(across)
+        beside = lax.ppermute(
+            jnp.concatenate(
+                [
+                    jnp.concatenate([head_of(a, 2 * x + 1 - core) for a in (keys, values)], axis=1),
+                    jnp.concatenate([head_of(a, 1 - core) for a in across], axis=1),
+                ],
+                axis=0,
+            ),
+            "ka",
+            [(i, i ^ 1) for i in range(4)],
+        )
+        near, far = jnp.bitwise_xor(me, 1), jnp.bitwise_xor(me, 3)
+        sources = [
+            (keys, 0, me, 0, me),
+            (values, 0, me, 1, me),
+            (across[0], 0, core, 0, jnp.bitwise_xor(me, 2)),
+            (across[1], 0, core, 1, jnp.bitwise_xor(me, 2)),
+        ]
+        for side in range(2):
+            for row, place in ((0, near), (rows, far)):
+                sources.append((beside, row, jnp.int32(side), side, place))
+        return rows, sources
     both = jnp.concatenate(
         [
             keys.reshape(rows, KEY_VALUE_HEADS, HEAD_SIZE),
@@ -164,7 +194,8 @@
     everything = lax.all_to_all(
         both.reshape(rows, groups * 2 * HEAD_SIZE), "ka", split_axis=1, concat_axis=0, tiled=True
     )
-    return [everything], [jnp.int32(0)]
+    first = jnp.int32(0)
+    return everything.shape[0], [(everything, 0, jnp.int32(side), side, first) for side in range(2)]
 
 
 ROW_TILE = 256
@@ -356,14 +387,16 @@
         return lax.ppermute(piece, "ka", ACROSS_CORE)
 
     tie = lax.optimization_barrier
-    kept_up, kept_down = hop([kept], [kept], 0)
-    taken = lax.ppermute(given, "pb", ACROSS_Y)
-    queries, keys, values, old = inputs
-    parts, places = own_head_keys_values(keys, values)
-    parts, kept_up[0], kept_down[0], taken = tie((parts, kept_up[0], kept_down[0], taken))
+    first = [*hop([kept], [kept], 0), lax.ppermute(given, "pb", ACROSS_Y)]
+
+    def gate(value):
+        value, first[:] = lax.optimization_barrier((value, first))
+        return value
+
+    attn = attend_with(inputs, gate)
+    kept_up, kept_down, taken = first
     kept_up, kept_down = hop(kept_up, kept_down, 1)
     taken_up, taken_down = hop([taken], [taken], 0)
-    attn = attend_with(queries, old, parts, places)
     attn, kept_up[1], kept_down[1] = tie((attn, kept_up[1], kept_down[1]))
     kept_end = lax.ppermute(kept_up[1] + kept_down[1], "pb", OUTWARD)
     across_y = lax.ppermute(attn, "pb", ACROSS_Y)
@@ -379,6 +412,7 @@
         ends.append(lax.ppermute(piece, "pb", OUTWARD))
         start += width
     corner = lax.ppermute(across_y, "ka", ACROSS_X)
+    corner, kept_end = tie((corner, kept_end))
     own_rows = [attn, other_core(attn), across_x, other_core(across_x)]
     other_rows = [across_y, other_core(across_y), corner, other_core(corner)]
 
@@ -419,14 +453,17 @@
 def shards(queries, keys, values, block_ids, counts, refresh, cached_attn, wo):
     groups = lax.axis_size("ka")
 
-    def attend_with(queries, old, parts, places):
-        return attend(block_ids[0, 0], counts[0, 0], refresh[0, 0], queries, old, parts, places)
-
+    def attend_with(inputs, gate=lambda x: x):
+        queries, keys, values, old = inputs
+        return attend(
+            block_ids[0, 0], counts[0, 0], refresh[0, 0], queries, old, own_head_keys_values(keys, values, gate)
+        )
+
+    inputs = (queries[0], keys, values, cached_attn[0])
     if lax.axis_size("pb") == 8 and groups == 4:
-        mixed = project(wo, (queries[0], keys, values, cached_attn[0]), attend_with)
+        mixed = project(wo, inputs, attend_with)
     else:
-        attn = attend_with(queries[0], cached_attn[0], *own_head_keys_values(keys, values))
-        attn_full = lax.all_gather(attn, "ka", axis=1, tiled=True)
+        attn_full = lax.all_gather(attend_with(inputs), "ka", axis=1, tiled=True)
         mixed = jnp.dot(
             attn_full, lax.all_gather(wo, "pb", axis=0, tiled=True), preferred_element_type=jnp.float32
         ).astype(jnp.bfloat16)

time: 191 us -> 190 us (level)
  waiting for transfers between devices: 116 us -> 96.7 us
  Pallas kernels: 27.7 us -> 44.6 us
  starting transfers between devices: 37.1 us -> 33.9 us
  local copies, waits for them, and re-layouts: 5.55 us -> 8.49 us
    ppermute x4, waiting for transfers between devices: 68.1 us -> 33.4 us  [hop(): down = down + [lax.ppermute(down[-1], 'pb', DOWN[step])]]
    pallas_call x1, Pallas kernels: 1.82 us -> 18.7 us  [attend(): pl.pallas_call(functools.partial(attention_kernel, heads, slots, part_row...]
    ppermute x4, waiting for transfers between devices: 14.4 us -> 21.7 us  [the longest x2 21.7 us: own_head_keys_values(): lax.ppermute(heads_of(a, 1 - x), 'ka', [(i, i ^ 2) for i in range(4)])]
    ppermute x1, waiting for transfers between devices: 0.01 us -> 5.56 us  [project(): corner = lax.ppermute(across_y, 'ka', ACROSS_X)]
    ppermute x3, waiting for transfers between devices: 12.2 us -> 16.2 us  [project(): received.append(lax.ppermute(other, 'pb', ACROSS_Y))]
    ppermute x4, waiting for transfers between devices: 3 us -> 0.01 us  [hop(): up = up + [lax.ppermute(up[-1], 'pb', UP[step])]]
    ppermute x4, starting transfers between devices: 5.89 us -> 3.68 us  [the longest x2 2.03 us: own_head_keys_values(): lax.ppermute(heads_of(a, 1 - x), 'ka', [(i, i ^ 2) for i in range(4)])]
    ppermute x4, starting transfers between devices: 12.1 us -> 14.2 us  [hop(): up = up + [lax.ppermute(up[-1], 'pb', UP[step])]]
  transfers between devices with their start and end apart: 26 -> 26, of which waited for: 10 -> 9; matrix products, arithmetic and copies ran while one was open for 2% -> 3% of each run, Pallas kernels for 13% -> 23%
where the time goes in v11:
time: 190 us; the launch traced here: 189 us
  waiting for transfers between devices  96.7 us (51%)
  Pallas kernels  44.6 us (23%)
  starting transfers between devices  33.9 us (18%)
  local copies, waits for them, and re-layouts  8.49 us (4%)
  other arithmetic  3.67 us (2%)
    ppermute x4, waiting for transfers between devices, hop(): down = down + [lax.ppermute(down[-1], 'pb', DOWN[step])]  33.4 us
    pallas_call x5, Pallas kernels, slab_product(): pl.pallas_call(functools.partial(slab_product_kernel, kind, tuple((distan...  23.9 us
    ppermute x2, waiting for transfers between devices, own_head_keys_values(): lax.ppermute(heads_of(a, 1 - x), 'ka', [(i, i ^ 2) for i in range(4)])  21.7 us
    pallas_call x1, Pallas kernels, attend(): pl.pallas_call(functools.partial(attention_kernel, heads, slots, part_row...  18.7 us
    ppermute x3, waiting for transfers between devices, project(): received.append(lax.ppermute(other, 'pb', ACROSS_Y))  16.2 us
    ppermute x1, waiting for transfers between devices, project(): kept_end = lax.ppermute(kept_up[1] + kept_down[1], 'pb', OUTWARD)  15.7 us
    ppermute x4, starting transfers between devices, hop(): up = up + [lax.ppermute(up[-1], 'pb', UP[step])]  14.2 us
    ppermute x1, waiting for transfers between devices, project(): corner = lax.ppermute(across_y, 'ka', ACROSS_X)  5.56 us
  transfers between devices with their start and end apart: 26, of which 9 were waited for; matrix products, arithmetic and copies ran while one was open for 3% of the time, Pallas kernels for 23%

profile of v11, /device:TPU:0, one launch (start us, length us, event | category | flops | bytes accessed | tf_op | source)
XLA Modules:
  0.0 189.2 jit_solution(1240536193499768281)
XLA Ops:
  0.0 2.8 %constant_dynamic-slice_fusion.6 = (bf16[512,1024]{1,0:T(8,128)(2,1)}, bf16[512,1024]{1,0:T(8,128)(2,1)S(1)}) fusion(bf16[512,2048]{1,0:T(8,128)(2,1)} %param.15, s32[]{:T(128)S(6)} %select_n.40, s32[]{:T(128)S(6)} %select_n.39), kind=kLoop, calls=%fused_computation.10 | loop fusion | bytes 4194312 | tf_op jit(solution)/shard_map/dynamic_slice | solution.py:378
  2.8 5.9 %collective-permute-start.2 = (bf16[512,1024]{1,0:T(8,128)(2,1)S(1)}, bf16[512,1024]{1,0:T(8,128)(2,1)}, u32[]{:S(2)}, u32[]{:S(2)}) collective-permute-start(bf16[512,1024]{1,0:T(8,128)(2,1)S(1)} %get-tuple-element.38.refs_8_), channel_id=1, source_target_pairs={{0,8},{4,12},{8,16},{12,20},{16,24},{20,28},{1,9},{5,13},{9,17},{1... | collective-permute-start | bytes 3145736 | tf_op jit(solution)/shard_map/ppermute | solution.py:382
  8.7 1.3 collective-permute-start.3
  10.0 1.6 collective-permute-start.4
  12.4 1.5 collective-permute-start.1
  15.4 12.2 %collective-permute-done.1.refs_3_ = bf16[1024,256]{1,0:T(8,128)(2,1)} collective-permute-done((bf16[1024,256]{1,0:T(8,128)(2,1)}, bf16[1024,256]{1,0:T(8,128)(2,1)}, u32[]{:S(2)}, u32[]{:S(2)}) %collective-permute-start.1) | collective-permute-done | bytes 524320 | tf_op jit(solution)/shard_map/ppermute | solution.py:160
  27.6 9.5 %collective-permute-done.refs_2_ = bf16[1024,256]{1,0:T(8,128)(2,1)} collective-permute-done((bf16[1024,256]{1,0:T(8,128)(2,1)}, bf16[1024,256]{1,0:T(8,128)(2,1)}, u32[]{:S(2)}, u32[]{:S(2)}) %collective-permute-start) | collective-permute-done | bytes 524320 | tf_op jit(solution)/shard_map/ppermute | solution.py:160
  39.1 1.3 collective-permute-start.7
  41.8 6.8 %collective-permute-start.11 = (bf16[512,1024]{1,0:T(8,128)(2,1)}, bf16[512,1024]{1,0:T(8,128)(2,1)S(1)}, u32[]{:S(2)}, u32[]{:S(2)}) collective-permute-start(bf16[512,1024]{1,0:T(8,128)(2,1)} %collective-permute-done.4.refs_8_), channel_id=1, source_target_pairs={{0,8},{4,12},{8,16},{12,20},{16,24},{20,28},{1,9},{5,13},{9,17},{1... | collective-permute-start | bytes 3145736 | tf_op jit(solution)/shard_map/ppermute | solution.py:382
  48.7 1.3 collective-permute-start.12
  51.0 18.7 %attend.1.refs_0_ = bf16[512,1024]{1,0:T(8,128)(2,1)S(1)} custom-call(s32[34]{0:T(128)S(1)} %concatenate.12.meta_ref, bf16[512,1024]{1,0:T(8,128)(2,1)} %bitcast.15, bf16[512,1024]{1,0:T(8,128)(2,1)} %bitcast.16, bf16[1024,512]{1,0:T(8,128)(2,1)} %refs_0_, bf16[1024,512]{1,0:T(8,128)(2,1)} %refs_1_, bf16[1024,256]{1,0:T(8,128)(2,1)} %collective-permute-done.refs_2_, ...), custom_call_target="tpu_custom_call" | custom-call | flops 1048576 | bytes 1048576 | tf_op jit(solution)/shard_map/attend/pallas_call | solution.py:118
  69.7 1.6 collective-permute-start.10
  71.5 1.6 add.51
  73.1 1.3 collective-permute-start.16
  74.5 17.4 %collective-permute-done.12.refs_11_.refs_10_ = bf16[512,1024]{1,0:T(8,128)(2,1)S(1)} collective-permute-done((bf16[512,1024]{1,0:T(8,128)(2,1)}, bf16[512,1024]{1,0:T(8,128)(2,1)S(1)}, u32[]{:S(2)}, u32[]{:S(2)}) %collective-permute-start.12) | collective-permute-done | bytes 1048608 | tf_op jit(solution)/shard_map/ppermute | solution.py:383
  91.9 2.9 %collective-permute-done.10.refs_2_ = bf16[512,1024]{1,0:T(8,128)(2,1)S(1)} collective-permute-done((bf16[512,1024]{1,0:T(8,128)(2,1)S(1)}, bf16[512,1024]{1,0:T(8,128)(2,1)S(1)}, u32[]{:S(2)}, u32[]{:S(2)}) %collective-permute-start.10) | collective-permute-done | bytes 1048608 | tf_op jit(solution)/shard_map/ppermute | solution.py:403
  94.8 1.2 collective-permute-done.9.refs_4_
  97.2 1.3 collective-permute-start.19
  98.6 15.7 %collective-permute-done.16.refs_13_ = bf16[512,1024]{1,0:T(8,128)(2,1)S(1)} collective-permute-done((bf16[512,1024]{1,0:T(8,128)(2,1)S(1)}, bf16[512,1024]{1,0:T(8,128)(2,1)S(1)}, u32[]{:S(2)}, u32[]{:S(2)}) %collective-permute-start.16) | collective-permute-done | bytes 1048608 | tf_op jit(solution)/shard_map/ppermute | solution.py:401
  114.4 5.6 %collective-permute-done.15.refs_6_ = bf16[512,1024]{1,0:T(8,128)(2,1)} collective-permute-done((bf16[512,1024]{1,0:T(8,128)(2,1)S(1)}, bf16[512,1024]{1,0:T(8,128)(2,1)}, u32[]{:S(2)}, u32[]{:S(2)}) %collective-permute-start.15) | collective-permute-done | bytes 1048608 | tf_op jit(solution)/shard_map/ppermute | solution.py:414
  120.4 16.0 %collective-permute-done.19.refs_12_ = bf16[512,1024]{1,0:T(8,128)(2,1)S(1)} collective-permute-done((bf16[512,1024]{1,0:T(8,128)(2,1)S(1)}, bf16[512,1024]{1,0:T(8,128)(2,1)S(1)}, u32[]{:S(2)}, u32[]{:S(2)}) %collective-permute-start.19) | collective-permute-done | bytes 1048608 | tf_op jit(solution)/shard_map/ppermute | solution.py:383
  137.5 1.3 collective-permute-start.21
  138.8 1.3 collective-permute-start.20
  141.9 1.5 collective-permute-start.22
  143.5 8.8 %product_kept.1.refs_13_ = f32[1024,1024]{1,0:T(8,128)S(1)} custom-call(s32[3]{0:T(128)S(1)} %pad_add_fusion.where_ref, bf16[512,1024]{1,0:T(8,128)(2,1)} %copy-done, bf16[512,1024]{1,0:T(8,128)(2,1)} %copy-done.4, bf16[512,1024]{1,0:T(8,128)(2,1)} %copy-done.2, bf16[512,1024]{1,0:T(8,128)(2,1)} %copy-done.5, bf16[512,1024]{1,0:T(8,128)(2,1)} %copy-done.3, ...), custom_call_target="tpu_custom_call" | custom-call | flops 1048576 | bytes 1048576 | tf_op jit(solution)/shard_map/product_kept/pallas_call | solution.py:299
  152.3 7.1 %product_near.1 = (f32[1024,384]{1,0:T(8,128)S(1)}, f32[1024,384]{1,0:T(8,128)S(1)}, f32[1024,256]{1,0:T(8,128)S(1)}) custom-call(s32[3]{0:T(128)S(1)} %pad_add_fusion.where_ref, bf16[512,1024]{1,0:T(8,128)(2,1)} %copy-done, bf16[512,1024]{1,0:T(8,128)(2,1)} %copy-done.4, bf16[512,1024]{1,0:T(8,128)(2,1)} %copy-done.2, bf16[512,1024]{1,0:T(8,128)(2,1)} %copy-done.5, ...), custom_call_target="tpu_custom_call" | custom-call | flops 1048576 | bytes 1048576 | tf_op jit(solution)/shard_map/product_near/pallas_call | solution.py:299
  159.4 2.8 %product_far.4 = (bf16[512,384]{1,0:T(8,128)(2,1)S(1)}, bf16[512,384]{1,0:T(8,128)(2,1)S(1)}) custom-call(s32[3]{0:T(128)S(1)} %pad_add_fusion.where_ref, bf16[512,1024]{1,0:T(8,128)(2,1)} %copy-done, bf16[512,1024]{1,0:T(8,128)(2,1)} %copy-done.4, bf16[512,1024]{1,0:T(8,128)(2,1)} %copy-done.2, bf16[512,1024]{1,0:T(8,128)(2,1)} %copy-done.5, ...), custom_call_target="tpu_custom_call" | custom-call | flops 1048576 | bytes 1048576 | tf_op jit(solution)/shard_map/product_far/pallas_call | solution.py:299
  163.5 2.7 %product_far.3 = (bf16[512,384]{1,0:T(8,128)(2,1)S(1)}, bf16[512,384]{1,0:T(8,128)(2,1)S(1)}) custom-call(s32[3]{0:T(128)S(1)} %pad_add_fusion.where_ref, bf16[512,1024]{1,0:T(8,128)(2,1)} %copy-done, bf16[512,1024]{1,0:T(8,128)(2,1)} %copy-done.4, bf16[512,1024]{1,0:T(8,128)(2,1)} %copy-done.2, bf16[512,1024]{1,0:T(8,128)(2,1)} %copy-done.5, ...), custom_call_target="tpu_custom_call" | custom-call | flops 1048576 | bytes 1048576 | tf_op jit(solution)/shard_map/product_far/pallas_call | solution.py:299
  166.2 1.6 collective-permute-start.23
  167.9 2.4 %product_far.5 = (bf16[512,256]{1,0:T(8,128)(2,1)S(1)}, bf16[512,256]{1,0:T(8,128)(2,1)S(1)}) custom-call(s32[3]{0:T(128)S(1)} %pad_add_fusion.where_ref, bf16[512,1024]{1,0:T(8,128)(2,1)} %copy-done, bf16[512,1024]{1,0:T(8,128)(2,1)} %copy-done.4, bf16[512,1024]{1,0:T(8,128)(2,1)} %copy-done.2, bf16[512,1024]{1,0:T(8,128)(2,1)} %copy-done.5, ...), custom_call_target="tpu_custom_call" | custom-call | flops 1048576 | bytes 1048576 | tf_op jit(solution)/shard_map/product_far/pallas_call | solution.py:299
  170.9 16.2 %collective-permute-done.25.refs_5_ = bf16[512,256]{1,0:T(8,128)(2,1)S(1)} collective-permute-done((bf16[512,256]{1,0:T(8,128)(2,1)S(1)}, bf16[512,256]{1,0:T(8,128)(2,1)S(1)}, u32[]{:S(2)}, u32[]{:S(2)}) %collective-permute-start.25) | collective-permute-done | bytes 262176 | tf_op jit(solution)/shard_map/ppermute | solution.py:448
  187.1 2.0 %finish.1 = bf16[512,2048]{1,0:T(8,128)(2,1)} custom-call(s32[3]{0:T(128)} %copy-done.1, bf16[512,384]{1,0:T(8,128)(2,1)S(1)} %get-tuple-element.55.refs_0_, bf16[512,384]{1,0:T(8,128)(2,1)S(1)} %get-tuple-element.57.refs_1_, bf16[512,256]{1,0:T(8,128)(2,1)S(1)} %get-tuple-element.59.refs_2_, bf16[512,384]{1,0:T(8,128)(2,1)S(1)} %collective-permute-done.23.refs_3_, ...), custom_call_target="tpu_custom_call" | custom-call | flops 1048576 | bytes 1048576 | tf_op jit(solution)/shard_map/finish/pallas_call | solution.py:351
  (74 shorter events, 12.2 us)
Async XLA Ops:
  2.8 34.3 %collective-permute-start.2 = (bf16[512,1024]{1,0:T(8,128)(2,1)S(1)}, bf16[512,1024]{1,0:T(8,128)(2,1)}, u32[]{:S(2)}, u32[]{:S(2)}) collective-permute-start(bf16[512,1024]{1,0:T(8,128)(2,1)S(1)} %get-tuple-element.38.refs_8_), channel_id=1, source_target_pairs={{0,8},{4,12},{8,16},{12,20},{16,24},{20,28},{1,9},{5,13},{9,17},{1... | collective-permute-start | bytes 3145736 | tf_op jit(solution)/shard_map/ppermute | solution.py:382
  8.7 28.4 %collective-permute-start.3 = (bf16[512,1024]{1,0:T(8,128)(2,1)S(1)}, bf16[512,1024]{1,0:T(8,128)(2,1)}, u32[]{:S(2)}, u32[]{:S(2)}) collective-permute-start(bf16[512,1024]{1,0:T(8,128)(2,1)S(1)} %get-tuple-element.38.refs_8_), channel_id=1, source_target_pairs={{8,0},{12,4},{16,8},{20,12},{24,16},{28,20},{9,1},{13,5},{17,9},{2... | collective-permute-start | bytes 3145736 | tf_op jit(solution)/shard_map/ppermute | solution.py:383
  10.0 27.1 %collective-permute-start.4 = (bf16[512,1024]{1,0:T(8,128)(2,1)}, bf16[512,1024]{1,0:T(8,128)(2,1)}, u32[]{:S(2)}, u32[]{:S(2)}) collective-permute-start(bf16[512,1024]{1,0:T(8,128)(2,1)} %get-tuple-element.39), channel_id=1, source_target_pairs={{0,4},{4,0},{8,12},{12,8},{16,20},{20,16},{24,28},{28,24},{1,5},{5... | collective-permute-start | bytes 3145736 | tf_op jit(solution)/shard_map/ppermute | solution.py:390
  12.4 15.2 %collective-permute-start.1 = (bf16[1024,256]{1,0:T(8,128)(2,1)}, bf16[1024,256]{1,0:T(8,128)(2,1)}, u32[]{:S(2)}, u32[]{:S(2)}) collective-permute-start(bf16[1024,256]{1,0:T(8,128)(2,1)} %constant_dynamic-slice_fusion.4), channel_id=1, source_target_pairs={{0,2},{1,3},{2,0},{3,1},{4,6},{5,7},{6,4},{7,5},{8,10},{9,11},{10,... | collective-permute-start | bytes 1572872 | tf_op jit(solution)/shard_map/ppermute | solution.py:160
  14.8 22.3 %collective-permute-start = (bf16[1024,256]{1,0:T(8,128)(2,1)}, bf16[1024,256]{1,0:T(8,128)(2,1)}, u32[]{:S(2)}, u32[]{:S(2)}) collective-permute-start(bf16[1024,256]{1,0:T(8,128)(2,1)} %constant_dynamic-slice_fusion.5), channel_id=1, source_target_pairs={{0,2},{1,3},{2,0},{3,1},{4,6},{5,7},{6,4},{7,5},{8,10},{9,11},{10,... | collective-permute-start | bytes 1572872 | tf_op jit(solution)/shard_map/ppermute | solution.py:160
  38.3 11.7 %collective-permute-start.5 = (bf16[2048,256]{1,0:T(8,128)(2,1)S(1)}, bf16[2048,256]{1,0:T(8,128)(2,1)S(1)}, u32[]{:S(2)}, u32[]{:S(2)}) collective-permute-start(bf16[2048,256]{1,0:T(8,128)(2,1)S(1)} %maximum_maximum_fusion), channel_id=1, source_target_pairs={{0,1},{1,0},{2,3},{3,2},{4,5},{5,4},{6,7},{7,6},{8,9},{9,8},{10,11... | collective-permute-start | bytes 3145736 | tf_op jit(solution)/shard_map/ppermute | solution.py:164
  38.4 31.3 %collective-permute-start.6 = (bf16[512,1024]{1,0:T(8,128)(2,1)}, bf16[512,1024]{1,0:T(8,128)(2,1)S(1)}, u32[]{:S(2)}, u32[]{:S(2)}) collective-permute-start(bf16[512,1024]{1,0:T(8,128)(2,1)} %collective-permute-done.2.refs_9_), channel_id=1, source_target_pairs={{8,16},{12,20},{16,24},{20,28},{9,17},{13,21},{17,25},{21,29},{10,... | collective-permute-start | bytes 3145736 | tf_op jit(solution)/shard_map/ppermute | solution.py:382
  39.1 30.6 %collective-permute-start.7 = (bf16[512,1024]{1,0:T(8,128)(2,1)}, bf16[512,1024]{1,0:T(8,128)(2,1)}, u32[]{:S(2)}, u32[]{:S(2)}) collective-permute-start(bf16[512,1024]{1,0:T(8,128)(2,1)} %collective-permute-done.3.refs_11_), channel_id=1, source_target_pairs={{8,0},{12,4},{16,8},{20,12},{9,1},{13,5},{17,9},{21,13},{10,2},{14... | collective-permute-start | bytes 3145736 | tf_op jit(solution)/shard_map/ppermute | solution.py:383
  41.8 32.6 %collective-permute-start.11 = (bf16[512,1024]{1,0:T(8,128)(2,1)}, bf16[512,1024]{1,0:T(8,128)(2,1)S(1)}, u32[]{:S(2)}, u32[]{:S(2)}) collective-permute-start(bf16[512,1024]{1,0:T(8,128)(2,1)} %collective-permute-done.4.refs_8_), channel_id=1, source_target_pairs={{0,8},{4,12},{8,16},{12,20},{16,24},{20,28},{1,9},{5,13},{9,17},{1... | collective-permute-start | bytes 3145736 | tf_op jit(solution)/shard_map/ppermute | solution.py:382
  48.7 43.2 %collective-permute-start.12 = (bf16[512,1024]{1,0:T(8,128)(2,1)}, bf16[512,1024]{1,0:T(8,128)(2,1)S(1)}, u32[]{:S(2)}, u32[]{:S(2)}) collective-permute-start(bf16[512,1024]{1,0:T(8,128)(2,1)} %collective-permute-done.4.refs_8_), channel_id=1, source_target_pairs={{8,0},{12,4},{16,8},{20,12},{24,16},{28,20},{9,1},{13,5},{17,9},{2... | collective-permute-start | bytes 3145736 | tf_op jit(solution)/shard_map/ppermute | solution.py:383
  69.7 67.8 %copy-start = (bf16[512,1024]{1,0:T(8,128)(2,1)}, bf16[512,1024]{1,0:T(8,128)(2,1)S(1)}, u32[]{:S(2)}) copy-start(bf16[512,1024]{1,0:T(8,128)(2,1)S(1)} %attend.1.refs_0_) | copy-start | bytes 3145732
  69.7 73.8 %copy-start.12 = (bf16[512,1024]{1,0:T(8,128)(2,1)}, bf16[512,1024]{1,0:T(8,128)(2,1)S(1)}, u32[]{:S(2)}) copy-start(bf16[512,1024]{1,0:T(8,128)(2,1)S(1)} %collective-permute-done.6.refs_10_) | copy-start | bytes 3145732
  69.7 25.0 %collective-permute-start.10 = (bf16[512,1024]{1,0:T(8,128)(2,1)S(1)}, bf16[512,1024]{1,0:T(8,128)(2,1)S(1)}, u32[]{:S(2)}, u32[]{:S(2)}) collective-permute-start(bf16[512,1024]{1,0:T(8,128)(2,1)S(1)} %attend.1.refs_0_), channel_id=1, source_target_pairs={{0,2},{1,3},{2,0},{3,1},{4,6},{5,7},{6,4},{7,5},{8,10},{9,11},{10,... | collective-permute-start | bytes 3145736 | tf_op jit(solution)/shard_map/ppermute | solution.py:403
  71.3 24.7 %collective-permute-start.9 = (bf16[512,1024]{1,0:T(8,128)(2,1)S(1)}, bf16[512,1024]{1,0:T(8,128)(2,1)S(1)}, u32[]{:S(2)}, u32[]{:S(2)}) collective-permute-start(bf16[512,1024]{1,0:T(8,128)(2,1)S(1)} %attend.1.refs_0_), channel_id=1, source_target_pairs={{0,4},{4,0},{8,12},{12,8},{16,20},{20,16},{24,28},{28,24},{1,5},{5... | collective-permute-start | bytes 3145736 | tf_op jit(solution)/shard_map/ppermute | solution.py:402
  73.1 41.2 %collective-permute-start.16 = (bf16[512,1024]{1,0:T(8,128)(2,1)S(1)}, bf16[512,1024]{1,0:T(8,128)(2,1)S(1)}, u32[]{:S(2)}, u32[]{:S(2)}) collective-permute-start(bf16[512,1024]{1,0:T(8,128)(2,1)S(1)} %add.51), channel_id=1, source_target_pairs={{8,0},{12,4},{16,24},{20,28},{9,1},{13,5},{17,25},{21,29},{10,2},{... | collective-permute-start | bytes 3145736 | tf_op jit(solution)/shard_map/ppermute | solution.py:401
  74.4 66.5 %copy-start.6 = (bf16[512,1024]{1,0:T(8,128)(2,1)}, bf16[512,1024]{1,0:T(8,128)(2,1)S(1)}, u32[]{:S(2)}) copy-start(bf16[512,1024]{1,0:T(8,128)(2,1)S(1)} %collective-permute-done.11.refs_9_) | copy-start | bytes 3145732
  91.9 49.0 %copy-start.7 = (bf16[512,1024]{1,0:T(8,128)(2,1)}, bf16[512,1024]{1,0:T(8,128)(2,1)S(1)}, u32[]{:S(2)}) copy-start(bf16[512,1024]{1,0:T(8,128)(2,1)S(1)} %collective-permute-done.12.refs_11_.refs_10_) | copy-start | bytes 3145732
  94.8 48.7 %copy-start.2 = (bf16[512,1024]{1,0:T(8,128)(2,1)}, bf16[512,1024]{1,0:T(8,128)(2,1)S(1)}, u32[]{:S(2)}) copy-start(bf16[512,1024]{1,0:T(8,128)(2,1)S(1)} %collective-permute-done.10.refs_2_) | copy-start | bytes 3145732
  96.0 47.5 %copy-start.3 = (bf16[512,1024]{1,0:T(8,128)(2,1)}, bf16[512,1024]{1,0:T(8,128)(2,1)S(1)}, u32[]{:S(2)}) copy-start(bf16[512,1024]{1,0:T(8,128)(2,1)S(1)} %collective-permute-done.9.refs_4_) | copy-start | bytes 3145732
  96.0 23.9 %collective-permute-start.15 = (bf16[512,1024]{1,0:T(8,128)(2,1)S(1)}, bf16[512,1024]{1,0:T(8,128)(2,1)}, u32[]{:S(2)}, u32[]{:S(2)}) collective-permute-start(bf16[512,1024]{1,0:T(8,128)(2,1)S(1)} %collective-permute-done.9.refs_4_), channel_id=1, source_target_pairs={{0,2},{1,3},{2,0},{3,1},{4,6},{5,7},{6,4},{7,5},{8,10},{9,11},{10,... | collective-permute-start | bytes 3145736 | tf_op jit(solution)/shard_map/ppermute | solution.py:414
  96.5 23.4 %collective-permute-start.18 = (bf16[512,1024]{1,0:T(8,128)(2,1)S(1)}, bf16[512,1024]{1,0:T(8,128)(2,1)S(1)}, u32[]{:S(2)}, u32[]{:S(2)}) collective-permute-start(bf16[512,1024]{1,0:T(8,128)(2,1)S(1)} %collective-permute-done.11.refs_9_), channel_id=1, source_target_pairs={{8,16},{12,20},{16,24},{20,28},{9,17},{13,21},{17,25},{21,29},{10,... | collective-permute-start | bytes 3145736 | tf_op jit(solution)/shard_map/ppermute | solution.py:382
  97.2 39.2 %collective-permute-start.19 = (bf16[512,1024]{1,0:T(8,128)(2,1)S(1)}, bf16[512,1024]{1,0:T(8,128)(2,1)S(1)}, u32[]{:S(2)}, u32[]{:S(2)}) collective-permute-start(bf16[512,1024]{1,0:T(8,128)(2,1)S(1)} %collective-permute-done.12.refs_11_.refs_10_), channel_id=1, source_target_pairs={{8,0},{12,4},{16,8},{20,12},{9,1},{13,5},{17,9},{21,13},{10,2},{14... | collective-permute-start | bytes 3145736 | tf_op jit(solution)/shard_map/ppermute | solution.py:383
  98.5 40.3 %collective-permute-start.8 = (bf16[512,1024]{1,0:T(8,128)(2,1)S(1)}, bf16[512,1024]{1,0:T(8,128)(2,1)S(1)}, u32[]{:S(2)}, u32[]{:S(2)}) collective-permute-start(bf16[512,1024]{1,0:T(8,128)(2,1)S(1)} %attend.1.refs_0_), channel_id=1, source_target_pairs={{0,1},{1,0},{2,3},{3,2},{4,5},{5,4},{6,7},{7,6},{8,9},{9,8},{10,11... | collective-permute-start | bytes 3145736 | tf_op jit(solution)/shard_map/ppermute | solution.py:387
  114.4 26.5 %collective-permute-start.13 = (bf16[512,1024]{1,0:T(8,128)(2,1)S(1)}, bf16[512,1024]{1,0:T(8,128)(2,1)S(1)}, u32[]{:S(2)}, u32[]{:S(2)}) collective-permute-start(bf16[512,1024]{1,0:T(8,128)(2,1)S(1)} %collective-permute-done.10.refs_2_), channel_id=1, source_target_pairs={{0,1},{1,0},{2,3},{3,2},{4,5},{5,4},{6,7},{7,6},{8,9},{9,8},{10,11... | collective-permute-start | bytes 3145736 | tf_op jit(solution)/shard_map/ppermute | solution.py:387
  119.9 23.6 %collective-permute-start.14 = (bf16[512,1024]{1,0:T(8,128)(2,1)S(1)}, bf16[512,1024]{1,0:T(8,128)(2,1)}, u32[]{:S(2)}, u32[]{:S(2)}) collective-permute-start(bf16[512,1024]{1,0:T(8,128)(2,1)S(1)} %collective-permute-done.9.refs_4_), channel_id=1, source_target_pairs={{0,1},{1,0},{2,3},{3,2},{4,5},{5,4},{6,7},{7,6},{8,9},{9,8},{10,11... | collective-permute-start | bytes 3145736 | tf_op jit(solution)/shard_map/ppermute | solution.py:387
  119.9 23.5 %collective-permute-start.17 = (bf16[512,1024]{1,0:T(8,128)(2,1)}, bf16[512,1024]{1,0:T(8,128)(2,1)}, u32[]{:S(2)}, u32[]{:S(2)}) collective-permute-start(bf16[512,1024]{1,0:T(8,128)(2,1)} %collective-permute-done.15.refs_6_), channel_id=1, source_target_pairs={{0,1},{1,0},{2,3},{3,2},{4,5},{5,4},{6,7},{7,6},{8,9},{9,8},{10,11... | collective-permute-start | bytes 3145736 | tf_op jit(solution)/shard_map/ppermute | solution.py:387
  137.5 21.9 %collective-permute-start.21 = (bf16[512,384]{1,0:T(8,128)(2,1)}, bf16[512,384]{1,0:T(8,128)(2,1)}, u32[]{:S(2)}, u32[]{:S(2)}) collective-permute-start(bf16[512,384]{1,0:T(8,128)(2,1)} %get-tuple-element.63), channel_id=1, source_target_pairs={{8,0},{12,4},{16,24},{20,28},{9,1},{13,5},{17,25},{21,29},{10,2},{... | collective-permute-start | bytes 1179656 | tf_op jit(solution)/shard_map/ppermute | solution.py:412
  138.8 23.9 %collective-permute-start.20 = (bf16[512,384]{1,0:T(8,128)(2,1)}, bf16[512,384]{1,0:T(8,128)(2,1)S(1)}, u32[]{:S(2)}, u32[]{:S(2)}) collective-permute-start(bf16[512,384]{1,0:T(8,128)(2,1)} %get-tuple-element.64), channel_id=1, source_target_pairs={{8,0},{12,4},{16,24},{20,28},{9,1},{13,5},{17,25},{21,29},{10,2},{... | collective-permute-start | bytes 1179656 | tf_op jit(solution)/shard_map/ppermute | solution.py:412
  141.9 26.0 %collective-permute-start.22 = (bf16[512,256]{1,0:T(8,128)(2,1)}, bf16[512,256]{1,0:T(8,128)(2,1)}, u32[]{:S(2)}, u32[]{:S(2)}) collective-permute-start(bf16[512,256]{1,0:T(8,128)(2,1)} %slice_add_fusion.2), channel_id=1, source_target_pairs={{8,0},{12,4},{16,24},{20,28},{9,1},{13,5},{17,25},{21,29},{10,2},{... | collective-permute-start | bytes 786440 | tf_op jit(solution)/shard_map/ppermute | solution.py:412
  162.2 24.8 %collective-permute-start.24 = (bf16[512,384]{1,0:T(8,128)(2,1)S(1)}, bf16[512,384]{1,0:T(8,128)(2,1)S(1)}, u32[]{:S(2)}, u32[]{:S(2)}) collective-permute-start(bf16[512,384]{1,0:T(8,128)(2,1)S(1)} %get-tuple-element.61), channel_id=1, source_target_pairs={{0,4},{4,0},{8,12},{12,8},{16,20},{20,16},{24,28},{28,24},{1,5},{5... | collective-permute-start | bytes 1179656 | tf_op jit(solution)/shard_map/ppermute | solution.py:448
  166.2 20.8 %collective-permute-start.23 = (bf16[512,384]{1,0:T(8,128)(2,1)S(1)}, bf16[512,384]{1,0:T(8,128)(2,1)S(1)}, u32[]{:S(2)}, u32[]{:S(2)}) collective-permute-start(bf16[512,384]{1,0:T(8,128)(2,1)S(1)} %get-tuple-element.60), channel_id=1, source_target_pairs={{0,4},{4,0},{8,12},{12,8},{16,20},{20,16},{24,28},{28,24},{1,5},{5... | collective-permute-start | bytes 1179656 | tf_op jit(solution)/shard_map/ppermute | solution.py:448
  170.3 16.7 %collective-permute-start.25 = (bf16[512,256]{1,0:T(8,128)(2,1)S(1)}, bf16[512,256]{1,0:T(8,128)(2,1)S(1)}, u32[]{:S(2)}, u32[]{:S(2)}) collective-permute-start(bf16[512,256]{1,0:T(8,128)(2,1)S(1)} %get-tuple-element.62), channel_id=1, source_target_pairs={{0,4},{4,0},{8,12},{12,8},{16,20},{20,16},{24,28},{28,24},{1,5},{5... | collective-permute-start | bytes 786440 | tf_op jit(solution)/shard_map/ppermute | solution.py:448
  (12 other events, 168.5 us)

commit v12 on v9

--- a/solution.py
+++ b/solution.py
@@ -303,40 +303,43 @@
     )
 
 
-def last_product_kernel(block_ref, left_slab, right_slab, base_ref, out_ref, staged, sems):
-    half = left_slab.shape[1]
+def last_product_kernel(start, block_ref, slab_ref, base_ref, *refs):
+    out_ref, staged, sems = refs[-3:]
+    columns = pl.ds(start, slab_ref.shape[1])
 
     def tile_copy(tile):
         at = pl.ds(tile * ROW_TILE, ROW_TILE)
-        return pltpu.make_async_copy(staged.at[at, :], out_ref.at[at, :], sems.at[tile])
+        return pltpu.make_async_copy(staged.at[at, :], out_ref.at[at, columns], sems.at[tile])
 
     tiles = block_ref.shape[0] // ROW_TILE
     for tile in range(tiles):
         at = pl.ds(tile * ROW_TILE, ROW_TILE)
-        for slab, start in ((left_slab, 0), (right_slab, half)):
-            columns = pl.ds(start, half)
-            product = jnp.dot(block_ref[at, :], slab[...], preferred_element_type=jnp.float32)
-            staged[at, columns] = (product + base_ref[at, columns]).astype(jnp.bfloat16)
+        product = jnp.dot(block_ref[at, :], slab_ref[...], preferred_element_type=jnp.float32)
+        staged[at, :] = (product + base_ref[at, columns]).astype(jnp.bfloat16)
         tile_copy(tile).start()
     for tile in range(tiles):
         tile_copy(tile).wait()
 
 
-def last_product(block, left_slab, right_slab, base):
+def last_product(block, slab, base, start, partly=None):
     rows, columns = base.shape
+    operands = pinned([block, slab, base], pltpu.VMEM)
+    if partly is not None:
+        operands.append(partly)
     return pl.pallas_call(
-        last_product_kernel,
+        functools.partial(last_product_kernel, start),
         out_shape=jax.ShapeDtypeStruct((rows, columns), jnp.bfloat16),
-        in_specs=[IN_VMEM] * 4,
+        in_specs=[IN_VMEM] * 3 + [IN_HBM] * (partly is not None),
         out_specs=IN_HBM,
         scratch_shapes=[
-            pltpu.VMEM((rows, columns), jnp.bfloat16),
+            pltpu.VMEM((rows, slab.shape[1]), jnp.bfloat16),
             pltpu.SemaphoreType.DMA((rows // ROW_TILE,)),
         ],
+        input_output_aliases={} if partly is None else {3: 0},
         compiler_params=pltpu.CompilerParams(vmem_limit_bytes=8 << 20),
         cost_estimate=SMALL_COST,
         name="last_product",
-    )(*pinned([block, left_slab, right_slab, base], pltpu.VMEM))
+    )(*operands)
 
 
 def project_ring(wo, inputs, attend_with):
@@ -347,8 +350,10 @@
     backward = [(b, a) for a, b in forward]
     half = columns // 2
     far = pb_size // 2
-    parts = [wo[:, :half], wo[:, half:]]
-    inputs, parts[0], parts[1] = lax.optimization_barrier((inputs, parts[0], parts[1]))
+    parts = [wo[:, :half]]
+    wo, parts[0] = lax.optimization_barrier((wo, parts[0]))
+    parts.append(wo[:, half:])
+    inputs, parts[1] = lax.optimization_barrier((inputs, parts[1]))
     slabs = [[(0, part)] for part in parts]
     moving = [[part, part] for part in parts]
 
@@ -399,7 +404,8 @@
     early, late = (0, -1, 1, -2, 2), (-3, 3)
     (base,) = ring_product(where, blocks, steps(early), chosen(early))
     base, block = ring_product(where, blocks, steps(late), chosen(late), base, far)
-    return last_product(block, at_step[0][far], at_step[1][far], base)
+    left = last_product(block, at_step[0][far], base, 0)
+    return last_product(block, at_step[1][far], base, half, left)
 
 
 def shards(queries, keys, values, block_ids, counts, refresh, cached_attn, wo):

time: 168 us -> 167 us (level)
  Pallas kernels: 39.2 us -> 23.1 us
  waiting for transfers between devices: 98.2 us -> 114 us
    pallas_call x1, Pallas kernels: 18.7 us -> 1.85 us  [attend(): pl.pallas_call(functools.partial(attention_kernel, heads, slots, part_row...]
    ppermute x7, waiting for transfers between devices: 49.3 us -> 64.7 us  [travel(): moving[part][1] = lax.ppermute(moving[part][1], 'pb', backward)]
    ppermute x7, waiting for transfers between devices: 24.6 us -> 29.3 us  [travel(): moving[part][0] = lax.ppermute(moving[part][0], 'pb', forward)]
    ppermute x1, waiting for transfers between devices: 3.79 us -> 0.01 us  [project_ring(): across = lax.ppermute(attn, 'ka', [(i, i ^ 2) for i in range(4)])]
  transfers between devices with their start and end apart: 20 -> 20, of which waited for: 10 -> 10; matrix products, arithmetic and copies ran while one was open for 3% -> 4% of each run, Pallas kernels for 22% -> 13%
where the time goes in v12:
time: 167 us
  waiting for transfers between devices  114 us (68%)
  Pallas kernels  23.1 us (14%)
  starting transfers between devices  20.1 us (12%)
  local copies, waits for them, and re-layouts  8.11 us (5%)
    ppermute x7, waiting for transfers between devices, travel(): moving[part][1] = lax.ppermute(moving[part][1], 'pb', backward)  64.7 us
    ppermute x7, waiting for transfers between devices, travel(): moving[part][0] = lax.ppermute(moving[part][0], 'pb', forward)  29.3 us
    ppermute x2, waiting for transfers between devices, own_head_keys_values(): lax.ppermute(heads_of(a, 1 - x), 'ka', [(i, i ^ 2) for i in range(4)])  20.1 us
    pallas_call x2, Pallas kernels, ring_product(): pl.pallas_call(functools.partial(ring_product_kernel, steps, spare_step),...  18.4 us
    ppermute x7, starting transfers between devices, travel(): moving[part][0] = lax.ppermute(moving[part][0], 'pb', forward)  10.4 us
    ppermute x7, starting transfers between devices, travel(): moving[part][1] = lax.ppermute(moving[part][1], 'pb', backward)  5.96 us
  transfers between devices with their start and end apart: 20, of which 10 were waited for; matrix products, arithmetic and copies ran while one was open for 4% of the time, Pallas kernels for 13%

profile of v12, /device:TPU:0, one launch (start us, length us, event | category | flops | bytes accessed | tf_op | source)
XLA Modules:
  0.0 167.0 jit_solution(7453650277895039605)
XLA Ops:
  0.0 1.4 slice.6.refs_4_
  1.5 3.1 %collective-permute-start.2 = (bf16[512,1024]{1,0:T(8,128)(2,1)S(1)}, bf16[512,1024]{1,0:T(8,128)(2,1)}, u32[]{:S(2)}, u32[]{:S(2)}) collective-permute-start(bf16[512,1024]{1,0:T(8,128)(2,1)S(1)} %slice.6.refs_4_), channel_id=1, source_target_pairs={{0,8},{8,16},{16,24},{24,28},{28,20},{20,12},{12,4},{4,0},{1,9},{9... | collective-permute-start | bytes 3145736 | tf_op jit(solution)/shard_map/ppermute | solution.py:363
  4.7 2.0 %collective-permute-start.15 = (bf16[512,1024]{1,0:T(8,128)(2,1)S(1)}, bf16[512,1024]{1,0:T(8,128)(2,1)}, u32[]{:S(2)}, u32[]{:S(2)}) collective-permute-start(bf16[512,1024]{1,0:T(8,128)(2,1)S(1)} %slice.7.refs_9_), channel_id=1, source_target_pairs={{8,0},{16,8},{24,16},{28,24},{20,28},{12,20},{4,12},{0,4},{9,1},{1... | collective-permute-start | bytes 3145736 | tf_op jit(solution)/shard_map/ppermute | solution.py:365
  6.7 1.9 %constant_dynamic-slice_fusion.4 = bf16[1024,256]{1,0:T(8,128)(2,1)} fusion(bf16[1024,512]{1,0:T(8,128)(2,1)} %refs_1_, s32[]{:T(128)S(6)} %select_n.29), kind=kLoop, calls=%fused_computation.5 | loop fusion | bytes 1048580 | tf_op jit(solution)/shard_map/dynamic_slice | solution.py:154
  8.6 1.5 collective-permute-start.1
  10.1 0.8 constant_dynamic-slice_fusion.5
  11.4 1.0 constant_dynamic-slice_fusion.2
  12.4 11.3 %collective-permute-done.1.refs_3_ = bf16[1024,256]{1,0:T(8,128)(2,1)} collective-permute-done((bf16[1024,256]{1,0:T(8,128)(2,1)}, bf16[1024,256]{1,0:T(8,128)(2,1)}, u32[]{:S(2)}, u32[]{:S(2)}) %collective-permute-start.1) | collective-permute-done | bytes 524320 | tf_op jit(solution)/shard_map/ppermute | solution.py:160
  24.1 8.8 %collective-permute-done.refs_2_ = bf16[1024,256]{1,0:T(8,128)(2,1)} collective-permute-done((bf16[1024,256]{1,0:T(8,128)(2,1)}, bf16[1024,256]{1,0:T(8,128)(2,1)}, u32[]{:S(2)}, u32[]{:S(2)}) %collective-permute-start) | collective-permute-done | bytes 524320 | tf_op jit(solution)/shard_map/ppermute | solution.py:160
  32.9 1.1 constant_dynamic-slice_fusion
  34.2 1.6 collective-permute-start.10
  36.3 16.9 %collective-permute-done.15.refs_11_ = bf16[512,1024]{1,0:T(8,128)(2,1)} collective-permute-done((bf16[512,1024]{1,0:T(8,128)(2,1)S(1)}, bf16[512,1024]{1,0:T(8,128)(2,1)}, u32[]{:S(2)}, u32[]{:S(2)}) %collective-permute-start.15) | collective-permute-done | bytes 1048608 | tf_op jit(solution)/shard_map/ppermute | solution.py:365
  54.6 2.1 %collective-permute-start.13 = (bf16[512,1024]{1,0:T(8,128)(2,1)}, bf16[512,1024]{1,0:T(8,128)(2,1)}, u32[]{:S(2)}, u32[]{:S(2)}) collective-permute-start(bf16[512,1024]{1,0:T(8,128)(2,1)} %collective-permute-done.12.refs_10_), channel_id=1, source_target_pairs={{0,8},{8,16},{16,24},{24,28},{28,20},{20,12},{12,4},{4,0},{1,9},{9... | collective-permute-start | bytes 3145736 | tf_op jit(solution)/shard_map/ppermute | solution.py:363
  56.7 1.0 copy-done.1
  57.7 1.8 %attend.1.refs_0_ = bf16[512,1024]{1,0:T(8,128)(2,1)S(1)} custom-call(s32[34]{0:T(128)S(1)} %concatenate.16.meta_ref, bf16[512,1024]{1,0:T(8,128)(2,1)} %bitcast.15, bf16[512,1024]{1,0:T(8,128)(2,1)} %bitcast.16, bf16[1024,512]{1,0:T(8,128)(2,1)} %refs_0_, bf16[1024,512]{1,0:T(8,128)(2,1)} %refs_1_, bf16[1024,256]{1,0:T(8,128)(2,1)} %collective-permute-done.refs_2_, ...), custom_call_target="tpu_custom_call" | custom-call | flops 1048576 | bytes 1048576 | tf_op jit(solution)/shard_map/attend/pallas_call | solution.py:118
  59.6 16.1 %collective-permute-done.10.refs_8_ = bf16[512,1024]{1,0:T(8,128)(2,1)} collective-permute-done((bf16[512,1024]{1,0:T(8,128)(2,1)}, bf16[512,1024]{1,0:T(8,128)(2,1)}, u32[]{:S(2)}, u32[]{:S(2)}) %collective-permute-start.10) | collective-permute-done | bytes 1048608 | tf_op jit(solution)/shard_map/ppermute | solution.py:365
  75.7 1.5 collective-permute-start.6
  77.2 1.6 collective-permute-start.9
  78.8 17.9 %collective-permute-done.16.refs_13_ = bf16[512,1024]{1,0:T(8,128)(2,1)} collective-permute-done((bf16[512,1024]{1,0:T(8,128)(2,1)}, bf16[512,1024]{1,0:T(8,128)(2,1)}, u32[]{:S(2)}, u32[]{:S(2)}) %collective-permute-start.16) | collective-permute-done | bytes 1048608 | tf_op jit(solution)/shard_map/ppermute | solution.py:365
  97.0 1.7 %collective-permute-start.11 = (bf16[512,1024]{1,0:T(8,128)(2,1)}, bf16[512,1024]{1,0:T(8,128)(2,1)}, u32[]{:S(2)}, u32[]{:S(2)}) collective-permute-start(bf16[512,1024]{1,0:T(8,128)(2,1)} %collective-permute-done.10.refs_8_), channel_id=1, source_target_pairs={{8,0},{16,8},{24,16},{28,24},{20,28},{12,20},{4,12},{0,4},{9,1},{1... | collective-permute-start | bytes 3145736 | tf_op jit(solution)/shard_map/ppermute | solution.py:365
  98.7 0.8 collective-permute-start.14
  99.5 19.0 %collective-permute-done.9.refs_4_ = bf16[512,1024]{1,0:T(8,128)(2,1)} collective-permute-done((bf16[512,1024]{1,0:T(8,128)(2,1)}, bf16[512,1024]{1,0:T(8,128)(2,1)}, u32[]{:S(2)}, u32[]{:S(2)}) %collective-permute-start.9) | collective-permute-done | bytes 1048608 | tf_op jit(solution)/shard_map/ppermute | solution.py:363
  118.5 2.1 %collective-permute-start.19 = (bf16[512,1024]{1,0:T(8,128)(2,1)}, bf16[512,1024]{1,0:T(8,128)(2,1)S(1)}, u32[]{:S(2)}, u32[]{:S(2)}) collective-permute-start(bf16[512,1024]{1,0:T(8,128)(2,1)} %collective-permute-done.9.refs_4_), channel_id=1, source_target_pairs={{0,8},{8,16},{16,24},{24,28},{28,20},{20,12},{12,4},{4,0},{1,9},{9... | collective-permute-start | bytes 3145736 | tf_op jit(solution)/shard_map/ppermute | solution.py:363
  120.6 2.5 %collective-permute-done.17.refs_7_ = bf16[512,1024]{1,0:T(8,128)(2,1)} collective-permute-done((bf16[512,1024]{1,0:T(8,128)(2,1)}, bf16[512,1024]{1,0:T(8,128)(2,1)}, u32[]{:S(2)}, u32[]{:S(2)}) %collective-permute-start.17) | collective-permute-done | bytes 1048608 | tf_op jit(solution)/shard_map/ppermute | solution.py:365
  123.4 0.7 fusion
  124.2 11.7 %ring_product.2.refs_8_ = f32[512,2048]{1,0:T(8,128)S(1)} custom-call(s32[9]{0:T(128)S(1)} %pad_add_fusion.where_ref, bf16[512,1024]{1,0:T(8,128)(2,1)} %copy-done, bf16[512,1024]{1,0:T(8,128)(2,1)} %copy-done.2, bf16[512,1024]{1,0:T(8,128)(2,1)} %copy-done.3, bf16[512,1024]{1,0:T(8,128)(2,1)} %collective-permute-done.7.refs_3_, ...), custom_call_target="tpu_custom_call" | custom-call | flops 1048576 | bytes 1048576 | tf_op jit(solution)/shard_map/ring_product/pallas_call | solution.py:285
  135.9 9.7 %collective-permute-done.11.refs_5_ = bf16[512,1024]{1,0:T(8,128)(2,1)} collective-permute-done((bf16[512,1024]{1,0:T(8,128)(2,1)}, bf16[512,1024]{1,0:T(8,128)(2,1)}, u32[]{:S(2)}, u32[]{:S(2)}) %collective-permute-start.11) | collective-permute-done | bytes 1048608 | tf_op jit(solution)/shard_map/ppermute | solution.py:365
  145.6 6.6 %ring_product.3 = (f32[512,2048]{1,0:T(8,128)S(1)}, bf16[512,512]{1,0:T(8,128)(2,1)S(1)}) custom-call(s32[9]{0:T(128)S(1)} %pad_add_fusion.where_ref, bf16[512,1024]{1,0:T(8,128)(2,1)} %copy-done, bf16[512,1024]{1,0:T(8,128)(2,1)} %copy-done.2, bf16[512,1024]{1,0:T(8,128)(2,1)} %copy-done.3, bf16[512,1024]{1,0:T(8,128)(2,1)} %collective-permute-done.7.refs_3_, ...), custom_call_target="tpu_custom_call" | custom-call | flops 1048576 | bytes 1048576 | tf_op jit(solution)/shard_map/ring_product/pallas_call | solution.py:285
  152.2 10.3 %collective-permute-done.19.slab_ref = bf16[512,1024]{1,0:T(8,128)(2,1)S(1)} collective-permute-done((bf16[512,1024]{1,0:T(8,128)(2,1)}, bf16[512,1024]{1,0:T(8,128)(2,1)S(1)}, u32[]{:S(2)}, u32[]{:S(2)}) %collective-permute-start.19) | collective-permute-done | bytes 1048608 | tf_op jit(solution)/shard_map/ppermute | solution.py:363
  162.5 1.5 last_product.2.refs_0_
  163.9 1.6 collective-permute-done.18.slab_ref
  165.5 1.5 last_product.3
  (41 shorter events, 2.6 us)
Async XLA Ops:
  0.0 4.6 %copy-start.7 = (bf16[512,2048]{1,0:T(8,128)(2,1)S(1)}, bf16[512,2048]{1,0:T(8,128)(2,1)}, u32[]{:S(2)}) copy-start(bf16[512,2048]{1,0:T(8,128)(2,1)} %param.16) | copy-start | bytes 6291460
  1.4 9.4 %copy-start.4 = (bf16[512,1024]{1,0:T(8,128)(2,1)}, bf16[512,1024]{1,0:T(8,128)(2,1)S(1)}, u32[]{:S(2)}) copy-start(bf16[512,1024]{1,0:T(8,128)(2,1)S(1)} %slice.6.refs_4_) | copy-start | bytes 3145732
  1.5 8.6 %copy-start.6 = (bf16[1024,512]{1,0:T(8,128)(2,1)S(1)}, bf16[1024,512]{1,0:T(8,128)(2,1)}, u32[]{:S(2)}) copy-start(bf16[1024,512]{1,0:T(8,128)(2,1)} %refs_0_) | copy-start | bytes 3145732
  1.5 31.5 %collective-permute-start.2 = (bf16[512,1024]{1,0:T(8,128)(2,1)S(1)}, bf16[512,1024]{1,0:T(8,128)(2,1)}, u32[]{:S(2)}, u32[]{:S(2)}) collective-permute-start(bf16[512,1024]{1,0:T(8,128)(2,1)S(1)} %slice.6.refs_4_), channel_id=1, source_target_pairs={{0,8},{8,16},{16,24},{24,28},{28,20},{20,12},{12,4},{4,0},{1,9},{9... | collective-permute-start | bytes 3145736 | tf_op jit(solution)/shard_map/ppermute | solution.py:363
  4.5 28.4 %collective-permute-start.3 = (bf16[512,1024]{1,0:T(8,128)(2,1)S(1)}, bf16[512,1024]{1,0:T(8,128)(2,1)}, u32[]{:S(2)}, u32[]{:S(2)}) collective-permute-start(bf16[512,1024]{1,0:T(8,128)(2,1)S(1)} %slice.6.refs_4_), channel_id=1, source_target_pairs={{8,0},{16,8},{24,16},{28,24},{20,28},{12,20},{4,12},{0,4},{9,1},{1... | collective-permute-start | bytes 3145736 | tf_op jit(solution)/shard_map/ppermute | solution.py:365
  4.7 29.4 %copy-start.5 = (bf16[512,1024]{1,0:T(8,128)(2,1)}, bf16[512,1024]{1,0:T(8,128)(2,1)S(1)}, u32[]{:S(2)}) copy-start(bf16[512,1024]{1,0:T(8,128)(2,1)S(1)} %slice.7.refs_9_) | copy-start | bytes 3145732
  4.7 48.5 %collective-permute-start.15 = (bf16[512,1024]{1,0:T(8,128)(2,1)S(1)}, bf16[512,1024]{1,0:T(8,128)(2,1)}, u32[]{:S(2)}, u32[]{:S(2)}) collective-permute-start(bf16[512,1024]{1,0:T(8,128)(2,1)S(1)} %slice.7.refs_9_), channel_id=1, source_target_pairs={{8,0},{16,8},{24,16},{28,24},{20,28},{12,20},{4,12},{0,4},{9,1},{1... | collective-permute-start | bytes 3145736 | tf_op jit(solution)/shard_map/ppermute | solution.py:365
  8.6 15.2 %collective-permute-start.1 = (bf16[1024,256]{1,0:T(8,128)(2,1)}, bf16[1024,256]{1,0:T(8,128)(2,1)}, u32[]{:S(2)}, u32[]{:S(2)}) collective-permute-start(bf16[1024,256]{1,0:T(8,128)(2,1)} %constant_dynamic-slice_fusion.4), channel_id=1, source_target_pairs={{0,2},{1,3},{2,0},{3,1},{4,6},{5,7},{6,4},{7,5},{8,10},{9,11},{10,... | collective-permute-start | bytes 1572872 | tf_op jit(solution)/shard_map/ppermute | solution.py:160
  10.9 22.1 %collective-permute-start = (bf16[1024,256]{1,0:T(8,128)(2,1)}, bf16[1024,256]{1,0:T(8,128)(2,1)}, u32[]{:S(2)}, u32[]{:S(2)}) collective-permute-start(bf16[1024,256]{1,0:T(8,128)(2,1)} %constant_dynamic-slice_fusion.5), channel_id=1, source_target_pairs={{0,2},{1,3},{2,0},{3,1},{4,6},{5,7},{6,4},{7,5},{8,10},{9,11},{10,... | collective-permute-start | bytes 1572872 | tf_op jit(solution)/shard_map/ppermute | solution.py:160
  11.4 43.1 %copy-start.8 = (s32[1,1,16]{2,1,0:T(1,128)S(1)}, s32[1,1,16]{2,1,0:T(1,128)}, u32[]{:S(2)}) copy-start(s32[1,1,16]{2,1,0:T(1,128)} %param.12) | copy-start | bytes 196
  23.7 30.9 %collective-permute-start.12 = (bf16[512,1024]{1,0:T(8,128)(2,1)S(1)}, bf16[512,1024]{1,0:T(8,128)(2,1)}, u32[]{:S(2)}, u32[]{:S(2)}) collective-permute-start(bf16[512,1024]{1,0:T(8,128)(2,1)S(1)} %slice.7.refs_9_), channel_id=1, source_target_pairs={{0,8},{8,16},{16,24},{24,28},{28,20},{20,12},{12,4},{4,0},{1,9},{9... | collective-permute-start | bytes 3145736 | tf_op jit(solution)/shard_map/ppermute | solution.py:363
  34.1 22.6 %collective-permute-start.4 = (bf16[2048,256]{1,0:T(8,128)(2,1)S(1)}, bf16[2048,256]{1,0:T(8,128)(2,1)S(1)}, u32[]{:S(2)}, u32[]{:S(2)}) collective-permute-start(bf16[2048,256]{1,0:T(8,128)(2,1)S(1)} %maximum_maximum_fusion), channel_id=1, source_target_pairs={{0,1},{1,0},{2,3},{3,2},{4,5},{5,4},{6,7},{7,6},{8,9},{9,8},{10,11... | collective-permute-start | bytes 3145736 | tf_op jit(solution)/shard_map/ppermute | solution.py:164
  34.2 41.5 %collective-permute-start.10 = (bf16[512,1024]{1,0:T(8,128)(2,1)}, bf16[512,1024]{1,0:T(8,128)(2,1)}, u32[]{:S(2)}, u32[]{:S(2)}) collective-permute-start(bf16[512,1024]{1,0:T(8,128)(2,1)} %collective-permute-done.3.refs_6_), channel_id=1, source_target_pairs={{8,0},{16,8},{24,16},{28,24},{20,28},{12,20},{4,12},{0,4},{9,1},{1... | collective-permute-start | bytes 3145736 | tf_op jit(solution)/shard_map/ppermute | solution.py:365
  35.9 41.3 %collective-permute-start.8 = (bf16[512,1024]{1,0:T(8,128)(2,1)}, bf16[512,1024]{1,0:T(8,128)(2,1)}, u32[]{:S(2)}, u32[]{:S(2)}) collective-permute-start(bf16[512,1024]{1,0:T(8,128)(2,1)} %collective-permute-done.2.refs_5_), channel_id=1, source_target_pairs={{0,8},{8,16},{16,24},{24,28},{28,20},{20,12},{12,4},{4,0},{1,9},{9... | collective-permute-start | bytes 3145736 | tf_op jit(solution)/shard_map/ppermute | solution.py:363
  53.2 43.5 %collective-permute-start.16 = (bf16[512,1024]{1,0:T(8,128)(2,1)}, bf16[512,1024]{1,0:T(8,128)(2,1)}, u32[]{:S(2)}, u32[]{:S(2)}) collective-permute-start(bf16[512,1024]{1,0:T(8,128)(2,1)} %collective-permute-done.15.refs_11_), channel_id=1, source_target_pairs={{8,0},{16,8},{24,16},{28,24},{20,28},{12,20},{4,12},{0,4},{9,1},{1... | collective-permute-start | bytes 3145736 | tf_op jit(solution)/shard_map/ppermute | solution.py:365
  54.6 42.3 %collective-permute-start.13 = (bf16[512,1024]{1,0:T(8,128)(2,1)}, bf16[512,1024]{1,0:T(8,128)(2,1)}, u32[]{:S(2)}, u32[]{:S(2)}) collective-permute-start(bf16[512,1024]{1,0:T(8,128)(2,1)} %collective-permute-done.12.refs_10_), channel_id=1, source_target_pairs={{0,8},{8,16},{16,24},{24,28},{28,20},{20,12},{12,4},{4,0},{1,9},{9... | collective-permute-start | bytes 3145736 | tf_op jit(solution)/shard_map/ppermute | solution.py:363
  56.7 1.0 copy-start.1
  59.5 64.6 %copy-start = (bf16[512,1024]{1,0:T(8,128)(2,1)}, bf16[512,1024]{1,0:T(8,128)(2,1)S(1)}, u32[]{:S(2)}) copy-start(bf16[512,1024]{1,0:T(8,128)(2,1)S(1)} %attend.1.refs_0_) | copy-start | bytes 3145732
  59.5 37.4 %collective-permute-start.5 = (bf16[512,1024]{1,0:T(8,128)(2,1)S(1)}, bf16[512,1024]{1,0:T(8,128)(2,1)S(1)}, u32[]{:S(2)}, u32[]{:S(2)}) collective-permute-start(bf16[512,1024]{1,0:T(8,128)(2,1)S(1)} %attend.1.refs_0_), channel_id=1, source_target_pairs={{0,1},{1,0},{2,3},{3,2},{4,5},{5,4},{6,7},{7,6},{8,9},{9,8},{10,11... | collective-permute-start | bytes 3145736 | tf_op jit(solution)/shard_map/ppermute | solution.py:387
  75.7 23.1 %collective-permute-start.6 = (bf16[512,1024]{1,0:T(8,128)(2,1)S(1)}, bf16[512,1024]{1,0:T(8,128)(2,1)S(1)}, u32[]{:S(2)}, u32[]{:S(2)}) collective-permute-start(bf16[512,1024]{1,0:T(8,128)(2,1)S(1)} %attend.1.refs_0_), channel_id=1, source_target_pairs={{0,2},{1,3},{2,0},{3,1},{4,6},{5,7},{6,4},{7,5},{8,10},{9,11},{10,... | collective-permute-start | bytes 3145736 | tf_op jit(solution)/shard_map/ppermute | solution.py:386
  77.2 41.3 %collective-permute-start.9 = (bf16[512,1024]{1,0:T(8,128)(2,1)}, bf16[512,1024]{1,0:T(8,128)(2,1)}, u32[]{:S(2)}, u32[]{:S(2)}) collective-permute-start(bf16[512,1024]{1,0:T(8,128)(2,1)} %collective-permute-done.8.refs_7_), channel_id=1, source_target_pairs={{0,8},{8,16},{16,24},{24,28},{28,20},{20,12},{12,4},{4,0},{1,9},{9... | collective-permute-start | bytes 3145736 | tf_op jit(solution)/shard_map/ppermute | solution.py:363
  96.7 26.4 %collective-permute-start.17 = (bf16[512,1024]{1,0:T(8,128)(2,1)}, bf16[512,1024]{1,0:T(8,128)(2,1)}, u32[]{:S(2)}, u32[]{:S(2)}) collective-permute-start(bf16[512,1024]{1,0:T(8,128)(2,1)} %collective-permute-done.16.refs_13_), channel_id=1, source_target_pairs={{8,0},{16,8},{24,16},{28,24},{20,28},{12,20},{4,12},{0,4},{9,1},{1... | collective-permute-start | bytes 3145736 | tf_op jit(solution)/shard_map/ppermute | solution.py:365
  97.0 27.2 %collective-permute-start.7 = (bf16[512,1024]{1,0:T(8,128)(2,1)S(1)}, bf16[512,1024]{1,0:T(8,128)(2,1)}, u32[]{:S(2)}, u32[]{:S(2)}) collective-permute-start(bf16[512,1024]{1,0:T(8,128)(2,1)S(1)} %attend.1.refs_0_), channel_id=1, source_target_pairs={{0,3},{1,2},{2,1},{3,0},{4,7},{5,6},{6,5},{7,4},{8,11},{9,10},{10,... | collective-permute-start | bytes 3145736 | tf_op jit(solution)/shard_map/ppermute | solution.py:388
  97.0 23.6 %copy-start.2 = (bf16[512,1024]{1,0:T(8,128)(2,1)}, bf16[512,1024]{1,0:T(8,128)(2,1)S(1)}, u32[]{:S(2)}) copy-start(bf16[512,1024]{1,0:T(8,128)(2,1)S(1)} %collective-permute-done.5.refs_1_) | copy-start | bytes 3145732
  97.0 48.6 %collective-permute-start.11 = (bf16[512,1024]{1,0:T(8,128)(2,1)}, bf16[512,1024]{1,0:T(8,128)(2,1)}, u32[]{:S(2)}, u32[]{:S(2)}) collective-permute-start(bf16[512,1024]{1,0:T(8,128)(2,1)} %collective-permute-done.10.refs_8_), channel_id=1, source_target_pairs={{8,0},{16,8},{24,16},{28,24},{20,28},{12,20},{4,12},{0,4},{9,1},{1... | collective-permute-start | bytes 3145736 | tf_op jit(solution)/shard_map/ppermute | solution.py:365
  98.7 24.4 %copy-start.3 = (bf16[512,1024]{1,0:T(8,128)(2,1)}, bf16[512,1024]{1,0:T(8,128)(2,1)S(1)}, u32[]{:S(2)}) copy-start(bf16[512,1024]{1,0:T(8,128)(2,1)S(1)} %collective-permute-done.6.refs_2_) | copy-start | bytes 3145732
  98.7 46.8 %collective-permute-start.14 = (bf16[512,1024]{1,0:T(8,128)(2,1)}, bf16[512,1024]{1,0:T(8,128)(2,1)}, u32[]{:S(2)}, u32[]{:S(2)}) collective-permute-start(bf16[512,1024]{1,0:T(8,128)(2,1)} %collective-permute-done.13.refs_12_), channel_id=1, source_target_pairs={{0,8},{8,16},{16,24},{24,28},{28,20},{20,12},{12,4},{4,0},{1,9},{9... | collective-permute-start | bytes 3145736 | tf_op jit(solution)/shard_map/ppermute | solution.py:363
  118.5 44.0 %collective-permute-start.19 = (bf16[512,1024]{1,0:T(8,128)(2,1)}, bf16[512,1024]{1,0:T(8,128)(2,1)S(1)}, u32[]{:S(2)}, u32[]{:S(2)}) collective-permute-start(bf16[512,1024]{1,0:T(8,128)(2,1)} %collective-permute-done.9.refs_4_), channel_id=1, source_target_pairs={{0,8},{8,16},{16,24},{24,28},{28,20},{20,12},{12,4},{4,0},{1,9},{9... | collective-permute-start | bytes 3145736 | tf_op jit(solution)/shard_map/ppermute | solution.py:363
  123.1 42.4 %collective-permute-start.18 = (bf16[512,1024]{1,0:T(8,128)(2,1)}, bf16[512,1024]{1,0:T(8,128)(2,1)S(1)}, u32[]{:S(2)}, u32[]{:S(2)}) collective-permute-start(bf16[512,1024]{1,0:T(8,128)(2,1)} %collective-permute-done.17.refs_7_), channel_id=1, source_target_pairs={{8,0},{16,8},{24,16},{28,24},{20,28},{12,20},{4,12},{0,4},{9,1},{1... | collective-permute-start | bytes 3145736 | tf_op jit(solution)/shard_map/ppermute | solution.py:365

commit v13 on v12

--- a/solution.py
+++ b/solution.py
@@ -372,8 +372,8 @@
                 slabs[part].append((hop, moving[part][1]))
 
     def gate(value):
-        value, moving[0][0], moving[0][1] = lax.optimization_barrier(
-            (value, moving[0][0], moving[0][1])
+        value, moving[0][0], moving[1][1] = lax.optimization_barrier(
+            (value, moving[0][0], moving[1][1])
         )
         return value
 

time: 167 us -> 168 us (level)
    ppermute x7, waiting for transfers between devices: 64.7 us -> 21.9 us  [travel(): moving[part][1] = lax.ppermute(moving[part][1], 'pb', backward)]
    ppermute x7, waiting for transfers between devices: 29.3 us -> 70.7 us  [travel(): moving[part][0] = lax.ppermute(moving[part][0], 'pb', forward)]
    ppermute x7, starting transfers between devices: 10.4 us -> 5.95 us  [travel(): moving[part][0] = lax.ppermute(moving[part][0], 'pb', forward)]
    ppermute x7, starting transfers between devices: 5.96 us -> 10.2 us  [travel(): moving[part][1] = lax.ppermute(moving[part][1], 'pb', backward)]
  transfers between devices with their start and end apart: 20 -> 20, of which waited for: 10 -> 12; matrix products, arithmetic and copies ran while one was open for 4% -> 4% of each run, Pallas kernels for 13% -> 13%
where the time goes in v13:
time: 168 us
  waiting for transfers between devices  113 us (67%)
  Pallas kernels  23.1 us (14%)
  starting transfers between devices  20.2 us (12%)
  local copies, waits for them, and re-layouts  8.57 us (5%)
    ppermute x7, waiting for transfers between devices, travel(): moving[part][0] = lax.ppermute(moving[part][0], 'pb', forward)  70.7 us
    ppermute x7, waiting for transfers between devices, travel(): moving[part][1] = lax.ppermute(moving[part][1], 'pb', backward)  21.9 us
    ppermute x2, waiting for transfers between devices, own_head_keys_values(): lax.ppermute(heads_of(a, 1 - x), 'ka', [(i, i ^ 2) for i in range(4)])  20.4 us
    pallas_call x2, Pallas kernels, ring_product(): pl.pallas_call(functools.partial(ring_product_kernel, steps, spare_step),...  18.4 us
    ppermute x7, starting transfers between devices, travel(): moving[part][1] = lax.ppermute(moving[part][1], 'pb', backward)  10.2 us
    ppermute x7, starting transfers between devices, travel(): moving[part][0] = lax.ppermute(moving[part][0], 'pb', forward)  5.95 us
  transfers between devices with their start and end apart: 20, of which 12 were waited for; matrix products, arithmetic and copies ran while one was open for 4% of the time, Pallas kernels for 13%

profile of v13, /device:TPU:0, one launch (start us, length us, event | category | flops | bytes accessed | tf_op | source)
XLA Modules:
  0.0 167.5 jit_solution(5331394238576912042)
XLA Ops:
  0.0 1.4 slice.6.refs_4_
  2.0 3.0 %collective-permute-start.3 = (bf16[512,1024]{1,0:T(8,128)(2,1)S(1)}, bf16[512,1024]{1,0:T(8,128)(2,1)}, u32[]{:S(2)}, u32[]{:S(2)}) collective-permute-start(bf16[512,1024]{1,0:T(8,128)(2,1)S(1)} %slice.7.refs_9_), channel_id=1, source_target_pairs={{8,0},{16,8},{24,16},{28,24},{20,28},{12,20},{4,12},{0,4},{9,1},{1... | collective-permute-start | bytes 3145736 | tf_op jit(solution)/shard_map/ppermute | solution.py:365
  5.2 2.0 %collective-permute-start.13 = (bf16[512,1024]{1,0:T(8,128)(2,1)S(1)}, bf16[512,1024]{1,0:T(8,128)(2,1)}, u32[]{:S(2)}, u32[]{:S(2)}) collective-permute-start(bf16[512,1024]{1,0:T(8,128)(2,1)S(1)} %slice.7.refs_9_), channel_id=1, source_target_pairs={{0,8},{8,16},{16,24},{24,28},{28,20},{20,12},{12,4},{4,0},{1,9},{9... | collective-permute-start | bytes 3145736 | tf_op jit(solution)/shard_map/ppermute | solution.py:363
  7.1 1.9 %constant_dynamic-slice_fusion.4 = bf16[1024,256]{1,0:T(8,128)(2,1)} fusion(bf16[1024,512]{1,0:T(8,128)(2,1)} %refs_1_, s32[]{:T(128)S(6)} %select_n.29), kind=kLoop, calls=%fused_computation.5 | loop fusion | bytes 1048580 | tf_op jit(solution)/shard_map/dynamic_slice | solution.py:154
  9.0 1.5 collective-permute-start.1
  10.5 0.8 constant_dynamic-slice_fusion.5
  11.9 1.0 constant_dynamic-slice_fusion.2
  12.9 11.3 %collective-permute-done.1.refs_3_ = bf16[1024,256]{1,0:T(8,128)(2,1)} collective-permute-done((bf16[1024,256]{1,0:T(8,128)(2,1)}, bf16[1024,256]{1,0:T(8,128)(2,1)}, u32[]{:S(2)}, u32[]{:S(2)}) %collective-permute-start.1) | collective-permute-done | bytes 524320 | tf_op jit(solution)/shard_map/ppermute | solution.py:160
  24.3 9.1 %collective-permute-done.refs_2_ = bf16[1024,256]{1,0:T(8,128)(2,1)} collective-permute-done((bf16[1024,256]{1,0:T(8,128)(2,1)}, bf16[1024,256]{1,0:T(8,128)(2,1)}, u32[]{:S(2)}, u32[]{:S(2)}) %collective-permute-start) | collective-permute-done | bytes 524320 | tf_op jit(solution)/shard_map/ppermute | solution.py:160
  33.4 1.1 constant_dynamic-slice_fusion
  34.5 1.1 maximum_maximum_fusion
  35.9 1.7 %collective-permute-start.8 = (bf16[512,1024]{1,0:T(8,128)(2,1)}, bf16[512,1024]{1,0:T(8,128)(2,1)}, u32[]{:S(2)}, u32[]{:S(2)}) collective-permute-start(bf16[512,1024]{1,0:T(8,128)(2,1)} %collective-permute-done.2.refs_5_), channel_id=1, source_target_pairs={{0,8},{8,16},{16,24},{24,28},{28,20},{20,12},{12,4},{4,0},{1,9},{9... | collective-permute-start | bytes 3145736 | tf_op jit(solution)/shard_map/ppermute | solution.py:363
  37.6 16.1 %collective-permute-done.13.refs_10_ = bf16[512,1024]{1,0:T(8,128)(2,1)} collective-permute-done((bf16[512,1024]{1,0:T(8,128)(2,1)S(1)}, bf16[512,1024]{1,0:T(8,128)(2,1)}, u32[]{:S(2)}, u32[]{:S(2)}) %collective-permute-start.13) | collective-permute-done | bytes 1048608 | tf_op jit(solution)/shard_map/ppermute | solution.py:363
  55.2 2.0 %collective-permute-start.11 = (bf16[512,1024]{1,0:T(8,128)(2,1)}, bf16[512,1024]{1,0:T(8,128)(2,1)}, u32[]{:S(2)}, u32[]{:S(2)}) collective-permute-start(bf16[512,1024]{1,0:T(8,128)(2,1)} %collective-permute-done.10.refs_6_), channel_id=1, source_target_pairs={{8,0},{16,8},{24,16},{28,24},{20,28},{12,20},{4,12},{0,4},{9,1},{1... | collective-permute-start | bytes 3145736 | tf_op jit(solution)/shard_map/ppermute | solution.py:365
  57.2 1.0 copy-done.1
  58.2 1.8 %attend.1.refs_0_ = bf16[512,1024]{1,0:T(8,128)(2,1)S(1)} custom-call(s32[34]{0:T(128)S(1)} %concatenate.16.meta_ref, bf16[512,1024]{1,0:T(8,128)(2,1)} %bitcast.15, bf16[512,1024]{1,0:T(8,128)(2,1)} %bitcast.16, bf16[1024,512]{1,0:T(8,128)(2,1)} %refs_0_, bf16[1024,512]{1,0:T(8,128)(2,1)} %refs_1_, bf16[1024,256]{1,0:T(8,128)(2,1)} %collective-permute-done.refs_2_, ...), custom_call_target="tpu_custom_call" | custom-call | flops 1048576 | bytes 1048576 | tf_op jit(solution)/shard_map/attend/pallas_call | solution.py:118
  60.1 14.0 %collective-permute-done.16.refs_13_ = bf16[512,1024]{1,0:T(8,128)(2,1)} collective-permute-done((bf16[512,1024]{1,0:T(8,128)(2,1)}, bf16[512,1024]{1,0:T(8,128)(2,1)}, u32[]{:S(2)}, u32[]{:S(2)}) %collective-permute-start.16) | collective-permute-done | bytes 1048608 | tf_op jit(solution)/shard_map/ppermute | solution.py:365
  74.1 2.0 %collective-permute-start.6 = (bf16[512,1024]{1,0:T(8,128)(2,1)S(1)}, bf16[512,1024]{1,0:T(8,128)(2,1)S(1)}, u32[]{:S(2)}, u32[]{:S(2)}) collective-permute-start(bf16[512,1024]{1,0:T(8,128)(2,1)S(1)} %attend.1.refs_0_), channel_id=1, source_target_pairs={{0,2},{1,3},{2,0},{3,1},{4,6},{5,7},{6,4},{7,5},{8,10},{9,11},{10,... | collective-permute-start | bytes 3145736 | tf_op jit(solution)/shard_map/ppermute | solution.py:386
  76.2 1.5 collective-permute-start.9
  77.7 21.0 %collective-permute-done.14.refs_12_ = bf16[512,1024]{1,0:T(8,128)(2,1)} collective-permute-done((bf16[512,1024]{1,0:T(8,128)(2,1)}, bf16[512,1024]{1,0:T(8,128)(2,1)}, u32[]{:S(2)}, u32[]{:S(2)}) %collective-permute-start.14) | collective-permute-done | bytes 1048608 | tf_op jit(solution)/shard_map/ppermute | solution.py:363
  98.6 1.6 collective-permute-start.17
  100.7 1.6 collective-permute-start.12
  102.3 18.8 %collective-permute-done.9.refs_4_ = bf16[512,1024]{1,0:T(8,128)(2,1)} collective-permute-done((bf16[512,1024]{1,0:T(8,128)(2,1)}, bf16[512,1024]{1,0:T(8,128)(2,1)}, u32[]{:S(2)}, u32[]{:S(2)}) %collective-permute-start.9) | collective-permute-done | bytes 1048608 | tf_op jit(solution)/shard_map/ppermute | solution.py:363
  121.2 3.9 %collective-permute-done.17.refs_7_ = bf16[512,1024]{1,0:T(8,128)(2,1)} collective-permute-done((bf16[512,1024]{1,0:T(8,128)(2,1)}, bf16[512,1024]{1,0:T(8,128)(2,1)}, u32[]{:S(2)}, u32[]{:S(2)}) %collective-permute-start.17) | collective-permute-done | bytes 1048608 | tf_op jit(solution)/shard_map/ppermute | solution.py:365
  125.1 1.6 collective-permute-start.18
  127.4 11.7 %ring_product.2.refs_8_ = f32[512,2048]{1,0:T(8,128)S(1)} custom-call(s32[9]{0:T(128)S(1)} %pad_add_fusion.where_ref, bf16[512,1024]{1,0:T(8,128)(2,1)} %copy-done, bf16[512,1024]{1,0:T(8,128)(2,1)} %copy-done.2, bf16[512,1024]{1,0:T(8,128)(2,1)} %copy-done.3, bf16[512,1024]{1,0:T(8,128)(2,1)} %collective-permute-done.7.refs_3_, ...), custom_call_target="tpu_custom_call" | custom-call | flops 1048576 | bytes 1048576 | tf_op jit(solution)/shard_map/ring_product/pallas_call | solution.py:285
  139.2 4.4 %collective-permute-done.15.refs_6_ = bf16[512,1024]{1,0:T(8,128)(2,1)} collective-permute-done((bf16[512,1024]{1,0:T(8,128)(2,1)}, bf16[512,1024]{1,0:T(8,128)(2,1)}, u32[]{:S(2)}, u32[]{:S(2)}) %collective-permute-start.15) | collective-permute-done | bytes 1048608 | tf_op jit(solution)/shard_map/ppermute | solution.py:363
  143.6 3.9 %collective-permute-done.12.refs_5_ = bf16[512,1024]{1,0:T(8,128)(2,1)} collective-permute-done((bf16[512,1024]{1,0:T(8,128)(2,1)}, bf16[512,1024]{1,0:T(8,128)(2,1)}, u32[]{:S(2)}, u32[]{:S(2)}) %collective-permute-start.12) | collective-permute-done | bytes 1048608 | tf_op jit(solution)/shard_map/ppermute | solution.py:365
  147.5 6.6 %ring_product.3 = (f32[512,2048]{1,0:T(8,128)S(1)}, bf16[512,512]{1,0:T(8,128)(2,1)S(1)}) custom-call(s32[9]{0:T(128)S(1)} %pad_add_fusion.where_ref, bf16[512,1024]{1,0:T(8,128)(2,1)} %copy-done, bf16[512,1024]{1,0:T(8,128)(2,1)} %copy-done.2, bf16[512,1024]{1,0:T(8,128)(2,1)} %copy-done.3, bf16[512,1024]{1,0:T(8,128)(2,1)} %collective-permute-done.7.refs_3_, ...), custom_call_target="tpu_custom_call" | custom-call | flops 1048576 | bytes 1048576 | tf_op jit(solution)/shard_map/ring_product/pallas_call | solution.py:285
  154.2 10.3 %collective-permute-done.19.slab_ref = bf16[512,1024]{1,0:T(8,128)(2,1)S(1)} collective-permute-done((bf16[512,1024]{1,0:T(8,128)(2,1)}, bf16[512,1024]{1,0:T(8,128)(2,1)S(1)}, u32[]{:S(2)}, u32[]{:S(2)}) %collective-permute-start.19) | collective-permute-done | bytes 1048608 | tf_op jit(solution)/shard_map/ppermute | solution.py:363
  164.5 1.5 last_product.2.refs_0_
  166.0 1.5 last_product.3
  (41 shorter events, 3.4 us)
Async XLA Ops:
  0.0 1.9 %copy-start.7 = (bf16[512,2048]{1,0:T(8,128)(2,1)S(1)}, bf16[512,2048]{1,0:T(8,128)(2,1)}, u32[]{:S(2)}) copy-start(bf16[512,2048]{1,0:T(8,128)(2,1)} %param.16) | copy-start | bytes 6291460
  1.9 22.3 %copy-start.4 = (bf16[512,1024]{1,0:T(8,128)(2,1)}, bf16[512,1024]{1,0:T(8,128)(2,1)S(1)}, u32[]{:S(2)}) copy-start(bf16[512,1024]{1,0:T(8,128)(2,1)S(1)} %slice.6.refs_4_) | copy-start | bytes 3145732
  1.9 8.6 %copy-start.6 = (bf16[1024,512]{1,0:T(8,128)(2,1)S(1)}, bf16[1024,512]{1,0:T(8,128)(2,1)}, u32[]{:S(2)}) copy-start(bf16[1024,512]{1,0:T(8,128)(2,1)} %refs_0_) | copy-start | bytes 3145732
  2.0 32.5 %copy-start.5 = (bf16[512,1024]{1,0:T(8,128)(2,1)}, bf16[512,1024]{1,0:T(8,128)(2,1)S(1)}, u32[]{:S(2)}) copy-start(bf16[512,1024]{1,0:T(8,128)(2,1)S(1)} %slice.7.refs_9_) | copy-start | bytes 3145732
  2.0 31.4 %collective-permute-start.3 = (bf16[512,1024]{1,0:T(8,128)(2,1)S(1)}, bf16[512,1024]{1,0:T(8,128)(2,1)}, u32[]{:S(2)}, u32[]{:S(2)}) collective-permute-start(bf16[512,1024]{1,0:T(8,128)(2,1)S(1)} %slice.7.refs_9_), channel_id=1, source_target_pairs={{8,0},{16,8},{24,16},{28,24},{20,28},{12,20},{4,12},{0,4},{9,1},{1... | collective-permute-start | bytes 3145736 | tf_op jit(solution)/shard_map/ppermute | solution.py:365
  5.0 28.4 %collective-permute-start.2 = (bf16[512,1024]{1,0:T(8,128)(2,1)S(1)}, bf16[512,1024]{1,0:T(8,128)(2,1)}, u32[]{:S(2)}, u32[]{:S(2)}) collective-permute-start(bf16[512,1024]{1,0:T(8,128)(2,1)S(1)} %slice.6.refs_4_), channel_id=1, source_target_pairs={{0,8},{8,16},{16,24},{24,28},{28,20},{20,12},{12,4},{4,0},{1,9},{9... | collective-permute-start | bytes 3145736 | tf_op jit(solution)/shard_map/ppermute | solution.py:363
  5.2 48.5 %collective-permute-start.13 = (bf16[512,1024]{1,0:T(8,128)(2,1)S(1)}, bf16[512,1024]{1,0:T(8,128)(2,1)}, u32[]{:S(2)}, u32[]{:S(2)}) collective-permute-start(bf16[512,1024]{1,0:T(8,128)(2,1)S(1)} %slice.7.refs_9_), channel_id=1, source_target_pairs={{0,8},{8,16},{16,24},{24,28},{28,20},{20,12},{12,4},{4,0},{1,9},{9... | collective-permute-start | bytes 3145736 | tf_op jit(solution)/shard_map/ppermute | solution.py:363
  9.0 15.2 %collective-permute-start.1 = (bf16[1024,256]{1,0:T(8,128)(2,1)}, bf16[1024,256]{1,0:T(8,128)(2,1)}, u32[]{:S(2)}, u32[]{:S(2)}) collective-permute-start(bf16[1024,256]{1,0:T(8,128)(2,1)} %constant_dynamic-slice_fusion.4), channel_id=1, source_target_pairs={{0,2},{1,3},{2,0},{3,1},{4,6},{5,7},{6,4},{7,5},{8,10},{9,11},{10,... | collective-permute-start | bytes 1572872 | tf_op jit(solution)/shard_map/ppermute | solution.py:160
  11.3 22.1 %collective-permute-start = (bf16[1024,256]{1,0:T(8,128)(2,1)}, bf16[1024,256]{1,0:T(8,128)(2,1)}, u32[]{:S(2)}, u32[]{:S(2)}) collective-permute-start(bf16[1024,256]{1,0:T(8,128)(2,1)} %constant_dynamic-slice_fusion.5), channel_id=1, source_target_pairs={{0,2},{1,3},{2,0},{3,1},{4,6},{5,7},{6,4},{7,5},{8,10},{9,11},{10,... | collective-permute-start | bytes 1572872 | tf_op jit(solution)/shard_map/ppermute | solution.py:160
  11.9 43.2 %copy-start.8 = (s32[1,1,16]{2,1,0:T(1,128)S(1)}, s32[1,1,16]{2,1,0:T(1,128)}, u32[]{:S(2)}) copy-start(s32[1,1,16]{2,1,0:T(1,128)} %param.12) | copy-start | bytes 196
  24.2 31.0 %collective-permute-start.10 = (bf16[512,1024]{1,0:T(8,128)(2,1)S(1)}, bf16[512,1024]{1,0:T(8,128)(2,1)}, u32[]{:S(2)}, u32[]{:S(2)}) collective-permute-start(bf16[512,1024]{1,0:T(8,128)(2,1)S(1)} %slice.6.refs_4_), channel_id=1, source_target_pairs={{8,0},{16,8},{24,16},{28,24},{20,28},{12,20},{4,12},{0,4},{9,1},{1... | collective-permute-start | bytes 3145736 | tf_op jit(solution)/shard_map/ppermute | solution.py:365
  35.6 21.6 %collective-permute-start.4 = (bf16[2048,256]{1,0:T(8,128)(2,1)}, bf16[2048,256]{1,0:T(8,128)(2,1)S(1)}, u32[]{:S(2)}, u32[]{:S(2)}) collective-permute-start(bf16[2048,256]{1,0:T(8,128)(2,1)} %maximum_maximum_fusion), channel_id=1, source_target_pairs={{0,1},{1,0},{2,3},{3,2},{4,5},{5,4},{6,7},{7,6},{8,9},{9,8},{10,11... | collective-permute-start | bytes 3145736 | tf_op jit(solution)/shard_map/ppermute | solution.py:164
  35.6 38.6 %collective-permute-start.16 = (bf16[512,1024]{1,0:T(8,128)(2,1)}, bf16[512,1024]{1,0:T(8,128)(2,1)}, u32[]{:S(2)}, u32[]{:S(2)}) collective-permute-start(bf16[512,1024]{1,0:T(8,128)(2,1)} %collective-permute-done.3.refs_11_), channel_id=1, source_target_pairs={{8,0},{16,8},{24,16},{28,24},{20,28},{12,20},{4,12},{0,4},{9,1},{1... | collective-permute-start | bytes 3145736 | tf_op jit(solution)/shard_map/ppermute | solution.py:365
  35.9 40.3 %collective-permute-start.8 = (bf16[512,1024]{1,0:T(8,128)(2,1)}, bf16[512,1024]{1,0:T(8,128)(2,1)}, u32[]{:S(2)}, u32[]{:S(2)}) collective-permute-start(bf16[512,1024]{1,0:T(8,128)(2,1)} %collective-permute-done.2.refs_5_), channel_id=1, source_target_pairs={{0,8},{8,16},{16,24},{24,28},{28,20},{20,12},{12,4},{4,0},{1,9},{9... | collective-permute-start | bytes 3145736 | tf_op jit(solution)/shard_map/ppermute | solution.py:363
  53.7 44.9 %collective-permute-start.14 = (bf16[512,1024]{1,0:T(8,128)(2,1)}, bf16[512,1024]{1,0:T(8,128)(2,1)}, u32[]{:S(2)}, u32[]{:S(2)}) collective-permute-start(bf16[512,1024]{1,0:T(8,128)(2,1)} %collective-permute-done.13.refs_10_), channel_id=1, source_target_pairs={{0,8},{8,16},{16,24},{24,28},{28,20},{20,12},{12,4},{4,0},{1,9},{9... | collective-permute-start | bytes 3145736 | tf_op jit(solution)/shard_map/ppermute | solution.py:363
  55.2 45.0 %collective-permute-start.11 = (bf16[512,1024]{1,0:T(8,128)(2,1)}, bf16[512,1024]{1,0:T(8,128)(2,1)}, u32[]{:S(2)}, u32[]{:S(2)}) collective-permute-start(bf16[512,1024]{1,0:T(8,128)(2,1)} %collective-permute-done.10.refs_6_), channel_id=1, source_target_pairs={{8,0},{16,8},{24,16},{28,24},{20,28},{12,20},{4,12},{0,4},{9,1},{1... | collective-permute-start | bytes 3145736 | tf_op jit(solution)/shard_map/ppermute | solution.py:365
  57.2 1.0 copy-start.1
  60.0 67.4 %copy-start = (bf16[512,1024]{1,0:T(8,128)(2,1)}, bf16[512,1024]{1,0:T(8,128)(2,1)S(1)}, u32[]{:S(2)}) copy-start(bf16[512,1024]{1,0:T(8,128)(2,1)S(1)} %attend.1.refs_0_) | copy-start | bytes 3145732
  60.0 40.2 %collective-permute-start.5 = (bf16[512,1024]{1,0:T(8,128)(2,1)S(1)}, bf16[512,1024]{1,0:T(8,128)(2,1)S(1)}, u32[]{:S(2)}, u32[]{:S(2)}) collective-permute-start(bf16[512,1024]{1,0:T(8,128)(2,1)S(1)} %attend.1.refs_0_), channel_id=1, source_target_pairs={{0,1},{1,0},{2,3},{3,2},{4,5},{5,4},{6,7},{7,6},{8,9},{9,8},{10,11... | collective-permute-start | bytes 3145736 | tf_op jit(solution)/shard_map/ppermute | solution.py:387
  74.1 26.6 %collective-permute-start.6 = (bf16[512,1024]{1,0:T(8,128)(2,1)S(1)}, bf16[512,1024]{1,0:T(8,128)(2,1)S(1)}, u32[]{:S(2)}, u32[]{:S(2)}) collective-permute-start(bf16[512,1024]{1,0:T(8,128)(2,1)S(1)} %attend.1.refs_0_), channel_id=1, source_target_pairs={{0,2},{1,3},{2,0},{3,1},{4,6},{5,7},{6,4},{7,5},{8,10},{9,11},{10,... | collective-permute-start | bytes 3145736 | tf_op jit(solution)/shard_map/ppermute | solution.py:386
  76.2 44.9 %collective-permute-start.9 = (bf16[512,1024]{1,0:T(8,128)(2,1)}, bf16[512,1024]{1,0:T(8,128)(2,1)}, u32[]{:S(2)}, u32[]{:S(2)}) collective-permute-start(bf16[512,1024]{1,0:T(8,128)(2,1)} %collective-permute-done.8.refs_7_), channel_id=1, source_target_pairs={{0,8},{8,16},{16,24},{24,28},{28,20},{20,12},{12,4},{4,0},{1,9},{9... | collective-permute-start | bytes 3145736 | tf_op jit(solution)/shard_map/ppermute | solution.py:363
  98.6 26.4 %collective-permute-start.17 = (bf16[512,1024]{1,0:T(8,128)(2,1)}, bf16[512,1024]{1,0:T(8,128)(2,1)}, u32[]{:S(2)}, u32[]{:S(2)}) collective-permute-start(bf16[512,1024]{1,0:T(8,128)(2,1)} %collective-permute-done.16.refs_13_), channel_id=1, source_target_pairs={{8,0},{16,8},{24,16},{28,24},{20,28},{12,20},{4,12},{0,4},{9,1},{1... | collective-permute-start | bytes 3145736 | tf_op jit(solution)/shard_map/ppermute | solution.py:365
  100.2 27.2 %collective-permute-start.7 = (bf16[512,1024]{1,0:T(8,128)(2,1)S(1)}, bf16[512,1024]{1,0:T(8,128)(2,1)}, u32[]{:S(2)}, u32[]{:S(2)}) collective-permute-start(bf16[512,1024]{1,0:T(8,128)(2,1)S(1)} %attend.1.refs_0_), channel_id=1, source_target_pairs={{0,3},{1,2},{2,1},{3,0},{4,7},{5,6},{6,5},{7,4},{8,11},{9,10},{10,... | collective-permute-start | bytes 3145736 | tf_op jit(solution)/shard_map/ppermute | solution.py:388
  100.2 21.0 %copy-start.2 = (bf16[512,1024]{1,0:T(8,128)(2,1)}, bf16[512,1024]{1,0:T(8,128)(2,1)S(1)}, u32[]{:S(2)}) copy-start(bf16[512,1024]{1,0:T(8,128)(2,1)S(1)} %collective-permute-done.5.refs_1_) | copy-start | bytes 3145732
  100.2 43.3 %collective-permute-start.15 = (bf16[512,1024]{1,0:T(8,128)(2,1)}, bf16[512,1024]{1,0:T(8,128)(2,1)}, u32[]{:S(2)}, u32[]{:S(2)}) collective-permute-start(bf16[512,1024]{1,0:T(8,128)(2,1)} %collective-permute-done.14.refs_12_), channel_id=1, source_target_pairs={{0,8},{8,16},{16,24},{24,28},{28,20},{20,12},{12,4},{4,0},{1,9},{9... | collective-permute-start | bytes 3145736 | tf_op jit(solution)/shard_map/ppermute | solution.py:363
  100.7 24.3 %copy-start.3 = (bf16[512,1024]{1,0:T(8,128)(2,1)}, bf16[512,1024]{1,0:T(8,128)(2,1)S(1)}, u32[]{:S(2)}) copy-start(bf16[512,1024]{1,0:T(8,128)(2,1)S(1)} %collective-permute-done.6.refs_2_) | copy-start | bytes 3145732
  100.7 46.8 %collective-permute-start.12 = (bf16[512,1024]{1,0:T(8,128)(2,1)}, bf16[512,1024]{1,0:T(8,128)(2,1)}, u32[]{:S(2)}, u32[]{:S(2)}) collective-permute-start(bf16[512,1024]{1,0:T(8,128)(2,1)} %collective-permute-done.11.refs_8_), channel_id=1, source_target_pairs={{8,0},{16,8},{24,16},{28,24},{20,28},{12,20},{4,12},{0,4},{9,1},{1... | collective-permute-start | bytes 3145736 | tf_op jit(solution)/shard_map/ppermute | solution.py:365
  121.1 43.4 %collective-permute-start.19 = (bf16[512,1024]{1,0:T(8,128)(2,1)}, bf16[512,1024]{1,0:T(8,128)(2,1)S(1)}, u32[]{:S(2)}, u32[]{:S(2)}) collective-permute-start(bf16[512,1024]{1,0:T(8,128)(2,1)} %collective-permute-done.9.refs_4_), channel_id=1, source_target_pairs={{0,8},{8,16},{16,24},{24,28},{28,20},{20,12},{12,4},{4,0},{1,9},{9... | collective-permute-start | bytes 3145736 | tf_op jit(solution)/shard_map/ppermute | solution.py:363
  125.1 41.0 %collective-permute-start.18 = (bf16[512,1024]{1,0:T(8,128)(2,1)}, bf16[512,1024]{1,0:T(8,128)(2,1)S(1)}, u32[]{:S(2)}, u32[]{:S(2)}) collective-permute-start(bf16[512,1024]{1,0:T(8,128)(2,1)} %collective-permute-done.17.refs_7_), channel_id=1, source_target_pairs={{8,0},{16,8},{24,16},{28,24},{20,28},{12,20},{4,12},{0,4},{9,1},{1... | collective-permute-start | bytes 3145736 | tf_op jit(solution)/shard_map/ppermute | solution.py:365

commit v14 on v12

--- a/solution.py
+++ b/solution.py
@@ -382,6 +382,10 @@
     keep(1)
     for hop in range(2, far + 1):
         travel(hop)
+        if hop == 2:
+            attn, moving[0][:], moving[1][:] = lax.optimization_barrier(
+                (attn, moving[0], moving[1])
+            )
         keep(hop)
     across = lax.ppermute(attn, "ka", [(i, i ^ 2) for i in range(4)])
     beside = lax.ppermute(attn, "ka", [(i, i ^ 1) for i in range(4)])

time: 167 us -> 177 us (1.060)
  waiting for transfers between devices: 114 us -> 122 us
    ppermute x1, waiting for transfers between devices: 0.01 us -> 22.2 us  [project_ring(): across = lax.ppermute(attn, 'ka', [(i, i ^ 2) for i in range(4)])]
    ppermute x7, waiting for transfers between devices: 64.7 us -> 43 us  [travel(): moving[part][1] = lax.ppermute(moving[part][1], 'pb', backward)]
    ppermute x1, waiting for transfers between devices: 0.01 us -> 17.4 us  [project_ring(): corner = lax.ppermute(attn, 'ka', [(i, i ^ 3) for i in range(4)])]
    ppermute x7, waiting for transfers between devices: 29.3 us -> 21.6 us  [travel(): moving[part][0] = lax.ppermute(moving[part][0], 'pb', forward)]
    ppermute x2, starting transfers between devices: 2.03 us -> 4.74 us  [own_head_keys_values(): lax.ppermute(heads_of(a, 1 - x), 'ka', [(i, i ^ 2) for i in range(4)])]
    ppermute x2, waiting for transfers between devices: 20.1 us -> 17.8 us  [own_head_keys_values(): lax.ppermute(heads_of(a, 1 - x), 'ka', [(i, i ^ 2) for i in range(4)])]
  transfers between devices with their start and end apart: 20 -> 20, of which waited for: 10 -> 10; matrix products, arithmetic and copies ran while one was open for 4% -> 2% of each run, Pallas kernels for 13% -> 12%
where the time goes in v14:
time: 177 us; the launch traced here: 176 us
  waiting for transfers between devices  122 us (69%)
  Pallas kernels  23.1 us (13%)
  starting transfers between devices  20.4 us (12%)
  local copies, waits for them, and re-layouts  9.36 us (5%)
    ppermute x7, waiting for transfers between devices, travel(): moving[part][1] = lax.ppermute(moving[part][1], 'pb', backward)  43 us
    ppermute x1, waiting for transfers between devices, project_ring(): across = lax.ppermute(attn, 'ka', [(i, i ^ 2) for i in range(4)])  22.2 us
    ppermute x7, waiting for transfers between devices, travel(): moving[part][0] = lax.ppermute(moving[part][0], 'pb', forward)  21.6 us
    pallas_call x2, Pallas kernels, ring_product(): pl.pallas_call(functools.partial(ring_product_kernel, steps, spare_step),...  18.4 us
    ppermute x2, waiting for transfers between devices, own_head_keys_values(): lax.ppermute(heads_of(a, 1 - x), 'ka', [(i, i ^ 2) for i in range(4)])  17.8 us
    ppermute x1, waiting for transfers between devices, project_ring(): corner = lax.ppermute(attn, 'ka', [(i, i ^ 3) for i in range(4)])  17.4 us
    ppermute x7, starting transfers between devices, travel(): moving[part][0] = lax.ppermute(moving[part][0], 'pb', forward)  10 us
    ppermute x2, starting transfers between devices, own_head_keys_values(): lax.ppermute(heads_of(a, 1 - x), 'ka', [(i, i ^ 2) for i in range(4)])  4.74 us
  transfers between devices with their start and end apart: 20, of which 10 were waited for; matrix products, arithmetic and copies ran while one was open for 2% of the time, Pallas kernels for 12%

profile of v14, /device:TPU:0, one launch (start us, length us, event | category | flops | bytes accessed | tf_op | source)
XLA Modules:
  0.0 176.5 jit_solution(14389924278968805824)
XLA Ops:
  0.0 1.4 slice.6.refs_4_
  2.0 1.9 %constant_dynamic-slice_fusion.4 = bf16[1024,256]{1,0:T(8,128)(2,1)S(1)} fusion(bf16[1024,512]{1,0:T(8,128)(2,1)} %refs_1_, s32[]{:T(128)S(6)} %select_n.29), kind=kLoop, calls=%fused_computation.5 | loop fusion | bytes 1048580 | tf_op jit(solution)/shard_map/dynamic_slice | solution.py:154
  3.9 3.0 %collective-permute-start.1 = (bf16[1024,256]{1,0:T(8,128)(2,1)S(1)}, bf16[1024,256]{1,0:T(8,128)(2,1)S(1)}, u32[]{:S(2)}, u32[]{:S(2)}) collective-permute-start(bf16[1024,256]{1,0:T(8,128)(2,1)S(1)} %constant_dynamic-slice_fusion.4), channel_id=1, source_target_pairs={{0,2},{1,3},{2,0},{3,1},{4,6},{5,7},{6,4},{7,5},{8,10},{9,11},{10,... | collective-permute-start | bytes 1572872 | tf_op jit(solution)/shard_map/ppermute | solution.py:160
  6.9 1.6 collective-permute-start.2
  9.0 1.5 collective-permute-start.9
  11.0 0.8 constant_dynamic-slice_fusion.5
  11.8 7.0 %collective-permute-done.1.refs_3_ = bf16[1024,256]{1,0:T(8,128)(2,1)S(1)} collective-permute-done((bf16[1024,256]{1,0:T(8,128)(2,1)S(1)}, bf16[1024,256]{1,0:T(8,128)(2,1)S(1)}, u32[]{:S(2)}, u32[]{:S(2)}) %collective-permute-start.1) | collective-permute-done | bytes 524320 | tf_op jit(solution)/shard_map/ppermute | solution.py:160
  18.9 0.8 copy-done.8
  19.6 1.7 collective-permute-start
  21.4 1.0 constant_dynamic-slice_fusion.2
  22.4 10.8 %collective-permute-done.refs_2_ = bf16[1024,256]{1,0:T(8,128)(2,1)} collective-permute-done((bf16[1024,256]{1,0:T(8,128)(2,1)}, bf16[1024,256]{1,0:T(8,128)(2,1)}, u32[]{:S(2)}, u32[]{:S(2)}) %collective-permute-start) | collective-permute-done | bytes 524320 | tf_op jit(solution)/shard_map/ppermute | solution.py:160
  33.2 1.5 collective-permute-done.3.refs_6_
  34.7 1.1 constant_dynamic-slice_fusion
  36.0 1.6 collective-permute-start.5
  38.1 19.1 %collective-permute-done.9.refs_11_ = bf16[512,1024]{1,0:T(8,128)(2,1)} collective-permute-done((bf16[512,1024]{1,0:T(8,128)(2,1)S(1)}, bf16[512,1024]{1,0:T(8,128)(2,1)}, u32[]{:S(2)}, u32[]{:S(2)}) %collective-permute-start.9) | collective-permute-done | bytes 1048608 | tf_op jit(solution)/shard_map/ppermute | solution.py:365
  57.6 1.6 collective-permute-start.8
  60.6 1.0 copy-done.1
  61.6 1.8 %attend.1.refs_0_ = bf16[512,1024]{1,0:T(8,128)(2,1)S(1)} custom-call(s32[34]{0:T(128)S(1)} %concatenate.16.meta_ref, bf16[512,1024]{1,0:T(8,128)(2,1)} %bitcast.15, bf16[512,1024]{1,0:T(8,128)(2,1)} %bitcast.16, bf16[1024,512]{1,0:T(8,128)(2,1)} %refs_0_, bf16[1024,512]{1,0:T(8,128)(2,1)} %refs_1_, bf16[1024,256]{1,0:T(8,128)(2,1)} %collective-permute-done.refs_2_, ...), custom_call_target="tpu_custom_call" | custom-call | flops 1048576 | bytes 1048576 | tf_op jit(solution)/shard_map/attend/pallas_call | solution.py:118
  63.5 14.6 %collective-permute-done.5.refs_7_ = bf16[512,1024]{1,0:T(8,128)(2,1)} collective-permute-done((bf16[512,1024]{1,0:T(8,128)(2,1)}, bf16[512,1024]{1,0:T(8,128)(2,1)}, u32[]{:S(2)}, u32[]{:S(2)}) %collective-permute-start.5) | collective-permute-done | bytes 1048608 | tf_op jit(solution)/shard_map/ppermute | solution.py:363
  78.1 1.6 collective-permute-done.6.refs_8_
  79.7 20.7 %collective-permute-done.10.refs_13_ = bf16[512,1024]{1,0:T(8,128)(2,1)} collective-permute-done((bf16[512,1024]{1,0:T(8,128)(2,1)}, bf16[512,1024]{1,0:T(8,128)(2,1)}, u32[]{:S(2)}, u32[]{:S(2)}) %collective-permute-start.10) | collective-permute-done | bytes 1048608 | tf_op jit(solution)/shard_map/ppermute | solution.py:365
  100.9 1.6 collective-permute-start.14
  102.9 0.8 collective-permute-start.13
  104.2 22.2 %collective-permute-done.12.refs_2_ = bf16[512,1024]{1,0:T(8,128)(2,1)S(1)} collective-permute-done((bf16[512,1024]{1,0:T(8,128)(2,1)S(1)}, bf16[512,1024]{1,0:T(8,128)(2,1)S(1)}, u32[]{:S(2)}, u32[]{:S(2)}) %collective-permute-start.12) | collective-permute-done | bytes 1048608 | tf_op jit(solution)/shard_map/ppermute | solution.py:390
  126.3 1.6 collective-permute-start.16
  127.9 1.6 collective-permute-start.19
  130.8 17.4 %collective-permute-done.13.refs_3_ = bf16[512,1024]{1,0:T(8,128)(2,1)} collective-permute-done((bf16[512,1024]{1,0:T(8,128)(2,1)S(1)}, bf16[512,1024]{1,0:T(8,128)(2,1)}, u32[]{:S(2)}, u32[]{:S(2)}) %collective-permute-start.13) | collective-permute-done | bytes 1048608 | tf_op jit(solution)/shard_map/ppermute | solution.py:392
  148.1 11.7 %ring_product.2.refs_8_ = f32[512,2048]{1,0:T(8,128)S(1)} custom-call(s32[9]{0:T(128)S(1)} %pad_add_fusion.where_ref, bf16[512,1024]{1,0:T(8,128)(2,1)} %copy-done, bf16[512,1024]{1,0:T(8,128)(2,1)} %copy-done.2, bf16[512,1024]{1,0:T(8,128)(2,1)} %copy-done.3, bf16[512,1024]{1,0:T(8,128)(2,1)} %collective-permute-done.13.refs_3_, ...), custom_call_target="tpu_custom_call" | custom-call | flops 1048576 | bytes 1048576 | tf_op jit(solution)/shard_map/ring_product/pallas_call | solution.py:285
  159.9 6.6 %ring_product.3 = (f32[512,2048]{1,0:T(8,128)S(1)}, bf16[512,512]{1,0:T(8,128)(2,1)S(1)}) custom-call(s32[9]{0:T(128)S(1)} %pad_add_fusion.where_ref, bf16[512,1024]{1,0:T(8,128)(2,1)} %copy-done, bf16[512,1024]{1,0:T(8,128)(2,1)} %copy-done.2, bf16[512,1024]{1,0:T(8,128)(2,1)} %copy-done.3, bf16[512,1024]{1,0:T(8,128)(2,1)} %collective-permute-done.13.refs_3_, ...), custom_call_target="tpu_custom_call" | custom-call | flops 1048576 | bytes 1048576 | tf_op jit(solution)/shard_map/ring_product/pallas_call | solution.py:285
  166.5 7.0 %collective-permute-done.19.slab_ref = bf16[512,1024]{1,0:T(8,128)(2,1)S(1)} collective-permute-done((bf16[512,1024]{1,0:T(8,128)(2,1)}, bf16[512,1024]{1,0:T(8,128)(2,1)S(1)}, u32[]{:S(2)}, u32[]{:S(2)}) %collective-permute-start.19) | collective-permute-done | bytes 1048608 | tf_op jit(solution)/shard_map/ppermute | solution.py:363
  173.5 1.5 last_product.2.refs_0_
  175.0 1.5 last_product.3
  (43 shorter events, 5.5 us)
Async XLA Ops:
  0.0 1.9 %copy-start.7 = (bf16[512,2048]{1,0:T(8,128)(2,1)S(1)}, bf16[512,2048]{1,0:T(8,128)(2,1)}, u32[]{:S(2)}) copy-start(bf16[512,2048]{1,0:T(8,128)(2,1)} %param.16) | copy-start | bytes 6291460
  1.9 9.9 %copy-start.4 = (bf16[512,1024]{1,0:T(8,128)(2,1)}, bf16[512,1024]{1,0:T(8,128)(2,1)S(1)}, u32[]{:S(2)}) copy-start(bf16[512,1024]{1,0:T(8,128)(2,1)S(1)} %slice.6.refs_4_) | copy-start | bytes 3145732
  1.9 9.1 %copy-start.6 = (bf16[1024,512]{1,0:T(8,128)(2,1)S(1)}, bf16[1024,512]{1,0:T(8,128)(2,1)}, u32[]{:S(2)}) copy-start(bf16[1024,512]{1,0:T(8,128)(2,1)} %refs_0_) | copy-start | bytes 3145732
  2.0 33.8 %copy-start.5 = (bf16[512,1024]{1,0:T(8,128)(2,1)}, bf16[512,1024]{1,0:T(8,128)(2,1)S(1)}, u32[]{:S(2)}) copy-start(bf16[512,1024]{1,0:T(8,128)(2,1)S(1)} %slice.7.refs_9_) | copy-start | bytes 3145732
  3.9 14.9 %collective-permute-start.1 = (bf16[1024,256]{1,0:T(8,128)(2,1)S(1)}, bf16[1024,256]{1,0:T(8,128)(2,1)S(1)}, u32[]{:S(2)}, u32[]{:S(2)}) collective-permute-start(bf16[1024,256]{1,0:T(8,128)(2,1)S(1)} %constant_dynamic-slice_fusion.4), channel_id=1, source_target_pairs={{0,2},{1,3},{2,0},{3,1},{4,6},{5,7},{6,4},{7,5},{8,10},{9,11},{10,... | collective-permute-start | bytes 1572872 | tf_op jit(solution)/shard_map/ppermute | solution.py:160
  6.9 26.2 %collective-permute-start.2 = (bf16[512,1024]{1,0:T(8,128)(2,1)S(1)}, bf16[512,1024]{1,0:T(8,128)(2,1)}, u32[]{:S(2)}, u32[]{:S(2)}) collective-permute-start(bf16[512,1024]{1,0:T(8,128)(2,1)S(1)} %slice.6.refs_4_), channel_id=1, source_target_pairs={{0,8},{8,16},{16,24},{24,28},{28,20},{20,12},{12,4},{4,0},{1,9},{9... | collective-permute-start | bytes 3145736 | tf_op jit(solution)/shard_map/ppermute | solution.py:363
  8.5 26.2 %collective-permute-start.3 = (bf16[512,1024]{1,0:T(8,128)(2,1)S(1)}, bf16[512,1024]{1,0:T(8,128)(2,1)}, u32[]{:S(2)}, u32[]{:S(2)}) collective-permute-start(bf16[512,1024]{1,0:T(8,128)(2,1)S(1)} %slice.6.refs_4_), channel_id=1, source_target_pairs={{8,0},{16,8},{24,16},{28,24},{20,28},{12,20},{4,12},{0,4},{9,1},{1... | collective-permute-start | bytes 3145736 | tf_op jit(solution)/shard_map/ppermute | solution.py:365
  9.0 48.2 %collective-permute-start.9 = (bf16[512,1024]{1,0:T(8,128)(2,1)S(1)}, bf16[512,1024]{1,0:T(8,128)(2,1)}, u32[]{:S(2)}, u32[]{:S(2)}) collective-permute-start(bf16[512,1024]{1,0:T(8,128)(2,1)S(1)} %slice.7.refs_9_), channel_id=1, source_target_pairs={{8,0},{16,8},{24,16},{28,24},{20,28},{12,20},{4,12},{0,4},{9,1},{1... | collective-permute-start | bytes 3145736 | tf_op jit(solution)/shard_map/ppermute | solution.py:365
  10.5 47.2 %collective-permute-start.7 = (bf16[512,1024]{1,0:T(8,128)(2,1)S(1)}, bf16[512,1024]{1,0:T(8,128)(2,1)}, u32[]{:S(2)}, u32[]{:S(2)}) collective-permute-start(bf16[512,1024]{1,0:T(8,128)(2,1)S(1)} %slice.7.refs_9_), channel_id=1, source_target_pairs={{0,8},{8,16},{16,24},{24,28},{28,20},{20,12},{12,4},{4,0},{1,9},{9... | collective-permute-start | bytes 3145736 | tf_op jit(solution)/shard_map/ppermute | solution.py:363
  18.9 0.8 copy-start.8
  19.6 13.5 %collective-permute-start = (bf16[1024,256]{1,0:T(8,128)(2,1)}, bf16[1024,256]{1,0:T(8,128)(2,1)}, u32[]{:S(2)}, u32[]{:S(2)}) collective-permute-start(bf16[1024,256]{1,0:T(8,128)(2,1)} %constant_dynamic-slice_fusion.5), channel_id=1, source_target_pairs={{0,2},{1,3},{2,0},{3,1},{4,6},{5,7},{6,4},{7,5},{8,10},{9,11},{10,... | collective-permute-start | bytes 1572872 | tf_op jit(solution)/shard_map/ppermute | solution.py:160
  21.4 39.1 %copy-start.9 = (s32[1,1,16]{2,1,0:T(1,128)S(1)}, s32[1,1,16]{2,1,0:T(1,128)}, u32[]{:S(2)}) copy-start(s32[1,1,16]{2,1,0:T(1,128)} %param.12) | copy-start | bytes 196
  35.9 24.7 %collective-permute-start.4 = (bf16[2048,256]{1,0:T(8,128)(2,1)S(1)}, bf16[2048,256]{1,0:T(8,128)(2,1)S(1)}, u32[]{:S(2)}, u32[]{:S(2)}) collective-permute-start(bf16[2048,256]{1,0:T(8,128)(2,1)S(1)} %maximum_maximum_fusion), channel_id=1, source_target_pairs={{0,1},{1,0},{2,3},{3,2},{4,5},{5,4},{6,7},{7,6},{8,9},{9,8},{10,11... | collective-permute-start | bytes 3145736 | tf_op jit(solution)/shard_map/ppermute | solution.py:164
  36.0 42.1 %collective-permute-start.5 = (bf16[512,1024]{1,0:T(8,128)(2,1)}, bf16[512,1024]{1,0:T(8,128)(2,1)}, u32[]{:S(2)}, u32[]{:S(2)}) collective-permute-start(bf16[512,1024]{1,0:T(8,128)(2,1)} %collective-permute-done.2.refs_5_), channel_id=1, source_target_pairs={{0,8},{8,16},{16,24},{24,28},{28,20},{20,12},{12,4},{4,0},{1,9},{9... | collective-permute-start | bytes 3145736 | tf_op jit(solution)/shard_map/ppermute | solution.py:363
  37.6 42.0 %collective-permute-start.6 = (bf16[512,1024]{1,0:T(8,128)(2,1)}, bf16[512,1024]{1,0:T(8,128)(2,1)}, u32[]{:S(2)}, u32[]{:S(2)}) collective-permute-start(bf16[512,1024]{1,0:T(8,128)(2,1)} %collective-permute-done.3.refs_6_), channel_id=1, source_target_pairs={{8,0},{16,8},{24,16},{28,24},{20,28},{12,20},{4,12},{0,4},{9,1},{1... | collective-permute-start | bytes 3145736 | tf_op jit(solution)/shard_map/ppermute | solution.py:365
  57.2 43.2 %collective-permute-start.10 = (bf16[512,1024]{1,0:T(8,128)(2,1)}, bf16[512,1024]{1,0:T(8,128)(2,1)}, u32[]{:S(2)}, u32[]{:S(2)}) collective-permute-start(bf16[512,1024]{1,0:T(8,128)(2,1)} %collective-permute-done.9.refs_11_), channel_id=1, source_target_pairs={{8,0},{16,8},{24,16},{28,24},{20,28},{12,20},{4,12},{0,4},{9,1},{1... | collective-permute-start | bytes 3145736 | tf_op jit(solution)/shard_map/ppermute | solution.py:365
  57.6 42.7 %collective-permute-start.8 = (bf16[512,1024]{1,0:T(8,128)(2,1)}, bf16[512,1024]{1,0:T(8,128)(2,1)}, u32[]{:S(2)}, u32[]{:S(2)}) collective-permute-start(bf16[512,1024]{1,0:T(8,128)(2,1)} %collective-permute-done.7.refs_10_), channel_id=1, source_target_pairs={{0,8},{8,16},{16,24},{24,28},{28,20},{20,12},{12,4},{4,0},{1,9},{9... | collective-permute-start | bytes 3145736 | tf_op jit(solution)/shard_map/ppermute | solution.py:363
  60.6 1.0 copy-start.1
  63.5 84.7 %copy-start = (bf16[512,1024]{1,0:T(8,128)(2,1)}, bf16[512,1024]{1,0:T(8,128)(2,1)S(1)}, u32[]{:S(2)}) copy-start(bf16[512,1024]{1,0:T(8,128)(2,1)S(1)} %attend.1.refs_0_) | copy-start | bytes 3145732
  100.4 3.3 %collective-permute-start.11 = (bf16[512,1024]{1,0:T(8,128)(2,1)S(1)}, bf16[512,1024]{1,0:T(8,128)(2,1)S(1)}, u32[]{:S(2)}, u32[]{:S(2)}) collective-permute-start(bf16[512,1024]{1,0:T(8,128)(2,1)S(1)} %attend.1.refs_0_), channel_id=1, source_target_pairs={{0,1},{1,0},{2,3},{3,2},{4,5},{5,4},{6,7},{7,6},{8,9},{9,8},{10,11... | collective-permute-start | bytes 3145736 | tf_op jit(solution)/shard_map/ppermute | solution.py:391
  100.4 26.0 %collective-permute-start.12 = (bf16[512,1024]{1,0:T(8,128)(2,1)S(1)}, bf16[512,1024]{1,0:T(8,128)(2,1)S(1)}, u32[]{:S(2)}, u32[]{:S(2)}) collective-permute-start(bf16[512,1024]{1,0:T(8,128)(2,1)S(1)} %attend.1.refs_0_), channel_id=1, source_target_pairs={{0,2},{1,3},{2,0},{3,1},{4,6},{5,7},{6,4},{7,5},{8,10},{9,11},{10,... | collective-permute-start | bytes 3145736 | tf_op jit(solution)/shard_map/ppermute | solution.py:390
  100.9 27.0 %collective-permute-start.14 = (bf16[512,1024]{1,0:T(8,128)(2,1)}, bf16[512,1024]{1,0:T(8,128)(2,1)}, u32[]{:S(2)}, u32[]{:S(2)}) collective-permute-start(bf16[512,1024]{1,0:T(8,128)(2,1)} %collective-permute-done.5.refs_7_), channel_id=1, source_target_pairs={{0,8},{8,16},{16,24},{24,28},{28,20},{20,12},{12,4},{4,0},{1,9},{9... | collective-permute-start | bytes 3145736 | tf_op jit(solution)/shard_map/ppermute | solution.py:363
  102.5 27.0 %collective-permute-start.17 = (bf16[512,1024]{1,0:T(8,128)(2,1)}, bf16[512,1024]{1,0:T(8,128)(2,1)}, u32[]{:S(2)}, u32[]{:S(2)}) collective-permute-start(bf16[512,1024]{1,0:T(8,128)(2,1)} %collective-permute-done.10.refs_13_), channel_id=1, source_target_pairs={{8,0},{16,8},{24,16},{28,24},{20,28},{12,20},{4,12},{0,4},{9,1},{1... | collective-permute-start | bytes 3145736 | tf_op jit(solution)/shard_map/ppermute | solution.py:365
  102.9 45.2 %collective-permute-start.13 = (bf16[512,1024]{1,0:T(8,128)(2,1)S(1)}, bf16[512,1024]{1,0:T(8,128)(2,1)}, u32[]{:S(2)}, u32[]{:S(2)}) collective-permute-start(bf16[512,1024]{1,0:T(8,128)(2,1)S(1)} %attend.1.refs_0_), channel_id=1, source_target_pairs={{0,3},{1,2},{2,1},{3,0},{4,7},{5,6},{6,5},{7,4},{8,11},{9,10},{10,... | collective-permute-start | bytes 3145736 | tf_op jit(solution)/shard_map/ppermute | solution.py:392
  103.7 25.8 %copy-start.2 = (bf16[512,1024]{1,0:T(8,128)(2,1)}, bf16[512,1024]{1,0:T(8,128)(2,1)S(1)}, u32[]{:S(2)}) copy-start(bf16[512,1024]{1,0:T(8,128)(2,1)S(1)} %collective-permute-done.11.refs_1_) | copy-start | bytes 3145732
  103.7 56.2 %collective-permute-start.15 = (bf16[512,1024]{1,0:T(8,128)(2,1)}, bf16[512,1024]{1,0:T(8,128)(2,1)}, u32[]{:S(2)}, u32[]{:S(2)}) collective-permute-start(bf16[512,1024]{1,0:T(8,128)(2,1)} %collective-permute-done.6.refs_8_), channel_id=1, source_target_pairs={{8,0},{16,8},{24,16},{28,24},{20,28},{12,20},{4,12},{0,4},{9,1},{1... | collective-permute-start | bytes 3145736 | tf_op jit(solution)/shard_map/ppermute | solution.py:365
  126.3 3.2 %copy-start.3 = (bf16[512,1024]{1,0:T(8,128)(2,1)}, bf16[512,1024]{1,0:T(8,128)(2,1)S(1)}, u32[]{:S(2)}) copy-start(bf16[512,1024]{1,0:T(8,128)(2,1)S(1)} %collective-permute-done.12.refs_2_) | copy-start | bytes 3145732
  126.3 33.5 %collective-permute-start.16 = (bf16[512,1024]{1,0:T(8,128)(2,1)}, bf16[512,1024]{1,0:T(8,128)(2,1)}, u32[]{:S(2)}, u32[]{:S(2)}) collective-permute-start(bf16[512,1024]{1,0:T(8,128)(2,1)} %collective-permute-done.8.refs_12_), channel_id=1, source_target_pairs={{0,8},{8,16},{16,24},{24,28},{28,20},{20,12},{12,4},{4,0},{1,9},{9... | collective-permute-start | bytes 3145736 | tf_op jit(solution)/shard_map/ppermute | solution.py:363
  127.9 45.6 %collective-permute-start.19 = (bf16[512,1024]{1,0:T(8,128)(2,1)}, bf16[512,1024]{1,0:T(8,128)(2,1)S(1)}, u32[]{:S(2)}, u32[]{:S(2)}) collective-permute-start(bf16[512,1024]{1,0:T(8,128)(2,1)} %collective-permute-done.14.refs_4_), channel_id=1, source_target_pairs={{0,8},{8,16},{16,24},{24,28},{28,20},{20,12},{12,4},{4,0},{1,9},{9... | collective-permute-start | bytes 3145736 | tf_op jit(solution)/shard_map/ppermute | solution.py:363
  129.5 45.5 %collective-permute-start.18 = (bf16[512,1024]{1,0:T(8,128)(2,1)}, bf16[512,1024]{1,0:T(8,128)(2,1)S(1)}, u32[]{:S(2)}, u32[]{:S(2)}) collective-permute-start(bf16[512,1024]{1,0:T(8,128)(2,1)} %collective-permute-done.17.refs_7_), channel_id=1, source_target_pairs={{8,0},{16,8},{24,16},{28,24},{20,28},{12,20},{4,12},{0,4},{9,1},{1... | collective-permute-start | bytes 3145736 | tf_op jit(solution)/shard_map/ppermute | solution.py:365

commit v15 on v13

--- a/solution.py
+++ b/solution.py
@@ -372,8 +372,8 @@
                 slabs[part].append((hop, moving[part][1]))
 
     def gate(value):
-        value, moving[0][0], moving[1][1] = lax.optimization_barrier(
-            (value, moving[0][0], moving[1][1])
+        value, moving[1][1], moving[0][0], moving[0][1] = lax.optimization_barrier(
+            (value, moving[1][1], moving[0][0], moving[0][1])
         )
         return value
 

time: 168 us -> 172 us (1.024)
  waiting for transfers between devices: 113 us -> 118 us
    ppermute x7, waiting for transfers between devices: 21.9 us -> 63.8 us  [travel(): moving[part][1] = lax.ppermute(moving[part][1], 'pb', backward)]
    ppermute x7, waiting for transfers between devices: 70.7 us -> 34.1 us  [travel(): moving[part][0] = lax.ppermute(moving[part][0], 'pb', forward)]
    ppermute x7, starting transfers between devices: 10.2 us -> 13.3 us  [travel(): moving[part][1] = lax.ppermute(moving[part][1], 'pb', backward)]
    ppermute x7, starting transfers between devices: 5.95 us -> 3.34 us  [travel(): moving[part][0] = lax.ppermute(moving[part][0], 'pb', forward)]
  transfers between devices with their start and end apart: 20 -> 20, of which waited for: 12 -> 11; matrix products, arithmetic and copies ran while one was open for 4% -> 3% of each run, Pallas kernels for 13% -> 13%
where the time goes in v15:
time: 172 us
  waiting for transfers between devices  118 us (69%)
  Pallas kernels  23.1 us (13%)
  starting transfers between devices  20.5 us (12%)
  local copies, waits for them, and re-layouts  8.56 us (5%)
    ppermute x7, waiting for transfers between devices, travel(): moving[part][1] = lax.ppermute(moving[part][1], 'pb', backward)  63.8 us
    ppermute x7, waiting for transfers between devices, travel(): moving[part][0] = lax.ppermute(moving[part][0], 'pb', forward)  34.1 us
    ppermute x2, waiting for transfers between devices, own_head_keys_values(): lax.ppermute(heads_of(a, 1 - x), 'ka', [(i, i ^ 2) for i in range(4)])  20.4 us
    pallas_call x2, Pallas kernels, ring_product(): pl.pallas_call(functools.partial(ring_product_kernel, steps, spare_step),...  18.4 us
    ppermute x7, starting transfers between devices, travel(): moving[part][1] = lax.ppermute(moving[part][1], 'pb', backward)  13.3 us
  transfers between devices with their start and end apart: 20, of which 11 were waited for; matrix products, arithmetic and copies ran while one was open for 3% of the time, Pallas kernels for 13%

profile of v15, /device:TPU:0, one launch (start us, length us, event | category | flops | bytes accessed | tf_op | source)
XLA Modules:
  0.0 172.1 jit_solution(1448511127060115317)
XLA Ops:
  0.0 1.4 slice.6.refs_4_
  2.0 3.0 %collective-permute-start.2 = (bf16[512,1024]{1,0:T(8,128)(2,1)S(1)}, bf16[512,1024]{1,0:T(8,128)(2,1)}, u32[]{:S(2)}, u32[]{:S(2)}) collective-permute-start(bf16[512,1024]{1,0:T(8,128)(2,1)S(1)} %slice.7.refs_9_), channel_id=1, source_target_pairs={{8,0},{16,8},{24,16},{28,24},{20,28},{12,20},{4,12},{0,4},{9,1},{1... | collective-permute-start | bytes 3145736 | tf_op jit(solution)/shard_map/ppermute | solution.py:365
  5.2 1.9 %collective-permute-start.4 = (bf16[512,1024]{1,0:T(8,128)(2,1)S(1)}, bf16[512,1024]{1,0:T(8,128)(2,1)}, u32[]{:S(2)}, u32[]{:S(2)}) collective-permute-start(bf16[512,1024]{1,0:T(8,128)(2,1)S(1)} %slice.6.refs_4_), channel_id=1, source_target_pairs={{8,0},{16,8},{24,16},{28,24},{20,28},{12,20},{4,12},{0,4},{9,1},{1... | collective-permute-start | bytes 3145736 | tf_op jit(solution)/shard_map/ppermute | solution.py:365
  7.1 1.9 %constant_dynamic-slice_fusion.4 = bf16[1024,256]{1,0:T(8,128)(2,1)} fusion(bf16[1024,512]{1,0:T(8,128)(2,1)} %refs_1_, s32[]{:T(128)S(6)} %select_n.29), kind=kLoop, calls=%fused_computation.5 | loop fusion | bytes 1048580 | tf_op jit(solution)/shard_map/dynamic_slice | solution.py:154
  8.9 1.5 collective-permute-start.1
  10.4 0.8 constant_dynamic-slice_fusion.5
  11.3 0.5 collective-permute-start
  11.8 1.0 constant_dynamic-slice_fusion.2
  12.8 11.3 %collective-permute-done.1.refs_3_ = bf16[1024,256]{1,0:T(8,128)(2,1)} collective-permute-done((bf16[1024,256]{1,0:T(8,128)(2,1)}, bf16[1024,256]{1,0:T(8,128)(2,1)}, u32[]{:S(2)}, u32[]{:S(2)}) %collective-permute-start.1) | collective-permute-done | bytes 524320 | tf_op jit(solution)/shard_map/ppermute | solution.py:160
  24.3 9.1 %collective-permute-done.refs_2_ = bf16[1024,256]{1,0:T(8,128)(2,1)} collective-permute-done((bf16[1024,256]{1,0:T(8,128)(2,1)}, bf16[1024,256]{1,0:T(8,128)(2,1)}, u32[]{:S(2)}, u32[]{:S(2)}) %collective-permute-start) | collective-permute-done | bytes 524320 | tf_op jit(solution)/shard_map/ppermute | solution.py:160
  33.3 17.5 %collective-permute-done.4.refs_6_ = bf16[512,1024]{1,0:T(8,128)(2,1)} collective-permute-done((bf16[512,1024]{1,0:T(8,128)(2,1)S(1)}, bf16[512,1024]{1,0:T(8,128)(2,1)}, u32[]{:S(2)}, u32[]{:S(2)}) %collective-permute-start.4) | collective-permute-done | bytes 1048608 | tf_op jit(solution)/shard_map/ppermute | solution.py:365
  50.8 1.1 constant_dynamic-slice_fusion
  52.1 1.7 %collective-permute-start.11 = (bf16[512,1024]{1,0:T(8,128)(2,1)}, bf16[512,1024]{1,0:T(8,128)(2,1)}, u32[]{:S(2)}, u32[]{:S(2)}) collective-permute-start(bf16[512,1024]{1,0:T(8,128)(2,1)} %collective-permute-done.4.refs_6_), channel_id=1, source_target_pairs={{8,0},{16,8},{24,16},{28,24},{20,28},{12,20},{4,12},{0,4},{9,1},{1... | collective-permute-start | bytes 3145736 | tf_op jit(solution)/shard_map/ppermute | solution.py:365
  54.2 1.7 collective-permute-start.16
  57.7 1.0 copy-done.1
  58.7 1.8 %attend.1.refs_0_ = bf16[512,1024]{1,0:T(8,128)(2,1)S(1)} custom-call(s32[34]{0:T(128)S(1)} %concatenate.16.meta_ref, bf16[512,1024]{1,0:T(8,128)(2,1)} %bitcast.15, bf16[512,1024]{1,0:T(8,128)(2,1)} %bitcast.16, bf16[1024,512]{1,0:T(8,128)(2,1)} %refs_0_, bf16[1024,512]{1,0:T(8,128)(2,1)} %refs_1_, bf16[1024,256]{1,0:T(8,128)(2,1)} %collective-permute-done.refs_2_, ...), custom_call_target="tpu_custom_call" | custom-call | flops 1048576 | bytes 1048576 | tf_op jit(solution)/shard_map/attend/pallas_call | solution.py:118
  60.6 17.8 %collective-permute-done.11.refs_8_ = bf16[512,1024]{1,0:T(8,128)(2,1)} collective-permute-done((bf16[512,1024]{1,0:T(8,128)(2,1)}, bf16[512,1024]{1,0:T(8,128)(2,1)}, u32[]{:S(2)}, u32[]{:S(2)}) %collective-permute-start.11) | collective-permute-done | bytes 1048608 | tf_op jit(solution)/shard_map/ppermute | solution.py:365
  78.4 1.7 collective-permute-start.7
  80.2 1.5 collective-permute-start.10
  81.7 18.8 %collective-permute-done.16.refs_13_ = bf16[512,1024]{1,0:T(8,128)(2,1)} collective-permute-done((bf16[512,1024]{1,0:T(8,128)(2,1)}, bf16[512,1024]{1,0:T(8,128)(2,1)}, u32[]{:S(2)}, u32[]{:S(2)}) %collective-permute-start.16) | collective-permute-done | bytes 1048608 | tf_op jit(solution)/shard_map/ppermute | solution.py:365
  100.5 1.7 collective-permute-start.17
  102.6 1.6 collective-permute-start.12
  104.8 20.3 %collective-permute-done.10.refs_4_ = bf16[512,1024]{1,0:T(8,128)(2,1)} collective-permute-done((bf16[512,1024]{1,0:T(8,128)(2,1)}, bf16[512,1024]{1,0:T(8,128)(2,1)}, u32[]{:S(2)}, u32[]{:S(2)}) %collective-permute-start.10) | collective-permute-done | bytes 1048608 | tf_op jit(solution)/shard_map/ppermute | solution.py:363
  125.5 1.4 collective-permute-done.17.refs_7_
  126.8 1.7 collective-permute-start.18
  128.5 0.7 fusion
  129.3 11.7 %ring_product.2.refs_8_ = f32[512,2048]{1,0:T(8,128)S(1)} custom-call(s32[9]{0:T(128)S(1)} %pad_add_fusion.where_ref, bf16[512,1024]{1,0:T(8,128)(2,1)} %copy-done, bf16[512,1024]{1,0:T(8,128)(2,1)} %copy-done.2, bf16[512,1024]{1,0:T(8,128)(2,1)} %copy-done.3, bf16[512,1024]{1,0:T(8,128)(2,1)} %collective-permute-done.8.refs_3_, ...), custom_call_target="tpu_custom_call" | custom-call | flops 1048576 | bytes 1048576 | tf_op jit(solution)/shard_map/ring_product/pallas_call | solution.py:285
  141.1 8.3 %collective-permute-done.12.refs_5_ = bf16[512,1024]{1,0:T(8,128)(2,1)} collective-permute-done((bf16[512,1024]{1,0:T(8,128)(2,1)}, bf16[512,1024]{1,0:T(8,128)(2,1)}, u32[]{:S(2)}, u32[]{:S(2)}) %collective-permute-start.12) | collective-permute-done | bytes 1048608 | tf_op jit(solution)/shard_map/ppermute | solution.py:365
  149.3 6.6 %ring_product.3 = (f32[512,2048]{1,0:T(8,128)S(1)}, bf16[512,512]{1,0:T(8,128)(2,1)S(1)}) custom-call(s32[9]{0:T(128)S(1)} %pad_add_fusion.where_ref, bf16[512,1024]{1,0:T(8,128)(2,1)} %copy-done, bf16[512,1024]{1,0:T(8,128)(2,1)} %copy-done.2, bf16[512,1024]{1,0:T(8,128)(2,1)} %copy-done.3, bf16[512,1024]{1,0:T(8,128)(2,1)} %collective-permute-done.8.refs_3_, ...), custom_call_target="tpu_custom_call" | custom-call | flops 1048576 | bytes 1048576 | tf_op jit(solution)/shard_map/ring_product/pallas_call | solution.py:285
  155.9 13.2 %collective-permute-done.19.slab_ref = bf16[512,1024]{1,0:T(8,128)(2,1)S(1)} collective-permute-done((bf16[512,1024]{1,0:T(8,128)(2,1)}, bf16[512,1024]{1,0:T(8,128)(2,1)S(1)}, u32[]{:S(2)}, u32[]{:S(2)}) %collective-permute-start.19) | collective-permute-done | bytes 1048608 | tf_op jit(solution)/shard_map/ppermute | solution.py:363
  169.2 1.5 last_product.2.refs_0_
  170.6 1.5 last_product.3
  (41 shorter events, 3.4 us)
Async XLA Ops:
  0.0 1.9 %copy-start.7 = (bf16[512,2048]{1,0:T(8,128)(2,1)S(1)}, bf16[512,2048]{1,0:T(8,128)(2,1)}, u32[]{:S(2)}) copy-start(bf16[512,2048]{1,0:T(8,128)(2,1)} %param.16) | copy-start | bytes 6291460
  1.9 9.4 %copy-start.4 = (bf16[512,1024]{1,0:T(8,128)(2,1)}, bf16[512,1024]{1,0:T(8,128)(2,1)S(1)}, u32[]{:S(2)}) copy-start(bf16[512,1024]{1,0:T(8,128)(2,1)S(1)} %slice.6.refs_4_) | copy-start | bytes 3145732
  1.9 8.5 %copy-start.6 = (bf16[1024,512]{1,0:T(8,128)(2,1)S(1)}, bf16[1024,512]{1,0:T(8,128)(2,1)}, u32[]{:S(2)}) copy-start(bf16[1024,512]{1,0:T(8,128)(2,1)} %refs_0_) | copy-start | bytes 3145732
  2.0 49.9 %copy-start.5 = (bf16[512,1024]{1,0:T(8,128)(2,1)}, bf16[512,1024]{1,0:T(8,128)(2,1)S(1)}, u32[]{:S(2)}) copy-start(bf16[512,1024]{1,0:T(8,128)(2,1)S(1)} %slice.7.refs_9_) | copy-start | bytes 3145732
  2.0 31.3 %collective-permute-start.2 = (bf16[512,1024]{1,0:T(8,128)(2,1)S(1)}, bf16[512,1024]{1,0:T(8,128)(2,1)}, u32[]{:S(2)}, u32[]{:S(2)}) collective-permute-start(bf16[512,1024]{1,0:T(8,128)(2,1)S(1)} %slice.7.refs_9_), channel_id=1, source_target_pairs={{8,0},{16,8},{24,16},{28,24},{20,28},{12,20},{4,12},{0,4},{9,1},{1... | collective-permute-start | bytes 3145736 | tf_op jit(solution)/shard_map/ppermute | solution.py:365
  5.0 28.3 %collective-permute-start.3 = (bf16[512,1024]{1,0:T(8,128)(2,1)S(1)}, bf16[512,1024]{1,0:T(8,128)(2,1)}, u32[]{:S(2)}, u32[]{:S(2)}) collective-permute-start(bf16[512,1024]{1,0:T(8,128)(2,1)S(1)} %slice.6.refs_4_), channel_id=1, source_target_pairs={{0,8},{8,16},{16,24},{24,28},{28,20},{20,12},{12,4},{4,0},{1,9},{9... | collective-permute-start | bytes 3145736 | tf_op jit(solution)/shard_map/ppermute | solution.py:363
  5.2 45.7 %collective-permute-start.4 = (bf16[512,1024]{1,0:T(8,128)(2,1)S(1)}, bf16[512,1024]{1,0:T(8,128)(2,1)}, u32[]{:S(2)}, u32[]{:S(2)}) collective-permute-start(bf16[512,1024]{1,0:T(8,128)(2,1)S(1)} %slice.6.refs_4_), channel_id=1, source_target_pairs={{8,0},{16,8},{24,16},{28,24},{20,28},{12,20},{4,12},{0,4},{9,1},{1... | collective-permute-start | bytes 3145736 | tf_op jit(solution)/shard_map/ppermute | solution.py:365
  8.9 15.2 %collective-permute-start.1 = (bf16[1024,256]{1,0:T(8,128)(2,1)}, bf16[1024,256]{1,0:T(8,128)(2,1)}, u32[]{:S(2)}, u32[]{:S(2)}) collective-permute-start(bf16[1024,256]{1,0:T(8,128)(2,1)} %constant_dynamic-slice_fusion.4), channel_id=1, source_target_pairs={{0,2},{1,3},{2,0},{3,1},{4,6},{5,7},{6,4},{7,5},{8,10},{9,11},{10,... | collective-permute-start | bytes 1572872 | tf_op jit(solution)/shard_map/ppermute | solution.py:160
  11.3 22.1 %collective-permute-start = (bf16[1024,256]{1,0:T(8,128)(2,1)}, bf16[1024,256]{1,0:T(8,128)(2,1)}, u32[]{:S(2)}, u32[]{:S(2)}) collective-permute-start(bf16[1024,256]{1,0:T(8,128)(2,1)} %constant_dynamic-slice_fusion.5), channel_id=1, source_target_pairs={{0,2},{1,3},{2,0},{3,1},{4,6},{5,7},{6,4},{7,5},{8,10},{9,11},{10,... | collective-permute-start | bytes 1572872 | tf_op jit(solution)/shard_map/ppermute | solution.py:160
  11.8 45.4 %copy-start.8 = (s32[1,1,16]{2,1,0:T(1,128)S(1)}, s32[1,1,16]{2,1,0:T(1,128)}, u32[]{:S(2)}) copy-start(s32[1,1,16]{2,1,0:T(1,128)} %param.12) | copy-start | bytes 196
  24.1 33.2 %collective-permute-start.13 = (bf16[512,1024]{1,0:T(8,128)(2,1)S(1)}, bf16[512,1024]{1,0:T(8,128)(2,1)}, u32[]{:S(2)}, u32[]{:S(2)}) collective-permute-start(bf16[512,1024]{1,0:T(8,128)(2,1)S(1)} %slice.7.refs_9_), channel_id=1, source_target_pairs={{0,8},{8,16},{16,24},{24,28},{28,20},{20,12},{12,4},{4,0},{1,9},{9... | collective-permute-start | bytes 3145736 | tf_op jit(solution)/shard_map/ppermute | solution.py:363
  52.0 5.7 %collective-permute-start.5 = (bf16[2048,256]{1,0:T(8,128)(2,1)S(1)}, bf16[2048,256]{1,0:T(8,128)(2,1)S(1)}, u32[]{:S(2)}, u32[]{:S(2)}) collective-permute-start(bf16[2048,256]{1,0:T(8,128)(2,1)S(1)} %maximum_maximum_fusion), channel_id=1, source_target_pairs={{0,1},{1,0},{2,3},{3,2},{4,5},{5,4},{6,7},{7,6},{8,9},{9,8},{10,11... | collective-permute-start | bytes 3145736 | tf_op jit(solution)/shard_map/ppermute | solution.py:164
  52.1 26.3 %collective-permute-start.11 = (bf16[512,1024]{1,0:T(8,128)(2,1)}, bf16[512,1024]{1,0:T(8,128)(2,1)}, u32[]{:S(2)}, u32[]{:S(2)}) collective-permute-start(bf16[512,1024]{1,0:T(8,128)(2,1)} %collective-permute-done.4.refs_6_), channel_id=1, source_target_pairs={{8,0},{16,8},{24,16},{28,24},{20,28},{12,20},{4,12},{0,4},{9,1},{1... | collective-permute-start | bytes 3145736 | tf_op jit(solution)/shard_map/ppermute | solution.py:365
  53.8 26.3 %collective-permute-start.9 = (bf16[512,1024]{1,0:T(8,128)(2,1)}, bf16[512,1024]{1,0:T(8,128)(2,1)}, u32[]{:S(2)}, u32[]{:S(2)}) collective-permute-start(bf16[512,1024]{1,0:T(8,128)(2,1)} %collective-permute-done.3.refs_5_), channel_id=1, source_target_pairs={{0,8},{8,16},{16,24},{24,28},{28,20},{20,12},{12,4},{4,0},{1,9},{9... | collective-permute-start | bytes 3145736 | tf_op jit(solution)/shard_map/ppermute | solution.py:363
  54.2 46.3 %collective-permute-start.16 = (bf16[512,1024]{1,0:T(8,128)(2,1)}, bf16[512,1024]{1,0:T(8,128)(2,1)}, u32[]{:S(2)}, u32[]{:S(2)}) collective-permute-start(bf16[512,1024]{1,0:T(8,128)(2,1)} %collective-permute-done.2.refs_11_), channel_id=1, source_target_pairs={{8,0},{16,8},{24,16},{28,24},{20,28},{12,20},{4,12},{0,4},{9,1},{1... | collective-permute-start | bytes 3145736 | tf_op jit(solution)/shard_map/ppermute | solution.py:365
  57.3 45.3 %collective-permute-start.14 = (bf16[512,1024]{1,0:T(8,128)(2,1)}, bf16[512,1024]{1,0:T(8,128)(2,1)}, u32[]{:S(2)}, u32[]{:S(2)}) collective-permute-start(bf16[512,1024]{1,0:T(8,128)(2,1)} %collective-permute-done.13.refs_10_), channel_id=1, source_target_pairs={{0,8},{8,16},{16,24},{24,28},{28,20},{20,12},{12,4},{4,0},{1,9},{9... | collective-permute-start | bytes 3145736 | tf_op jit(solution)/shard_map/ppermute | solution.py:363
  57.7 1.0 copy-start.1
  60.5 68.8 %copy-start = (bf16[512,1024]{1,0:T(8,128)(2,1)}, bf16[512,1024]{1,0:T(8,128)(2,1)S(1)}, u32[]{:S(2)}) copy-start(bf16[512,1024]{1,0:T(8,128)(2,1)S(1)} %attend.1.refs_0_) | copy-start | bytes 3145732
  60.5 42.1 %collective-permute-start.6 = (bf16[512,1024]{1,0:T(8,128)(2,1)S(1)}, bf16[512,1024]{1,0:T(8,128)(2,1)S(1)}, u32[]{:S(2)}, u32[]{:S(2)}) collective-permute-start(bf16[512,1024]{1,0:T(8,128)(2,1)S(1)} %attend.1.refs_0_), channel_id=1, source_target_pairs={{0,1},{1,0},{2,3},{3,2},{4,5},{5,4},{6,7},{7,6},{8,9},{9,8},{10,11... | collective-permute-start | bytes 3145736 | tf_op jit(solution)/shard_map/ppermute | solution.py:387
  78.4 25.8 %collective-permute-start.7 = (bf16[512,1024]{1,0:T(8,128)(2,1)S(1)}, bf16[512,1024]{1,0:T(8,128)(2,1)S(1)}, u32[]{:S(2)}, u32[]{:S(2)}) collective-permute-start(bf16[512,1024]{1,0:T(8,128)(2,1)S(1)} %attend.1.refs_0_), channel_id=1, source_target_pairs={{0,2},{1,3},{2,0},{3,1},{4,6},{5,7},{6,4},{7,5},{8,10},{9,11},{10,... | collective-permute-start | bytes 3145736 | tf_op jit(solution)/shard_map/ppermute | solution.py:386
  80.2 44.9 %collective-permute-start.10 = (bf16[512,1024]{1,0:T(8,128)(2,1)}, bf16[512,1024]{1,0:T(8,128)(2,1)}, u32[]{:S(2)}, u32[]{:S(2)}) collective-permute-start(bf16[512,1024]{1,0:T(8,128)(2,1)} %collective-permute-done.9.refs_7_), channel_id=1, source_target_pairs={{0,8},{8,16},{16,24},{24,28},{28,20},{20,12},{12,4},{4,0},{1,9},{9... | collective-permute-start | bytes 3145736 | tf_op jit(solution)/shard_map/ppermute | solution.py:363
  100.5 26.4 %collective-permute-start.17 = (bf16[512,1024]{1,0:T(8,128)(2,1)}, bf16[512,1024]{1,0:T(8,128)(2,1)}, u32[]{:S(2)}, u32[]{:S(2)}) collective-permute-start(bf16[512,1024]{1,0:T(8,128)(2,1)} %collective-permute-done.16.refs_13_), channel_id=1, source_target_pairs={{8,0},{16,8},{24,16},{28,24},{20,28},{12,20},{4,12},{0,4},{9,1},{1... | collective-permute-start | bytes 3145736 | tf_op jit(solution)/shard_map/ppermute | solution.py:365
  102.6 26.7 %collective-permute-start.8 = (bf16[512,1024]{1,0:T(8,128)(2,1)S(1)}, bf16[512,1024]{1,0:T(8,128)(2,1)}, u32[]{:S(2)}, u32[]{:S(2)}) collective-permute-start(bf16[512,1024]{1,0:T(8,128)(2,1)S(1)} %attend.1.refs_0_), channel_id=1, source_target_pairs={{0,3},{1,2},{2,1},{3,0},{4,7},{5,6},{6,5},{7,4},{8,11},{9,10},{10,... | collective-permute-start | bytes 3145736 | tf_op jit(solution)/shard_map/ppermute | solution.py:388
  102.6 22.8 %copy-start.2 = (bf16[512,1024]{1,0:T(8,128)(2,1)}, bf16[512,1024]{1,0:T(8,128)(2,1)S(1)}, u32[]{:S(2)}) copy-start(bf16[512,1024]{1,0:T(8,128)(2,1)S(1)} %collective-permute-done.6.refs_1_) | copy-start | bytes 3145732
  102.6 46.7 %collective-permute-start.12 = (bf16[512,1024]{1,0:T(8,128)(2,1)}, bf16[512,1024]{1,0:T(8,128)(2,1)}, u32[]{:S(2)}, u32[]{:S(2)}) collective-permute-start(bf16[512,1024]{1,0:T(8,128)(2,1)} %collective-permute-done.11.refs_8_), channel_id=1, source_target_pairs={{8,0},{16,8},{24,16},{28,24},{20,28},{12,20},{4,12},{0,4},{9,1},{1... | collective-permute-start | bytes 3145736 | tf_op jit(solution)/shard_map/ppermute | solution.py:365
  104.3 22.6 %copy-start.3 = (bf16[512,1024]{1,0:T(8,128)(2,1)}, bf16[512,1024]{1,0:T(8,128)(2,1)S(1)}, u32[]{:S(2)}) copy-start(bf16[512,1024]{1,0:T(8,128)(2,1)S(1)} %collective-permute-done.7.refs_2_) | copy-start | bytes 3145732
  104.3 45.0 %collective-permute-start.15 = (bf16[512,1024]{1,0:T(8,128)(2,1)}, bf16[512,1024]{1,0:T(8,128)(2,1)}, u32[]{:S(2)}, u32[]{:S(2)}) collective-permute-start(bf16[512,1024]{1,0:T(8,128)(2,1)} %collective-permute-done.14.refs_12_), channel_id=1, source_target_pairs={{0,8},{8,16},{16,24},{24,28},{28,20},{20,12},{12,4},{4,0},{1,9},{9... | collective-permute-start | bytes 3145736 | tf_op jit(solution)/shard_map/ppermute | solution.py:363
  125.1 44.1 %collective-permute-start.19 = (bf16[512,1024]{1,0:T(8,128)(2,1)}, bf16[512,1024]{1,0:T(8,128)(2,1)S(1)}, u32[]{:S(2)}, u32[]{:S(2)}) collective-permute-start(bf16[512,1024]{1,0:T(8,128)(2,1)} %collective-permute-done.10.refs_4_), channel_id=1, source_target_pairs={{0,8},{8,16},{16,24},{24,28},{28,20},{20,12},{12,4},{4,0},{1,9},{9... | collective-permute-start | bytes 3145736 | tf_op jit(solution)/shard_map/ppermute | solution.py:363
  126.8 43.8 %collective-permute-start.18 = (bf16[512,1024]{1,0:T(8,128)(2,1)}, bf16[512,1024]{1,0:T(8,128)(2,1)S(1)}, u32[]{:S(2)}, u32[]{:S(2)}) collective-permute-start(bf16[512,1024]{1,0:T(8,128)(2,1)} %collective-permute-done.17.refs_7_), channel_id=1, source_target_pairs={{8,0},{16,8},{24,16},{28,24},{20,28},{12,20},{4,12},{0,4},{9,1},{1... | collective-permute-start | bytes 3145736 | tf_op jit(solution)/shard_map/ppermute | solution.py:365

commit v16 on v15

--- a/solution.py
+++ b/solution.py
@@ -371,14 +371,8 @@
             if hop < far or part == 1:
                 slabs[part].append((hop, moving[part][1]))
 
-    def gate(value):
-        value, moving[1][1], moving[0][0], moving[0][1] = lax.optimization_barrier(
-            (value, moving[1][1], moving[0][0], moving[0][1])
-        )
-        return value
-
     travel(1)
-    attn = attend_with(inputs, gate)
+    attn = attend_with(inputs)
     keep(1)
     for hop in range(2, far + 1):
         travel(hop)

time: 172 us -> 168 us (0.977)
  waiting for transfers between devices: 118 us -> 95.9 us
  Pallas kernels: 23.1 us -> 40 us
    ppermute x7, waiting for transfers between devices: 63.8 us -> 3.17 us  [travel(): moving[part][1] = lax.ppermute(moving[part][1], 'pb', backward)]
    ppermute x7, waiting for transfers between devices: 34.1 us -> 71.1 us  [travel(): moving[part][0] = lax.ppermute(moving[part][0], 'pb', forward)]
    pallas_call x1, Pallas kernels: 1.85 us -> 18.7 us  [attend(): pl.pallas_call(functools.partial(attention_kernel, heads, slots, part_row...]
    ppermute x7, starting transfers between devices: 13.3 us -> 2.56 us  [travel(): moving[part][1] = lax.ppermute(moving[part][1], 'pb', backward)]
    ppermute x7, starting transfers between devices: 3.34 us -> 14 us  [travel(): moving[part][0] = lax.ppermute(moving[part][0], 'pb', forward)]
    ppermute x1, waiting for transfers between devices: 0.01 us -> 2.12 us  [project_ring(): across = lax.ppermute(attn, 'ka', [(i, i ^ 2) for i in range(4)])]
  transfers between devices with their start and end apart: 20 -> 20, of which waited for: 11 -> 10; matrix products, arithmetic and copies ran while one was open for 3% -> 5% of each run, Pallas kernels for 13% -> 23%
where the time goes in v16:
time: 168 us
  waiting for transfers between devices  95.9 us (57%)
  Pallas kernels  40 us (24%)
  starting transfers between devices  20.2 us (12%)
  local copies, waits for them, and re-layouts  9.42 us (6%)
    ppermute x7, waiting for transfers between devices, travel(): moving[part][0] = lax.ppermute(moving[part][0], 'pb', forward)  71.1 us
    ppermute x2, waiting for transfers between devices, own_head_keys_values(): lax.ppermute(heads_of(a, 1 - x), 'ka', [(i, i ^ 2) for i in range(4)])  19.5 us
    pallas_call x1, Pallas kernels, attend(): pl.pallas_call(functools.partial(attention_kernel, heads, slots, part_row...  18.7 us
    pallas_call x2, Pallas kernels, ring_product(): pl.pallas_call(functools.partial(ring_product_kernel, steps, spare_step),...  18.4 us
    ppermute x7, starting transfers between devices, travel(): moving[part][0] = lax.ppermute(moving[part][0], 'pb', forward)  14 us
  transfers between devices with their start and end apart: 20, of which 10 were waited for; matrix products, arithmetic and copies ran while one was open for 5% of the time, Pallas kernels for 23%

profile of v16, /device:TPU:0, one launch (start us, length us, event | category | flops | bytes accessed | tf_op | source)
XLA Modules:
  0.0 168.2 jit_solution(14319942835233814965)
XLA Ops:
  0.0 1.4 slice.6.refs_4_
  2.0 3.1 %collective-permute-start.12 = (bf16[512,1024]{1,0:T(8,128)(2,1)S(1)}, bf16[512,1024]{1,0:T(8,128)(2,1)}, u32[]{:S(2)}, u32[]{:S(2)}) collective-permute-start(bf16[512,1024]{1,0:T(8,128)(2,1)S(1)} %slice.7.refs_9_), channel_id=1, source_target_pairs={{0,8},{8,16},{16,24},{24,28},{28,20},{20,12},{12,4},{4,0},{1,9},{9... | collective-permute-start | bytes 3145736 | tf_op jit(solution)/shard_map/ppermute | solution.py:363
  5.1 2.0 %collective-permute-start.6 = (bf16[512,1024]{1,0:T(8,128)(2,1)S(1)}, bf16[512,1024]{1,0:T(8,128)(2,1)}, u32[]{:S(2)}, u32[]{:S(2)}) collective-permute-start(bf16[512,1024]{1,0:T(8,128)(2,1)S(1)} %slice.6.refs_4_), channel_id=1, source_target_pairs={{0,8},{8,16},{16,24},{24,28},{28,20},{20,12},{12,4},{4,0},{1,9},{9... | collective-permute-start | bytes 3145736 | tf_op jit(solution)/shard_map/ppermute | solution.py:363
  7.1 1.9 %constant_dynamic-slice_fusion.4 = bf16[1024,256]{1,0:T(8,128)(2,1)} fusion(bf16[1024,512]{1,0:T(8,128)(2,1)} %refs_1_, s32[]{:T(128)S(6)} %select_n.29), kind=kLoop, calls=%fused_computation.5 | loop fusion | bytes 1048580 | tf_op jit(solution)/shard_map/dynamic_slice | solution.py:154
  9.0 1.5 collective-permute-start.1
  11.9 1.0 constant_dynamic-slice_fusion.2
  12.9 11.3 %collective-permute-done.1.refs_3_ = bf16[1024,256]{1,0:T(8,128)(2,1)} collective-permute-done((bf16[1024,256]{1,0:T(8,128)(2,1)}, bf16[1024,256]{1,0:T(8,128)(2,1)}, u32[]{:S(2)}, u32[]{:S(2)}) %collective-permute-start.1) | collective-permute-done | bytes 524320 | tf_op jit(solution)/shard_map/ppermute | solution.py:160
  24.2 1.0 constant_dynamic-slice_fusion
  25.2 8.2 %collective-permute-done.refs_2_ = bf16[1024,256]{1,0:T(8,128)(2,1)} collective-permute-done((bf16[1024,256]{1,0:T(8,128)(2,1)}, bf16[1024,256]{1,0:T(8,128)(2,1)}, u32[]{:S(2)}, u32[]{:S(2)}) %collective-permute-start) | collective-permute-done | bytes 524320 | tf_op jit(solution)/shard_map/ppermute | solution.py:160
  33.4 1.0 constant_dynamic-slice_fusion.1
  34.3 1.1 maximum_maximum_fusion
  35.4 1.6 collective-permute-start.13
  37.0 14.6 %collective-permute-done.6.refs_5_ = bf16[512,1024]{1,0:T(8,128)(2,1)} collective-permute-done((bf16[512,1024]{1,0:T(8,128)(2,1)S(1)}, bf16[512,1024]{1,0:T(8,128)(2,1)}, u32[]{:S(2)}, u32[]{:S(2)}) %collective-permute-start.6) | collective-permute-done | bytes 1048608 | tf_op jit(solution)/shard_map/ppermute | solution.py:363
  51.6 2.1 %collective-permute-start.7 = (bf16[512,1024]{1,0:T(8,128)(2,1)}, bf16[512,1024]{1,0:T(8,128)(2,1)}, u32[]{:S(2)}, u32[]{:S(2)}) collective-permute-start(bf16[512,1024]{1,0:T(8,128)(2,1)} %collective-permute-done.6.refs_5_), channel_id=1, source_target_pairs={{0,8},{8,16},{16,24},{24,28},{28,20},{20,12},{12,4},{4,0},{1,9},{9... | collective-permute-start | bytes 3145736 | tf_op jit(solution)/shard_map/ppermute | solution.py:363
  55.1 2.0 %collective-permute-start.10 = (bf16[512,1024]{1,0:T(8,128)(2,1)}, bf16[512,1024]{1,0:T(8,128)(2,1)}, u32[]{:S(2)}, u32[]{:S(2)}) collective-permute-start(bf16[512,1024]{1,0:T(8,128)(2,1)} %collective-permute-done.9.refs_6_), channel_id=1, source_target_pairs={{8,0},{16,8},{24,16},{28,24},{20,28},{12,20},{4,12},{0,4},{9,1},{1... | collective-permute-start | bytes 3145736 | tf_op jit(solution)/shard_map/ppermute | solution.py:365
  57.2 1.0 copy-done.1
  58.1 18.7 %attend.1.refs_0_ = bf16[512,1024]{1,0:T(8,128)(2,1)S(1)} custom-call(s32[34]{0:T(128)S(1)} %concatenate.16.meta_ref, bf16[512,1024]{1,0:T(8,128)(2,1)} %bitcast.15, bf16[512,1024]{1,0:T(8,128)(2,1)} %bitcast.16, bf16[1024,512]{1,0:T(8,128)(2,1)} %refs_0_, bf16[1024,512]{1,0:T(8,128)(2,1)} %refs_1_, bf16[1024,256]{1,0:T(8,128)(2,1)} %collective-permute-done.refs_2_, ...), custom_call_target="tpu_custom_call" | custom-call | flops 1048576 | bytes 1048576 | tf_op jit(solution)/shard_map/attend/pallas_call | solution.py:118
  76.9 1.6 collective-permute-start.4
  78.5 17.2 %collective-permute-done.7.refs_7_ = bf16[512,1024]{1,0:T(8,128)(2,1)} collective-permute-done((bf16[512,1024]{1,0:T(8,128)(2,1)}, bf16[512,1024]{1,0:T(8,128)(2,1)}, u32[]{:S(2)}, u32[]{:S(2)}) %collective-permute-start.7) | collective-permute-done | bytes 1048608 | tf_op jit(solution)/shard_map/ppermute | solution.py:363
  95.7 1.8 %collective-permute-start.8 = (bf16[512,1024]{1,0:T(8,128)(2,1)}, bf16[512,1024]{1,0:T(8,128)(2,1)}, u32[]{:S(2)}, u32[]{:S(2)}) collective-permute-start(bf16[512,1024]{1,0:T(8,128)(2,1)} %collective-permute-done.7.refs_7_), channel_id=1, source_target_pairs={{0,8},{8,16},{16,24},{24,28},{28,20},{20,12},{12,4},{4,0},{1,9},{9... | collective-permute-start | bytes 3145736 | tf_op jit(solution)/shard_map/ppermute | solution.py:363
  97.7 1.4 collective-permute-done.10.refs_8_
  99.1 1.6 collective-permute-start.14
  100.7 2.1 %collective-permute-done.4.refs_2_ = bf16[512,1024]{1,0:T(8,128)(2,1)S(1)} collective-permute-done((bf16[512,1024]{1,0:T(8,128)(2,1)S(1)}, bf16[512,1024]{1,0:T(8,128)(2,1)S(1)}, u32[]{:S(2)}, u32[]{:S(2)}) %collective-permute-start.4) | collective-permute-done | bytes 1048608 | tf_op jit(solution)/shard_map/ppermute | solution.py:380
  102.9 19.3 %collective-permute-done.8.refs_4_ = bf16[512,1024]{1,0:T(8,128)(2,1)} collective-permute-done((bf16[512,1024]{1,0:T(8,128)(2,1)}, bf16[512,1024]{1,0:T(8,128)(2,1)}, u32[]{:S(2)}, u32[]{:S(2)}) %collective-permute-start.8) | collective-permute-done | bytes 1048608 | tf_op jit(solution)/shard_map/ppermute | solution.py:363
  122.1 1.8 %collective-permute-start.19 = (bf16[512,1024]{1,0:T(8,128)(2,1)}, bf16[512,1024]{1,0:T(8,128)(2,1)S(1)}, u32[]{:S(2)}, u32[]{:S(2)}) collective-permute-start(bf16[512,1024]{1,0:T(8,128)(2,1)} %collective-permute-done.8.refs_4_), channel_id=1, source_target_pairs={{0,8},{8,16},{16,24},{24,28},{28,20},{20,12},{12,4},{4,0},{1,9},{9... | collective-permute-start | bytes 3145736 | tf_op jit(solution)/shard_map/ppermute | solution.py:363
  125.0 11.7 %ring_product.2.refs_8_ = f32[512,2048]{1,0:T(8,128)S(1)} custom-call(s32[9]{0:T(128)S(1)} %pad_add_fusion.where_ref, bf16[512,1024]{1,0:T(8,128)(2,1)} %copy-done, bf16[512,1024]{1,0:T(8,128)(2,1)} %copy-done.2, bf16[512,1024]{1,0:T(8,128)(2,1)} %copy-done.3, bf16[512,1024]{1,0:T(8,128)(2,1)} %collective-permute-done.5.refs_3_, ...), custom_call_target="tpu_custom_call" | custom-call | flops 1048576 | bytes 1048576 | tf_op jit(solution)/shard_map/ring_product/pallas_call | solution.py:285
  136.7 7.9 %collective-permute-done.14.refs_6_ = bf16[512,1024]{1,0:T(8,128)(2,1)} collective-permute-done((bf16[512,1024]{1,0:T(8,128)(2,1)}, bf16[512,1024]{1,0:T(8,128)(2,1)}, u32[]{:S(2)}, u32[]{:S(2)}) %collective-permute-start.14) | collective-permute-done | bytes 1048608 | tf_op jit(solution)/shard_map/ppermute | solution.py:363
  144.6 1.8 %collective-permute-done.11.refs_5_ = bf16[512,1024]{1,0:T(8,128)(2,1)} collective-permute-done((bf16[512,1024]{1,0:T(8,128)(2,1)}, bf16[512,1024]{1,0:T(8,128)(2,1)}, u32[]{:S(2)}, u32[]{:S(2)}) %collective-permute-start.11) | collective-permute-done | bytes 1048608 | tf_op jit(solution)/shard_map/ppermute | solution.py:365
  146.4 6.6 %ring_product.3 = (f32[512,2048]{1,0:T(8,128)S(1)}, bf16[512,512]{1,0:T(8,128)(2,1)S(1)}) custom-call(s32[9]{0:T(128)S(1)} %pad_add_fusion.where_ref, bf16[512,1024]{1,0:T(8,128)(2,1)} %copy-done, bf16[512,1024]{1,0:T(8,128)(2,1)} %copy-done.2, bf16[512,1024]{1,0:T(8,128)(2,1)} %copy-done.3, bf16[512,1024]{1,0:T(8,128)(2,1)} %collective-permute-done.5.refs_3_, ...), custom_call_target="tpu_custom_call" | custom-call | flops 1048576 | bytes 1048576 | tf_op jit(solution)/shard_map/ring_product/pallas_call | solution.py:285
  153.0 12.2 %collective-permute-done.19.slab_ref = bf16[512,1024]{1,0:T(8,128)(2,1)S(1)} collective-permute-done((bf16[512,1024]{1,0:T(8,128)(2,1)}, bf16[512,1024]{1,0:T(8,128)(2,1)S(1)}, u32[]{:S(2)}, u32[]{:S(2)}) %collective-permute-start.19) | collective-permute-done | bytes 1048608 | tf_op jit(solution)/shard_map/ppermute | solution.py:363
  165.2 1.5 last_product.2.refs_0_
  166.7 1.5 last_product.3
  (42 shorter events, 3.4 us)
Async XLA Ops:
  0.0 1.9 %copy-start.7 = (bf16[512,2048]{1,0:T(8,128)(2,1)S(1)}, bf16[512,2048]{1,0:T(8,128)(2,1)}, u32[]{:S(2)}) copy-start(bf16[512,2048]{1,0:T(8,128)(2,1)} %param.16) | copy-start | bytes 6291460
  1.9 22.3 %copy-start.4 = (bf16[512,1024]{1,0:T(8,128)(2,1)}, bf16[512,1024]{1,0:T(8,128)(2,1)S(1)}, u32[]{:S(2)}) copy-start(bf16[512,1024]{1,0:T(8,128)(2,1)S(1)} %slice.6.refs_4_) | copy-start | bytes 3145732
  1.9 8.6 %copy-start.6 = (bf16[1024,512]{1,0:T(8,128)(2,1)S(1)}, bf16[1024,512]{1,0:T(8,128)(2,1)}, u32[]{:S(2)}) copy-start(bf16[1024,512]{1,0:T(8,128)(2,1)} %refs_0_) | copy-start | bytes 3145732
  2.0 32.3 %copy-start.5 = (bf16[512,1024]{1,0:T(8,128)(2,1)}, bf16[512,1024]{1,0:T(8,128)(2,1)S(1)}, u32[]{:S(2)}) copy-start(bf16[512,1024]{1,0:T(8,128)(2,1)S(1)} %slice.7.refs_9_) | copy-start | bytes 3145732
  2.0 33.4 %collective-permute-start.12 = (bf16[512,1024]{1,0:T(8,128)(2,1)S(1)}, bf16[512,1024]{1,0:T(8,128)(2,1)}, u32[]{:S(2)}, u32[]{:S(2)}) collective-permute-start(bf16[512,1024]{1,0:T(8,128)(2,1)S(1)} %slice.7.refs_9_), channel_id=1, source_target_pairs={{0,8},{8,16},{16,24},{24,28},{28,20},{20,12},{12,4},{4,0},{1,9},{9... | collective-permute-start | bytes 3145736 | tf_op jit(solution)/shard_map/ppermute | solution.py:363
  5.1 48.6 %collective-permute-start.15 = (bf16[512,1024]{1,0:T(8,128)(2,1)S(1)}, bf16[512,1024]{1,0:T(8,128)(2,1)}, u32[]{:S(2)}, u32[]{:S(2)}) collective-permute-start(bf16[512,1024]{1,0:T(8,128)(2,1)S(1)} %slice.7.refs_9_), channel_id=1, source_target_pairs={{8,0},{16,8},{24,16},{28,24},{20,28},{12,20},{4,12},{0,4},{9,1},{1... | collective-permute-start | bytes 3145736 | tf_op jit(solution)/shard_map/ppermute | solution.py:365
  5.1 46.5 %collective-permute-start.6 = (bf16[512,1024]{1,0:T(8,128)(2,1)S(1)}, bf16[512,1024]{1,0:T(8,128)(2,1)}, u32[]{:S(2)}, u32[]{:S(2)}) collective-permute-start(bf16[512,1024]{1,0:T(8,128)(2,1)S(1)} %slice.6.refs_4_), channel_id=1, source_target_pairs={{0,8},{8,16},{16,24},{24,28},{28,20},{20,12},{12,4},{4,0},{1,9},{9... | collective-permute-start | bytes 3145736 | tf_op jit(solution)/shard_map/ppermute | solution.py:363
  9.0 15.2 %collective-permute-start.1 = (bf16[1024,256]{1,0:T(8,128)(2,1)}, bf16[1024,256]{1,0:T(8,128)(2,1)}, u32[]{:S(2)}, u32[]{:S(2)}) collective-permute-start(bf16[1024,256]{1,0:T(8,128)(2,1)} %constant_dynamic-slice_fusion.4), channel_id=1, source_target_pairs={{0,2},{1,3},{2,0},{3,1},{4,6},{5,7},{6,4},{7,5},{8,10},{9,11},{10,... | collective-permute-start | bytes 1572872 | tf_op jit(solution)/shard_map/ppermute | solution.py:160
  11.3 22.1 %collective-permute-start = (bf16[1024,256]{1,0:T(8,128)(2,1)}, bf16[1024,256]{1,0:T(8,128)(2,1)}, u32[]{:S(2)}, u32[]{:S(2)}) collective-permute-start(bf16[1024,256]{1,0:T(8,128)(2,1)} %constant_dynamic-slice_fusion.5), channel_id=1, source_target_pairs={{0,2},{1,3},{2,0},{3,1},{4,6},{5,7},{6,4},{7,5},{8,10},{9,11},{10,... | collective-permute-start | bytes 1572872 | tf_op jit(solution)/shard_map/ppermute | solution.py:160
  11.9 43.2 %copy-start.8 = (s32[1,1,16]{2,1,0:T(1,128)S(1)}, s32[1,1,16]{2,1,0:T(1,128)}, u32[]{:S(2)}) copy-start(s32[1,1,16]{2,1,0:T(1,128)} %param.12) | copy-start | bytes 196
  24.2 31.0 %collective-permute-start.9 = (bf16[512,1024]{1,0:T(8,128)(2,1)S(1)}, bf16[512,1024]{1,0:T(8,128)(2,1)}, u32[]{:S(2)}, u32[]{:S(2)}) collective-permute-start(bf16[512,1024]{1,0:T(8,128)(2,1)S(1)} %slice.6.refs_4_), channel_id=1, source_target_pairs={{8,0},{16,8},{24,16},{28,24},{20,28},{12,20},{4,12},{0,4},{9,1},{1... | collective-permute-start | bytes 3145736 | tf_op jit(solution)/shard_map/ppermute | solution.py:365
  35.4 21.7 %collective-permute-start.2 = (bf16[2048,256]{1,0:T(8,128)(2,1)}, bf16[2048,256]{1,0:T(8,128)(2,1)S(1)}, u32[]{:S(2)}, u32[]{:S(2)}) collective-permute-start(bf16[2048,256]{1,0:T(8,128)(2,1)} %maximum_maximum_fusion), channel_id=1, source_target_pairs={{0,1},{1,0},{2,3},{3,2},{4,5},{5,4},{6,7},{7,6},{8,9},{9,8},{10,11... | collective-permute-start | bytes 3145736 | tf_op jit(solution)/shard_map/ppermute | solution.py:164
  35.4 41.5 %collective-permute-start.13 = (bf16[512,1024]{1,0:T(8,128)(2,1)}, bf16[512,1024]{1,0:T(8,128)(2,1)}, u32[]{:S(2)}, u32[]{:S(2)}) collective-permute-start(bf16[512,1024]{1,0:T(8,128)(2,1)} %collective-permute-done.12.refs_10_), channel_id=1, source_target_pairs={{0,8},{8,16},{16,24},{24,28},{28,20},{20,12},{12,4},{4,0},{1,9},{9... | collective-permute-start | bytes 3145736 | tf_op jit(solution)/shard_map/ppermute | solution.py:363
  51.6 44.1 %collective-permute-start.7 = (bf16[512,1024]{1,0:T(8,128)(2,1)}, bf16[512,1024]{1,0:T(8,128)(2,1)}, u32[]{:S(2)}, u32[]{:S(2)}) collective-permute-start(bf16[512,1024]{1,0:T(8,128)(2,1)} %collective-permute-done.6.refs_5_), channel_id=1, source_target_pairs={{0,8},{8,16},{16,24},{24,28},{28,20},{20,12},{12,4},{4,0},{1,9},{9... | collective-permute-start | bytes 3145736 | tf_op jit(solution)/shard_map/ppermute | solution.py:363
  53.7 43.8 %collective-permute-start.16 = (bf16[512,1024]{1,0:T(8,128)(2,1)}, bf16[512,1024]{1,0:T(8,128)(2,1)}, u32[]{:S(2)}, u32[]{:S(2)}) collective-permute-start(bf16[512,1024]{1,0:T(8,128)(2,1)} %collective-permute-done.15.refs_11_), channel_id=1, source_target_pairs={{8,0},{16,8},{24,16},{28,24},{20,28},{12,20},{4,12},{0,4},{9,1},{1... | collective-permute-start | bytes 3145736 | tf_op jit(solution)/shard_map/ppermute | solution.py:365
  55.1 44.0 %collective-permute-start.10 = (bf16[512,1024]{1,0:T(8,128)(2,1)}, bf16[512,1024]{1,0:T(8,128)(2,1)}, u32[]{:S(2)}, u32[]{:S(2)}) collective-permute-start(bf16[512,1024]{1,0:T(8,128)(2,1)} %collective-permute-done.9.refs_6_), channel_id=1, source_target_pairs={{8,0},{16,8},{24,16},{28,24},{20,28},{12,20},{4,12},{0,4},{9,1},{1... | collective-permute-start | bytes 3145736 | tf_op jit(solution)/shard_map/ppermute | solution.py:365
  57.2 1.0 copy-start.1
  76.8 48.1 %copy-start = (bf16[512,1024]{1,0:T(8,128)(2,1)}, bf16[512,1024]{1,0:T(8,128)(2,1)S(1)}, u32[]{:S(2)}) copy-start(bf16[512,1024]{1,0:T(8,128)(2,1)S(1)} %attend.1.refs_0_) | copy-start | bytes 3145732
  76.9 22.3 %collective-permute-start.3 = (bf16[512,1024]{1,0:T(8,128)(2,1)S(1)}, bf16[512,1024]{1,0:T(8,128)(2,1)S(1)}, u32[]{:S(2)}, u32[]{:S(2)}) collective-permute-start(bf16[512,1024]{1,0:T(8,128)(2,1)S(1)} %attend.1.refs_0_), channel_id=1, source_target_pairs={{0,1},{1,0},{2,3},{3,2},{4,5},{5,4},{6,7},{7,6},{8,9},{9,8},{10,11... | collective-permute-start | bytes 3145736 | tf_op jit(solution)/shard_map/ppermute | solution.py:381
  76.9 25.9 %collective-permute-start.4 = (bf16[512,1024]{1,0:T(8,128)(2,1)S(1)}, bf16[512,1024]{1,0:T(8,128)(2,1)S(1)}, u32[]{:S(2)}, u32[]{:S(2)}) collective-permute-start(bf16[512,1024]{1,0:T(8,128)(2,1)S(1)} %attend.1.refs_0_), channel_id=1, source_target_pairs={{0,2},{1,3},{2,0},{3,1},{4,6},{5,7},{6,4},{7,5},{8,10},{9,11},{10,... | collective-permute-start | bytes 3145736 | tf_op jit(solution)/shard_map/ppermute | solution.py:380
  95.7 26.4 %collective-permute-start.8 = (bf16[512,1024]{1,0:T(8,128)(2,1)}, bf16[512,1024]{1,0:T(8,128)(2,1)}, u32[]{:S(2)}, u32[]{:S(2)}) collective-permute-start(bf16[512,1024]{1,0:T(8,128)(2,1)} %collective-permute-done.7.refs_7_), channel_id=1, source_target_pairs={{0,8},{8,16},{16,24},{24,28},{28,20},{20,12},{12,4},{4,0},{1,9},{9... | collective-permute-start | bytes 3145736 | tf_op jit(solution)/shard_map/ppermute | solution.py:363
  97.5 26.4 %collective-permute-start.17 = (bf16[512,1024]{1,0:T(8,128)(2,1)}, bf16[512,1024]{1,0:T(8,128)(2,1)}, u32[]{:S(2)}, u32[]{:S(2)}) collective-permute-start(bf16[512,1024]{1,0:T(8,128)(2,1)} %collective-permute-done.16.refs_13_), channel_id=1, source_target_pairs={{8,0},{16,8},{24,16},{28,24},{20,28},{12,20},{4,12},{0,4},{9,1},{1... | collective-permute-start | bytes 3145736 | tf_op jit(solution)/shard_map/ppermute | solution.py:365
  99.1 25.9 %collective-permute-start.5 = (bf16[512,1024]{1,0:T(8,128)(2,1)S(1)}, bf16[512,1024]{1,0:T(8,128)(2,1)}, u32[]{:S(2)}, u32[]{:S(2)}) collective-permute-start(bf16[512,1024]{1,0:T(8,128)(2,1)S(1)} %attend.1.refs_0_), channel_id=1, source_target_pairs={{0,3},{1,2},{2,1},{3,0},{4,7},{5,6},{6,5},{7,4},{8,11},{9,10},{10,... | collective-permute-start | bytes 3145736 | tf_op jit(solution)/shard_map/ppermute | solution.py:382
  99.1 24.8 %copy-start.2 = (bf16[512,1024]{1,0:T(8,128)(2,1)}, bf16[512,1024]{1,0:T(8,128)(2,1)S(1)}, u32[]{:S(2)}) copy-start(bf16[512,1024]{1,0:T(8,128)(2,1)S(1)} %collective-permute-done.3.refs_1_) | copy-start | bytes 3145732
  99.1 45.5 %collective-permute-start.14 = (bf16[512,1024]{1,0:T(8,128)(2,1)}, bf16[512,1024]{1,0:T(8,128)(2,1)}, u32[]{:S(2)}, u32[]{:S(2)}) collective-permute-start(bf16[512,1024]{1,0:T(8,128)(2,1)} %collective-permute-done.13.refs_12_), channel_id=1, source_target_pairs={{0,8},{8,16},{16,24},{24,28},{28,20},{20,12},{12,4},{4,0},{1,9},{9... | collective-permute-start | bytes 3145736 | tf_op jit(solution)/shard_map/ppermute | solution.py:363
  102.9 21.1 %copy-start.3 = (bf16[512,1024]{1,0:T(8,128)(2,1)}, bf16[512,1024]{1,0:T(8,128)(2,1)S(1)}, u32[]{:S(2)}) copy-start(bf16[512,1024]{1,0:T(8,128)(2,1)S(1)} %collective-permute-done.4.refs_2_) | copy-start | bytes 3145732
  102.9 43.5 %collective-permute-start.11 = (bf16[512,1024]{1,0:T(8,128)(2,1)}, bf16[512,1024]{1,0:T(8,128)(2,1)}, u32[]{:S(2)}, u32[]{:S(2)}) collective-permute-start(bf16[512,1024]{1,0:T(8,128)(2,1)} %collective-permute-done.10.refs_8_), channel_id=1, source_target_pairs={{8,0},{16,8},{24,16},{28,24},{20,28},{12,20},{4,12},{0,4},{9,1},{1... | collective-permute-start | bytes 3145736 | tf_op jit(solution)/shard_map/ppermute | solution.py:365
  122.1 43.1 %collective-permute-start.19 = (bf16[512,1024]{1,0:T(8,128)(2,1)}, bf16[512,1024]{1,0:T(8,128)(2,1)S(1)}, u32[]{:S(2)}, u32[]{:S(2)}) collective-permute-start(bf16[512,1024]{1,0:T(8,128)(2,1)} %collective-permute-done.8.refs_4_), channel_id=1, source_target_pairs={{0,8},{8,16},{16,24},{24,28},{28,20},{20,12},{12,4},{4,0},{1,9},{9... | collective-permute-start | bytes 3145736 | tf_op jit(solution)/shard_map/ppermute | solution.py:363
  123.9 42.8 %collective-permute-start.18 = (bf16[512,1024]{1,0:T(8,128)(2,1)}, bf16[512,1024]{1,0:T(8,128)(2,1)S(1)}, u32[]{:S(2)}, u32[]{:S(2)}) collective-permute-start(bf16[512,1024]{1,0:T(8,128)(2,1)} %collective-permute-done.17.refs_7_), channel_id=1, source_target_pairs={{8,0},{16,8},{24,16},{28,24},{20,28},{12,20},{4,12},{0,4},{9,1},{1... | collective-permute-start | bytes 3145736 | tf_op jit(solution)/shard_map/ppermute | solution.py:365
